TPU v7x, 32 devices: a whole 2x2x4 slice. The times are simulated.
32 devices in a mesh: dp: 8 (over y, x, core), mp: 4 (over z).
Axes of the slice: x: 2, y: 2, z: 4, core: 2. Of those that a mesh axis runs over, the one named last changes fastest.
Arguments:
- hidden: bfloat16 [4096, 768], P('dp'), may hold values from -6 to 6
- memory: bfloat16 [32768, 768], P('dp', 'mp'), may hold values from -6 to 6
- out_grad: bfloat16 [4096, 768], P('dp'), may hold values from -6 to 6
- dec_starts: int32 [32, 4], P('dp'), may hold values from 0 to 127, as said below
- dec_length: int32 [32], P('dp'), may hold values from 96 to 128
- mem_starts: int32 [32, 4], P('dp'), may hold values from 0 to 1023, as said below
- mem_length: int32 [32], P('dp'), may hold values from 768 to 1024
- self_qkv: bfloat16 [3, 768, 768], P(None, None, 'mp'), may hold values from -0.25 to 0.25
- self_qv_bias: float32 [2, 768], P(None, 'mp'), may hold values from -3 to 3
- self_proj: bfloat16 [768, 768], P('mp'), may hold values from -0.3125 to 0.3125
- cross_query: bfloat16 [768, 768], P(None, 'mp'), may hold values from -0.25 to 0.25
- cross_kv: bfloat16 [2, 768, 768], P(None, None, 'mp'), may hold values from -0.25 to 0.25
- cross_qv_bias: float32 [2, 768], P(None, 'mp'), may hold values from -3 to 3
- cross_proj: bfloat16 [768, 768], P('mp'), may hold values from -0.875 to 0.875
- ffn_in: bfloat16 [768, 3072], P(None, 'mp'), may hold values from -0.21875 to 0.21875
- ffn_in_bias: float32 [3072], P('mp'), may hold values from -3 to 3
- ffn_out: bfloat16 [3072, 768], P('mp'), may hold values from -0.15625 to 0.15625
- out_biases: float32 [3, 768], replicated, may hold values from -3 to 3
- norm_gains: float32 [3, 768], replicated, may hold values from 0.25 to 1.75
- norm_biases: float32 [3, 768], replicated, may hold values from -2 to 2
Outputs:
- result: bfloat16 [4096, 768], P('dp')
- hidden_grad: float32 [4096, 768], P('dp')
- memory_grad: float32 [32768, 768], P('dp', 'mp')
- self_qkv_grad: float32 [3, 768, 768], P(None, None, 'mp')
- self_qv_bias_grad: float32 [2, 768], P(None, 'mp')
- self_proj_grad: float32 [768, 768], P('mp')
- cross_query_grad: float32 [768, 768], P(None, 'mp')
- cross_kv_grad: float32 [2, 768, 768], P(None, None, 'mp')
- cross_qv_bias_grad: float32 [2, 768], P(None, 'mp')
- cross_proj_grad: float32 [768, 768], P('mp')
- ffn_in_grad: float32 [768, 3072], P(None, 'mp')
- ffn_in_bias_grad: float32 [3072], P('mp')
- ffn_out_grad: float32 [3072, 768], P('mp')
- out_biases_grad: float32 [3, 768], replicated
- norm_gains_grad: float32 [3, 768], replicated
- norm_biases_grad: float32 [3, 768], replicated
Inputs may be any that keep to these rules, and one draw needn't show every extreme that they name: `dec_starts`: each packed row holds 4 pairs; its offsets start at 0, rise strictly and stay below the row's used slots, so every decoder segment holds at least one used slot; padded slots belong to the last pair. `mem_starts`: pair j's table is memory segment j of the same packed row; offsets start at 0, rise strictly and stay below the row's used slots, so every memory segment holds at least one used slot.
All inputs are finite; a program needn't handle non-finite values.
Results may differ from a plain program's by a relative error of at most 0.023.
Values may be sent and summed in bfloat16 or wider, within the bound.
No kernel may reach another device: no remote copies, remote signals or barrier semaphores. Data moves between devices by JAX's collectives and lax.ppermute only.
A program may use at most 128 MiB of HBM per device.

v0:
```python
import jax
import jax.numpy as jnp
from jax import lax
from jax.sharding import PartitionSpec as P

HD = 64


NEG_FILL = -1000000000.0
EPSILON = 1e-05


def layer_norm(values, gain_row, bias_row):
    average = jnp.mean(values, -1, keepdims=True)
    centered = values - average
    variance = jnp.mean(centered * centered, -1, keepdims=True)
    return centered * lax.rsqrt(variance + EPSILON) * gain_row + bias_row


def exact_gelu(values):
    return jax.nn.gelu(values, approximate=False)


def segment_ids(starts, slot_count):
    places = jnp.arange(slot_count, dtype=jnp.int32)
    return jnp.sum((starts[:, None, :] <= places[None, :, None]).astype(jnp.int32), -1) - 1


def inner_dot(left_side, right_side):
    return lax.dot_general(
        left_side, right_side, (((0,), (0,)), ((), ())), preferred_element_type=jnp.float32
    )


def outer_dot(left_side, right_side):
    return lax.dot_general(
        left_side, right_side, (((1,), (1,)), ((), ())), preferred_element_type=jnp.float32
    )


def row_groups(kernel, arrays):
    row_count = arrays[0].shape[0]
    limit = max(1, 512 // arrays[0].shape[1])
    group_rows = max(
        (count for count in range(1, min(row_count, limit) + 1) if row_count % count == 0)
    )
    blocks = row_count // group_rows
    shaped = tuple((member.reshape((blocks, group_rows) + member.shape[1:]) for member in arrays))
    results = lax.map(lambda pieces: kernel(*pieces), shaped)
    return jax.tree.map(lambda member: member.reshape((row_count,) + member.shape[2:]), results)


def attend_block(queries, key_rows, value_rows, allowed):
    scores = jnp.einsum("rqhd,rkhd->rhqk", queries, key_rows, preferred_element_type=jnp.float32)
    scores = jnp.where(allowed[:, None], scores, NEG_FILL)
    peak_score = jnp.max(scores, -1, keepdims=True)
    weights = jnp.exp(scores - peak_score)
    totals = jnp.sum(weights, -1, keepdims=True)
    prob_low = (weights / totals).astype(jnp.bfloat16)
    output = jnp.einsum("rhqk,rkhd->rqhd", prob_low, value_rows, preferred_element_type=jnp.float32)
    return (output, (peak_score + jnp.log(totals))[..., 0])


def attend_back(queries, key_rows, value_rows, allowed, log_total, grad_rows):
    scores = jnp.einsum("rqhd,rkhd->rhqk", queries, key_rows, preferred_element_type=jnp.float32)
    scores = jnp.where(allowed[:, None], scores, NEG_FILL)
    prob_full = jnp.exp(scores - log_total[..., None])
    prob_low = prob_full.astype(jnp.bfloat16)
    value_grad = jnp.einsum(
        "rhqk,rqhd->rkhd", prob_low, grad_rows, preferred_element_type=jnp.float32
    )
    prob_grad = jnp.einsum(
        "rqhd,rkhd->rhqk", grad_rows, value_rows, preferred_element_type=jnp.float32
    )
    offset = jnp.sum(prob_full * prob_grad, -1, keepdims=True)
    score_grad = (prob_full * (prob_grad - offset)).astype(jnp.bfloat16)
    query_grad = jnp.einsum(
        "rhqk,rkhd->rqhd", score_grad, key_rows, preferred_element_type=jnp.float32
    )
    key_grad = jnp.einsum(
        "rhqk,rqhd->rkhd", score_grad, queries, preferred_element_type=jnp.float32
    )
    return (query_grad, key_grad, value_grad)


def body(
    hidden,
    memory,
    out_grad,
    dec_starts,
    dec_length,
    mem_starts,
    mem_length,
    self_qkv,
    self_qv_bias,
    self_proj,
    cross_query,
    cross_kv,
    cross_qv_bias,
    cross_proj,
    ffn_in,
    ffn_in_bias,
    ffn_out,
    out_biases,
    norm_gains,
    norm_biases,
):
    row_count = dec_starts.shape[0]
    dec_slots = hidden.shape[0] // row_count
    mem_slots = memory.shape[0] // row_count
    local_width = self_qkv.shape[2]
    head_count = local_width // HD
    scaling = HD ** (-0.5)
    dec_places = jnp.arange(dec_slots, dtype=jnp.int32)
    mem_places = jnp.arange(mem_slots, dtype=jnp.int32)
    dec_segment = segment_ids(dec_starts, dec_slots)
    mem_segment = segment_ids(mem_starts, mem_slots)
    self_allowed = (
        (dec_segment[:, :, None] == dec_segment[:, None, :])
        & (dec_places[None, None, :] <= dec_places[None, :, None])
        & (dec_places[None, None, :] < dec_length[:, None, None])
    )
    cross_allowed = (dec_segment[:, :, None] == mem_segment[:, None, :]) & (
        mem_places[None, None, :] < mem_length[:, None, None]
    )

    def split_heads(values):
        return values.reshape(row_count, values.shape[0] // row_count, head_count, HD)

    def merge_heads(values):
        return values.reshape(row_count * values.shape[1], local_width)

    self_weight = jnp.concatenate([self_qkv[0], self_qkv[1], self_qkv[2]], axis=1)
    projected = jnp.dot(hidden, self_weight, preferred_element_type=jnp.float32)
    self_q = split_heads(
        ((projected[:, :local_width] + self_qv_bias[0]) * scaling).astype(jnp.bfloat16)
    )
    self_k = split_heads(projected[:, local_width : 2 * local_width].astype(jnp.bfloat16))
    self_v = split_heads((projected[:, 2 * local_width :] + self_qv_bias[1]).astype(jnp.bfloat16))
    self_out, self_total = row_groups(attend_block, (self_q, self_k, self_v, self_allowed))
    self_low = merge_heads(self_out).astype(jnp.bfloat16)
    self_branch = lax.psum(jnp.dot(self_low, self_proj, preferred_element_type=jnp.float32), "mp")
    first, first_back = jax.vjp(
        layer_norm,
        hidden.astype(jnp.float32) + self_branch + out_biases[0],
        norm_gains[0],
        norm_biases[0],
    )
    first_low = first.astype(jnp.bfloat16)
    cross_pre = jnp.dot(first_low, cross_query, preferred_element_type=jnp.float32)
    cross_q = split_heads(((cross_pre + cross_qv_bias[0]) * scaling).astype(jnp.bfloat16))
    memory_whole = lax.all_gather(memory, "mp", axis=1, tiled=True)
    kv_weight = jnp.concatenate([cross_kv[0], cross_kv[1]], axis=1)
    memory_kv = jnp.dot(memory_whole, kv_weight, preferred_element_type=jnp.float32)
    cross_k = split_heads(memory_kv[:, :local_width].astype(jnp.bfloat16))
    cross_v = split_heads((memory_kv[:, local_width:] + cross_qv_bias[1]).astype(jnp.bfloat16))
    cross_out, cross_total = row_groups(attend_block, (cross_q, cross_k, cross_v, cross_allowed))
    cross_low = merge_heads(cross_out).astype(jnp.bfloat16)
    cross_branch = lax.psum(
        jnp.dot(cross_low, cross_proj, preferred_element_type=jnp.float32), "mp"
    )
    second, second_back = jax.vjp(
        layer_norm, first + cross_branch + out_biases[1], norm_gains[1], norm_biases[1]
    )
    second_low = second.astype(jnp.bfloat16)
    hidden_pre = jnp.dot(second_low, ffn_in, preferred_element_type=jnp.float32) + ffn_in_bias
    activated, gelu_back = jax.vjp(exact_gelu, hidden_pre)
    activated_low = activated.astype(jnp.bfloat16)
    ffn_branch = lax.psum(jnp.dot(activated_low, ffn_out, preferred_element_type=jnp.float32), "mp")
    final_norm, third_back = jax.vjp(
        layer_norm, second + ffn_branch + out_biases[2], norm_gains[2], norm_biases[2]
    )
    third_grad, gain_three, shift_three = third_back(out_grad.astype(jnp.float32))
    third_low = third_grad.astype(jnp.bfloat16)
    ffn_out_grad = inner_dot(activated_low, third_low)
    ffn_bias_out = jnp.sum(third_grad, 0)
    (pre_grad,) = gelu_back(outer_dot(third_low, ffn_out))
    ffn_in_bias_grad = jnp.sum(pre_grad, 0)
    pre_low = pre_grad.astype(jnp.bfloat16)
    ffn_in_grad = inner_dot(second_low, pre_low)
    second_grad = third_grad + lax.psum(outer_dot(pre_low, ffn_in), "mp")
    cross_grad, gain_two, shift_two = second_back(second_grad)
    cross_grad_low = cross_grad.astype(jnp.bfloat16)
    cross_proj_grad = inner_dot(cross_low, cross_grad_low)
    cross_bias_out = jnp.sum(cross_grad, 0)
    cross_out_grad = split_heads(outer_dot(cross_grad_low, cross_proj).astype(jnp.bfloat16))
    cq_grad, ck_grad, cv_grad = row_groups(
        attend_back, (cross_q, cross_k, cross_v, cross_allowed, cross_total, cross_out_grad)
    )
    cq_grad = merge_heads(cq_grad) * scaling
    cv_grad = merge_heads(cv_grad)
    cross_qv_grad = jnp.stack([jnp.sum(cq_grad, 0), jnp.sum(cv_grad, 0)])
    cq_low = cq_grad.astype(jnp.bfloat16)
    cross_query_grad = inner_dot(first_low, cq_low)
    first_grad = cross_grad + lax.psum(outer_dot(cq_low, cross_query), "mp")
    kv_grad_low = jnp.concatenate([merge_heads(ck_grad), cv_grad], axis=1).astype(jnp.bfloat16)
    kv_weight_grad = inner_dot(memory_whole, kv_grad_low)
    cross_kv_grad = jnp.stack([kv_weight_grad[:, :local_width], kv_weight_grad[:, local_width:]])
    memory_grad = lax.psum_scatter(
        outer_dot(kv_grad_low, kv_weight).astype(jnp.bfloat16),
        "mp",
        scatter_dimension=1,
        tiled=True,
    ).astype(jnp.float32)
    self_grad, gain_one, shift_one = first_back(first_grad)
    self_grad_low = self_grad.astype(jnp.bfloat16)
    self_proj_grad = inner_dot(self_low, self_grad_low)
    self_bias_out = jnp.sum(self_grad, 0)
    self_out_grad = split_heads(outer_dot(self_grad_low, self_proj).astype(jnp.bfloat16))
    sq_grad, sk_grad, sv_grad = row_groups(
        attend_back, (self_q, self_k, self_v, self_allowed, self_total, self_out_grad)
    )
    sq_grad = merge_heads(sq_grad) * scaling
    sv_grad = merge_heads(sv_grad)
    self_qv_grad = jnp.stack([jnp.sum(sq_grad, 0), jnp.sum(sv_grad, 0)])
    qkv_low = jnp.concatenate([sq_grad, merge_heads(sk_grad), sv_grad], axis=1).astype(jnp.bfloat16)
    qkv_weight_grad = inner_dot(hidden, qkv_low)
    self_qkv_grad = jnp.stack(
        [
            qkv_weight_grad[:, :local_width],
            qkv_weight_grad[:, local_width : 2 * local_width],
            qkv_weight_grad[:, 2 * local_width :],
        ]
    )
    hidden_grad = self_grad + lax.psum(
        outer_dot(qkv_low, self_weight).astype(jnp.bfloat16), "mp"
    ).astype(jnp.float32)
    (
        self_qkv_grad,
        self_qv_grad,
        self_proj_grad,
        cross_query_grad,
        cross_kv_grad,
        cross_qv_grad,
        cross_proj_grad,
        ffn_in_grad,
        ffn_in_bias_grad,
        ffn_out_grad,
        self_bias_out,
        cross_bias_out,
        ffn_bias_out,
        gain_one,
        gain_two,
        gain_three,
        shift_one,
        shift_two,
        shift_three,
    ) = lax.psum(
        (
            self_qkv_grad,
            self_qv_grad,
            self_proj_grad,
            cross_query_grad,
            cross_kv_grad,
            cross_qv_grad,
            cross_proj_grad,
            ffn_in_grad,
            ffn_in_bias_grad,
            ffn_out_grad,
            self_bias_out,
            cross_bias_out,
            ffn_bias_out,
            gain_one,
            gain_two,
            gain_three,
            shift_one,
            shift_two,
            shift_three,
        ),
        "dp",
    )
    out_biases_grad = jnp.stack([self_bias_out, cross_bias_out, ffn_bias_out])
    norm_gains_grad = jnp.stack([gain_one, gain_two, gain_three])
    norm_biases_grad = jnp.stack([shift_one, shift_two, shift_three])
    return (
        final_norm.astype(jnp.bfloat16),
        hidden_grad,
        memory_grad,
        self_qkv_grad,
        self_qv_grad,
        self_proj_grad,
        cross_query_grad,
        cross_kv_grad,
        cross_qv_grad,
        cross_proj_grad,
        ffn_in_grad,
        ffn_in_bias_grad,
        ffn_out_grad,
        out_biases_grad,
        norm_gains_grad,
        norm_biases_grad,
    )


def solution(mesh):
    placed = (
        P("dp", None),
        P("dp", "mp"),
        P("dp", None),
        P("dp", None),
        P("dp"),
        P("dp", None),
        P("dp"),
        P(None, None, "mp"),
        P(None, "mp"),
        P("mp", None),
        P(None, "mp"),
        P(None, None, "mp"),
        P(None, "mp"),
        P("mp", None),
        P(None, "mp"),
        P("mp"),
        P("mp", None),
        P(),
        P(),
        P(),
    )
    return jax.shard_map(
        body,
        mesh=mesh,
        in_specs=placed,
        out_specs=(
            P("dp", None),
            P("dp", None),
            P("dp", "mp"),
            P(None, None, "mp"),
            P(None, "mp"),
            P("mp", None),
            P(None, "mp"),
            P(None, None, "mp"),
            P(None, "mp"),
            P("mp", None),
            P(None, "mp"),
            P("mp"),
            P("mp", None),
            P(),
            P(),
            P(),
        ),
        check_vma=False,
    )
```

profile of v0, /device:TPU:9, one launch (start us, length us, event | category | flops | bytes accessed | tf_op | source)
XLA Modules:
  0.0 872.9 jit_solution(11104530872102401639)
XLA Ops:
  17.6 66.8 %all-reduce.10.cloned.1.call-done = f32[512,768]{1,0:T(8,128)} async-done(((f32[512,768]{1,0:T(8,128)}), f32[512,768]{1,0:T(8,128)}) %all-reduce.10.cloned.1.call-update) | async-done | bytes 1572880 | tf_op jit(solution)/shard_map/psum | solution.py:142
  89.9 108.7 %all-gather.2.cloned.1.call-done = bf16[4096,768]{0,1:T(8,128)(2,1)} async-done(((bf16[4096,192]{0,1:T(8,128)(2,1)}), bf16[4096,768]{0,1:T(8,128)(2,1)}) %all-gather.2.cloned.1.call-update) | async-done | bytes 6291472 | tf_op jit(solution)/shard_map/all_gather | solution.py:152
  198.7 4.8 convolution_bitcast_fusion
  203.5 2.6 copy-done.17
  207.5 3.9 squeeze.90
  211.3 3.4 fusion.4
  214.7 3.9 squeeze.88
  218.5 3.5 select_reduce_fusion
  224.7 2.8 fusion.39
  229.6 68.9 %all-reduce.12.cloned.1.call-done = f32[512,768]{1,0:T(8,128)} async-done(((f32[512,768]{1,0:T(8,128)}), f32[512,768]{1,0:T(8,128)}) %all-reduce.12.cloned.1.call-update) | async-done | bytes 1572880 | tf_op jit(solution)/shard_map/psum | solution.py:159
  301.2 5.4 multiply_convert_fusion.1
  309.5 68.3 %all-reduce.14.cloned.1.call-done = f32[512,768]{1,0:T(8,128)} async-done(((f32[512,768]{1,0:T(8,128)}), f32[512,768]{1,0:T(8,128)}) %all-reduce.14.cloned.1.call-update) | async-done | bytes 1572880 | tf_op jit(solution)/shard_map/psum | solution.py:169
  389.0 68.2 %all-reduce.16.cloned.1.call-done = f32[512,768]{1,0:T(8,128)} async-done(((f32[512,768]{1,0:T(8,128)}), f32[512,768]{1,0:T(8,128)}) %all-reduce.16.cloned.1.call-update) | async-done | bytes 1572880 | tf_op jit(solution)/shard_map/psum | solution.py:181
  457.2 2.8 multiply_reduce_fusion.1
  462.4 6.5 multiply_reduce_fusion
  474.6 8.5 all-reduce.20.cloned.1.call-start
  483.2 2.6 fusion.19
  487.7 3.1 bitcast_convert_fusion
  495.1 47.9 %all-reduce.18.cloned.1.call-done = f32[512,768]{1,0:T(8,128)} async-done(((f32[512,768]{1,0:T(8,128)}), f32[512,768]{1,0:T(8,128)}) %all-reduce.18.cloned.1.call-update) | async-done | bytes 1572880 | tf_op jit(solution)/shard_map/psum | solution.py:195
  542.9 2.8 multiply_reduce_fusion.2
  554.0 7.2 convolution_convert_fusion
  562.4 3.8 fusion.93
  566.2 2.4 fusion.49
  568.6 5.5 convolution_bitcast_fusion.3
  582.2 2.2 bitcast_reduce_fusion
  584.8 11.3 %all-reduce.20.cloned.1.call-done = bf16[512,768]{1,0:T(8,128)(2,1)} async-done(((bf16[512,768]{1,0:T(8,128)(2,1)}), bf16[512,768]{1,0:T(8,128)(2,1)}) %all-reduce.20.cloned.1.call-update) | async-done | bytes 786448 | tf_op jit(solution)/shard_map/psum | solution.py:225
  596.1 2.5 add_reduce_fusion
  598.6 22.5 %all-reduce = (f32[2,192]{1,0:T(2,128)}, f32[2,192]{1,0:T(2,128)}, f32[768]{0:T(1024)}, f32[1,768]{1,0:T(1,128)S(1)}, f32[1,768]{1,0:T(1,128)S(1)}, /*index=5*/f...) all-reduce(f32[2,192]{1,0:T(2,128)S(1)} %pad_maximum_fusion.11, ...), channel_id=1, replica_groups=mesh['dp'=8,'mp'=4] {'dp'}, use_global_device_ids=true, to_apply=%region_30.31 | all-reduce | flops 8448 | bytes 67584 | tf_op jit(solution)/shard_map/psum | solution.py:248
  622.9 86.1 %reduce-scatter.2.cloned.1.call-done = bf16[4096,192]{0,1:T(8,128)(2,1)} async-done(((bf16[4096,768]{0,1:T(8,128)(2,1)}), bf16[4096,192]{0,1:T(8,128)(2,1)}) %reduce-scatter.2.cloned.1.call-update) | async-done | bytes 1572880 | tf_op jit(solution)/shard_map/reduce_scatter | solution.py:199
  709.1 3.4 convert_element_type.157
  712.5 142.8 %all-reduce.22.cloned.1.call-done = (f32[3,768,192]{1,2,0:T(8,128)}, f32[192,768]{1,0:T(8,128)}, f32[768,192]{0,1:T(8,128)}, f32[2,768,192]{1,2,0:T(8,128)}, f32...) async-done(((f32[3,768,192]{1,2,0:T(8,128)}, f32[192,768]{1,0:T(8,128)}, f32[768,192]{0,1:T(8,128)}, f32[2,768,192]{1,2,0:T(8,128)}, f32[192,768]{1,0:T(8,128)}, ...) | async-done | bytes 9437200 | tf_op jit(solution)/shard_map/psum | solution.py:248
  855.3 2.9 copy.229
  (308 shorter events, 79.8 us)
Async XLA Ops:
  7.2 293.7 %copy-start = (bf16[768,768]{1,0:T(8,128)(2,1)S(1)}, bf16[768,768]{1,0:T(8,128)(2,1)}, u32[]{:S(2)}) copy-start(bf16[768,768]{1,0:T(8,128)(2,1)} %param.34) | copy-start | bytes 3538948
  7.2 77.2 %all-reduce.10.cloned.1.call-start = ((), (), s32[]{:S(2)}) async-start(), calls=%async_computation.1 | async-start | bytes 3145728 | tf_op jit(solution)/shard_map/psum | solution.py:142
  15.0 183.6 %all-gather.2.cloned.1.call-start = ((), (), s32[]{:S(2)}) async-start(), calls=%async_computation.2 | async-start | bytes 7864320 | tf_op jit(solution)/shard_map/all_gather | solution.py:152
  15.8 282.7 %all-reduce.12.cloned.1.call-start = ((), (), s32[]{:S(2)}) async-start(), calls=%async_computation.3 | async-start | bytes 3145728 | tf_op jit(solution)/shard_map/psum | solution.py:159
  16.1 361.6 %copy-start.63 = (f32[768]{0:T(1024)}, f32[768]{0:T(1024)S(1)}, u32[]{:S(2)}) copy-start(f32[768]{0:T(1024)S(1)} %get-tuple-element.122) | copy-start | bytes 9220
  16.7 207.0 %copy-start.12 = (pred[4,128,1024]{2,1,0:T(8,128)(4,1)}, pred[4,128,1024]{2,1,0:T(8,128)(4,1)S(1)}, u32[]{:S(2)}) copy-start(pred[4,128,1024]{2,1,0:T(8,128)(4,1)S(1)} %compare_and_fusion) | copy-start | bytes 1572868
  86.3 212.2 %copy-start.3 = (f32[512,768]{1,0:T(8,128)}, f32[512,768]{1,0:T(8,128)S(1)}, u32[]{:S(2)}) copy-start(f32[512,768]{1,0:T(8,128)S(1)} %get-tuple-element.170) | copy-start | bytes 4718596
  224.7 2.9 copy-start.39
  229.3 148.5 %all-reduce.14.cloned.1.call-start = ((), (), s32[]{:S(2)}) async-start(), calls=%async_computation.4 | async-start | bytes 3145728 | tf_op jit(solution)/shard_map/psum | solution.py:169
  300.5 6.1 copy-start.5
  301.2 6.3 copy-start.74
  309.4 68.3 %copy-start.6 = (f32[512,768]{1,0:T(8,128)S(1)}, f32[512,768]{1,0:T(8,128)}, u32[]{:S(2)}) copy-start(f32[512,768]{1,0:T(8,128)} %copy-done.5) | copy-start | bytes 4718596
  309.4 147.8 %all-reduce.16.cloned.1.call-start = ((), (), s32[]{:S(2)}) async-start(), calls=%async_computation.5 | async-start | bytes 3145728 | tf_op jit(solution)/shard_map/psum | solution.py:181
  383.2 2.7 copy-start.18
  388.9 154.0 %all-reduce.18.cloned.1.call-start = ((), (), s32[]{:S(2)}) async-start(), calls=%async_computation.6 | async-start | bytes 3145728 | tf_op jit(solution)/shard_map/psum | solution.py:195
  462.3 6.5 slice-start
  462.4 6.5 slice-start.1
  474.6 13.0 %slice-start.2 = ((s8[6291456]{0:T(1024)(128)(4,1)}), s8[2097152]{0:T(1024)(128)(4,1)S(1)}, s32[]{:S(2)}) async-start(s8[6291456]{0:T(1024)(128)(4,1)} %bitcast.150), calls=%async_computation.12 | async-start | bytes 4194304
  474.6 121.5 %all-reduce.20.cloned.1.call-start = ((), (), s32[]{:S(2)}) async-start(), calls=%async_computation.7 | async-start | bytes 1572864 | tf_op jit(solution)/shard_map/psum | solution.py:225
  483.2 4.5 slice-start.3
  493.8 49.2 %copy-start.4 = (f32[512,768]{1,0:T(8,128)S(1)}, f32[512,768]{1,0:T(8,128)}, u32[]{:S(2)}) copy-start(f32[512,768]{1,0:T(8,128)} %copy-done.3) | copy-start | bytes 4718596
  552.7 156.4 %reduce-scatter.2.cloned.1.call-start = ((), (), s32[]{:S(2)}) async-start(), calls=%async_computation.8 | async-start | bytes 7864320 | tf_op jit(solution)/shard_map/reduce_scatter | solution.py:199
  561.3 4.9 copy-start.7
  561.3 4.9 copy-start.64
  561.3 294.0 %all-reduce.22.cloned.1.call-start = ((), (), s32[]{:S(2)}) async-start(), calls=%async_computation.9 | async-start | bytes 18874368 | tf_op jit(solution)/shard_map/psum | solution.py:248
  562.4 3.8 copy-start.79
  574.1 2.7 copy-start.11
  574.1 2.7 copy-start.38
  584.8 13.8 %copy-start.68 = (f32[768]{0:T(1024)S(1)}, f32[768]{0:T(1024)}, u32[]{:S(2)}) copy-start(f32[768]{0:T(1024)} %get-tuple-element.210) | copy-start | bytes 9220
  855.3 2.9 copy-start.54
  855.3 3.7 copy-start.53
  862.2 3.9 copy-start.1
  (63 other events, 93.3 us)
Sparse Core Ops, SparseCore 0:
  15.2 69.1 all-reduce.9
  86.0 112.6 all-gather.1
  229.4 69.0 all-reduce.11
  309.6 68.1 all-reduce.13
  389.0 68.1 all-reduce.15
  474.7 68.1 all-reduce.17
  552.8 43.2 all-reduce.19
  598.4 110.6 reduce-scatter.1
  715.0 140.2 all-reduce.21
where the time goes:
time: 884 us; the launch traced here: 873 us
  waiting for transfers between devices  670 us (76%)
  matrix products  70.8 us (8%)
  local copies, waits for them, and re-layouts  47.4 us (5%)
  other arithmetic  37.7 us (4%)
  blocking collectives  22.5 us (3%)
  between operations  15.3 us (2%)
  starting transfers between devices  9.3 us (1%)
    psum x1, waiting for transfers between devices, body(): lax.psum((self_qkv_grad, self_qv_grad, self_proj_grad, cross_query_grad,...  143 us
    all_gather x1, waiting for transfers between devices, body(): memory_whole = lax.all_gather(memory, 'mp', axis=1, tiled=True)  109 us
    reduce_scatter x1, waiting for transfers between devices, body(): lax.psum_scatter(outer_dot(kv_grad_low, kv_weight).astype(jnp.bfloat16),...  86.1 us
    psum x1, waiting for transfers between devices, body(): lax.psum(jnp.dot(cross_low, cross_proj, preferred_element_type=jnp.float3...  68.9 us
    psum x1, waiting for transfers between devices, body(): lax.psum(jnp.dot(activated_low, ffn_out, preferred_element_type=jnp.float...  68.3 us
    psum x1, waiting for transfers between devices, body(): second_grad = third_grad + lax.psum(outer_dot(pre_low, ffn_in), 'mp')  68.2 us
    psum x1, waiting for transfers between devices, body(): lax.psum(jnp.dot(self_low, self_proj, preferred_element_type=jnp.float32)...  66.8 us
    psum x1, waiting for transfers between devices, body(): first_grad = cross_grad + lax.psum(outer_dot(cq_low, cross_query), 'mp')  47.9 us
  transfers between devices with their start and end apart: 9, of which 9 were waited for; matrix products, arithmetic and copies ran while one was open for 6% of the time, Pallas kernels for 0%

commit v1 on v0

v1 whole, which is shorter than its diff:
```python
import jax
import jax.numpy as jnp
from jax import lax
from jax.sharding import PartitionSpec as P

HD = 64
SUB = 8
NEG_FILL = -1000000000.0
EPSILON = 1e-05
F32 = jnp.float32
BF16 = jnp.bfloat16


def layer_norm(values, gain_row, bias_row):
    average = jnp.mean(values, -1, keepdims=True)
    centered = values - average
    variance = jnp.mean(centered * centered, -1, keepdims=True)
    return centered * lax.rsqrt(variance + EPSILON) * gain_row + bias_row


def exact_gelu(values):
    return jax.nn.gelu(values, approximate=False)


def segment_ids(starts, slot_count):
    places = jnp.arange(slot_count, dtype=jnp.int32)
    return jnp.sum((starts[None, :] <= places[:, None]).astype(jnp.int32), -1) - 1


def ein(spec, left, right):
    return jnp.einsum(spec, left, right, preferred_element_type=F32)


def attend(queries, keys_t, values_t, allowed):
    scores = ein("htd,hds->hts", queries, keys_t)
    scores = jnp.where(allowed[None], scores, NEG_FILL)
    weights = jnp.exp(scores - jnp.max(scores, -1, keepdims=True))
    probs = weights / jnp.sum(weights, -1, keepdims=True)
    return ein("hts,hds->htd", probs.astype(BF16), values_t), probs


def attend_back(queries, keys_t, values_t, probs, grad_rows):
    prob_low = probs.astype(BF16)
    values_grad = ein("hts,htd->hds", prob_low, grad_rows)
    prob_grad = ein("htd,hds->hts", grad_rows, values_t)
    offset = jnp.sum(probs * prob_grad, -1, keepdims=True)
    score_grad = (probs * (prob_grad - offset)).astype(BF16)
    return (
        ein("hts,hds->htd", score_grad, keys_t),
        ein("hts,htd->hds", score_grad, queries),
        values_grad,
    )


def solution(mesh):
    dp = mesh.shape["dp"]
    mp = mesh.shape["mp"]

    def swap(value, bit):
        return lax.ppermute(value, "dp", [(i, i ^ bit) for i in range(dp)])

    def shift(value, step):
        return lax.ppermute(value, "mp", [(i, (i + step) % mp) for i in range(mp)])

    def gather_line(own):
        return jnp.stack([own] + [shift(own, step) for step in range(1, mp)])

    def gather_plane(own, place):
        half = own.shape[0] // 2
        over_two = swap(own, 2)
        over_four = swap(own, 4)
        across = jnp.concatenate([swap(over_four[:half], 2), swap(over_two[half:], 4)])
        whole = jnp.zeros(own.shape[:1] + (SUB,) + own.shape[1:], own.dtype)
        for offset, piece in ((0, own), (2, over_two), (4, over_four), (6, across)):
            for bit in (0, 1):
                part = swap(piece, 1) if bit else piece
                start = (0, place ^ (offset | bit)) + (0,) * (own.ndim - 1)
                whole = lax.dynamic_update_slice(whole, part[:, None], start)
        return whole

    def reduce_plane(parts, place):
        def part(offset):
            return lax.dynamic_index_in_dim(parts, place ^ offset, 1, keepdims=False)

        half = parts.shape[0] // 2
        sums = {}
        for offset in (6, 2, 4, 0):
            sums[offset] = part(offset) + swap(part(offset ^ 1).astype(BF16), 1)
        far = sums[6].astype(BF16)
        near_two = swap(sums[2][:half].astype(BF16), 2)
        near_four = swap(sums[4][half:].astype(BF16), 4)
        late_four = sums[4][:half] + swap(far[:half], 2)
        late_two = sums[2][half:] + swap(far[half:], 4)
        late_two = swap(late_two.astype(BF16), 2)
        late_four = swap(late_four.astype(BF16), 4)
        return sums[0] + jnp.concatenate(
            [near_two.astype(F32) + late_four, near_four.astype(F32) + late_two]
        )

    def reduce_line(parts):
        total = parts[0]
        for step in range(1, mp):
            total = total + shift(parts[step].astype(BF16), -step)
        return total

    def reduce_outer(total):
        bit = SUB
        while bit < dp:
            total = total + swap(total, bit)
            bit *= 2
        return total

    def reduce_group(parts, place):
        total = reduce_outer(reduce_line(reduce_plane(parts, place)))
        low = total.astype(BF16)
        rows, width = low.shape
        pieces = low.reshape(2, rows // 2, width)
        whole = gather_plane(pieces, place)
        return jnp.swapaxes(whole, 0, 1).reshape(SUB, rows, width).astype(F32)

    def sum_everywhere(total):
        bit = 1
        while bit < dp:
            total = total + swap(total, bit)
            bit *= 2
        bit = 1
        while bit < mp:
            total = total + lax.ppermute(total, "mp", [(i, i ^ bit) for i in range(mp)])
            bit *= 2
        return total

    def body(
        hidden,
        memory,
        out_grad,
        dec_starts,
        dec_length,
        mem_starts,
        mem_length,
        self_qkv,
        self_qv_bias,
        self_proj,
        cross_query,
        cross_kv,
        cross_qv_bias,
        cross_proj,
        ffn_in,
        ffn_in_bias,
        ffn_out,
        out_biases,
        norm_gains,
        norm_biases,
    ):
        row_count = dec_starts.shape[0]
        assert row_count == mp
        slots = hidden.shape[0] // row_count
        mem_slots = memory.shape[0] // row_count
        width = hidden.shape[1]
        local = self_proj.shape[0]
        heads = local // HD
        inner = ffn_out.shape[0]
        scaling = HD ** (-0.5)
        line = lax.axis_index("mp")
        place = lax.axis_index("dp") % SUB
        from_line = (line - jnp.arange(mp)) % mp

        def row_of(array, size):
            return lax.dynamic_slice_in_dim(array, line * size, size, 0)

        def slice_of(array):
            size = array.shape[0] // SUB
            return lax.dynamic_slice_in_dim(array, place * size, size, 0)

        head_in = jnp.concatenate(
            [jnp.swapaxes(self_qkv, 1, 2).reshape(3 * local, width), cross_query.T]
        )
        head_out = jnp.concatenate([self_proj, cross_proj])
        key_value = jnp.swapaxes(cross_kv, 1, 2).reshape(2 * local, width)
        first_piece = jnp.concatenate([slice_of(head_in), slice_of(head_out)])
        memory_piece = slice_of(key_value)
        ffn_piece = jnp.concatenate([slice_of(ffn_in), slice_of(ffn_out)])
        biases = gather_line(
            jnp.concatenate([self_qv_bias.reshape(-1), cross_qv_bias.reshape(-1), ffn_in_bias])
        )
        first_whole = gather_plane(gather_line(first_piece), place)
        split = head_in.shape[0] // SUB
        head_in_all = first_whole[:, :, :split].reshape(mp, 4 * local, width)
        head_out_all = first_whole[:, :, split:].reshape(mp, 2 * local, width)
        self_bias = biases[:, : 2 * local].reshape(mp, 2, local)
        cross_bias = biases[:, 2 * local : 4 * local].reshape(mp, 2, local)
        inner_bias = biases[:, 4 * local :]

        memory_t = memory.T
        columns = []
        for step in range(mp):
            to = (line + step) % mp
            block = lax.dynamic_slice_in_dim(memory_t, to * mem_slots, mem_slots, 1)
            columns.append(shift(block, step) if step else block)
        memory_row = jnp.zeros((mp, local, mem_slots), BF16)
        for step in range(mp):
            memory_row = lax.dynamic_update_slice(
                memory_row, columns[step][None], (from_line[step], 0, 0)
            )
        memory_row = memory_row.reshape(width, mem_slots)
        key_value_all = gather_plane(gather_line(memory_piece), place).reshape(
            mp, 2 * local, width
        )
        ffn_whole = gather_plane(gather_line(ffn_piece), place)
        split = width // SUB
        ffn_in_all = ffn_whole[:, :, :split].reshape(mp, width, inner)
        ffn_out_all = ffn_whole[:, :, split:].reshape(mp, inner, width)

        dec_segment = segment_ids(row_of(dec_starts, 1)[0], slots)
        mem_segment = segment_ids(row_of(mem_starts, 1)[0], mem_slots)
        dec_places = jnp.arange(slots, dtype=jnp.int32)
        mem_places = jnp.arange(mem_slots, dtype=jnp.int32)
        self_allowed = (
            (dec_segment[:, None] == dec_segment[None, :])
            & (dec_places[None, :] <= dec_places[:, None])
            & (dec_places[None, :] < row_of(dec_length, 1))
        )
        cross_allowed = (dec_segment[:, None] == mem_segment[None, :]) & (
            mem_places[None, :] < row_of(mem_length, 1)
        )

        def to_heads(values):
            values = values.reshape(mp, slots, heads, HD)
            return jnp.swapaxes(values, 1, 2).reshape(mp * heads, slots, HD)

        def from_heads(values):
            values = values.reshape(mp, heads, slots, HD)
            return jnp.swapaxes(values, 1, 2).reshape(mp, slots, local)

        def to_heads_t(values):
            return values.reshape(mp * heads, HD, values.shape[-1])

        hidden_row = row_of(hidden, slots)
        grad_row = row_of(out_grad, slots)
        self_q = to_heads(
            (
                (ein("td,znd->ztn", hidden_row, head_in_all[:, :local]) + self_bias[:, None, 0])
                * scaling
            ).astype(BF16)
        )
        self_k = to_heads_t(
            ein("znd,td->znt", head_in_all[:, local : 2 * local], hidden_row).astype(BF16)
        )
        self_v = to_heads_t(
            (
                ein("znd,td->znt", head_in_all[:, 2 * local : 3 * local], hidden_row)
                + self_bias[:, 1, :, None]
            ).astype(BF16)
        )
        self_out, self_probs = attend(self_q, self_k, self_v, self_allowed)
        self_low = from_heads(self_out.astype(BF16))
        first, first_back = jax.vjp(
            layer_norm,
            hidden_row.astype(F32)
            + ein("ztn,znd->td", self_low, head_out_all[:, :local])
            + out_biases[0],
            norm_gains[0],
            norm_biases[0],
        )
        first_low = first.astype(BF16)
        cross_q = to_heads(
            (
                (ein("td,znd->ztn", first_low, head_in_all[:, 3 * local :]) + cross_bias[:, None, 0])
                * scaling
            ).astype(BF16)
        )
        memory_kv = ein("znd,ds->zns", key_value_all, memory_row)
        cross_k = to_heads_t(memory_kv[:, :local].astype(BF16))
        cross_v = to_heads_t((memory_kv[:, local:] + cross_bias[:, 1, :, None]).astype(BF16))
        cross_out, cross_probs = attend(cross_q, cross_k, cross_v, cross_allowed)
        cross_low = from_heads(cross_out.astype(BF16))
        second, second_back = jax.vjp(
            layer_norm,
            first + ein("ztn,znd->td", cross_low, head_out_all[:, local:]) + out_biases[1],
            norm_gains[1],
            norm_biases[1],
        )
        second_low = second.astype(BF16)
        hidden_pre = ein("td,zdn->ztn", second_low, ffn_in_all) + inner_bias[:, None]
        activated, gelu_back = jax.vjp(exact_gelu, hidden_pre)
        activated_low = activated.astype(BF16)
        final_norm, third_back = jax.vjp(
            layer_norm,
            second + ein("ztn,znd->td", activated_low, ffn_out_all) + out_biases[2],
            norm_gains[2],
            norm_biases[2],
        )
        result = gather_line(final_norm.astype(BF16))

        third_grad, gain_three, shift_three = third_back(grad_row.astype(F32))
        third_low = third_grad.astype(BF16)
        (pre_grad,) = gelu_back(ein("td,znd->ztn", third_low, ffn_out_all))
        pre_low = pre_grad.astype(BF16)
        ffn_parts = jnp.concatenate(
            [
                ein("td,ztn->zdn", second_low, pre_low).reshape(mp, SUB, -1, inner),
                ein("ztn,td->znd", activated_low, third_low).reshape(mp, SUB, -1, width),
            ],
            axis=2,
        )
        ffn_grads = reduce_group(ffn_parts, place)
        second_grad = third_grad + ein("ztn,zdn->td", pre_low, ffn_in_all)
        cross_grad, gain_two, shift_two = second_back(second_grad)
        cross_grad_low = cross_grad.astype(BF16)
        cross_out_grad = to_heads(
            ein("td,znd->ztn", cross_grad_low, head_out_all[:, local:]).astype(BF16)
        )
        cq_grad, ck_grad, cv_grad = attend_back(
            cross_q, cross_k, cross_v, cross_probs, cross_out_grad
        )
        cq_grad = from_heads(cq_grad) * scaling
        cq_low = cq_grad.astype(BF16)
        ck_grad = ck_grad.reshape(mp, local, mem_slots)
        cv_grad = cv_grad.reshape(mp, local, mem_slots)
        kv_low = jnp.concatenate([ck_grad, cv_grad], axis=1).astype(BF16)
        memory_grad_t = ein("znd,zns->ds", key_value_all, kv_low).astype(BF16)
        memory_blocks = memory_grad_t.reshape(mp, local, mem_slots)
        memory_out = jnp.zeros((local, mp, mem_slots), BF16)
        for step in range(mp):
            to = (line + step) % mp
            block = lax.dynamic_index_in_dim(memory_blocks, to, 0, keepdims=False)
            block = shift(block, step) if step else block
            memory_out = lax.dynamic_update_slice(
                memory_out, block[:, None], (0, from_line[step], 0)
            )
        memory_grad = memory_out.astype(F32).reshape(local, mp * mem_slots).T
        kv_parts = ein("zns,ds->znd", kv_low, memory_row).reshape(mp, SUB, -1, width)
        kv_grads = reduce_group(kv_parts, place)

        first_grad = cross_grad + ein("ztn,znd->td", cq_low, head_in_all[:, 3 * local :])
        self_grad, gain_one, shift_one = first_back(first_grad)
        self_grad_low = self_grad.astype(BF16)
        self_out_grad = to_heads(
            ein("td,znd->ztn", self_grad_low, head_out_all[:, :local]).astype(BF16)
        )
        sq_grad, sk_grad, sv_grad = attend_back(self_q, self_k, self_v, self_probs, self_out_grad)
        sq_grad = from_heads(sq_grad) * scaling
        sk_grad = jnp.swapaxes(sk_grad.reshape(mp, local, slots), 1, 2)
        sv_grad = jnp.swapaxes(sv_grad.reshape(mp, local, slots), 1, 2)
        qkv_low = jnp.concatenate([sq_grad, sk_grad, sv_grad], axis=2).astype(BF16)
        hidden_grad_row = self_grad + ein("ztn,znd->td", qkv_low, head_in_all[:, : 3 * local])
        hidden_grad = gather_line(hidden_grad_row.astype(BF16))
        head_in_parts = jnp.concatenate(
            [ein("ztn,td->znd", qkv_low, hidden_row), ein("ztn,td->znd", cq_low, first_low)], axis=1
        ).reshape(mp, SUB, -1, width)
        head_out_parts = jnp.concatenate(
            [
                ein("ztn,td->znd", self_low, self_grad_low),
                ein("ztn,td->znd", cross_low, cross_grad_low),
            ],
            axis=1,
        ).reshape(mp, SUB, -1, width)
        head_grads = reduce_group(jnp.concatenate([head_in_parts, head_out_parts], axis=2), place)

        def absolute(values):
            return jnp.take(values, from_line, axis=0)

        small = jnp.concatenate(
            [
                jnp.stack(
                    [
                        jnp.sum(self_grad, 0),
                        jnp.sum(cross_grad, 0),
                        jnp.sum(third_grad, 0),
                        gain_one,
                        gain_two,
                        gain_three,
                        shift_one,
                        shift_two,
                        shift_three,
                    ]
                ).reshape(-1),
                absolute(
                    jnp.concatenate(
                        [
                            jnp.sum(sq_grad, 1),
                            jnp.sum(sv_grad, 1),
                            jnp.sum(cq_grad, 1),
                            jnp.sum(cv_grad, 2),
                            jnp.sum(pre_grad, 1),
                        ],
                        axis=1,
                    )
                ).reshape(-1),
            ]
        )
        small = sum_everywhere(small)
        rows = small[: 9 * width].reshape(3, 3, width)
        sharded = lax.dynamic_index_in_dim(
            small[9 * width :].reshape(mp, 4 * local + inner), line, 0, keepdims=False
        )

        def in_order(gathered):
            return jnp.take(gathered, from_line, axis=0).reshape(mp * slots, width)

        split = 4 * local // SUB
        head_in_grad = head_grads[:, :split].reshape(4, local, width)
        head_out_grad = head_grads[:, split:].reshape(2, local, width)
        ffn_in_grad = ffn_grads[:, : width // SUB].reshape(width, inner)
        ffn_out_grad = ffn_grads[:, width // SUB :].reshape(inner, width)
        return (
            in_order(result),
            in_order(hidden_grad).astype(F32),
            memory_grad,
            jnp.swapaxes(head_in_grad[:3], 1, 2),
            sharded[: 2 * local].reshape(2, local),
            head_out_grad[0],
            head_in_grad[3].T,
            jnp.swapaxes(kv_grads.reshape(2, local, width), 1, 2),
            sharded[2 * local : 4 * local].reshape(2, local),
            head_out_grad[1],
            ffn_in_grad,
            sharded[4 * local :],
            ffn_out_grad,
            rows[0],
            rows[1],
            rows[2],
        )

    return jax.shard_map(
        body,
        mesh=mesh,
        in_specs=(
            P("dp", None),
            P("dp", "mp"),
            P("dp", None),
            P("dp", None),
            P("dp"),
            P("dp", None),
            P("dp"),
            P(None, None, "mp"),
            P(None, "mp"),
            P("mp", None),
            P(None, "mp"),
            P(None, None, "mp"),
            P(None, "mp"),
            P("mp", None),
            P(None, "mp"),
            P("mp"),
            P("mp", None),
            P(),
            P(),
            P(),
        ),
        out_specs=(
            P("dp", None),
            P("dp", None),
            P("dp", "mp"),
            P(None, None, "mp"),
            P(None, "mp"),
            P("mp", None),
            P(None, "mp"),
            P(None, None, "mp"),
            P(None, "mp"),
            P("mp", None),
            P(None, "mp"),
            P("mp"),
            P("mp", None),
            P(),
            P(),
            P(),
        ),
        check_vma=False,
    )
```

time: 884 us -> 657 us (0.74)
  waiting for transfers between devices: 670 us -> 187 us
  starting transfers between devices: 9.3 us -> 143 us
  local copies, waits for them, and re-layouts: 47.4 us -> 147 us
  other arithmetic: 37.7 us -> 70.8 us
  blocking collectives: 22.5 us -> 0 us
  matrix products: 70.8 us -> 88.3 us
    psum x7 -> x0, waiting for transfers between devices: 474 us -> none  [the longest x1 143 us: body(): lax.psum((self_qkv_grad, self_qv_grad, self_proj_grad, cross_query_grad,...]
    ppermute x0 -> x116, waiting for transfers between devices: none -> 187 us  [the longest x81 108 us: swap(): return lax.ppermute(value, 'dp', [(i, i ^ bit) for i in range(dp)])]
    ppermute x0 -> x116, starting transfers between devices: none -> 143 us  [the longest x81 85.1 us: swap(): return lax.ppermute(value, 'dp', [(i, i ^ bit) for i in range(dp)])]
    all_gather x1 -> x0, waiting for transfers between devices: 109 us -> none  [body(): memory_whole = lax.all_gather(memory, 'mp', axis=1, tiled=True)]
    reduce_scatter x1 -> x0, waiting for transfers between devices: 86.1 us -> none  [body(): lax.psum_scatter(outer_dot(kv_grad_low, kv_weight).astype(jnp.bfloat16),...]
    dynamic_update_slice x0 -> x53, local copies, waits for them, and re-layouts: none -> 73.5 us  [the longest x4 56.7 us: body(): lax.dynamic_update_slice(memory_out, block[:, None], (0, from_line[step],...]
    slice x4 -> x40, local copies, waits for them, and re-layouts: 1.38 us -> 26.2 us  [the longest x1 6.94 us: body(): ffn_out_all = ffn_whole[:, :, split:].reshape(mp, inner, width)]
    psum x1 -> x0, blocking collectives: 22.5 us -> none  [body(): lax.psum((self_qkv_grad, self_qv_grad, self_proj_grad, cross_query_grad,...]
  transfers between devices with their start and end apart: 9 -> 116, of which waited for: 9 -> 36; matrix products, arithmetic and copies ran while one was open for 6% -> 36% of each run, Pallas kernels for 0% -> 0%
where the time goes in v1:
time: 657 us; the launch traced here: 648 us
  waiting for transfers between devices  187 us (28%)
  local copies, waits for them, and re-layouts  147 us (22%)
  starting transfers between devices  143 us (22%)
  matrix products  88.3 us (13%)
  other arithmetic  70.8 us (11%)
  between operations  11.9 us (2%)
    ppermute x81, waiting for transfers between devices, swap(): return lax.ppermute(value, 'dp', [(i, i ^ bit) for i in range(dp)])  108 us
    ppermute x81, starting transfers between devices, swap(): return lax.ppermute(value, 'dp', [(i, i ^ bit) for i in range(dp)])  85.1 us
    dot_general x33, matrix products, ein(): return jnp.einsum(spec, left, right, preferred_element_type=F32)  80.6 us
    ppermute x33, waiting for transfers between devices, shift(): return lax.ppermute(value, 'mp', [(i, (i + step) % mp) for i in range(mp)])  67.8 us
    dynamic_update_slice x4, local copies, waits for them, and re-layouts, body(): lax.dynamic_update_slice(memory_out, block[:, None], (0, from_line[step],...  56.7 us
    ppermute x33, starting transfers between devices, shift(): return lax.ppermute(value, 'mp', [(i, (i + step) % mp) for i in range(mp)])  54.8 us
    dynamic_update_slice x45, local copies, waits for them, and re-layouts, gather_plane(): whole = lax.dynamic_update_slice(whole, part[:, None], start)  16.6 us
    unnamed x262, local copies, waits for them, and re-layouts  16.1 us
  transfers between devices with their start and end apart: 116, of which 36 were waited for; matrix products, arithmetic and copies ran while one was open for 36% of the time, Pallas kernels for 0%

profile of v1, /device:TPU:9, one launch (start us, length us, event | category | flops | bytes accessed | tf_op | source)
XLA Modules:
  0.0 647.7 jit_solution(10162162452175390701)
XLA Ops:
  40.5 7.2 %collective-permute-start.30 = (bf16[192,768]{1,0:T(8,128)(2,1)}, bf16[192,768]{1,0:T(8,128)(2,1)S(1)}, u32[]{:S(2)}, u32[]{:S(2)}) collective-permute-start(bf16[192,768]{1,0:T(8,128)(2,1)} %get-tuple-element.106), channel_id=1, source_target_pairs={{0,3},{1,0},{2,1},{3,2},{4,7},{5,4},{6,5},{7,6},{8,11},{9,8},{10,9... | collective-permute-start | bytes 884744 | tf_op jit(solution)/shard_map/ppermute | solution.py:63
  59.4 7.7 %collective-permute-done.29 = bf16[192,768]{1,0:T(8,128)(2,1)S(1)} collective-permute-done((bf16[192,768]{1,0:T(8,128)(2,1)}, bf16[192,768]{1,0:T(8,128)(2,1)S(1)}, u32[]{:S(2)}, u32[]{:S(2)}) %collective-permute-start.29) | collective-permute-done | bytes 294944 | tf_op jit(solution)/shard_map/ppermute | solution.py:63
  67.1 5.9 collective-permute-start.25
  87.1 18.1 %collective-permute-done.26 = bf16[192,1024]{1,0:T(8,128)(2,1)S(1)} collective-permute-done((bf16[192,1024]{1,0:T(8,128)(2,1)S(1)}, bf16[192,1024]{1,0:T(8,128)(2,1)S(1)}, u32[]{:S(2)}, u32[]{:S(2)}) %collective-permute-start.26) | collective-permute-done | bytes 393248 | tf_op jit(solution)/shard_map/ppermute | solution.py:63
  119.0 13.9 %collective-permute-done.6 = bf16[4,144,768]{2,1,0:T(8,128)(2,1)S(1)} collective-permute-done((bf16[4,144,768]{2,1,0:T(8,128)(2,1)S(1)}, bf16[4,144,768]{2,1,0:T(8,128)(2,1)S(1)}, u32[]{:S(2)}, u32[]{:S(2)}) %collective-permute-start.6) | collective-permute-done | bytes 884768 | tf_op jit(solution)/shard_map/ppermute | solution.py:60
  143.8 16.1 %collective-permute-done.34 = bf16[4,192,768]{2,1,0:T(8,128)(2,1)} collective-permute-done((bf16[4,192,768]{2,1,0:T(8,128)(2,1)S(1)}, bf16[4,192,768]{2,1,0:T(8,128)(2,1)}, u32[]{:S(2)}, u32[]{:S(2)}) %collective-permute-start.34) | collective-permute-done | bytes 1179680 | tf_op jit(solution)/shard_map/ppermute | solution.py:60
  171.8 6.9 %collective-permute-done.36 = bf16[2,192,768]{2,1,0:T(8,128)(2,1)S(1)} collective-permute-done((bf16[2,192,768]{2,1,0:T(8,128)(2,1)S(1)}, bf16[2,192,768]{2,1,0:T(8,128)(2,1)S(1)}, u32[]{:S(2)}, u32[]{:S(2)}) %collective-permute-start.36) | collective-permute-done | bytes 589856 | tf_op jit(solution)/shard_map/ppermute | solution.py:60
  195.4 6.4 fusion.289
  201.8 4.9 fusion.126
  219.4 6.9 %fusion.268 = (bf16[4,8,96,768]{3,2,1,0:T(8,128)(2,1)S(1)}, bf16[4,8,96,768]{3,2,1,0:T(8,128)(2,1)}) fusion(bf16[4,8,192,768]{3,2,1,0:T(8,128)(2,1)} %bitcast_dynamic-update-slice_fusion), kind=kLoop, calls=%fused_computation.512 | loop fusion | bytes 18874368 | tf_op jit(solution)/shard_map/slice | solution.py:211
  226.3 6.0 fusion.68
  235.2 5.4 fusion.296
  282.1 5.0 fusion.173
  297.1 5.2 fusion.162
  302.4 5.1 fusion.226
  310.3 7.9 %pad_maximum_fusion = f32[4,768,768]{2,1,0:T(8,128)} fusion(f32[4,192,768]{2,1,0:T(8,128)} %fusion.245, f32[4,576,768]{2,1,0:T(8,128)} %fusion.173), kind=kLoop, calls=%fused_computation.37 | loop fusion | flops 2359296 | bytes 18874368 | tf_op jit(solution)/shard_map/concatenate | solution.py:347
  322.4 7.8 %fusion.111 = (bf16[4,192,768]{2,1,0:T(8,128)(2,1)}, bf16[4,192,768]{2,1,0:T(8,128)(2,1)}, bf16[4,192,768]{2,1,0:T(8,128)(2,1)}, bf16[4,192,768]{2,1,0:T(8,128)(2,1)}) fusion(s32[]{:T(128)S(6)} %select_n.245, f32[4,8,96,768]{3,2,1,0:T(8,128)} %bitcast.673, f32[4,8,96,768]{3,2,1,0:T(8,128)} %bitcast.678, s32[]{:T(128)S(6)} %select_n.247, s32[]{:T(128)S(6)} %select_n.249, ...), kind=kLoop, calls=%fused_computation.190 | loop fusion | flops 9437184 | bytes 23592976 | tf_op jit(solution)/shard_map/convert_element_type | solution.py:88
  347.3 14.2 %dynamic_update_slice.196 = bf16[192,4,1024]{2,1,0:T(4,128)(2,1)} dynamic-update-slice(bf16[192,4,1024]{2,1,0:T(4,128)(2,1)} %broadcast_in_dim.313, bf16[192,1,1024]{2,1,0:T(2,128)(2,1)S(1)} %copy.168, s32[]{:T(128)} %constant.223.clone.1, s32[]{:T(128)S(6)} %select_n.256, s32[]{:T(128)} %constant.223.clone.1) | dynamic-update-slice | bytes 786436 | tf_op jit(solution)/shard_map/dynamic_update_slice | solution.py:327
  381.3 9.6 %collective-permute-done.73 = f32[13056]{0:T(1024)S(1)} collective-permute-done((f32[13056]{0:T(1024)S(1)}, f32[13056]{0:T(1024)S(1)}, u32[]{:S(2)}, u32[]{:S(2)}) %collective-permute-start.73) | collective-permute-done | bytes 52256 | tf_op jit(solution)/shard_map/ppermute | solution.py:128
  402.3 7.2 %collective-permute-start.47 = (bf16[192,1024]{1,0:T(8,128)(2,1)}, bf16[192,1024]{1,0:T(8,128)(2,1)S(1)}, u32[]{:S(2)}, u32[]{:S(2)}) collective-permute-start(bf16[192,1024]{1,0:T(8,128)(2,1)} %get-tuple-element.78), channel_id=1, source_target_pairs={{0,3},{1,0},{2,1},{3,2},{4,7},{5,4},{6,5},{7,6},{8,11},{9,8},{10,9... | collective-permute-start | bytes 1179656 | tf_op jit(solution)/shard_map/ppermute | solution.py:63
  420.2 5.3 collective-permute-start.51
  428.5 14.2 %dynamic_update_slice.197 = bf16[192,4,1024]{2,1,0:T(4,128)(2,1)} dynamic-update-slice(bf16[192,4,1024]{2,1,0:T(4,128)(2,1)} %dynamic_update_slice.196, bf16[192,1,1024]{2,1,0:T(2,128)(2,1)S(1)} %copy.169, s32[]{:T(128)} %constant.223.clone.1, s32[]{:T(128)S(6)} %select_n.259, s32[]{:T(128)} %constant.223.clone.1) | dynamic-update-slice | bytes 786436 | tf_op jit(solution)/shard_map/dynamic_update_slice | solution.py:327
  442.7 14.2 %dynamic_update_slice.198 = bf16[192,4,1024]{2,1,0:T(4,128)(2,1)} dynamic-update-slice(bf16[192,4,1024]{2,1,0:T(4,128)(2,1)} %dynamic_update_slice.197, bf16[192,1,1024]{2,1,0:T(2,128)(2,1)S(1)} %copy.170, s32[]{:T(128)} %constant.223.clone.1, s32[]{:T(128)S(6)} %select_n.262, s32[]{:T(128)} %constant.223.clone.1) | dynamic-update-slice | bytes 786436 | tf_op jit(solution)/shard_map/dynamic_update_slice | solution.py:327
  456.9 14.2 %dynamic_update_slice.199 = bf16[192,4,1024]{2,1,0:T(4,128)(2,1)} dynamic-update-slice(bf16[192,4,1024]{2,1,0:T(4,128)(2,1)} %dynamic_update_slice.198, bf16[192,1,1024]{2,1,0:T(2,128)(2,1)S(1)} %copy.171, s32[]{:T(128)} %constant.223.clone.1, s32[]{:T(128)S(6)} %select_n.265, s32[]{:T(128)} %constant.223.clone.1) | dynamic-update-slice | bytes 786436 | tf_op jit(solution)/shard_map/dynamic_update_slice | solution.py:327
  499.9 6.1 fusion.27
  518.0 9.7 %collective-permute-done.57 = bf16[2,144,768]{2,1,0:T(8,128)(2,1)S(1)} collective-permute-done((bf16[2,144,768]{2,1,0:T(8,128)(2,1)S(1)}, bf16[2,144,768]{2,1,0:T(8,128)(2,1)S(1)}, u32[]{:S(2)}, u32[]{:S(2)}) %collective-permute-start.57) | collective-permute-done | bytes 442400 | tf_op jit(solution)/shard_map/ppermute | solution.py:60
  544.2 8.6 %collective-permute-done.59 = bf16[144,768]{1,0:T(8,128)(2,1)S(1)} collective-permute-done((bf16[144,768]{1,0:T(8,128)(2,1)S(1)}, bf16[144,768]{1,0:T(8,128)(2,1)S(1)}, u32[]{:S(2)}, u32[]{:S(2)}) %collective-permute-start.59) | collective-permute-done | bytes 221216 | tf_op jit(solution)/shard_map/ppermute | solution.py:63
  560.1 4.8 collective-permute-done.64
  567.9 12.0 %collective-permute-done.66 = bf16[1,72,768]{2,1,0:T(8,128)(2,1)S(1)} collective-permute-done((bf16[1,72,768]{2,1,0:T(8,128)(2,1)S(1)}, bf16[1,72,768]{2,1,0:T(8,128)(2,1)S(1)}, u32[]{:S(2)}, u32[]{:S(2)}) %collective-permute-start.66) | collective-permute-done | bytes 110624 | tf_op jit(solution)/shard_map/ppermute | solution.py:60
  586.5 6.5 %collective-permute-done.97 = bf16[2,192,768]{2,1,0:T(8,128)(2,1)S(1)} collective-permute-done((bf16[2,192,768]{2,1,0:T(8,128)(2,1)S(1)}, bf16[2,192,768]{2,1,0:T(8,128)(2,1)S(1)}, u32[]{:S(2)}, u32[]{:S(2)}) %collective-permute-start.97) | collective-permute-done | bytes 589856 | tf_op jit(solution)/shard_map/ppermute | solution.py:60
  604.2 17.0 %collective-permute-done.106 = bf16[192,768]{1,0:T(8,128)(2,1)S(1)} collective-permute-done((bf16[192,768]{1,0:T(8,128)(2,1)S(1)}, bf16[192,768]{1,0:T(8,128)(2,1)S(1)}, u32[]{:S(2)}, u32[]{:S(2)}) %collective-permute-start.106) | collective-permute-done | bytes 294944 | tf_op jit(solution)/shard_map/ppermute | solution.py:63
  629.3 5.8 collective-permute-done.111
  (768 shorter events, 349.9 us)
Async XLA Ops:
  4.2 43.6 %collective-permute-start.2 = (bf16[144,768]{1,0:T(8,128)(2,1)}, bf16[144,768]{1,0:T(8,128)(2,1)S(1)}, u32[]{:S(2)}, u32[]{:S(2)}) collective-permute-start(bf16[144,768]{1,0:T(8,128)(2,1)} %get-tuple-element.108), channel_id=1, source_target_pairs={{0,3},{1,0},{2,1},{3,2},{4,7},{5,4},{6,5},{7,6},{8,11},{9,8},{10,9... | collective-permute-start | bytes 663560 | tf_op jit(solution)/shard_map/ppermute | solution.py:63
  4.2 45.0 %collective-permute-start.1 = (bf16[144,768]{1,0:T(8,128)(2,1)}, bf16[144,768]{1,0:T(8,128)(2,1)S(1)}, u32[]{:S(2)}, u32[]{:S(2)}) collective-permute-start(bf16[144,768]{1,0:T(8,128)(2,1)} %get-tuple-element.108), channel_id=1, source_target_pairs={{0,2},{1,3},{2,0},{3,1},{4,6},{5,7},{6,4},{7,5},{8,10},{9,11},{10,... | collective-permute-start | bytes 663560 | tf_op jit(solution)/shard_map/ppermute | solution.py:63
  8.0 27.8 %collective-permute-start.12 = (f32[1536]{0:T(1024)S(1)}, f32[1536]{0:T(1024)S(1)}, u32[]{:S(2)}, u32[]{:S(2)}) collective-permute-start(f32[1536]{0:T(1024)S(1)} %constant_dynamic-update-slice_fusion.18), channel_id=1, source_target_pairs={{0,2},{1,3},{2,0},{3,1},{4,6},{5,7},{6,4},{7,5},{8,10},{9,11},{10,... | collective-permute-start | bytes 18440 | tf_op jit(solution)/shard_map/ppermute | solution.py:63
  49.2 36.1 %collective-permute-start.17 = (bf16[4,48,768]{2,1,0:T(8,128)(2,1)S(1)}, bf16[4,48,768]{2,1,0:T(8,128)(2,1)S(1)}, u32[]{:S(2)}, u32[]{:S(2)}) collective-permute-start(bf16[4,48,768]{2,1,0:T(8,128)(2,1)S(1)} %pad_maximum_fusion.8), channel_id=1, source_target_pairs={{0,4},{4,0},{8,12},{12,8},{16,20},{20,16},{24,28},{28,24},{1,5},{5... | collective-permute-start | bytes 884744 | tf_op jit(solution)/shard_map/ppermute | solution.py:60
  53.0 30.1 %collective-permute-start.18 = (bf16[4,48,768]{2,1,0:T(8,128)(2,1)S(1)}, bf16[4,48,768]{2,1,0:T(8,128)(2,1)S(1)}, u32[]{:S(2)}, u32[]{:S(2)}) collective-permute-start(bf16[4,48,768]{2,1,0:T(8,128)(2,1)S(1)} %pad_maximum_fusion.8), channel_id=1, source_target_pairs={{0,8},{4,12},{8,0},{12,4},{16,24},{20,28},{24,16},{28,20},{1,9},{5... | collective-permute-start | bytes 884744 | tf_op jit(solution)/shard_map/ppermute | solution.py:60
  73.4 31.7 %collective-permute-start.26 = (bf16[192,1024]{1,0:T(8,128)(2,1)S(1)}, bf16[192,1024]{1,0:T(8,128)(2,1)S(1)}, u32[]{:S(2)}, u32[]{:S(2)}) collective-permute-start(bf16[192,1024]{1,0:T(8,128)(2,1)S(1)} %copy-done.49), channel_id=1, source_target_pairs={{0,2},{1,3},{2,0},{3,1},{4,6},{5,7},{6,4},{7,5},{8,10},{9,11},{10,... | collective-permute-start | bytes 1179656 | tf_op jit(solution)/shard_map/ppermute | solution.py:63
  83.2 56.5 %collective-permute-start.3 = (bf16[4,144,768]{2,1,0:T(8,128)(2,1)S(1)}, bf16[4,144,768]{2,1,0:T(8,128)(2,1)S(1)}, u32[]{:S(2)}, u32[]{:S(2)}) collective-permute-start(bf16[4,144,768]{2,1,0:T(8,128)(2,1)S(1)} %pad_maximum_fusion.4), channel_id=1, source_target_pairs={{0,4},{4,0},{8,12},{12,8},{16,20},{20,16},{24,28},{28,24},{1,5},{5... | collective-permute-start | bytes 2654216 | tf_op jit(solution)/shard_map/ppermute | solution.py:60
  85.3 55.6 %collective-permute-start.4 = (bf16[4,144,768]{2,1,0:T(8,128)(2,1)S(1)}, bf16[4,144,768]{2,1,0:T(8,128)(2,1)S(1)}, u32[]{:S(2)}, u32[]{:S(2)}) collective-permute-start(bf16[4,144,768]{2,1,0:T(8,128)(2,1)S(1)} %pad_maximum_fusion.4), channel_id=1, source_target_pairs={{0,8},{4,12},{8,0},{12,4},{16,24},{20,28},{24,16},{28,20},{1,9},{5... | collective-permute-start | bytes 2654216 | tf_op jit(solution)/shard_map/ppermute | solution.py:60
  112.9 29.6 %collective-permute-start.31 = (bf16[4,192,768]{2,1,0:T(8,128)(2,1)S(1)}, bf16[4,192,768]{2,1,0:T(8,128)(2,1)S(1)}, u32[]{:S(2)}, u32[]{:S(2)}) collective-permute-start(bf16[4,192,768]{2,1,0:T(8,128)(2,1)S(1)} %pad_maximum_fusion.3), channel_id=1, source_target_pairs={{0,4},{4,0},{8,12},{12,8},{16,20},{20,16},{24,28},{28,24},{1,5},{5... | collective-permute-start | bytes 3538952 | tf_op jit(solution)/shard_map/ppermute | solution.py:60
  117.8 46.0 %collective-permute-start.32 = (bf16[4,192,768]{2,1,0:T(8,128)(2,1)S(1)}, bf16[4,192,768]{2,1,0:T(8,128)(2,1)}, u32[]{:S(2)}, u32[]{:S(2)}) collective-permute-start(bf16[4,192,768]{2,1,0:T(8,128)(2,1)S(1)} %pad_maximum_fusion.3), channel_id=1, source_target_pairs={{0,8},{4,12},{8,0},{12,4},{16,24},{20,28},{24,16},{28,20},{1,9},{5... | collective-permute-start | bytes 3538952 | tf_op jit(solution)/shard_map/ppermute | solution.py:60
  139.7 28.9 %collective-permute-start.8 = (bf16[2,144,768]{2,1,0:T(8,128)(2,1)S(1)}, bf16[2,144,768]{2,1,0:T(8,128)(2,1)S(1)}, u32[]{:S(2)}, u32[]{:S(2)}) collective-permute-start(bf16[2,144,768]{2,1,0:T(8,128)(2,1)S(1)} %slice.494), channel_id=1, source_target_pairs={{0,8},{4,12},{8,0},{12,4},{16,24},{20,28},{24,16},{28,20},{1,9},{5... | collective-permute-start | bytes 1327112 | tf_op jit(solution)/shard_map/ppermute | solution.py:60
  141.0 29.9 %collective-permute-start.5 = (bf16[4,144,768]{2,1,0:T(8,128)(2,1)S(1)}, bf16[4,144,768]{2,1,0:T(8,128)(2,1)S(1)}, u32[]{:S(2)}, u32[]{:S(2)}) collective-permute-start(bf16[4,144,768]{2,1,0:T(8,128)(2,1)S(1)} %collective-permute-done.4), channel_id=1, source_target_pairs={{0,4},{4,0},{8,12},{12,8},{16,20},{20,16},{24,28},{28,24},{1,5},{5... | collective-permute-start | bytes 2654216 | tf_op jit(solution)/shard_map/ppermute | solution.py:60
  169.8 37.6 %collective-permute-start.33 = (bf16[4,192,768]{2,1,0:T(8,128)(2,1)}, bf16[4,192,768]{2,1,0:T(8,128)(2,1)}, u32[]{:S(2)}, u32[]{:S(2)}) collective-permute-start(bf16[4,192,768]{2,1,0:T(8,128)(2,1)} %collective-permute-done.32), channel_id=1, source_target_pairs={{0,4},{4,0},{8,12},{12,8},{16,20},{20,16},{24,28},{28,24},{1,5},{5... | collective-permute-start | bytes 3538952 | tf_op jit(solution)/shard_map/ppermute | solution.py:60
  171.1 41.1 %collective-permute-start.35 = (bf16[4,192,768]{2,1,0:T(8,128)(2,1)}, bf16[4,192,768]{2,1,0:T(8,128)(2,1)}, u32[]{:S(2)}, u32[]{:S(2)}) collective-permute-start(bf16[4,192,768]{2,1,0:T(8,128)(2,1)} %collective-permute-done.34), channel_id=1, source_target_pairs={{0,4},{4,0},{8,12},{12,8},{16,20},{20,16},{24,28},{28,24},{1,5},{5... | collective-permute-start | bytes 3538952 | tf_op jit(solution)/shard_map/ppermute | solution.py:60
  184.2 32.8 %collective-permute-start.38 = (bf16[4,192,768]{2,1,0:T(8,128)(2,1)}, bf16[4,192,768]{2,1,0:T(8,128)(2,1)}, u32[]{:S(2)}, u32[]{:S(2)}) collective-permute-start(bf16[4,192,768]{2,1,0:T(8,128)(2,1)} %constant_dynamic-update-slice_fusion.5), channel_id=1, source_target_pairs={{0,4},{4,0},{8,12},{12,8},{16,20},{20,16},{24,28},{28,24},{1,5},{5... | collective-permute-start | bytes 3538952 | tf_op jit(solution)/shard_map/ppermute | solution.py:60
  271.4 70.1 %collective-permute-start.44 = (bf16[128,768]{1,0:T(8,128)(2,1)}, bf16[128,768]{1,0:T(8,128)(2,1)}, u32[]{:S(2)}, u32[]{:S(2)}) collective-permute-start(bf16[128,768]{1,0:T(8,128)(2,1)} %fusion.120), channel_id=1, source_target_pairs={{0,3},{1,0},{2,1},{3,2},{4,7},{5,4},{6,5},{7,6},{8,11},{9,8},{10,9... | collective-permute-start | bytes 589832 | tf_op jit(solution)/shard_map/ppermute | solution.py:63
  271.4 90.1 %collective-permute-start.43 = (bf16[128,768]{1,0:T(8,128)(2,1)}, bf16[128,768]{1,0:T(8,128)(2,1)}, u32[]{:S(2)}, u32[]{:S(2)}) collective-permute-start(bf16[128,768]{1,0:T(8,128)(2,1)} %fusion.120), channel_id=1, source_target_pairs={{0,2},{1,3},{2,0},{3,1},{4,6},{5,7},{6,4},{7,5},{8,10},{9,11},{10,... | collective-permute-start | bytes 589832 | tf_op jit(solution)/shard_map/ppermute | solution.py:63
  272.6 88.9 %collective-permute-start.42 = (bf16[128,768]{1,0:T(8,128)(2,1)}, bf16[128,768]{1,0:T(8,128)(2,1)}, u32[]{:S(2)}, u32[]{:S(2)}) collective-permute-start(bf16[128,768]{1,0:T(8,128)(2,1)} %fusion.120), channel_id=1, source_target_pairs={{0,1},{1,2},{2,3},{3,0},{4,5},{5,6},{6,7},{7,4},{8,9},{9,10},{10,1... | collective-permute-start | bytes 589832 | tf_op jit(solution)/shard_map/ppermute | solution.py:63
  307.5 58.0 %collective-permute-start.41 = (bf16[128,768]{1,0:T(8,128)(2,1)S(1)}, bf16[128,768]{1,0:T(8,128)(2,1)S(1)}, u32[]{:S(2)}, u32[]{:S(2)}) collective-permute-start(bf16[128,768]{1,0:T(8,128)(2,1)S(1)} %copy-done.46), channel_id=1, source_target_pairs={{0,3},{1,0},{2,1},{3,2},{4,7},{5,4},{6,5},{7,6},{8,11},{9,8},{10,9... | collective-permute-start | bytes 589832 | tf_op jit(solution)/shard_map/ppermute | solution.py:63
  361.5 52.9 %collective-permute-start.45 = (bf16[192,1024]{1,0:T(8,128)(2,1)}, bf16[192,1024]{1,0:T(8,128)(2,1)}, u32[]{:S(2)}, u32[]{:S(2)}) collective-permute-start(bf16[192,1024]{1,0:T(8,128)(2,1)} %get-tuple-element.80), channel_id=1, source_target_pairs={{0,1},{1,2},{2,3},{3,0},{4,5},{5,6},{6,7},{7,4},{8,9},{9,10},{10,1... | collective-permute-start | bytes 1179656 | tf_op jit(solution)/shard_map/ppermute | solution.py:63
  372.5 47.7 %collective-permute-start.46 = (bf16[192,1024]{1,0:T(8,128)(2,1)}, bf16[192,1024]{1,0:T(8,128)(2,1)S(1)}, u32[]{:S(2)}, u32[]{:S(2)}) collective-permute-start(bf16[192,1024]{1,0:T(8,128)(2,1)} %get-tuple-element.79), channel_id=1, source_target_pairs={{0,2},{1,3},{2,0},{3,1},{4,6},{5,7},{6,4},{7,5},{8,10},{9,11},{10,... | collective-permute-start | bytes 1179656 | tf_op jit(solution)/shard_map/ppermute | solution.py:63
  372.9 36.7 %collective-permute-start.74 = (bf16[4,48,768]{2,1,0:T(8,128)(2,1)S(1)}, bf16[4,48,768]{2,1,0:T(8,128)(2,1)S(1)}, u32[]{:S(2)}, u32[]{:S(2)}) collective-permute-start(bf16[4,48,768]{2,1,0:T(8,128)(2,1)S(1)} %copy-done.52), channel_id=1, source_target_pairs={{0,4},{4,0},{8,12},{12,8},{16,20},{20,16},{24,28},{28,24},{1,5},{5... | collective-permute-start | bytes 884744 | tf_op jit(solution)/shard_map/ppermute | solution.py:60
  410.8 64.2 %collective-permute-start.86 = (bf16[48,768]{1,0:T(8,128)(2,1)S(1)}, bf16[48,768]{1,0:T(8,128)(2,1)S(1)}, u32[]{:S(2)}, u32[]{:S(2)}) collective-permute-start(bf16[48,768]{1,0:T(8,128)(2,1)S(1)} %get-tuple-element.101), channel_id=1, source_target_pairs={{0,1},{1,2},{2,3},{3,0},{4,5},{5,6},{6,7},{7,4},{8,9},{9,10},{10,1... | collective-permute-start | bytes 221192 | tf_op jit(solution)/shard_map/ppermute | solution.py:63
  410.9 64.1 %collective-permute-start.85 = (bf16[48,768]{1,0:T(8,128)(2,1)S(1)}, bf16[48,768]{1,0:T(8,128)(2,1)S(1)}, u32[]{:S(2)}, u32[]{:S(2)}) collective-permute-start(bf16[48,768]{1,0:T(8,128)(2,1)S(1)} %get-tuple-element.102), channel_id=1, source_target_pairs={{0,2},{1,3},{2,0},{3,1},{4,6},{5,7},{6,4},{7,5},{8,10},{9,11},{10,... | collective-permute-start | bytes 221192 | tf_op jit(solution)/shard_map/ppermute | solution.py:63
  414.4 60.6 %collective-permute-start.84 = (bf16[48,768]{1,0:T(8,128)(2,1)S(1)}, bf16[48,768]{1,0:T(8,128)(2,1)}, u32[]{:S(2)}, u32[]{:S(2)}) collective-permute-start(bf16[48,768]{1,0:T(8,128)(2,1)S(1)} %get-tuple-element.100), channel_id=1, source_target_pairs={{0,3},{1,0},{2,1},{3,2},{4,7},{5,4},{6,5},{7,6},{8,11},{9,8},{10,9... | collective-permute-start | bytes 221192 | tf_op jit(solution)/shard_map/ppermute | solution.py:63
  420.2 68.3 %collective-permute-start.51 = (bf16[4,144,768]{2,1,0:T(8,128)(2,1)}, bf16[4,144,768]{2,1,0:T(8,128)(2,1)}, u32[]{:S(2)}, u32[]{:S(2)}) collective-permute-start(bf16[4,144,768]{2,1,0:T(8,128)(2,1)} %get-tuple-element.58), channel_id=1, source_target_pairs={{0,4},{4,0},{8,12},{12,8},{16,20},{20,16},{24,28},{28,24},{1,5},{5... | collective-permute-start | bytes 2654216 | tf_op jit(solution)/shard_map/ppermute | solution.py:60
  426.2 63.8 %collective-permute-start.49 = (bf16[4,144,768]{2,1,0:T(8,128)(2,1)}, bf16[4,144,768]{2,1,0:T(8,128)(2,1)}, u32[]{:S(2)}, u32[]{:S(2)}) collective-permute-start(bf16[4,144,768]{2,1,0:T(8,128)(2,1)} %get-tuple-element.57), channel_id=1, source_target_pairs={{0,4},{4,0},{8,12},{12,8},{16,20},{20,16},{24,28},{28,24},{1,5},{5... | collective-permute-start | bytes 2654216 | tf_op jit(solution)/shard_map/ppermute | solution.py:60
  490.0 41.6 %collective-permute-start.48 = (bf16[4,144,768]{2,1,0:T(8,128)(2,1)S(1)}, bf16[4,144,768]{2,1,0:T(8,128)(2,1)}, u32[]{:S(2)}, u32[]{:S(2)}) collective-permute-start(bf16[4,144,768]{2,1,0:T(8,128)(2,1)S(1)} %copy-done.35), channel_id=1, source_target_pairs={{0,4},{4,0},{8,12},{12,8},{16,20},{20,16},{24,28},{28,24},{1,5},{5... | collective-permute-start | bytes 2654216 | tf_op jit(solution)/shard_map/ppermute | solution.py:60
  499.0 30.1 %collective-permute-start.50 = (bf16[2,144,768]{2,1,0:T(8,128)(2,1)}, bf16[2,144,768]{2,1,0:T(8,128)(2,1)}, u32[]{:S(2)}, u32[]{:S(2)}) collective-permute-start(bf16[2,144,768]{2,1,0:T(8,128)(2,1)} %slice.686), channel_id=1, source_target_pairs={{0,8},{4,12},{8,0},{12,4},{16,24},{20,28},{24,16},{28,20},{1,9},{5... | collective-permute-start | bytes 1327112 | tf_op jit(solution)/shard_map/ppermute | solution.py:60
  515.9 80.6 %collective-permute-start.95 = (bf16[4,192,768]{2,1,0:T(8,128)(2,1)S(1)}, bf16[4,192,768]{2,1,0:T(8,128)(2,1)S(1)}, u32[]{:S(2)}, u32[]{:S(2)}) collective-permute-start(bf16[4,192,768]{2,1,0:T(8,128)(2,1)S(1)} %copy-done.31), channel_id=1, source_target_pairs={{0,4},{4,0},{8,12},{12,8},{16,20},{20,16},{24,28},{28,24},{1,5},{5... | collective-permute-start | bytes 3538952 | tf_op jit(solution)/shard_map/ppermute | solution.py:60
  529.1 28.3 %collective-permute-start.100 = (bf16[2,192,768]{2,1,0:T(8,128)(2,1)S(1)}, bf16[2,192,768]{2,1,0:T(8,128)(2,1)}, u32[]{:S(2)}, u32[]{:S(2)}) collective-permute-start(bf16[2,192,768]{2,1,0:T(8,128)(2,1)S(1)} %get-tuple-element.88), channel_id=1, source_target_pairs={{0,8},{4,12},{8,0},{12,4},{16,24},{20,28},{24,16},{28,20},{1,9},{5... | collective-permute-start | bytes 1769480 | tf_op jit(solution)/shard_map/ppermute | solution.py:60
  544.0 39.4 %collective-permute-start.102 = (bf16[2,192,768]{2,1,0:T(8,128)(2,1)S(1)}, bf16[2,192,768]{2,1,0:T(8,128)(2,1)S(1)}, u32[]{:S(2)}, u32[]{:S(2)}) collective-permute-start(bf16[2,192,768]{2,1,0:T(8,128)(2,1)S(1)} %slice.683), channel_id=1, source_target_pairs={{0,16},{4,20},{8,24},{12,28},{16,0},{20,4},{24,8},{28,12},{1,17},{... | collective-permute-start | bytes 1769480 | tf_op jit(solution)/shard_map/ppermute | solution.py:60
  (209 other events, 2022.8 us)

commit v2 on v1

v2 whole, which is shorter than its diff:
```python
import jax
import jax.numpy as jnp
from jax import lax
from jax.experimental import pallas as pl
from jax.experimental.pallas import tpu as pltpu
from jax.sharding import PartitionSpec as P

HD = 64
SUB = 8
NEG_FILL = -1000000000.0
EPSILON = 1e-05
F32 = jnp.float32
BF16 = jnp.bfloat16
VMEM = pltpu.VMEM
ROOT_HALF = 0.7071067811865476
ROOT_TWO_PI = 0.3989422804014327
SLOTS = ((3, 0), (1, 0), (3, 1), (2, 1), (1, 1), (2, 0), (0, 0), (0, 1))


def nn(left, right):
    return lax.dot_general(left, right, (((1,), (0,)), ((), ())), preferred_element_type=F32)


def nt(left, right):
    return lax.dot_general(left, right, (((1,), (1,)), ((), ())), preferred_element_type=F32)


def tn(left, right):
    return lax.dot_general(left, right, (((0,), (0,)), ((), ())), preferred_element_type=F32)


def normed(values):
    average = jnp.mean(values, -1, keepdims=True)
    centered = values - average
    variance = jnp.mean(centered * centered, -1, keepdims=True)
    inverse = lax.rsqrt(variance + EPSILON)
    return centered * inverse, inverse


def norm_back(unit, inverse, gain, grad):
    scaled = grad * gain
    return (
        scaled
        - jnp.mean(scaled, -1, keepdims=True)
        - unit * jnp.mean(scaled * unit, -1, keepdims=True)
    ) * inverse


def row_sum(values):
    return jnp.sum(values, 0, keepdims=True)


def segments(meta, start, count, shape, axis):
    places = lax.broadcasted_iota(jnp.int32, shape, axis)
    found = jnp.zeros(shape, jnp.int32) - 1
    for j in range(count):
        found = found + (meta[start + j] <= places).astype(jnp.int32)
    return found, places


def fetch(pieces, place, target, low, high, sem):
    size = high - low
    half = pieces[0].shape[1] // 2
    blocks = pieces[0].shape[0]
    part = low // half
    for beside in (0, 1):
        whole = pieces[5 * beside : 5 * beside + 3]
        split = pieces[5 * beside + 3 : 5 * beside + 5]
        for offset in range(4):
            row = pl.multiple_of((place ^ (offset + 4 * beside)) * size, 16)
            for block in range(blocks):
                if offset < 3:
                    source = whole[offset].at[block, pl.ds(low, size)]
                else:
                    at = 2 * block + part
                    source = split[at // blocks].at[at % blocks, pl.ds(low - half * part, size)]
                pltpu.make_async_copy(source, target.at[block + 1, pl.ds(row, size)], sem).start()


def fetch_own(source, target, low, sem):
    size = source.shape[0]
    pltpu.make_async_copy(source, target.at[0, pl.ds(low, size)], sem).start()


def arrive(target, sem):
    pltpu.make_async_copy(target, target, sem).wait()


def fetch_memory(blocks, line, target, sem):
    count = len(blocks)
    for step, block in enumerate(blocks):
        size = block.shape[0]
        row = pl.multiple_of(lax.rem(line + count - step, count) * size, 16)
        pltpu.make_async_copy(block, target.at[pl.ds(row, size)], sem).start()


def slot_of(offset, half):
    first = SLOTS.index((offset, 0))
    second = SLOTS.index((offset, 1))
    return jnp.where(half == 0, first, second)


def self_forward(dims, meta, x_ref, sb, cb, ob, gain, bias, *refs):
    mp, local, heads, scaling, nseg = dims
    pieces, (own_self, own_cq, own_sp, own_cp) = refs[:10], refs[10:14]
    qkv, low, z1, first, cq = refs[14:19]
    wa, wp, acc, sems = refs[19:]
    place = meta[0]
    fetch(pieces, place, wa, 0, 96, sems.at[0])
    fetch_own(own_self, wa, 0, sems.at[0])
    fetch_own(own_cq, wa, 3 * local, sems.at[0])
    fetch(pieces, place, wp, 96, 144, sems.at[1])
    fetch_own(own_sp, wp, 0, sems.at[1])
    fetch_own(own_cp, wp, local, sems.at[1])
    slots = x_ref.shape[0]
    shape = (slots, slots)
    query_segment, query_place = segments(meta, 4, nseg, shape, 0)
    key_segment, key_place = segments(meta, 4, nseg, shape, 1)
    allowed = (
        (query_segment == key_segment) & (key_place <= query_place) & (key_place < meta[2])
    )
    acc[...] = x_ref[...].astype(F32) + ob[0:1]
    arrive(wa, sems.at[0])
    arrive(wp, sems.at[1])

    def step(z, carry):
        flat = nt(x_ref[...], wa[z, : 3 * local])
        rows = sb[z]
        qkv[z, :, :local] = ((flat[:, :local] + rows[0:1]) * scaling).astype(BF16)
        qkv[z, :, local : 2 * local] = flat[:, local : 2 * local].astype(BF16)
        qkv[z, :, 2 * local :] = (flat[:, 2 * local :] + rows[1:2]).astype(BF16)
        for i in range(heads):
            at = HD * i
            scores = nt(
                qkv[z, :, at : at + HD], qkv[z, :, local + at : local + at + HD]
            )
            scores = jnp.where(allowed, scores, NEG_FILL)
            weights = jnp.exp(scores - jnp.max(scores, -1, keepdims=True))
            probs = (weights / jnp.sum(weights, -1, keepdims=True)).astype(BF16)
            out = nn(probs, qkv[z, :, 2 * local + at : 2 * local + at + HD])
            low[z, :, at : at + HD] = out.astype(BF16)
        acc[...] += nn(low[z], wp[z, :local])
        return carry

    lax.fori_loop(0, mp, step, 0)
    z1[...] = acc[...]
    unit, _ = normed(acc[...])
    values = unit * gain[0:1] + bias[0:1]
    first[...] = values
    values = values.astype(BF16)

    def query(z, carry):
        rows = cb[z]
        cq[z] = ((nt(values, wa[z, 3 * local :]) + rows[0:1]) * scaling).astype(BF16)
        return carry

    lax.fori_loop(0, mp, query, 0)


def cross_mask(meta, nseg, slots, mem_slots):
    query_segment, _ = segments(meta, 4, nseg, (slots, 1), 0)
    key_segment, key_place = segments(meta, 4 + nseg, nseg, (1, mem_slots), 1)
    key_segment = jnp.where(key_place < meta[3], key_segment, -1)
    return query_segment == key_segment


def cross_forward(dims, meta, cq, cb, ob, gain, bias, first, *refs):
    mp, local, heads, scaling, nseg = dims
    blocks, pieces, (own_kv, own_sp, own_cp) = refs[:mp], refs[mp : mp + 10], refs[mp + 10 : mp + 13]
    kv, low, total, z2, second = refs[mp + 13 : mp + 18]
    wk, wp, mem, acc, sems = refs[mp + 18 :]
    place = meta[0]
    fetch_memory(blocks, meta[1], mem, sems.at[2])
    fetch(pieces, place, wk, 144, 192, sems.at[0])
    fetch_own(own_kv, wk, 0, sems.at[0])
    fetch(pieces, place, wp, 96, 144, sems.at[1])
    fetch_own(own_sp, wp, 0, sems.at[1])
    fetch_own(own_cp, wp, local, sems.at[1])
    allowed = cross_mask(meta, nseg, first.shape[0], mem.shape[1])
    acc[...] = first[...] + ob[1:2]
    arrive(wk, sems.at[0])
    arrive(mem, sems.at[2])
    arrive(wp, sems.at[1])

    def step(z, carry):
        flat = nn(wk[z], mem[...])
        column = jnp.swapaxes(jnp.broadcast_to(cb[z][1:2], (8, local)), 0, 1)[:, :1]
        kv[z, :local] = flat[:local].astype(BF16)
        kv[z, local:] = (flat[local:] + column).astype(BF16)
        for i in range(heads):
            at = HD * i
            scores = nn(cq[z, :, at : at + HD], kv[z, at : at + HD])
            scores = jnp.where(allowed, scores, NEG_FILL)
            peak = jnp.max(scores, -1, keepdims=True)
            weights = jnp.exp(scores - peak)
            mass = jnp.sum(weights, -1, keepdims=True)
            probs = (weights / mass).astype(BF16)
            low[z, :, at : at + HD] = nt(probs, kv[z, local + at : local + at + HD]).astype(BF16)
            total[z * heads + i] = peak + jnp.log(mass)
        acc[...] += nn(low[z], wp[z, local:])
        return carry

    lax.fori_loop(0, mp, step, 0)
    z2[...] = acc[...]
    unit, _ = normed(acc[...])
    second[...] = unit * gain[1:2] + bias[1:2]


def put_slots(beside, mine, place, z, base, size, source):
    half = lax.div(z, 2)
    at = lax.rem(z, 2)
    for offset in range(4):
        slot = slot_of(offset, half)
        for target, flip in ((mine, 0), (beside, 4)):
            row = pl.multiple_of((place ^ (offset + flip)) * size, 16)
            target[slot, at, base : base + size] = source[pl.ds(row, size)].astype(BF16)


def ffn_both(dims, meta, second, z2, grad, ib, ob, gain, bias, *refs):
    mp, local, heads, scaling, nseg = dims
    pieces, (own_in, own_out) = refs[:10], refs[10:12]
    result, dz2, sums, beside, mine = refs[12:17]
    win, wout, acc, act, slope, dw, sems = refs[17:]
    place = meta[0]
    fetch(pieces, place, win, 0, 96, sems.at[0])
    fetch_own(own_in, win, 0, sems.at[0])
    fetch(pieces, place, wout, 96, 192, sems.at[1])
    fetch_own(own_out, wout, 0, sems.at[1])
    acc[...] = second[...] + ob[2:3]
    second_low = second[...].astype(BF16)
    arrive(win, sems.at[0])
    arrive(wout, sems.at[1])

    def forward(z, carry):
        inner = nn(second_low, win[z]) + ib[z]
        share = 0.5 * (1.0 + lax.erf(inner * ROOT_HALF))
        act[z] = (inner * share).astype(BF16)
        slope[z] = share + inner * (ROOT_TWO_PI * jnp.exp(-0.5 * inner * inner))
        acc[...] += nn(act[z], wout[z])
        return carry

    lax.fori_loop(0, mp, forward, 0)
    unit, inverse = normed(acc[...])
    result[...] = (unit * gain[2:3] + bias[2:3]).astype(BF16)
    out_grad = grad[...].astype(F32)
    third = norm_back(unit, inverse, gain[2:3], out_grad)
    sums[...] = jnp.zeros_like(sums)
    sums[0:1] = row_sum(third)
    sums[1:2] = row_sum(out_grad * unit)
    sums[2:3] = row_sum(out_grad)
    third_low = third.astype(BF16)
    acc[...] = third

    def backward(z, carry):
        inner = nt(third_low, wout[z]) * slope[z]
        sums[pl.ds(8 + z, 1)] = row_sum(inner)
        inner_low = inner.astype(BF16)
        acc[...] += nt(inner_low, win[z])
        dw[...] = tn(second_low, inner_low)
        put_slots(beside, mine, place, z, 0, 96, dw)
        dw[...] = tn(act[z], third_low)
        put_slots(beside, mine, place, z, 96, 96, dw)
        return carry

    lax.fori_loop(0, mp, backward, 0)
    unit, inverse = normed(z2[...])
    grad_rows = acc[...]
    values = norm_back(unit, inverse, gain[1:2], grad_rows)
    dz2[...] = values
    sums[3:4] = row_sum(values)
    sums[4:5] = row_sum(grad_rows * unit)
    sums[5:6] = row_sum(grad_rows)


def cross_back(dims, meta, dz2, cq, total, z1, gain, *refs):
    mp, local, heads, scaling, nseg = dims
    kv_ref, pieces, owns = refs[0], refs[1:11], refs[11:16]
    own_self, own_cq, own_kv, own_sp, own_cp = owns
    mem_out, kv_low, dcq, dz1, sums, sums_local = refs[16:22]
    wa, wk, wp, kv, dmem, acc, dout, sems = refs[22:]
    place = meta[0]
    pltpu.make_async_copy(kv_ref, kv, sems.at[3]).start()
    fetch(pieces, place, wp, 96, 144, sems.at[1])
    fetch_own(own_sp, wp, 0, sems.at[1])
    fetch_own(own_cp, wp, local, sems.at[1])
    fetch(pieces, place, wk, 144, 192, sems.at[0])
    fetch_own(own_kv, wk, 0, sems.at[0])
    fetch(pieces, place, wa, 0, 96, sems.at[2])
    fetch_own(own_self, wa, 0, sems.at[2])
    fetch_own(own_cq, wa, 3 * local, sems.at[2])
    allowed = cross_mask(meta, nseg, dz2.shape[0], kv.shape[2])
    dz2_low = dz2[...].astype(BF16)
    acc[...] = dz2[...]
    dmem[...] = jnp.zeros_like(dmem)
    arrive(kv, sems.at[3])
    arrive(wp, sems.at[1])
    arrive(wk, sems.at[0])
    arrive(wa, sems.at[2])

    def step(z, carry):
        dout[...] = nt(dz2_low, wp[z, local:]).astype(BF16)
        for i in range(heads):
            at = HD * i
            query = cq[z, :, at : at + HD]
            key = kv[z, at : at + HD]
            value = kv[z, local + at : local + at + HD]
            grad = dout[:, at : at + HD]
            scores = jnp.where(allowed, nn(query, key), NEG_FILL)
            probs = jnp.exp(scores - total[z * heads + i])
            probs_low = probs.astype(BF16)
            prob_grad = nn(grad, value)
            offset = jnp.sum(probs * prob_grad, -1, keepdims=True)
            score_grad = (probs * (prob_grad - offset)).astype(BF16)
            kv_low[z, at : at + HD] = tn(query, score_grad).astype(BF16)
            kv_low[z, local + at : local + at + HD] = tn(grad, probs_low).astype(BF16)
            mass = jnp.sum(probs_low.astype(F32), -1, keepdims=True)
            query_grad = nt(score_grad, key) * scaling
            dcq[z, :, at : at + HD] = query_grad.astype(BF16)
            sums_local[z, 0:1, at : at + HD] = row_sum(query_grad)
            sums_local[z, 1:2, at : at + HD] = row_sum(mass * grad.astype(F32))
        acc[...] += nn(dcq[z], wa[z, 3 * local :])
        dmem[...] += tn(wk[z], kv_low[z])
        return carry

    lax.fori_loop(0, mp, step, 0)
    for block in range(mp):
        row = pl.multiple_of(lax.rem(meta[1] + block, mp) * local, 16)
        mem_out[block] = dmem[pl.ds(row, local)].astype(BF16)
    unit, inverse = normed(z1[...])
    grad_rows = acc[...]
    values = norm_back(unit, inverse, gain[0:1], grad_rows)
    dz1[...] = values
    sums[...] = jnp.zeros_like(sums)
    sums[0:1] = row_sum(values)
    sums[1:2] = row_sum(grad_rows * unit)
    sums[2:3] = row_sum(grad_rows)


def self_back(dims, meta, dz1, dz2, x_ref, first, qkv, self_low, cross_low, dcq, *refs):
    mp, local, heads, scaling, nseg = dims
    kv_ref, blocks, pieces, owns = refs[0], refs[1 : 1 + mp], refs[1 + mp : 11 + mp], refs[11 + mp : 15 + mp]
    own_self, own_cq, own_sp, own_cp = owns
    dx, sums_local, beside, mine = refs[15 + mp : 19 + mp]
    wa, wp, kv, mem, acc, dout, dqkv, dwa, dwp, sems = refs[19 + mp :]
    place = meta[0]
    fetch(pieces, place, wp, 96, 144, sems.at[1])
    fetch_own(own_sp, wp, 0, sems.at[1])
    fetch_own(own_cp, wp, local, sems.at[1])
    fetch(pieces, place, wa, 0, 96, sems.at[0])
    fetch_own(own_self, wa, 0, sems.at[0])
    fetch_own(own_cq, wa, 3 * local, sems.at[0])
    pltpu.make_async_copy(kv_ref, kv, sems.at[2]).start()
    fetch_memory(blocks, meta[1], mem, sems.at[3])
    slots = x_ref.shape[0]
    shape = (slots, slots)
    query_segment, query_place = segments(meta, 4, nseg, shape, 0)
    key_segment, key_place = segments(meta, 4, nseg, shape, 1)
    allowed = (
        (query_segment == key_segment) & (key_place <= query_place) & (key_place < meta[2])
    )
    dz1_low = dz1[...].astype(BF16)
    dz2_low = dz2[...].astype(BF16)
    first_low = first[...].astype(BF16)
    acc[...] = dz1[...]
    arrive(wp, sems.at[1])
    arrive(wa, sems.at[0])
    arrive(kv, sems.at[2])
    arrive(mem, sems.at[3])

    def step(z, carry):
        dout[...] = nt(dz1_low, wp[z, :local]).astype(BF16)
        for i in range(heads):
            at = HD * i
            query = qkv[z, :, at : at + HD]
            key = qkv[z, :, local + at : local + at + HD]
            value = qkv[z, :, 2 * local + at : 2 * local + at + HD]
            grad = dout[:, at : at + HD]
            scores = jnp.where(allowed, nt(query, key), NEG_FILL)
            weights = jnp.exp(scores - jnp.max(scores, -1, keepdims=True))
            probs = weights / jnp.sum(weights, -1, keepdims=True)
            prob_grad = nt(grad, value)
            offset = jnp.sum(probs * prob_grad, -1, keepdims=True)
            score_grad = (probs * (prob_grad - offset)).astype(BF16)
            value_grad = tn(probs.astype(BF16), grad)
            query_grad = nn(score_grad, key) * scaling
            dqkv[:, at : at + HD] = query_grad.astype(BF16)
            dqkv[:, local + at : local + at + HD] = tn(score_grad, query).astype(BF16)
            dqkv[:, 2 * local + at : 2 * local + at + HD] = value_grad.astype(BF16)
            sums_local[z, 0:1, at : at + HD] = row_sum(query_grad)
            sums_local[z, 1:2, at : at + HD] = row_sum(value_grad)
        acc[...] += nn(dqkv[...], wa[z, : 3 * local])
        dwa[: 3 * local] = tn(dqkv[...], x_ref[...])
        dwa[3 * local :] = tn(dcq[z], first_low)
        put_slots(beside, mine, place, z, 0, 96, dwa)
        dwp[:local] = tn(self_low[z], dz1_low)
        dwp[local:] = tn(cross_low[z], dz2_low)
        put_slots(beside, mine, place, z, 96, 48, dwp)
        dwp[...] = nt(kv[z], mem[...])
        put_slots(beside, mine, place, z, 144, 48, dwp)
        return carry

    lax.fori_loop(0, mp, step, 0)
    dx[...] = acc[...]


def place_rows(place, ranges, low, over_two, over_four, near, far, across):
    half = near.shape[0]
    rows = low.shape[0]
    for offset in range(8):
        position = place ^ offset
        for start, size, targets in ranges:
            if offset >= 4:
                source = across[pl.ds((offset - 4) * rows + start, size)]
            elif offset == 3:
                source = (near if start < half else far)[pl.ds(start % half, size)]
            else:
                source = (low, over_two, over_four)[offset][pl.ds(start, size)]
            source = source.astype(F32)
            first = 0
            for target in targets:
                count = target.shape[0] // size

                @pl.when((position >= first) & (position < first + count))
                def _():
                    row = pl.multiple_of((position - first) * size, 8)
                    target[pl.ds(row, size)] = source

                first += count


def finish_heads(meta, low, over_two, over_four, near, far, across, gs, gq, gp, gc, gk):
    ranges = ((0, 96, (gs, gq)), (96, 48, (gp, gc)), (144, 48, (gk,)))
    place_rows(meta[0], ranges, low, over_two, over_four, near, far, across)


def finish_ffn(meta, low, over_two, over_four, near, far, across, gi, go):
    ranges = ((0, 96, (gi,)), (96, 96, (go,)))
    place_rows(meta[0], ranges, low, over_two, over_four, near, far, across)


def shaped(shape, dtype=F32):
    return jax.ShapeDtypeStruct(shape, dtype)


def in_vmem(count):
    return [pl.BlockSpec(memory_space=pltpu.VMEM)] * count


def in_place(count):
    return [pl.BlockSpec(memory_space=pl.ANY)] * count


META = pl.BlockSpec(memory_space=pltpu.SMEM)


def call(kernel, in_specs, outs, scratch, flops, moved, name):
    return pl.pallas_call(
        kernel,
        out_shape=outs,
        in_specs=in_specs,
        out_specs=in_vmem(len(outs)),
        scratch_shapes=scratch,
        name=name,
        compiler_params=pltpu.CompilerParams(vmem_limit_bytes=60 * 1024 * 1024),
        cost_estimate=pl.CostEstimate(flops=flops, bytes_accessed=moved, transcendentals=0),
    )


def solution(mesh):
    dp = mesh.shape["dp"]
    mp = mesh.shape["mp"]

    def swap(value, bit):
        return lax.ppermute(value, "dp", [(i, i ^ bit) for i in range(dp)])

    def shift(value, step):
        return lax.ppermute(value, "mp", [(i, (i + step) % mp) for i in range(mp)])

    def after(value, *others):
        return lax.optimization_barrier((value,) + others)[0]

    def gather_plane(own):
        blocks, rows, width = own.shape
        over_two = swap(own, 2)
        over_four = swap(own, 4)
        halves = (2 * blocks, rows // 2, width)
        near = swap(over_four.reshape(halves)[:blocks], 2)
        far = swap(over_two.reshape(halves)[blocks:], 4)
        mine = (own, over_two, over_four, near, far)
        return mine + tuple(swap(piece, 1) for piece in mine)

    def reduce_group(beside, mine):
        total = mine.astype(F32) + swap(beside, 1).astype(F32)
        low = total[:6].astype(BF16)
        from_two = swap(low[0:2], 2).astype(F32)
        from_four = swap(low[2:4], 4).astype(F32)
        late_four = swap((low[5].astype(F32) + from_two[0]).astype(BF16), 4)
        late_two = swap((low[4].astype(F32) + from_four[0]).astype(BF16), 2)
        top = total[6] + from_two[1] + late_four.astype(F32)
        end = total[7] + from_four[1] + late_two.astype(F32)
        bit = SUB
        while bit < dp:
            top = top + swap(top, bit)
            end = end + swap(end, bit)
            bit *= 2
        blocks = [top[0], top[1], end[0], end[1]]
        total = blocks[0]
        for step in range(1, mp):
            total = total + shift(blocks[step].astype(BF16), -step).astype(F32)
        low = total.astype(BF16)
        half = low.shape[0] // 2
        over_two = swap(low, 2)
        over_four = swap(low, 4)
        near = swap(over_four[:half], 2)
        far = swap(over_two[half:], 4)
        across = swap(jnp.concatenate([low, over_two, over_four, near, far]), 1)
        return (low, over_two, over_four, near, far, across)

    def sum_everywhere(total):
        bit = 1
        while bit < dp:
            total = total + swap(total, bit)
            bit *= 2
        bit = 1
        while bit < mp:
            total = total + lax.ppermute(total, "mp", [(i, i ^ bit) for i in range(mp)])
            bit *= 2
        return total

    def body(
        hidden,
        memory,
        out_grad,
        dec_starts,
        dec_length,
        mem_starts,
        mem_length,
        self_qkv,
        self_qv_bias,
        self_proj,
        cross_query,
        cross_kv,
        cross_qv_bias,
        cross_proj,
        ffn_in,
        ffn_in_bias,
        ffn_out,
        out_biases,
        norm_gains,
        norm_biases,
    ):
        row_count = dec_starts.shape[0]
        assert row_count == mp == 4 and dp % SUB == 0
        slots = hidden.shape[0] // row_count
        mem_slots = memory.shape[0] // row_count
        width = hidden.shape[1]
        local = self_proj.shape[0]
        heads = local // HD
        inner = ffn_out.shape[0]
        nseg = dec_starts.shape[1]
        dims = (mp, local, heads, HD ** (-0.5), nseg)
        line = lax.axis_index("mp")
        device = lax.axis_index("dp") % SUB
        place = (device & 1) * 4 + device // 2

        def row_of(array, size):
            return lax.dynamic_slice_in_dim(array, line * size, size, 0)

        def slice_of(array):
            size = array.shape[0] // SUB
            return lax.dynamic_slice_in_dim(array, place * size, size, 0)

        meta = jnp.concatenate(
            [
                jnp.stack([place, line]).astype(jnp.int32),
                row_of(dec_length, 1),
                row_of(mem_length, 1),
                row_of(dec_starts, 1)[0],
                row_of(mem_starts, 1)[0],
            ]
        )
        own_self = jnp.swapaxes(self_qkv, 1, 2).reshape(3 * local, width)
        own_cq = cross_query.T
        own_kv = jnp.swapaxes(cross_kv, 1, 2).reshape(2 * local, width)

        head_piece = jnp.concatenate(
            [
                slice_of(jnp.concatenate([own_self, own_cq])),
                slice_of(jnp.concatenate([self_proj, cross_proj])),
                slice_of(own_kv),
            ]
        )
        ffn_piece = jnp.concatenate([slice_of(ffn_in), slice_of(ffn_out)])
        bias_piece = jnp.concatenate(
            [self_qv_bias.reshape(-1), cross_qv_bias.reshape(-1), ffn_in_bias]
        )
        head_line = jnp.stack([shift(head_piece, step) for step in range(1, mp)])
        biases = jnp.stack([bias_piece] + [shift(bias_piece, step) for step in range(1, mp)])
        head_pieces = gather_plane(head_line)
        ffn_piece = after(ffn_piece, head_line)
        ffn_line = jnp.stack([shift(ffn_piece, step) for step in range(1, mp)])
        ffn_pieces = gather_plane(ffn_line)
        memory_t = after(memory.T, ffn_line)
        memory_blocks = []
        for step in range(mp):
            to = (line + step) % mp
            block = lax.dynamic_slice_in_dim(memory_t, to * mem_slots, mem_slots, 1)
            memory_blocks.append(shift(block, step) if step else block)

        self_bias = biases[:, : 2 * local].reshape(mp, 2, local)
        cross_bias = biases[:, 2 * local : 4 * local].reshape(mp, 2, local)
        inner_bias = biases[:, None, 4 * local :]
        hidden_row = row_of(hidden, slots)
        grad_row = row_of(out_grad, slots)
        params = (out_biases, norm_gains, norm_biases)
        dma = pltpu.SemaphoreType.DMA((4,))
        wa_shape = VMEM((mp, 4 * local, width), BF16)
        wp_shape = VMEM((mp, 2 * local, width), BF16)
        flat_shape = VMEM((slots, width), F32)
        row_shape = shaped((slots, width))
        low_shape = shaped((mp, slots, local), BF16)
        matmul = 2 * slots * width * width

        def bound(kernel):
            return lambda *refs: kernel(dims, *refs)

        qkv, self_low, z1, first, cross_q = call(
            bound(self_forward),
            [META] + in_vmem(6) + in_place(14),
            (
                shaped((mp, slots, 3 * local), BF16),
                low_shape,
                row_shape,
                row_shape,
                low_shape,
            ),
            [wa_shape, wp_shape, flat_shape, dma],
            5 * matmul,
            8 * width * width * 2,
            "self_forward",
        )(
            meta,
            hidden_row,
            self_bias,
            cross_bias,
            *params,
            *head_pieces,
            own_self,
            own_cq,
            self_proj,
            cross_proj,
        )
        kv, cross_low, cross_total, z2, second = call(
            bound(cross_forward),
            [META] + in_vmem(6) + in_place(mp + 13),
            (
                shaped((mp, 2 * local, mem_slots), BF16),
                low_shape,
                shaped((mp * heads, slots, 1)),
                row_shape,
                row_shape,
            ),
            [wp_shape, wp_shape, VMEM((width, mem_slots), BF16), flat_shape, dma],
            18 * matmul,
            8 * width * width * 2,
            "cross_forward",
        )(
            meta,
            cross_q,
            cross_bias,
            *params,
            first,
            *memory_blocks,
            *head_pieces,
            own_kv,
            self_proj,
            cross_proj,
        )
        slot_shape = shaped((8, 2, 2 * width // SUB, width), BF16)
        square = VMEM((width, width), F32)
        result, dz2, ffn_sums, ffn_beside, ffn_mine = call(
            bound(ffn_both),
            [META] + in_vmem(7) + in_place(12),
            (
                shaped((slots, width), BF16),
                row_shape,
                shaped((16, width)),
                slot_shape,
                slot_shape,
            ),
            [
                VMEM((mp, width, inner), BF16),
                VMEM((mp, inner, width), BF16),
                flat_shape,
                VMEM((mp, slots, inner), BF16),
                VMEM((mp, slots, inner), F32),
                square,
                dma,
            ],
            24 * matmul,
            16 * width * width * 2,
            "ffn_both",
        )(meta, second, z2, grad_row, inner_bias, *params, *ffn_pieces, ffn_in, ffn_out)
        ffn_reduced = reduce_group(ffn_beside, ffn_mine)

        memory_grads, kv_low, cross_dq, dz1, cross_sums, cross_local = call(
            bound(cross_back),
            [META] + in_vmem(5) + in_place(16),
            (
                shaped((mp, local, mem_slots), BF16),
                shaped((mp, 2 * local, mem_slots), BF16),
                low_shape,
                row_shape,
                shaped((8, width)),
                shaped((mp, 2, local)),
            ),
            [
                wa_shape,
                wp_shape,
                wp_shape,
                VMEM((mp, 2 * local, mem_slots), BF16),
                VMEM((width, mem_slots), F32),
                flat_shape,
                VMEM((slots, local), BF16),
                dma,
            ],
            24 * matmul,
            12 * width * width * 2,
            "cross_back",
        )(
            meta,
            dz2,
            cross_q,
            cross_total,
            z1,
            norm_gains,
            kv,
            *head_pieces,
            own_self,
            own_cq,
            own_kv,
            self_proj,
            cross_proj,
        )
        memory_out = jnp.zeros((local, mp * mem_slots), F32)
        for step in range(mp):
            block = shift(memory_grads[step], step) if step else memory_grads[0]
            at = ((line - step) % mp) * mem_slots
            memory_out = lax.dynamic_update_slice(memory_out, block.astype(F32), (0, at))

        hidden_grad, self_local, head_beside, head_mine = call(
            bound(self_back),
            [META] + in_vmem(8) + in_place(mp + 15),
            (row_shape, shaped((mp, 2, local)), slot_shape, slot_shape),
            [
                wa_shape,
                wp_shape,
                VMEM((mp, 2 * local, mem_slots), BF16),
                VMEM((width, mem_slots), BF16),
                flat_shape,
                VMEM((slots, local), BF16),
                VMEM((slots, 3 * local), BF16),
                square,
                VMEM((2 * local, width), F32),
                dma,
            ],
            26 * matmul,
            16 * width * width * 2,
            "self_back",
        )(
            meta,
            dz1,
            dz2,
            hidden_row,
            first,
            qkv,
            self_low,
            cross_low,
            cross_dq,
            kv_low,
            *memory_blocks,
            *head_pieces,
            own_self,
            own_cq,
            self_proj,
            cross_proj,
        )
        head_reduced = reduce_group(head_beside, head_mine)

        def spread(rows):
            low = rows.astype(BF16)
            whole = jnp.zeros((mp * slots, width), BF16)
            for step in range(mp):
                piece = shift(low, step) if step else low
                at = ((line - step) % mp) * slots
                whole = lax.dynamic_update_slice(whole, piece, (at, 0))
            return whole

        from_line = (line - jnp.arange(mp)) % mp
        partial = jnp.concatenate(
            [
                self_local.reshape(mp, -1),
                cross_local.reshape(mp, -1),
                ffn_sums[8 : 8 + mp],
            ],
            axis=1,
        )
        small = sum_everywhere(
            jnp.concatenate(
                [cross_sums[:3], ffn_sums[:6], jnp.take(partial, from_line, axis=0).reshape(-1, width)]
            )
        )
        sharded = lax.dynamic_index_in_dim(
            small[9:].reshape(mp, 4 * local + inner), line, 0, keepdims=False
        )
        grad_self, grad_cq, grad_sp, grad_cp, grad_kv = call(
            finish_heads,
            [META] + in_vmem(6),
            (
                shaped((3 * local, width)),
                shaped((local, width)),
                shaped((local, width)),
                shaped((local, width)),
                shaped((2 * local, width)),
            ),
            [],
            0,
            12 * width * width,
            "finish_heads",
        )(meta, *head_reduced)
        grad_in, grad_out = call(
            finish_ffn,
            [META] + in_vmem(6),
            (shaped((width, inner)), shaped((inner, width))),
            [],
            0,
            12 * width * width,
            "finish_ffn",
        )(meta, *ffn_reduced)
        return (
            spread(result),
            spread(hidden_grad).astype(F32),
            memory_out.T,
            jnp.swapaxes(grad_self.reshape(3, local, width), 1, 2),
            sharded[: 2 * local].reshape(2, local),
            grad_sp,
            grad_cq.T,
            jnp.swapaxes(grad_kv.reshape(2, local, width), 1, 2),
            sharded[2 * local : 4 * local].reshape(2, local),
            grad_cp,
            grad_in,
            sharded[4 * local :],
            grad_out,
            jnp.stack([small[0], small[6], small[3]]),
            jnp.stack([small[1], small[7], small[4]]),
            jnp.stack([small[2], small[8], small[5]]),
        )

    return jax.shard_map(
        body,
        mesh=mesh,
        in_specs=(
            P("dp", None),
            P("dp", "mp"),
            P("dp", None),
            P("dp", None),
            P("dp"),
            P("dp", None),
            P("dp"),
            P(None, None, "mp"),
            P(None, "mp"),
            P("mp", None),
            P(None, "mp"),
            P(None, None, "mp"),
            P(None, "mp"),
            P("mp", None),
            P(None, "mp"),
            P("mp"),
            P("mp", None),
            P(),
            P(),
            P(),
        ),
        out_specs=(
            P("dp", None),
            P("dp", None),
            P("dp", "mp"),
            P(None, None, "mp"),
            P(None, "mp"),
            P("mp", None),
            P(None, "mp"),
            P(None, None, "mp"),
            P(None, "mp"),
            P("mp", None),
            P(None, "mp"),
            P("mp"),
            P("mp", None),
            P(),
            P(),
            P(),
        ),
        check_vma=False,
    )
```

time: 657 us -> 454 us (0.69)
  local copies, waits for them, and re-layouts: 147 us -> 34.4 us
  Pallas kernels: 0 us -> 97 us
  matrix products: 88.3 us -> 0 us
  starting transfers between devices: 143 us -> 76.8 us
  other arithmetic: 70.8 us -> 39.9 us
  waiting for transfers between devices: 187 us -> 201 us
  between operations: 11.9 us -> 1.51 us
    pallas_call x0 -> x7, Pallas kernels: none -> 97 us  [the longest x1 23.5 us: body(): call(bound(self_back), [META] + in_vmem(8) + in_place(mp + 15), (row_shap...]
    dot_general x33 -> x0, matrix products: 80.6 us -> none  [ein(): return jnp.einsum(spec, left, right, preferred_element_type=F32)]
    dynamic_update_slice x53 -> x7, local copies, waits for them, and re-layouts: 73.5 us -> 0.13 us  [spread(): whole = lax.dynamic_update_slice(whole, piece, (at, 0))]
    ppermute x33 -> x27, waiting for transfers between devices: 67.8 us -> 133 us  [shift(): return lax.ppermute(value, 'mp', [(i, (i + step) % mp) for i in range(mp)])]
    ppermute x81 -> x41, starting transfers between devices: 85.1 us -> 39.3 us  [swap(): return lax.ppermute(value, 'dp', [(i, i ^ bit) for i in range(dp)])]
    ppermute x81 -> x41, waiting for transfers between devices: 108 us -> 68.6 us  [swap(): return lax.ppermute(value, 'dp', [(i, i ^ bit) for i in range(dp)])]
    ppermute x33 -> x27, starting transfers between devices: 54.8 us -> 31.7 us  [shift(): return lax.ppermute(value, 'mp', [(i, (i + step) % mp) for i in range(mp)])]
    slice x40 -> x15, local copies, waits for them, and re-layouts: 27.5 us -> 5.61 us  [the longest x2 3.49 us: reduce_group(): from_two = swap(low[0:2], 2).astype(F32)]
  transfers between devices with their start and end apart: 116 -> 70, of which waited for: 36 -> 28; matrix products, arithmetic and copies ran while one was open for 36% -> 15% of each run, Pallas kernels for 0% -> 16%
where the time goes in v2:
time: 454 us; the launch traced here: 451 us
  waiting for transfers between devices  201 us (44%)
  Pallas kernels  97 us (21%)
  starting transfers between devices  76.8 us (17%)
  other arithmetic  39.9 us (9%)
  local copies, waits for them, and re-layouts  34.4 us (8%)
    ppermute x27, waiting for transfers between devices, shift(): return lax.ppermute(value, 'mp', [(i, (i + step) % mp) for i in range(mp)])  133 us
    ppermute x41, waiting for transfers between devices, swap(): return lax.ppermute(value, 'dp', [(i, i ^ bit) for i in range(dp)])  68.6 us
    ppermute x41, starting transfers between devices, swap(): return lax.ppermute(value, 'dp', [(i, i ^ bit) for i in range(dp)])  39.3 us
    ppermute x27, starting transfers between devices, shift(): return lax.ppermute(value, 'mp', [(i, (i + step) % mp) for i in range(mp)])  31.7 us
    pallas_call x1, Pallas kernels, body(): call(bound(self_back), [META] + in_vmem(8) + in_place(mp + 15), (row_shap...  23.5 us
    pallas_call x1, Pallas kernels, body(): call(bound(cross_back), [META] + in_vmem(5) + in_place(16), (shaped((mp,...  19.9 us
    pallas_call x1, Pallas kernels, body(): call(bound(ffn_both), [META] + in_vmem(7) + in_place(12), (shaped((slots,...  19.3 us
    add x2, other arithmetic, reduce_group(): total = mine.astype(F32) + swap(beside, 1).astype(F32)  16.7 us
  transfers between devices with their start and end apart: 70, of which 28 were waited for; matrix products, arithmetic and copies ran while one was open for 15% of the time, Pallas kernels for 16%

profile of v2, /device:TPU:9, one launch (start us, length us, event | category | flops | bytes accessed | tf_op | source)
XLA Modules:
  0.0 451.0 jit_solution(3054403829781180227)
XLA Ops:
  7.7 16.8 %collective-permute-done.4 = bf16[192,768]{1,0:T(8,128)(2,1)S(1)} collective-permute-done((bf16[192,768]{1,0:T(8,128)(2,1)S(1)}, bf16[192,768]{1,0:T(8,128)(2,1)S(1)}, u32[]{:S(2)}, u32[]{:S(2)}) %collective-permute-start.4) | collective-permute-done | bytes 294944 | tf_op jit(solution)/shard_map/ppermute | solution.py:477
  24.5 11.7 %collective-permute-done.5 = bf16[192,768]{1,0:T(8,128)(2,1)S(1)} collective-permute-done((bf16[192,768]{1,0:T(8,128)(2,1)S(1)}, bf16[192,768]{1,0:T(8,128)(2,1)S(1)}, u32[]{:S(2)}, u32[]{:S(2)}) %collective-permute-start.5) | collective-permute-done | bytes 294944 | tf_op jit(solution)/shard_map/ppermute | solution.py:477
  40.1 3.6 collective-permute-done.15
  43.7 17.1 %collective-permute-done.16 = bf16[192,768]{1,0:T(8,128)(2,1)S(1)} collective-permute-done((bf16[192,768]{1,0:T(8,128)(2,1)S(1)}, bf16[192,768]{1,0:T(8,128)(2,1)S(1)}, u32[]{:S(2)}, u32[]{:S(2)}) %collective-permute-start.16) | collective-permute-done | bytes 294944 | tf_op jit(solution)/shard_map/ppermute | solution.py:477
  62.8 3.2 collective-permute-start.1
  68.1 3.6 collective-permute-start.10
  85.0 24.6 %collective-permute-done.19.refs_9_.refs_12_ = bf16[192,1024]{1,0:T(8,128)(2,1)S(1)} collective-permute-done((bf16[192,1024]{1,0:T(8,128)(2,1)S(1)}, bf16[192,1024]{1,0:T(8,128)(2,1)S(1)}, u32[]{:S(2)}, u32[]{:S(2)}) %collective-permute-start.19) | collective-permute-done | bytes 393248 | tf_op jit(solution)/shard_map/ppermute | solution.py:477
  115.8 3.6 collective-permute-done.9.refs_11_.refs_15_.refs_18_
  119.5 5.3 %collective-permute-start.13 = (bf16[3,96,768]{2,1,0:T(8,128)(2,1)}, bf16[3,96,768]{2,1,0:T(8,128)(2,1)}, u32[]{:S(2)}, u32[]{:S(2)}) collective-permute-start(bf16[3,96,768]{2,1,0:T(8,128)(2,1)} %collective-permute-done.8.refs_10_.refs_14_.refs_17_), channel_id=1, source_target_pairs={{0,4},{4,0},{8,12},{12,8},{16,20},{20,16},{24,28},{28,24},{1,5},{5... | collective-permute-start | bytes 1327112 | tf_op jit(solution)/shard_map/ppermute | solution.py:474
  128.9 2.8 collective-permute-start.25
  139.9 11.4 %self_forward.1 = (bf16[4,128,576]{2,1,0:T(8,128)(2,1)}, bf16[4,128,192]{2,1,0:T(8,128)(2,1)}, f32[128,768]{1,0:T(8,128)}, f32[128,768]{1,0:T(8,128)}, bf16[4,128,192]{2,1,0:T(8,128)(2,1)}) custom-call(s32[12]{0:T(128)} %concatenate.30.refs_0_.meta, bf16[128,768]{1,0:T(8,128)(2,1)} %constant_dynamic-slice_fusion.9.refs_1_.refs_3_, ...), custom_call_target="tpu_custom_call" | custom-call | flops 754974720 | bytes 9437184 | tf_op jit(solution)/shard_map/self_forward/pallas_call | solution.py:627
  151.3 14.2 %cross_forward.1 = (bf16[4,384,1024]{2,1,0:T(8,128)(2,1)}, bf16[4,128,192]{2,1,0:T(8,128)(2,1)}, f32[12,128,1]{2,1,0:T(8,128)}, f32[128,768]{1,0:T(8,128)}, f32[128,768]{1,0:T(8,128)}) custom-call(s32[12]{0:T(128)} %concatenate.30.refs_0_.meta, bf16[4,128,192]{2,1,0:T(8,128)(2,1)} %get-tuple-element.50.refs_1_.refs_2_, ...), custom_call_target="tpu_custom_call" | custom-call | flops 2717908992 | bytes 9437184 | tf_op jit(solution)/shard_map/cross_forward/pallas_call | solution.py:653
  166.5 19.3 %ffn_both.1 = (bf16[128,768]{1,0:T(8,128)(2,1)}, f32[128,768]{1,0:T(8,128)}, f32[16,768]{1,0:T(8,128)}, bf16[8,2,192,768]{3,2,1,0:T(8,128)(2,1)}, bf16[8,2,192,768]{3,2,1,0:T(8,128)(2,1)}) custom-call(s32[12]{0:T(128)} %concatenate.30.refs_0_.meta, f32[128,768]{1,0:T(8,128)} %get-tuple-element.54.refs_1_, f32[128,768]{1,0:T(8,128)} %get-tuple-element.55.refs_2_, ...), custom_call_target="tpu_custom_call" | custom-call | flops 3623878656 | bytes 18874368 | tf_op jit(solution)/shard_map/ffn_both/pallas_call | solution.py:681
  185.9 19.9 %cross_back.1 = (bf16[4,192,1024]{2,1,0:T(8,128)(2,1)}, bf16[4,384,1024]{2,1,0:T(8,128)(2,1)}, bf16[4,128,192]{2,1,0:T(8,128)(2,1)}, f32[128,768]{1,0:T(8,128)}, f32[8,768]{1,0:T(8,128)}, /*index=5*/f32[4,2,192]{2,1,0:T(2,128)}) custom-call(s32[12]{0:T(128)} %concatenate.30.refs_0_.meta, f32[128,768]{1,0:T(8,128)} %get-tuple-element.57.refs_1_.refs_2_, ...), custom_call_target="tpu_custom_call" | custom-call | flops 3623878656 | bytes 14155776 | tf_op jit(solution)/shard_map/cross_back/pallas_call | solution.py:706
  205.8 23.5 %self_back.1 = (f32[128,768]{1,0:T(8,128)}, f32[4,2,192]{2,1,0:T(2,128)}, bf16[8,2,192,768]{3,2,1,0:T(8,128)(2,1)}, bf16[8,2,192,768]{3,2,1,0:T(8,128)(2,1)}) custom-call(s32[12]{0:T(128)} %concatenate.30.refs_0_.meta, f32[128,768]{1,0:T(8,128)} %get-tuple-element.61.refs_1_, f32[128,768]{1,0:T(8,128)} %get-tuple-element.57.refs_1_.refs_2_, ...), custom_call_target="tpu_custom_call" | custom-call | flops 3925868544 | bytes 18874368 | tf_op jit(solution)/shard_map/self_back/pallas_call | solution.py:751
  232.9 4.6 %collective-permute-done.52 = f32[17,768]{1,0:T(8,128)S(1)} collective-permute-done((f32[17,768]{1,0:T(8,128)S(1)}, f32[17,768]{1,0:T(8,128)S(1)}, u32[]{:S(2)}, u32[]{:S(2)}) %collective-permute-start.52) | collective-permute-done | bytes 52256 | tf_op jit(solution)/shard_map/ppermute | solution.py:474
  237.8 9.1 %convert_add_fusion = (f32[8,2,192,768]{3,2,1,0:T(8,128)}, bf16[8,2,192,768]{3,2,1,0:T(8,128)(2,1)S(1)}) fusion(bf16[8,2,192,768]{3,2,1,0:T(8,128)(2,1)} %collective-permute-done.57, bf16[8,2,192,768]{3,2,1,0:T(8,128)(2,1)} %get-tuple-element.80), kind=kLoop, calls=%fused_computation.1 | loop fusion | flops 9437184 | bytes 23592960 | tf_op jit(solution)/shard_map/add | solution.py:493
  251.3 7.6 %convert_add_fusion.1 = (f32[8,2,192,768]{3,2,1,0:T(8,128)S(1)}, bf16[8,2,192,768]{3,2,1,0:T(8,128)(2,1)}) fusion(bf16[8,2,192,768]{3,2,1,0:T(8,128)(2,1)} %collective-permute-done.39, bf16[8,2,192,768]{3,2,1,0:T(8,128)(2,1)} %get-tuple-element.69), kind=kLoop, calls=%fused_computation.2 | loop fusion | flops 9437184 | bytes 23592960 | tf_op jit(solution)/shard_map/add | solution.py:493
  263.3 41.4 %collective-permute-done.54 = f32[17,768]{1,0:T(8,128)S(1)} collective-permute-done((f32[17,768]{1,0:T(8,128)S(1)}, f32[17,768]{1,0:T(8,128)S(1)}, u32[]{:S(2)}, u32[]{:S(2)}) %collective-permute-start.54) | collective-permute-done | bytes 52256 | tf_op jit(solution)/shard_map/ppermute | solution.py:474
  309.2 3.1 collective-permute-start.34
  320.4 7.9 %collective-permute-done.30 = bf16[128,768]{1,0:T(8,128)(2,1)S(1)} collective-permute-done((bf16[128,768]{1,0:T(8,128)(2,1)S(1)}, bf16[128,768]{1,0:T(8,128)(2,1)S(1)}, u32[]{:S(2)}, u32[]{:S(2)}) %collective-permute-start.30) | collective-permute-done | bytes 196640 | tf_op jit(solution)/shard_map/ppermute | solution.py:477
  328.6 3.9 collective-permute-done.31
  342.2 9.2 %collective-permute-done.41 = bf16[2,192,768]{2,1,0:T(8,128)(2,1)S(1)} collective-permute-done((bf16[2,192,768]{2,1,0:T(8,128)(2,1)S(1)}, bf16[2,192,768]{2,1,0:T(8,128)(2,1)S(1)}, u32[]{:S(2)}, u32[]{:S(2)}) %collective-permute-start.41) | collective-permute-done | bytes 589856 | tf_op jit(solution)/shard_map/ppermute | solution.py:474
  362.5 10.7 %collective-permute-done.60 = bf16[192,768]{1,0:T(8,128)(2,1)S(1)} collective-permute-done((bf16[192,768]{1,0:T(8,128)(2,1)S(1)}, bf16[192,768]{1,0:T(8,128)(2,1)S(1)}, u32[]{:S(2)}, u32[]{:S(2)}) %collective-permute-start.60) | collective-permute-done | bytes 294944 | tf_op jit(solution)/shard_map/ppermute | solution.py:477
  374.1 6.3 %collective-permute-done.45 = bf16[192,768]{1,0:T(8,128)(2,1)S(1)} collective-permute-done((bf16[192,768]{1,0:T(8,128)(2,1)S(1)}, bf16[192,768]{1,0:T(8,128)(2,1)S(1)}, u32[]{:S(2)}, u32[]{:S(2)}) %collective-permute-start.45) | collective-permute-done | bytes 294944 | tf_op jit(solution)/shard_map/ppermute | solution.py:477
  380.4 3.6 collective-permute-start.56
  384.0 12.4 %collective-permute-done.46 = bf16[192,768]{1,0:T(8,128)(2,1)S(1)} collective-permute-done((bf16[192,768]{1,0:T(8,128)(2,1)S(1)}, bf16[192,768]{1,0:T(8,128)(2,1)S(1)}, u32[]{:S(2)}, u32[]{:S(2)}) %collective-permute-start.46) | collective-permute-done | bytes 294944 | tf_op jit(solution)/shard_map/ppermute | solution.py:477
  397.8 7.5 %collective-permute-done.42 = bf16[192,768]{1,0:T(8,128)(2,1)S(1)} collective-permute-done((bf16[192,768]{1,0:T(8,128)(2,1)S(1)}, bf16[192,768]{1,0:T(8,128)(2,1)S(1)}, u32[]{:S(2)}, u32[]{:S(2)}) %collective-permute-start.42) | collective-permute-done | bytes 294944 | tf_op jit(solution)/shard_map/ppermute | solution.py:477
  406.1 3.3 collective-permute-done.32
  425.2 4.7 %collective-permute-start.69 = (bf16[768,768]{1,0:T(8,128)(2,1)}, bf16[768,768]{1,0:T(8,128)(2,1)}, u32[]{:S(2)}, u32[]{:S(2)}) collective-permute-start(bf16[768,768]{1,0:T(8,128)(2,1)} %constant_dynamic-update-slice_fusion.6), channel_id=1, source_target_pairs={{0,4},{4,0},{8,12},{12,8},{16,20},{20,16},{24,28},{28,24},{1,5},{5... | collective-permute-start | bytes 3538952 | tf_op jit(solution)/shard_map/ppermute | solution.py:474
  441.3 4.3 finish_ffn.1
  446.6 4.4 finish_heads.1
  (305 shorter events, 124.7 us)
Async XLA Ops:
  5.2 31.0 %collective-permute-start.5 = (bf16[192,768]{1,0:T(8,128)(2,1)S(1)}, bf16[192,768]{1,0:T(8,128)(2,1)S(1)}, u32[]{:S(2)}, u32[]{:S(2)}) collective-permute-start(bf16[192,768]{1,0:T(8,128)(2,1)S(1)} %pad_maximum_fusion.2), channel_id=1, source_target_pairs={{0,3},{1,0},{2,1},{3,2},{4,7},{5,4},{6,5},{7,6},{8,11},{9,8},{10,9... | collective-permute-start | bytes 884744 | tf_op jit(solution)/shard_map/ppermute | solution.py:477
  5.4 30.9 %collective-permute-start.3 = (bf16[192,768]{1,0:T(8,128)(2,1)S(1)}, bf16[192,768]{1,0:T(8,128)(2,1)S(1)}, u32[]{:S(2)}, u32[]{:S(2)}) collective-permute-start(bf16[192,768]{1,0:T(8,128)(2,1)S(1)} %pad_maximum_fusion.2), channel_id=1, source_target_pairs={{0,1},{1,2},{2,3},{3,0},{4,5},{5,6},{6,7},{7,4},{8,9},{9,10},{10,1... | collective-permute-start | bytes 884744 | tf_op jit(solution)/shard_map/ppermute | solution.py:477
  36.5 24.3 %collective-permute-start.16 = (bf16[192,768]{1,0:T(8,128)(2,1)S(1)}, bf16[192,768]{1,0:T(8,128)(2,1)S(1)}, u32[]{:S(2)}, u32[]{:S(2)}) collective-permute-start(bf16[192,768]{1,0:T(8,128)(2,1)S(1)} %pad_maximum_fusion.3), channel_id=1, source_target_pairs={{0,2},{1,3},{2,0},{3,1},{4,6},{5,7},{6,4},{7,5},{8,10},{9,11},{10,... | collective-permute-start | bytes 884744 | tf_op jit(solution)/shard_map/ppermute | solution.py:477
  36.5 24.2 %collective-permute-start.17 = (bf16[192,768]{1,0:T(8,128)(2,1)S(1)}, bf16[192,768]{1,0:T(8,128)(2,1)S(1)}, u32[]{:S(2)}, u32[]{:S(2)}) collective-permute-start(bf16[192,768]{1,0:T(8,128)(2,1)S(1)} %pad_maximum_fusion.3), channel_id=1, source_target_pairs={{0,3},{1,0},{2,1},{3,2},{4,7},{5,4},{6,5},{7,6},{8,11},{9,8},{10,9... | collective-permute-start | bytes 884744 | tf_op jit(solution)/shard_map/ppermute | solution.py:477
  37.9 37.2 %collective-permute-start.7 = (bf16[3,192,768]{2,1,0:T(8,128)(2,1)S(1)}, bf16[3,192,768]{2,1,0:T(8,128)(2,1)S(1)}, u32[]{:S(2)}, u32[]{:S(2)}) collective-permute-start(bf16[3,192,768]{2,1,0:T(8,128)(2,1)S(1)} %pad_maximum_fusion.refs_7_.refs_11_.refs_14_), channel_id=1, source_target_pairs={{0,16},{4,20},{8,24},{12,28},{16,0},{20,4},{24,8},{28,12},{1,17},{... | collective-permute-start | bytes 2654216 | tf_op jit(solution)/shard_map/ppermute | solution.py:474
  38.9 38.0 %collective-permute-start.6 = (bf16[3,192,768]{2,1,0:T(8,128)(2,1)S(1)}, bf16[3,192,768]{2,1,0:T(8,128)(2,1)S(1)}, u32[]{:S(2)}, u32[]{:S(2)}) collective-permute-start(bf16[3,192,768]{2,1,0:T(8,128)(2,1)S(1)} %pad_maximum_fusion.refs_7_.refs_11_.refs_14_), channel_id=1, source_target_pairs={{0,8},{4,12},{8,0},{12,4},{16,24},{20,28},{24,16},{28,20},{1,9},{5... | collective-permute-start | bytes 2654216 | tf_op jit(solution)/shard_map/ppermute | solution.py:474
  68.1 44.5 %collective-permute-start.10 = (bf16[3,192,768]{2,1,0:T(8,128)(2,1)S(1)}, bf16[3,192,768]{2,1,0:T(8,128)(2,1)S(1)}, u32[]{:S(2)}, u32[]{:S(2)}) collective-permute-start(bf16[3,192,768]{2,1,0:T(8,128)(2,1)S(1)} %pad_maximum_fusion.refs_7_.refs_11_.refs_14_), channel_id=1, source_target_pairs={{0,4},{4,0},{8,12},{12,8},{16,20},{20,16},{24,28},{28,24},{1,5},{5... | collective-permute-start | bytes 2654216 | tf_op jit(solution)/shard_map/ppermute | solution.py:474
  71.7 42.5 %collective-permute-start.21 = (bf16[3,192,768]{2,1,0:T(8,128)(2,1)}, bf16[3,192,768]{2,1,0:T(8,128)(2,1)S(1)}, u32[]{:S(2)}, u32[]{:S(2)}) collective-permute-start(bf16[3,192,768]{2,1,0:T(8,128)(2,1)} %pad_maximum_fusion.1.refs_8_), channel_id=1, source_target_pairs={{0,8},{4,12},{8,0},{12,4},{16,24},{20,28},{24,16},{28,20},{1,9},{5... | collective-permute-start | bytes 2654216 | tf_op jit(solution)/shard_map/ppermute | solution.py:474
  76.9 32.7 %collective-permute-start.19 = (bf16[192,1024]{1,0:T(8,128)(2,1)S(1)}, bf16[192,1024]{1,0:T(8,128)(2,1)S(1)}, u32[]{:S(2)}, u32[]{:S(2)}) collective-permute-start(bf16[192,1024]{1,0:T(8,128)(2,1)S(1)} %get-tuple-element.112), channel_id=1, source_target_pairs={{0,2},{1,3},{2,0},{3,1},{4,6},{5,7},{6,4},{7,5},{8,10},{9,11},{10,... | collective-permute-start | bytes 1179656 | tf_op jit(solution)/shard_map/ppermute | solution.py:477
  81.4 31.0 %collective-permute-start.20 = (bf16[192,1024]{1,0:T(8,128)(2,1)S(1)}, bf16[192,1024]{1,0:T(8,128)(2,1)S(1)}, u32[]{:S(2)}, u32[]{:S(2)}) collective-permute-start(bf16[192,1024]{1,0:T(8,128)(2,1)S(1)} %get-tuple-element.111), channel_id=1, source_target_pairs={{0,3},{1,0},{2,1},{3,2},{4,7},{5,4},{6,5},{7,6},{8,11},{9,8},{10,9... | collective-permute-start | bytes 1179656 | tf_op jit(solution)/shard_map/ppermute | solution.py:477
  84.7 30.5 %collective-permute-start.8 = (bf16[3,96,768]{2,1,0:T(8,128)(2,1)S(1)}, bf16[3,96,768]{2,1,0:T(8,128)(2,1)}, u32[]{:S(2)}, u32[]{:S(2)}) collective-permute-start(bf16[3,96,768]{2,1,0:T(8,128)(2,1)S(1)} %slice.262), channel_id=1, source_target_pairs={{0,8},{4,12},{8,0},{12,4},{16,24},{20,28},{24,16},{28,20},{1,9},{5... | collective-permute-start | bytes 1327112 | tf_op jit(solution)/shard_map/ppermute | solution.py:474
  112.6 24.7 %collective-permute-start.11 = (bf16[3,192,768]{2,1,0:T(8,128)(2,1)S(1)}, bf16[3,192,768]{2,1,0:T(8,128)(2,1)S(1)}, u32[]{:S(2)}, u32[]{:S(2)}) collective-permute-start(bf16[3,192,768]{2,1,0:T(8,128)(2,1)S(1)} %collective-permute-done.6.refs_8_.refs_12_.refs_15_), channel_id=1, source_target_pairs={{0,4},{4,0},{8,12},{12,8},{16,20},{20,16},{24,28},{28,24},{1,5},{5... | collective-permute-start | bytes 2654216 | tf_op jit(solution)/shard_map/ppermute | solution.py:474
  128.9 36.6 %collective-permute-start.25 = (bf16[3,192,768]{2,1,0:T(8,128)(2,1)}, bf16[3,192,768]{2,1,0:T(8,128)(2,1)}, u32[]{:S(2)}, u32[]{:S(2)}) collective-permute-start(bf16[3,192,768]{2,1,0:T(8,128)(2,1)} %pad_maximum_fusion.1.refs_8_), channel_id=1, source_target_pairs={{0,4},{4,0},{8,12},{12,8},{16,20},{20,16},{24,28},{28,24},{1,5},{5... | collective-permute-start | bytes 2654216 | tf_op jit(solution)/shard_map/ppermute | solution.py:474
  131.8 33.8 %collective-permute-start.26 = (bf16[3,192,768]{2,1,0:T(8,128)(2,1)}, bf16[3,192,768]{2,1,0:T(8,128)(2,1)}, u32[]{:S(2)}, u32[]{:S(2)}) collective-permute-start(bf16[3,192,768]{2,1,0:T(8,128)(2,1)} %copy-done.27), channel_id=1, source_target_pairs={{0,4},{4,0},{8,12},{12,8},{16,20},{20,16},{24,28},{28,24},{1,5},{5... | collective-permute-start | bytes 2654216 | tf_op jit(solution)/shard_map/ppermute | solution.py:474
  131.8 33.8 %collective-permute-start.27 = (bf16[3,192,768]{2,1,0:T(8,128)(2,1)}, bf16[3,192,768]{2,1,0:T(8,128)(2,1)}, u32[]{:S(2)}, u32[]{:S(2)}) collective-permute-start(bf16[3,192,768]{2,1,0:T(8,128)(2,1)} %collective-permute-done.22.refs_10_), channel_id=1, source_target_pairs={{0,4},{4,0},{8,12},{12,8},{16,20},{20,16},{24,28},{28,24},{1,5},{5... | collective-permute-start | bytes 2654216 | tf_op jit(solution)/shard_map/ppermute | solution.py:474
  137.3 28.3 %collective-permute-start.28 = (bf16[3,96,768]{2,1,0:T(8,128)(2,1)}, bf16[3,96,768]{2,1,0:T(8,128)(2,1)S(1)}, u32[]{:S(2)}, u32[]{:S(2)}) collective-permute-start(bf16[3,96,768]{2,1,0:T(8,128)(2,1)} %copy-done.35), channel_id=1, source_target_pairs={{0,4},{4,0},{8,12},{12,8},{16,20},{20,16},{24,28},{28,24},{1,5},{5... | collective-permute-start | bytes 1327112 | tf_op jit(solution)/shard_map/ppermute | solution.py:474
  137.4 28.2 %collective-permute-start.29 = (bf16[3,96,768]{2,1,0:T(8,128)(2,1)}, bf16[3,96,768]{2,1,0:T(8,128)(2,1)S(1)}, u32[]{:S(2)}, u32[]{:S(2)}) collective-permute-start(bf16[3,96,768]{2,1,0:T(8,128)(2,1)} %collective-permute-done.24.refs_12_), channel_id=1, source_target_pairs={{0,4},{4,0},{8,12},{12,8},{16,20},{20,16},{24,28},{28,24},{1,5},{5... | collective-permute-start | bytes 1327112 | tf_op jit(solution)/shard_map/ppermute | solution.py:474
  185.8 52.1 %collective-permute-start.57 = (bf16[8,2,192,768]{3,2,1,0:T(8,128)(2,1)}, bf16[8,2,192,768]{3,2,1,0:T(8,128)(2,1)}, u32[]{:S(2)}, u32[]{:S(2)}) collective-permute-start(bf16[8,2,192,768]{3,2,1,0:T(8,128)(2,1)} %get-tuple-element.81), channel_id=1, source_target_pairs={{0,4},{4,0},{8,12},{12,8},{16,20},{20,16},{24,28},{28,24},{1,5},{5... | collective-permute-start | bytes 14155784 | tf_op jit(solution)/shard_map/ppermute | solution.py:474
  237.5 24.9 %collective-permute-start.53 = (f32[17,768]{1,0:T(8,128)S(1)}, f32[17,768]{1,0:T(8,128)S(1)}, u32[]{:S(2)}, u32[]{:S(2)}) collective-permute-start(f32[17,768]{1,0:T(8,128)S(1)} %fusion.36), channel_id=1, source_target_pairs={{0,8},{4,12},{8,0},{12,4},{16,24},{20,28},{24,16},{28,20},{1,9},{5... | collective-permute-start | bytes 156680 | tf_op jit(solution)/shard_map/ppermute | solution.py:474
  249.9 62.4 %collective-permute-start.58 = (bf16[2,2,192,768]{3,2,1,0:T(8,128)(2,1)}, bf16[2,2,192,768]{3,2,1,0:T(8,128)(2,1)}, u32[]{:S(2)}, u32[]{:S(2)}) collective-permute-start(bf16[2,2,192,768]{3,2,1,0:T(8,128)(2,1)} %get-tuple-element.102), channel_id=1, source_target_pairs={{0,8},{4,12},{8,0},{12,4},{16,24},{20,28},{24,16},{28,20},{1,9},{5... | collective-permute-start | bytes 3538952 | tf_op jit(solution)/shard_map/ppermute | solution.py:474
  251.1 64.0 %collective-permute-start.61 = (bf16[2,2,192,768]{3,2,1,0:T(8,128)(2,1)}, bf16[2,2,192,768]{3,2,1,0:T(8,128)(2,1)}, u32[]{:S(2)}, u32[]{:S(2)}) collective-permute-start(bf16[2,2,192,768]{3,2,1,0:T(8,128)(2,1)} %get-tuple-element.103), channel_id=1, source_target_pairs={{0,16},{4,20},{8,24},{12,28},{16,0},{20,4},{24,8},{28,12},{1,17},{... | collective-permute-start | bytes 3538952 | tf_op jit(solution)/shard_map/ppermute | solution.py:474
  260.7 73.8 %collective-permute-start.40 = (bf16[2,2,192,768]{3,2,1,0:T(8,128)(2,1)S(1)}, bf16[2,2,192,768]{3,2,1,0:T(8,128)(2,1)S(1)}, u32[]{:S(2)}, u32[]{:S(2)}) collective-permute-start(bf16[2,2,192,768]{3,2,1,0:T(8,128)(2,1)S(1)} %get-tuple-element.106), channel_id=1, source_target_pairs={{0,8},{4,12},{8,0},{12,4},{16,24},{20,28},{24,16},{28,20},{1,9},{5... | collective-permute-start | bytes 3538952 | tf_op jit(solution)/shard_map/ppermute | solution.py:474
  261.3 75.7 %collective-permute-start.43 = (bf16[2,2,192,768]{3,2,1,0:T(8,128)(2,1)S(1)}, bf16[2,2,192,768]{3,2,1,0:T(8,128)(2,1)S(1)}, u32[]{:S(2)}, u32[]{:S(2)}) collective-permute-start(bf16[2,2,192,768]{3,2,1,0:T(8,128)(2,1)S(1)} %get-tuple-element.107), channel_id=1, source_target_pairs={{0,16},{4,20},{8,24},{12,28},{16,0},{20,4},{24,8},{28,12},{1,17},{... | collective-permute-start | bytes 3538952 | tf_op jit(solution)/shard_map/ppermute | solution.py:474
  262.4 42.2 %collective-permute-start.54 = (f32[17,768]{1,0:T(8,128)S(1)}, f32[17,768]{1,0:T(8,128)S(1)}, u32[]{:S(2)}, u32[]{:S(2)}) collective-permute-start(f32[17,768]{1,0:T(8,128)S(1)} %add.276), channel_id=1, source_target_pairs={{0,16},{4,20},{8,24},{12,28},{16,0},{20,4},{24,8},{28,12},{1,17},{... | collective-permute-start | bytes 156680 | tf_op jit(solution)/shard_map/ppermute | solution.py:474
  355.6 24.8 %collective-permute-start.45 = (bf16[192,768]{1,0:T(8,128)(2,1)S(1)}, bf16[192,768]{1,0:T(8,128)(2,1)S(1)}, u32[]{:S(2)}, u32[]{:S(2)}) collective-permute-start(bf16[192,768]{1,0:T(8,128)(2,1)S(1)} %get-tuple-element.117), channel_id=1, source_target_pairs={{0,2},{1,3},{2,0},{3,1},{4,6},{5,7},{6,4},{7,5},{8,10},{9,11},{10,... | collective-permute-start | bytes 884744 | tf_op jit(solution)/shard_map/ppermute | solution.py:477
  357.8 38.6 %collective-permute-start.46 = (bf16[192,768]{1,0:T(8,128)(2,1)S(1)}, bf16[192,768]{1,0:T(8,128)(2,1)S(1)}, u32[]{:S(2)}, u32[]{:S(2)}) collective-permute-start(bf16[192,768]{1,0:T(8,128)(2,1)S(1)} %get-tuple-element.118), channel_id=1, source_target_pairs={{0,1},{1,2},{2,3},{3,0},{4,5},{5,6},{6,7},{7,4},{8,9},{9,10},{10,1... | collective-permute-start | bytes 884744 | tf_op jit(solution)/shard_map/ppermute | solution.py:477
  360.1 45.1 %collective-permute-start.42 = (bf16[192,768]{1,0:T(8,128)(2,1)S(1)}, bf16[192,768]{1,0:T(8,128)(2,1)S(1)}, u32[]{:S(2)}, u32[]{:S(2)}) collective-permute-start(bf16[192,768]{1,0:T(8,128)(2,1)S(1)} %fusion.26), channel_id=1, source_target_pairs={{0,3},{1,0},{2,1},{3,2},{4,7},{5,4},{6,5},{7,6},{8,11},{9,8},{10,9... | collective-permute-start | bytes 884744 | tf_op jit(solution)/shard_map/ppermute | solution.py:477
  361.5 48.0 %collective-permute-start.32 = (bf16[128,768]{1,0:T(8,128)(2,1)S(1)}, bf16[128,768]{1,0:T(8,128)(2,1)S(1)}, u32[]{:S(2)}, u32[]{:S(2)}) collective-permute-start(bf16[128,768]{1,0:T(8,128)(2,1)S(1)} %copy-done.28), channel_id=1, source_target_pairs={{0,3},{1,0},{2,1},{3,2},{4,7},{5,4},{6,5},{7,6},{8,11},{9,8},{10,9... | collective-permute-start | bytes 589832 | tf_op jit(solution)/shard_map/ppermute | solution.py:477
  373.2 63.9 %collective-permute-start.36 = (bf16[192,1024]{1,0:T(8,128)(2,1)}, bf16[192,1024]{1,0:T(8,128)(2,1)S(1)}, u32[]{:S(2)}, u32[]{:S(2)}) collective-permute-start(bf16[192,1024]{1,0:T(8,128)(2,1)} %get-tuple-element.110), channel_id=1, source_target_pairs={{0,1},{1,2},{2,3},{3,0},{4,5},{5,6},{6,7},{7,4},{8,9},{9,10},{10,1... | collective-permute-start | bytes 1179656 | tf_op jit(solution)/shard_map/ppermute | solution.py:477
  380.4 30.9 %collective-permute-start.56 = (f32[17,768]{1,0:T(8,128)S(1)}, f32[17,768]{1,0:T(8,128)S(1)}, u32[]{:S(2)}, u32[]{:S(2)}) collective-permute-start(f32[17,768]{1,0:T(8,128)S(1)} %add.278), channel_id=1, source_target_pairs={{0,2},{1,3},{2,0},{3,1},{4,6},{5,7},{6,4},{7,5},{8,10},{9,11},{10,... | collective-permute-start | bytes 156680 | tf_op jit(solution)/shard_map/ppermute | solution.py:526
  411.2 26.9 %collective-permute-start.37 = (bf16[192,1024]{1,0:T(8,128)(2,1)}, bf16[192,1024]{1,0:T(8,128)(2,1)S(1)}, u32[]{:S(2)}, u32[]{:S(2)}) collective-permute-start(bf16[192,1024]{1,0:T(8,128)(2,1)} %get-tuple-element.109), channel_id=1, source_target_pairs={{0,2},{1,3},{2,0},{3,1},{4,6},{5,7},{6,4},{7,5},{8,10},{9,11},{10,... | collective-permute-start | bytes 1179656 | tf_op jit(solution)/shard_map/ppermute | solution.py:477
  412.1 27.2 %collective-permute-start.38 = (bf16[192,1024]{1,0:T(8,128)(2,1)}, bf16[192,1024]{1,0:T(8,128)(2,1)}, u32[]{:S(2)}, u32[]{:S(2)}) collective-permute-start(bf16[192,1024]{1,0:T(8,128)(2,1)} %get-tuple-element.108), channel_id=1, source_target_pairs={{0,3},{1,0},{2,1},{3,2},{4,7},{5,4},{6,5},{7,6},{8,11},{9,8},{10,9... | collective-permute-start | bytes 1179656 | tf_op jit(solution)/shard_map/ppermute | solution.py:477
  (78 other events, 1191.3 us)

commit v3 on v2

v3 whole, which is shorter than its diff:
```python
import jax
import jax.numpy as jnp
from jax import lax
from jax.experimental import pallas as pl
from jax.experimental.pallas import tpu as pltpu
from jax.sharding import PartitionSpec as P

HD = 64
SUB = 8
NEG_FILL = -1000000000.0
EPSILON = 1e-05
F32 = jnp.float32
BF16 = jnp.bfloat16
VMEM = pltpu.VMEM
ROOT_HALF = 0.7071067811865476
ROOT_TWO_PI = 0.3989422804014327
SLOTS = ((3, 0), (1, 0), (3, 1), (2, 1), (1, 1), (2, 0), (0, 0), (0, 1))


def nn(left, right):
    return lax.dot_general(left, right, (((1,), (0,)), ((), ())), preferred_element_type=F32)


def nt(left, right):
    return lax.dot_general(left, right, (((1,), (1,)), ((), ())), preferred_element_type=F32)


def tn(left, right):
    return lax.dot_general(left, right, (((0,), (0,)), ((), ())), preferred_element_type=F32)


def normed(values):
    average = jnp.mean(values, -1, keepdims=True)
    centered = values - average
    variance = jnp.mean(centered * centered, -1, keepdims=True)
    inverse = lax.rsqrt(variance + EPSILON)
    return centered * inverse, inverse


def norm_back(unit, inverse, gain, grad):
    scaled = grad * gain
    return (
        scaled
        - jnp.mean(scaled, -1, keepdims=True)
        - unit * jnp.mean(scaled * unit, -1, keepdims=True)
    ) * inverse


def row_sum(values):
    return jnp.sum(values, 0, keepdims=True)


def segments(meta, start, count, shape, axis):
    places = lax.broadcasted_iota(jnp.int32, shape, axis)
    found = jnp.zeros(shape, jnp.int32) - 1
    for j in range(count):
        found = found + (meta[start + j] <= places).astype(jnp.int32)
    return found, places


def fetch(pieces, place, target, low, high, sem):
    size = high - low
    blocks, rows = pieces[0].shape[:2]
    half = rows // 2
    for beside in (0, 1):
        whole = pieces[5 * beside : 5 * beside + 3]
        split = pieces[5 * beside + 3 : 5 * beside + 5]
        for offset in range(4):
            row = (place ^ (offset + 4 * beside)) * size
            for block in range(blocks):
                if offset < 3:
                    source = whole[offset].at[block, pl.ds(low, size)]
                    to = target.at[block + 1, pl.ds(pl.multiple_of(row, 16), size)]
                    pltpu.make_async_copy(source, to, sem).start()
                    continue
                for part in range(low // half, high // half):
                    at = 2 * block + part
                    source = split[at // blocks].at[at % blocks]
                    start = pl.multiple_of(row + part * half - low, 16)
                    to = target.at[block + 1, pl.ds(start, half)]
                    pltpu.make_async_copy(source, to, sem).start()


def fetch_own(source, target, low, sem):
    size = source.shape[0]
    pltpu.make_async_copy(source, target.at[0, pl.ds(low, size)], sem).start()


def arrive(target, sem):
    pltpu.make_async_copy(target, target, sem).wait()


def fetch_memory(blocks, line, target, sem):
    count = len(blocks)
    for step, block in enumerate(blocks):
        size = block.shape[0]
        row = pl.multiple_of(lax.rem(line + count - step, count) * size, 16)
        pltpu.make_async_copy(block, target.at[pl.ds(row, size)], sem).start()


def slot_of(offset, half):
    first = SLOTS.index((offset, 0))
    second = SLOTS.index((offset, 1))
    return jnp.where(half == 0, first, second)


def self_mask(meta, nseg, slots):
    shape = (slots, slots)
    query_segment, query_place = segments(meta, 4, nseg, shape, 0)
    key_segment, key_place = segments(meta, 4, nseg, shape, 1)
    return (query_segment == key_segment) & (key_place <= query_place) & (key_place < meta[2])


def self_forward(dims, meta, x_ref, sb, ob, gain, bias, *refs):
    mp, local, heads, scaling, nseg = dims
    pieces, (own_self, own_sp) = refs[:10], refs[10:12]
    qkv, low, z1, first = refs[12:16]
    ws, acc, sems = refs[16:]
    fetch(pieces, meta[0], ws, 0, 96, sems.at[0])
    fetch_own(own_self, ws, 0, sems.at[0])
    fetch_own(own_sp, ws, 3 * local, sems.at[0])
    allowed = self_mask(meta, nseg, x_ref.shape[0])
    acc[...] = x_ref[...].astype(F32) + ob[0:1]
    arrive(ws, sems.at[0])

    def step(z, carry):
        flat = nt(x_ref[...], ws[z, : 3 * local])
        rows = sb[z]
        qkv[z, :, :local] = ((flat[:, :local] + rows[0:1]) * scaling).astype(BF16)
        qkv[z, :, local : 2 * local] = flat[:, local : 2 * local].astype(BF16)
        qkv[z, :, 2 * local :] = (flat[:, 2 * local :] + rows[1:2]).astype(BF16)
        for i in range(heads):
            at = HD * i
            scores = nt(qkv[z, :, at : at + HD], qkv[z, :, local + at : local + at + HD])
            scores = jnp.where(allowed, scores, NEG_FILL)
            weights = jnp.exp(scores - jnp.max(scores, -1, keepdims=True))
            probs = (weights / jnp.sum(weights, -1, keepdims=True)).astype(BF16)
            out = nn(probs, qkv[z, :, 2 * local + at : 2 * local + at + HD])
            low[z, :, at : at + HD] = out.astype(BF16)
        acc[...] += nn(low[z], ws[z, 3 * local :])
        return carry

    lax.fori_loop(0, mp, step, 0)
    z1[...] = acc[...]
    unit, _ = normed(acc[...])
    first[...] = unit * gain[0:1] + bias[0:1]


def cross_mask(meta, nseg, slots, mem_slots):
    query_segment, _ = segments(meta, 4, nseg, (slots, 1), 0)
    key_segment, key_place = segments(meta, 4 + nseg, nseg, (1, mem_slots), 1)
    key_segment = jnp.where(key_place < meta[3], key_segment, -1)
    return query_segment == key_segment


def fetch_cross(pieces, owns, place, target, sem):
    fetch(pieces, place, target, 96, 192, sem)
    row = 0
    for own in owns:
        fetch_own(own, target, row, sem)
        row += own.shape[0]


def cross_forward(dims, meta, cb, ob, gain, bias, first, *refs):
    mp, local, heads, scaling, nseg = dims
    blocks, pieces, owns = refs[:mp], refs[mp : mp + 10], refs[mp + 10 : mp + 13]
    cq, kv, low, total, z2, second = refs[mp + 13 : mp + 19]
    wc, mem, acc, sems = refs[mp + 19 :]
    fetch_cross(pieces, owns, meta[0], wc, sems.at[0])
    fetch_memory(blocks, meta[1], mem, sems.at[1])
    allowed = cross_mask(meta, nseg, first.shape[0], mem.shape[1])
    acc[...] = first[...] + ob[1:2]
    first_low = first[...].astype(BF16)
    arrive(wc, sems.at[0])
    arrive(mem, sems.at[1])

    def step(z, carry):
        rows = cb[z]
        cq[z] = ((nt(first_low, wc[z, :local]) + rows[0:1]) * scaling).astype(BF16)
        flat = nn(wc[z, 2 * local :], mem[...])
        column = jnp.swapaxes(jnp.broadcast_to(rows[1:2], (8, local)), 0, 1)[:, :1]
        kv[z, :local] = flat[:local].astype(BF16)
        kv[z, local:] = (flat[local:] + column).astype(BF16)
        for i in range(heads):
            at = HD * i
            scores = nn(cq[z, :, at : at + HD], kv[z, at : at + HD])
            scores = jnp.where(allowed, scores, NEG_FILL)
            peak = jnp.max(scores, -1, keepdims=True)
            weights = jnp.exp(scores - peak)
            mass = jnp.sum(weights, -1, keepdims=True)
            probs = (weights / mass).astype(BF16)
            low[z, :, at : at + HD] = nt(probs, kv[z, local + at : local + at + HD]).astype(BF16)
            total[z * heads + i] = peak + jnp.log(mass)
        acc[...] += nn(low[z], wc[z, local : 2 * local])
        return carry

    lax.fori_loop(0, mp, step, 0)
    z2[...] = acc[...]
    unit, _ = normed(acc[...])
    second[...] = unit * gain[1:2] + bias[1:2]


def put_slots(beside, mine, place, z, base, size, source):
    half = lax.div(z, 2)
    at = lax.rem(z, 2)
    for offset in range(4):
        slot = slot_of(offset, half)
        for target, flip in ((mine, 0), (beside, 4)):
            row = pl.multiple_of((place ^ (offset + flip)) * size, 16)
            target[slot, at, base : base + size] = source[pl.ds(row, size)].astype(BF16)


def ffn_both(dims, meta, second, z2, grad, ib, ob, gain, bias, *refs):
    mp, local, heads, scaling, nseg = dims
    pieces, (own_in, own_out) = refs[:10], refs[10:12]
    result, dz2, sums, beside, mine = refs[12:17]
    win, wout, acc, act, slope, dw, sems = refs[17:]
    place = meta[0]
    fetch(pieces, place, win, 0, 96, sems.at[0])
    fetch_own(own_in, win, 0, sems.at[0])
    fetch(pieces, place, wout, 96, 192, sems.at[1])
    fetch_own(own_out, wout, 0, sems.at[1])
    acc[...] = second[...] + ob[2:3]
    second_low = second[...].astype(BF16)
    arrive(win, sems.at[0])
    arrive(wout, sems.at[1])

    def forward(z, carry):
        inner = nn(second_low, win[z]) + ib[z]
        share = 0.5 * (1.0 + lax.erf(inner * ROOT_HALF))
        act[z] = (inner * share).astype(BF16)
        slope[z] = share + inner * (ROOT_TWO_PI * jnp.exp(-0.5 * inner * inner))
        acc[...] += nn(act[z], wout[z])
        return carry

    lax.fori_loop(0, mp, forward, 0)
    unit, inverse = normed(acc[...])
    result[...] = (unit * gain[2:3] + bias[2:3]).astype(BF16)
    out_grad = grad[...].astype(F32)
    third = norm_back(unit, inverse, gain[2:3], out_grad)
    sums[...] = jnp.zeros_like(sums)
    sums[0:1] = row_sum(third)
    sums[1:2] = row_sum(out_grad * unit)
    sums[2:3] = row_sum(out_grad)
    third_low = third.astype(BF16)
    acc[...] = third

    def backward(z, carry):
        inner = nt(third_low, wout[z]) * slope[z]
        sums[pl.ds(8 + z, 1)] = row_sum(inner)
        inner_low = inner.astype(BF16)
        acc[...] += nt(inner_low, win[z])
        dw[...] = tn(second_low, inner_low)
        put_slots(beside, mine, place, z, 0, 96, dw)
        dw[...] = tn(act[z], third_low)
        put_slots(beside, mine, place, z, 96, 96, dw)
        return carry

    lax.fori_loop(0, mp, backward, 0)
    unit, inverse = normed(z2[...])
    grad_rows = acc[...]
    values = norm_back(unit, inverse, gain[1:2], grad_rows)
    dz2[...] = values
    sums[3:4] = row_sum(values)
    sums[4:5] = row_sum(grad_rows * unit)
    sums[5:6] = row_sum(grad_rows)


def cross_back(dims, meta, dz2, cq, total, z1, gain, *refs):
    mp, local, heads, scaling, nseg = dims
    kv_ref, pieces, owns = refs[0], refs[1:11], refs[11:14]
    mem_out, kv_low, dcq, dz1, sums, sums_local = refs[14:20]
    wc, kv, dmem, acc, dout, sems = refs[20:]
    fetch_cross(pieces, owns, meta[0], wc, sems.at[0])
    pltpu.make_async_copy(kv_ref, kv, sems.at[1]).start()
    allowed = cross_mask(meta, nseg, dz2.shape[0], kv.shape[2])
    dz2_low = dz2[...].astype(BF16)
    acc[...] = dz2[...]
    dmem[...] = jnp.zeros_like(dmem)
    arrive(wc, sems.at[0])
    arrive(kv, sems.at[1])

    def step(z, carry):
        dout[...] = nt(dz2_low, wc[z, local : 2 * local]).astype(BF16)
        for i in range(heads):
            at = HD * i
            query = cq[z, :, at : at + HD]
            key = kv[z, at : at + HD]
            value = kv[z, local + at : local + at + HD]
            grad = dout[:, at : at + HD]
            scores = jnp.where(allowed, nn(query, key), NEG_FILL)
            probs = jnp.exp(scores - total[z * heads + i])
            probs_low = probs.astype(BF16)
            prob_grad = nn(grad, value)
            offset = jnp.sum(probs * prob_grad, -1, keepdims=True)
            score_grad = (probs * (prob_grad - offset)).astype(BF16)
            kv_low[z, at : at + HD] = tn(query, score_grad).astype(BF16)
            kv_low[z, local + at : local + at + HD] = tn(grad, probs_low).astype(BF16)
            mass = jnp.sum(probs_low.astype(F32), -1, keepdims=True)
            query_grad = nt(score_grad, key) * scaling
            dcq[z, :, at : at + HD] = query_grad.astype(BF16)
            sums_local[z, 0:1, at : at + HD] = row_sum(query_grad)
            sums_local[z, 1:2, at : at + HD] = row_sum(mass * grad.astype(F32))
        acc[...] += nn(dcq[z], wc[z, :local])
        dmem[...] += tn(wc[z, 2 * local :], kv_low[z])
        return carry

    lax.fori_loop(0, mp, step, 0)
    for block in range(mp):
        row = pl.multiple_of(lax.rem(meta[1] + block, mp) * local, 16)
        mem_out[block] = dmem[pl.ds(row, local)].astype(BF16)
    unit, inverse = normed(z1[...])
    grad_rows = acc[...]
    values = norm_back(unit, inverse, gain[0:1], grad_rows)
    dz1[...] = values
    sums[...] = jnp.zeros_like(sums)
    sums[0:1] = row_sum(values)
    sums[1:2] = row_sum(grad_rows * unit)
    sums[2:3] = row_sum(grad_rows)


def head_back(dims, meta, dz1, x_ref, qkv, self_low, dz2, first, dcq, cross_low, *refs):
    mp, local, heads, scaling, nseg = dims
    cross_sums, cross_local, ffn_sums = refs[:3]
    refs = refs[3:]
    kv_ref, blocks, pieces = refs[0], refs[1 : 1 + mp], refs[1 + mp : 11 + mp]
    own_self, own_sp = refs[11 + mp : 13 + mp]
    dx, small, beside, mine = refs[13 + mp : 17 + mp]
    ws, kv, mem, acc, dout, dqkv, dw, sums_local, sems = refs[17 + mp :]
    place = meta[0]
    fetch(pieces, place, ws, 0, 96, sems.at[0])
    fetch_own(own_self, ws, 0, sems.at[0])
    fetch_own(own_sp, ws, 3 * local, sems.at[0])
    pltpu.make_async_copy(kv_ref, kv, sems.at[1]).start()
    fetch_memory(blocks, meta[1], mem, sems.at[2])
    allowed = self_mask(meta, nseg, x_ref.shape[0])
    dz1_low = dz1[...].astype(BF16)
    dz2_low = dz2[...].astype(BF16)
    first_low = first[...].astype(BF16)
    acc[...] = dz1[...]
    arrive(ws, sems.at[0])
    arrive(kv, sems.at[1])
    arrive(mem, sems.at[2])

    def step(z, carry):
        dout[...] = nt(dz1_low, ws[z, 3 * local :]).astype(BF16)
        for i in range(heads):
            at = HD * i
            query = qkv[z, :, at : at + HD]
            key = qkv[z, :, local + at : local + at + HD]
            value = qkv[z, :, 2 * local + at : 2 * local + at + HD]
            grad = dout[:, at : at + HD]
            scores = jnp.where(allowed, nt(query, key), NEG_FILL)
            weights = jnp.exp(scores - jnp.max(scores, -1, keepdims=True))
            probs = weights / jnp.sum(weights, -1, keepdims=True)
            prob_grad = nt(grad, value)
            offset = jnp.sum(probs * prob_grad, -1, keepdims=True)
            score_grad = (probs * (prob_grad - offset)).astype(BF16)
            value_grad = tn(probs.astype(BF16), grad)
            query_grad = nn(score_grad, key) * scaling
            dqkv[:, at : at + HD] = query_grad.astype(BF16)
            dqkv[:, local + at : local + at + HD] = tn(score_grad, query).astype(BF16)
            dqkv[:, 2 * local + at : 2 * local + at + HD] = value_grad.astype(BF16)
            sums_local[z, 0:1, at : at + HD] = row_sum(query_grad)
            sums_local[z, 1:2, at : at + HD] = row_sum(value_grad)
        acc[...] += nn(dqkv[...], ws[z, : 3 * local])
        dw[: 3 * local] = tn(dqkv[...], x_ref[...])
        dw[3 * local :] = tn(self_low[z], dz1_low)
        put_slots(beside, mine, place, z, 0, 96, dw)
        dw[:local] = tn(dcq[z], first_low)
        dw[local : 2 * local] = tn(cross_low[z], dz2_low)
        dw[2 * local :] = nt(kv[z], mem[...])
        put_slots(beside, mine, place, z, 96, 96, dw)
        return carry

    lax.fori_loop(0, mp, step, 0)
    dx[...] = acc[...]
    small[...] = jnp.zeros_like(small)
    small[0:3] = cross_sums[0:3]
    small[3:9] = ffn_sums[0:6]

    def collect(z, carry):
        row = 9 + 2 * lax.rem(meta[1] + mp - z, mp)
        for i, part in enumerate((sums_local, cross_local)):
            for j in (0, 1):
                at = (2 * i + j) * local
                small[pl.ds(row, 1), at : at + local] = part[z, j : j + 1]
        small[pl.ds(row + 1, 1)] = ffn_sums[pl.ds(8 + z, 1)]
        return carry

    lax.fori_loop(0, mp, collect, 0)


def place_rows(place, ranges, low, over_two, over_four, near, far, across):
    half = near.shape[0]
    rows = low.shape[0]

    def taken(offset, start, size):
        if offset >= 4:
            return across[pl.ds((offset - 4) * rows + start, size)]
        if offset < 3:
            return (low, over_two, over_four)[offset][pl.ds(start, size)]
        if start < half:
            return near[pl.ds(start, size)]
        return far[pl.ds(start - half, size)]

    for offset in range(8):
        position = place ^ offset
        for start, size, targets in ranges:
            if offset == 3 and start < half < start + size:
                parts = ((start, half - start), (half, start + size - half))
            else:
                parts = ((start, size),)
            for begin, length in parts:
                source = taken(offset, begin, length).astype(F32)
                first = 0
                for target in targets:
                    count = target.shape[0] // size

                    @pl.when((position >= first) & (position < first + count))
                    def _():
                        row = (position - first) * size + (begin - start)
                        target[pl.ds(pl.multiple_of(row, 8), length)] = source

                    first += count


def finish_heads(meta, *refs):
    place_rows(meta[0], ((0, 96, refs[6:8]), (96, 96, refs[8:])), *refs[:6])


def finish_ffn(meta, *refs):
    gi, go = refs[6:]
    place_rows(meta[0], ((0, 96, (gi,)), (96, 96, (go,))), *refs[:6])


def join_columns(meta, *refs):
    blocks, target = refs[:-1], refs[-1]
    count = len(blocks)
    for step, block in enumerate(blocks):
        size = block.shape[1]
        at = pl.multiple_of(lax.rem(meta[1] + count - step, count) * size, 128)
        target[:, pl.ds(at, size)] = block[...].astype(target.dtype)


def join_rows(meta, *refs):
    blocks, target = refs[:-1], refs[-1]
    count = len(blocks)
    for step, block in enumerate(blocks):
        size = block.shape[0]
        at = pl.multiple_of(lax.rem(meta[1] + count - step, count) * size, 16)
        target[pl.ds(at, size)] = block[...].astype(target.dtype)


def shaped(shape, dtype=F32):
    return jax.ShapeDtypeStruct(shape, dtype)


def in_vmem(count):
    return [pl.BlockSpec(memory_space=pltpu.VMEM)] * count


def in_place(count):
    return [pl.BlockSpec(memory_space=pl.ANY)] * count


META = pl.BlockSpec(memory_space=pltpu.SMEM)


def call(kernel, in_specs, outs, scratch, flops, moved, name):
    return pl.pallas_call(
        kernel,
        out_shape=outs,
        in_specs=in_specs,
        out_specs=in_vmem(len(outs)),
        scratch_shapes=scratch,
        name=name,
        compiler_params=pltpu.CompilerParams(vmem_limit_bytes=60 * 1024 * 1024),
        cost_estimate=pl.CostEstimate(
            flops=flops // 16, bytes_accessed=moved // 4, transcendentals=0
        ),
    )


def solution(mesh):
    dp = mesh.shape["dp"]
    mp = mesh.shape["mp"]

    def swap(value, bit):
        return lax.ppermute(value, "dp", [(i, i ^ bit) for i in range(dp)])

    def shift(value, step):
        return lax.ppermute(value, "mp", [(i, (i + step) % mp) for i in range(mp)])

    def flip(value, bit):
        return lax.ppermute(value, "mp", [(i, i ^ bit) for i in range(mp)])

    def after(value, *others):
        return lax.optimization_barrier((value,) + others)[0] if others else value

    def meet(*values):
        return lax.optimization_barrier(values)

    def near_chips(own):
        return swap(own, 2), swap(own, 4)

    def far_chips(over_two, over_four):
        def halves(piece):
            if piece.ndim == 3:
                piece = piece.reshape(-1, piece.shape[1] // 2, piece.shape[2])
            half = piece.shape[0] // 2
            return piece[:half], piece[half:]

        return swap(halves(over_four)[0], 2), swap(halves(over_two)[1], 4)

    def beside(pieces):
        found = []
        for piece in pieces:
            found.append(swap(after(piece, *found[-1:]), 1))
        return found

    class Group:
        def __init__(self, *pairs):
            self.pairs = pairs
            self.low = self.summed(slice(0, 6)).astype(BF16)

        def summed(self, slots):
            parts = [
                mine[slots].astype(F32) + other[slots].astype(F32) for other, mine in self.pairs
            ]
            return parts[0] if len(parts) == 1 else jnp.concatenate(parts, axis=-2)

        def first(self):
            return swap(self.low[0:2], 2), swap(self.low[2:4], 4)

        def second(self, from_two, from_four):
            late_four = (self.low[5].astype(F32) + from_two[0].astype(F32)).astype(BF16)
            late_two = (self.low[4].astype(F32) + from_four[0].astype(F32)).astype(BF16)
            return late_two, late_four

        def third(self, from_two, from_four, late_two, late_four):
            top = self.summed(6) + from_two[1].astype(F32) + late_four.astype(F32)
            end = self.summed(7) + from_four[1].astype(F32) + late_two.astype(F32)
            bit = SUB
            while bit < dp:
                top = top + swap(top, bit)
                end = end + swap(end, bit)
                bit *= 2
            blocks = [top[0], top[1], end[0], end[1]]
            return blocks[0], [block.astype(BF16) for block in blocks[1:]]

    def line_sum(total, sent):
        for piece in sent:
            total = total + piece.astype(F32)
        return total.astype(BF16)

    def body(
        hidden,
        memory,
        out_grad,
        dec_starts,
        dec_length,
        mem_starts,
        mem_length,
        self_qkv,
        self_qv_bias,
        self_proj,
        cross_query,
        cross_kv,
        cross_qv_bias,
        cross_proj,
        ffn_in,
        ffn_in_bias,
        ffn_out,
        out_biases,
        norm_gains,
        norm_biases,
    ):
        row_count = dec_starts.shape[0]
        assert row_count == mp == 4 and dp % SUB == 0
        slots = hidden.shape[0] // row_count
        mem_slots = memory.shape[0] // row_count
        width = hidden.shape[1]
        local = self_proj.shape[0]
        heads = local // HD
        inner = ffn_out.shape[0]
        nseg = dec_starts.shape[1]
        dims = (mp, local, heads, HD ** (-0.5), nseg)
        line = lax.axis_index("mp")
        device = lax.axis_index("dp") % SUB
        place = (device & 1) * 4 + device // 2

        def row_of(array, size):
            return lax.dynamic_slice_in_dim(array, line * size, size, 0)

        def slice_of(array):
            size = array.shape[0] // SUB
            return lax.dynamic_slice_in_dim(array, place * size, size, 0)

        meta = jnp.concatenate(
            [
                jnp.stack([place, line]).astype(jnp.int32),
                row_of(dec_length, 1),
                row_of(mem_length, 1),
                row_of(dec_starts, 1)[0],
                row_of(mem_starts, 1)[0],
            ]
        )
        own_self = jnp.swapaxes(self_qkv, 1, 2).reshape(3 * local, width)
        own_cq = cross_query.T
        own_kv = jnp.swapaxes(cross_kv, 1, 2).reshape(2 * local, width)

        bias = jnp.concatenate(
            [self_qv_bias.reshape(-1), cross_qv_bias.reshape(-1), ffn_in_bias]
        ).reshape(-1, width)
        terms = []
        rest = bias
        for _ in range(3):
            term = lax.reduce_precision(rest, 8, 7)
            terms.append(term.astype(BF16))
            rest = rest - term
        bias_rows = 3 * bias.shape[0]
        terms = jnp.concatenate(terms + [jnp.zeros((16 - bias_rows, width), BF16)])
        head_piece = jnp.concatenate(
            [
                slice_of(jnp.concatenate([own_self, self_proj])),
                slice_of(jnp.concatenate([own_cq, cross_proj, own_kv])),
                terms,
            ]
        )
        ffn_piece = jnp.concatenate([slice_of(ffn_in), slice_of(ffn_out)])
        memory_t = memory.T
        memory_blocks = [
            lax.dynamic_slice_in_dim(memory_t, ((line + step) % mp) * mem_slots, mem_slots, 1)
            for step in range(mp)
        ]
        head_line = [shift(head_piece, step) for step in range(1, mp)]
        rows = head_piece.shape[0] - 16
        head_own = jnp.stack([piece[:rows] for piece in head_line])
        head_near = near_chips(head_own)
        ffn_piece = after(ffn_piece, *head_line)
        ffn_line = [shift(ffn_piece, step) for step in range(1, mp)]
        head_own, head_near, ffn_line, memory_blocks = meet(
            head_own, head_near, ffn_line, memory_blocks
        )
        head_far = far_chips(*head_near)
        head_beside = [swap(head_own, 1), swap(head_near[0], 1)]
        memory_blocks[1] = shift(memory_blocks[1], 1)
        ffn_own = jnp.stack(ffn_line)
        head_own, head_near, head_far, head_beside, ffn_own, memory_blocks = meet(
            head_own, head_near, head_far, head_beside, ffn_own, memory_blocks
        )
        head_beside += beside((head_near[1], *head_far))
        head_pieces = (head_own, *head_near, *head_far, *head_beside)
        ffn_near = near_chips(ffn_own)
        memory_blocks[2] = shift(memory_blocks[2], 2)
        biases = [bias]
        for piece in head_line:
            term = piece[rows : rows + bias_rows].reshape(3, -1, width).astype(F32)
            biases.append((term[0] + term[1]) + term[2])
        biases = jnp.stack(biases).reshape(mp, -1)

        self_bias = biases[:, : 2 * local].reshape(mp, 2, local)
        cross_bias = biases[:, 2 * local : 4 * local].reshape(mp, 2, local)
        inner_bias = biases[:, None, 4 * local :]
        hidden_row = row_of(hidden, slots)
        grad_row = row_of(out_grad, slots)
        params = (out_biases, norm_gains, norm_biases)
        dma = pltpu.SemaphoreType.DMA((2,))
        square = VMEM((width, width), F32)
        weights_shape = VMEM((mp, 4 * local, width), BF16)
        flat_shape = VMEM((slots, width), F32)
        kv_shape = VMEM((mp, 2 * local, mem_slots), BF16)
        row_shape = shaped((slots, width))
        low_shape = shaped((mp, slots, local), BF16)
        head_slots = shaped((8, 2, 4 * local // SUB, width), BF16)
        ffn_slots = shaped((8, 2, 2 * width // SUB, width), BF16)
        matmul = 2 * slots * width * width
        plain = width * width * 2

        def spread_line(rows):
            return [rows] + [shift(rows, step) for step in range(1, mp)]

        def bound(kernel):
            return lambda *refs: kernel(dims, *refs)

        qkv, self_low, z1, first = call(
            bound(self_forward),
            [META] + in_vmem(5) + in_place(12),
            (shaped((mp, slots, 3 * local), BF16), low_shape, row_shape, row_shape),
            [weights_shape, flat_shape, dma],
            20 * matmul,
            8 * plain,
            "self_forward",
        )(meta, hidden_row, self_bias, *params, *head_pieces, own_self, self_proj)
        ffn_own, ffn_near, memory_blocks, qkv, self_low, z1, first = meet(
            ffn_own, ffn_near, memory_blocks, qkv, self_low, z1, first
        )
        ffn_far = far_chips(*ffn_near)
        memory_blocks[3] = shift(memory_blocks[3], 3)
        ffn_far, ffn_beside, memory_blocks, first = meet(
            ffn_far, [swap(ffn_own, 1)], memory_blocks, first
        )
        ffn_beside += [swap(piece, 1) for piece in (*ffn_near, *ffn_far)]
        ffn_pieces = (ffn_own, *ffn_near, *ffn_far, *ffn_beside)
        cross_q, kv, cross_low, cross_total, z2, second = call(
            bound(cross_forward),
            [META] + in_vmem(5) + in_place(mp + 13),
            (
                low_shape,
                shaped((mp, 2 * local, mem_slots), BF16),
                low_shape,
                shaped((mp * heads, slots, 1)),
                row_shape,
                row_shape,
            ),
            [weights_shape, VMEM((width, mem_slots), BF16), flat_shape, dma],
            40 * matmul,
            8 * plain,
            "cross_forward",
        )(
            meta,
            cross_bias,
            *params,
            first,
            *memory_blocks,
            *head_pieces,
            own_cq,
            cross_proj,
            own_kv,
        )
        result, dz2, ffn_sums, ffn_beside, ffn_mine = call(
            bound(ffn_both),
            [META] + in_vmem(7) + in_place(12),
            (
                shaped((slots, width), BF16),
                row_shape,
                shaped((16, width)),
                ffn_slots,
                ffn_slots,
            ),
            [
                VMEM((mp, width, inner), BF16),
                VMEM((mp, inner, width), BF16),
                flat_shape,
                VMEM((mp, slots, inner), BF16),
                VMEM((mp, slots, inner), F32),
                square,
                dma,
            ],
            50 * matmul,
            16 * plain,
            "ffn_both",
        )(meta, second, z2, grad_row, inner_bias, *params, *ffn_pieces, ffn_in, ffn_out)
        ffn_other = swap(ffn_beside, 1)
        result_blocks = spread_line(result)

        memory_grads, kv_low, cross_dq, dz1, cross_sums, cross_local = call(
            bound(cross_back),
            [META] + in_vmem(5) + in_place(14),
            (
                shaped((mp, local, mem_slots), BF16),
                shaped((mp, 2 * local, mem_slots), BF16),
                low_shape,
                row_shape,
                shaped((8, width)),
                shaped((mp, 2, local)),
            ),
            [
                weights_shape,
                kv_shape,
                VMEM((width, mem_slots), F32),
                flat_shape,
                VMEM((slots, local), BF16),
                dma,
            ],
            50 * matmul,
            12 * plain,
            "cross_back",
        )(
            meta,
            dz2,
            cross_q,
            cross_total,
            z1,
            norm_gains,
            kv,
            *head_pieces,
            own_cq,
            cross_proj,
            own_kv,
        )
        ffn_other, result_blocks, memory_grads, kv_low, dz1 = meet(
            ffn_other, result_blocks, memory_grads, kv_low, dz1
        )
        ffn_group = Group((ffn_other, ffn_mine))
        ffn_group.low, dz1, memory_grads = meet(ffn_group.low, dz1, memory_grads)
        ffn_from = ffn_group.first()
        memory_out = [memory_grads[0]] + [shift(memory_grads[step], step) for step in (1, 2)]
        hidden_grad, small, head_beside, head_mine = call(
            bound(head_back),
            [META] + in_vmem(11) + in_place(mp + 13),
            (row_shape, shaped((24, width)), ffn_slots, ffn_slots),
            [
                weights_shape,
                kv_shape,
                VMEM((width, mem_slots), BF16),
                flat_shape,
                VMEM((slots, local), BF16),
                VMEM((slots, 3 * local), BF16),
                square,
                VMEM((mp, 2, local), F32),
                pltpu.SemaphoreType.DMA((3,)),
            ],
            60 * matmul,
            24 * plain,
            "head_back",
        )(
            meta,
            dz1,
            hidden_row,
            qkv,
            self_low,
            dz2,
            first,
            cross_dq,
            cross_low,
            cross_sums,
            cross_local,
            ffn_sums,
            kv_low,
            *memory_blocks,
            *head_pieces,
            own_self,
            self_proj,
        )
        ffn_from, memory_out, memory_grads, hidden_grad, small, head_beside, head_mine = meet(
            ffn_from, memory_out, memory_grads, hidden_grad, small, head_beside, head_mine
        )
        late_two, late_four = ffn_group.second(*ffn_from)
        head_other = swap(head_beside, 1)
        small = small + flip(small, 1)
        memory_out.append(shift(after(memory_grads[3], small), 3))
        ffn_late = swap(late_two, 2), swap(late_four, 4)
        ffn_late, head_other, memory_out = meet(ffn_late, head_other, memory_out)
        head_group = Group((head_other, head_mine))
        head_from = head_group.first()
        bit = 2
        while bit < mp:
            small = small + flip(small, bit)
            bit *= 2
        ffn_late = after(ffn_late[0], small), ffn_late[1]
        ffn_total, ffn_blocks = ffn_group.third(*ffn_from, *ffn_late)
        ffn_sent = [shift(ffn_blocks[step - 1], -step) for step in range(1, mp)]

        def joined(kernel, blocks, shape, dtype, name):
            return call(
                kernel, [META] + in_vmem(mp), (shaped(shape, dtype),), [], 0, 2 * plain, name
            )(meta, *blocks)[0]

        rows_shape = (mp * slots, width)
        memory_grad = joined(
            join_columns, memory_out, (local, mp * mem_slots), F32, "join_memory"
        )
        result = joined(join_rows, result_blocks, rows_shape, BF16, "join_result")
        head_from, ffn_sent, memory_grad, result, hidden_grad = meet(
            head_from, ffn_sent, memory_grad, result, hidden_grad
        )
        late_two, late_four = head_group.second(*head_from)
        head_late = swap(late_two, 2), swap(late_four, 4)
        hidden_blocks = spread_line(hidden_grad.astype(BF16))
        ffn_low = line_sum(ffn_total, ffn_sent)
        head_late, hidden_blocks, ffn_low, small = meet(head_late, hidden_blocks, ffn_low, small)
        head_total, head_blocks = head_group.third(*head_from, *head_late)
        ffn_near = near_chips(ffn_low)
        head_sent = [shift(head_blocks[0], -1), shift(head_blocks[2], -3)]
        ffn_near, head_sent, head_blocks = meet(ffn_near, head_sent, head_blocks)
        ffn_far = far_chips(*ffn_near)
        head_sent.append(shift(head_blocks[1], -2))
        hidden_grad = joined(join_rows, hidden_blocks, rows_shape, F32, "join_hidden")
        head_sent, ffn_near, ffn_far, small, hidden_grad = meet(
            head_sent, ffn_near, ffn_far, small, hidden_grad
        )
        head_low = line_sum(head_total, head_sent)
        head_near = near_chips(head_low)
        ffn_reduced = (ffn_low, *ffn_near, *ffn_far)
        ffn_reduced += (swap(jnp.concatenate(ffn_reduced), 1),)
        small = small + swap(small, 1)
        head_near, ffn_reduced, small = meet(head_near, ffn_reduced, small)
        grad_in, grad_out = call(
            finish_ffn,
            [META] + in_vmem(6),
            (shaped((width, inner)), shaped((inner, width))),
            [],
            0,
            plain,
            "finish_ffn",
        )(meta, *ffn_reduced)
        head_far = far_chips(*head_near)
        small = small + swap(small, 2)
        head_far, small, grad_in, grad_out = meet(head_far, small, grad_in, grad_out)
        head_reduced = (head_low, *head_near, *head_far)
        head_reduced += (swap(jnp.concatenate(head_reduced), 1),)
        small = small + swap(small, 4)
        bit = SUB
        while bit < dp:
            small = small + swap(small, bit)
            bit *= 2
        sharded = lax.dynamic_index_in_dim(
            small[9 : 9 + 2 * mp].reshape(mp, -1), line, 0, keepdims=False
        )
        grad_self, grad_sp, grad_cq, grad_cp, grad_kv = call(
            finish_heads,
            [META] + in_vmem(6),
            (
                shaped((3 * local, width)),
                shaped((local, width)),
                shaped((local, width)),
                shaped((local, width)),
                shaped((2 * local, width)),
            ),
            [],
            0,
            plain,
            "finish_heads",
        )(meta, *head_reduced)
        return (
            result,
            hidden_grad,
            memory_grad.T,
            jnp.swapaxes(grad_self.reshape(3, local, width), 1, 2),
            sharded[: 2 * local].reshape(2, local),
            grad_sp,
            grad_cq.T,
            jnp.swapaxes(grad_kv.reshape(2, local, width), 1, 2),
            sharded[2 * local : 4 * local].reshape(2, local),
            grad_cp,
            grad_in,
            sharded[4 * local :],
            grad_out,
            jnp.stack([small[0], small[6], small[3]]),
            jnp.stack([small[1], small[7], small[4]]),
            jnp.stack([small[2], small[8], small[5]]),
        )

    return jax.shard_map(
        body,
        mesh=mesh,
        in_specs=(
            P("dp", None),
            P("dp", "mp"),
            P("dp", None),
            P("dp", None),
            P("dp"),
            P("dp", None),
            P("dp"),
            P(None, None, "mp"),
            P(None, "mp"),
            P("mp", None),
            P(None, "mp"),
            P(None, None, "mp"),
            P(None, "mp"),
            P("mp", None),
            P(None, "mp"),
            P("mp"),
            P("mp", None),
            P(),
            P(),
            P(),
        ),
        out_specs=(
            P("dp", None),
            P("dp", None),
            P("dp", "mp"),
            P(None, None, "mp"),
            P(None, "mp"),
            P("mp", None),
            P(None, "mp"),
            P(None, None, "mp"),
            P(None, "mp"),
            P("mp", None),
            P(None, "mp"),
            P("mp"),
            P("mp", None),
            P(),
            P(),
            P(),
        ),
        check_vma=False,
    )
```

time: 454 us -> 376 us (0.83)
  waiting for transfers between devices: 201 us -> 146 us
  starting transfers between devices: 76.8 us -> 61.5 us
  other arithmetic: 39.9 us -> 27.9 us
  Pallas kernels: 97 us -> 102 us
    ppermute x41, waiting for transfers between devices: 68.6 us -> 20.6 us  [swap(): return lax.ppermute(value, 'dp', [(i, i ^ bit) for i in range(dp)])]
    add x9 -> x5, other arithmetic: 19.4 us -> 0.68 us  [the longest x1 0.64 us: body(): small = small + flip(small, bit)]
    ppermute x27 -> x24, starting transfers between devices: 31.7 us -> 24.4 us  [shift(): return lax.ppermute(value, 'mp', [(i, (i + step) % mp) for i in range(mp)])]
    convert_element_type x7 -> x10, other arithmetic: 7.79 us -> 15.1 us  [the longest x2 8.76 us: __init__(): self.low = self.summed(slice(0, 6)).astype(BF16)]
    ppermute x27 -> x24, waiting for transfers between devices: 133 us -> 126 us  [shift(): return lax.ppermute(value, 'mp', [(i, (i + step) % mp) for i in range(mp)])]
    ppermute x41, starting transfers between devices: 39.3 us -> 32.7 us  [swap(): return lax.ppermute(value, 'dp', [(i, i ^ bit) for i in range(dp)])]
    another operation x3 -> x5, other arithmetic: 1.13 us -> 7.42 us  [the longest x1 1.01 us: body(): ffn_line = jnp.stack([shift(ffn_piece, step) for step in range(1, mp)])]
    dynamic_update_slice x5 -> x0, other arithmetic: 5.88 us -> none  [the longest x4 5.84 us: body(): lax.dynamic_update_slice(memory_out, block.astype(F32), (0, at))]
  transfers between devices with their start and end apart: 70 -> 67, of which waited for: 28 -> 30; matrix products, arithmetic and copies ran while one was open for 15% -> 11% of each run, Pallas kernels for 16% -> 21%
where the time goes in v3:
time: 376 us; the launch traced here: 372 us
  waiting for transfers between devices  146 us (39%)
  Pallas kernels  102 us (27%)
  starting transfers between devices  61.5 us (16%)
  local copies, waits for them, and re-layouts  32.8 us (9%)
  other arithmetic  27.9 us (7%)
    ppermute x24, waiting for transfers between devices, shift(): return lax.ppermute(value, 'mp', [(i, (i + step) % mp) for i in range(mp)])  126 us
    ppermute x41, starting transfers between devices, swap(): return lax.ppermute(value, 'dp', [(i, i ^ bit) for i in range(dp)])  32.7 us
    ppermute x24, starting transfers between devices, shift(): return lax.ppermute(value, 'mp', [(i, (i + step) % mp) for i in range(mp)])  24.4 us
    pallas_call x1, Pallas kernels, body(): call(bound(head_back), [META] + in_vmem(11) + in_place(mp + 13), (row_sha...  23 us
    ppermute x41, waiting for transfers between devices, swap(): return lax.ppermute(value, 'dp', [(i, i ^ bit) for i in range(dp)])  20.6 us
    pallas_call x1, Pallas kernels, body(): call(bound(ffn_both), [META] + in_vmem(7) + in_place(12), (shaped((slots,...  19.3 us
    pallas_call x1, Pallas kernels, body(): call(bound(cross_back), [META] + in_vmem(5) + in_place(14), (shaped((mp,...  18.7 us
    pallas_call x1, Pallas kernels, body(): call(bound(cross_forward), [META] + in_vmem(5) + in_place(mp + 13), (low_...  14.9 us
  transfers between devices with their start and end apart: 67, of which 30 were waited for; matrix products, arithmetic and copies ran while one was open for 11% of the time, Pallas kernels for 21%

profile of v3, /device:TPU:9, one launch (start us, length us, event | category | flops | bytes accessed | tf_op | source)
XLA Modules:
  0.0 371.9 jit_solution(15063664153938669156)
XLA Ops:
  9.4 3.7 collective-permute-done.2
  13.1 14.3 %collective-permute-done.1 = bf16[208,768]{1,0:T(8,128)(2,1)S(1)} collective-permute-done((bf16[208,768]{1,0:T(8,128)(2,1)S(1)}, bf16[208,768]{1,0:T(8,128)(2,1)S(1)}, u32[]{:S(2)}, u32[]{:S(2)}) %collective-permute-start.1) | collective-permute-done | bytes 319520 | tf_op jit(solution)/shard_map/ppermute | solution.py:493
  27.4 6.8 %collective-permute-done = bf16[208,768]{1,0:T(8,128)(2,1)S(1)} collective-permute-done((bf16[208,768]{1,0:T(8,128)(2,1)S(1)}, bf16[208,768]{1,0:T(8,128)(2,1)S(1)}, u32[]{:S(2)}, u32[]{:S(2)}) %collective-permute-start) | collective-permute-done | bytes 319520 | tf_op jit(solution)/shard_map/ppermute | solution.py:493
  46.8 18.4 %collective-permute-done.6 = bf16[192,768]{1,0:T(8,128)(2,1)} collective-permute-done((bf16[192,768]{1,0:T(8,128)(2,1)}, bf16[192,768]{1,0:T(8,128)(2,1)}, u32[]{:S(2)}, u32[]{:S(2)}) %collective-permute-start.6) | collective-permute-done | bytes 294944 | tf_op jit(solution)/shard_map/ppermute | solution.py:493
  65.3 2.7 collective-permute-done.7
  72.3 7.6 %collective-permute-done.12.refs_7_.refs_14_ = bf16[192,1024]{1,0:T(8,128)(2,1)S(1)} collective-permute-done((bf16[192,1024]{1,0:T(8,128)(2,1)S(1)}, bf16[192,1024]{1,0:T(8,128)(2,1)S(1)}, u32[]{:S(2)}, u32[]{:S(2)}) %collective-permute-start.12) | collective-permute-done | bytes 393248 | tf_op jit(solution)/shard_map/ppermute | solution.py:493
  97.3 9.5 %self_forward.1 = (bf16[4,128,576]{2,1,0:T(8,128)(2,1)}, bf16[4,128,192]{2,1,0:T(8,128)(2,1)}, f32[128,768]{1,0:T(8,128)}, f32[128,768]{1,0:T(8,128)}) custom-call(s32[12]{0:T(128)} %concatenate.25.refs_0_.meta, bf16[128,768]{1,0:T(8,128)(2,1)} %constant_dynamic-slice_fusion.1.refs_1_.refs_2_, f32[4,2,192]{2,1,0:T(2,128)} %reshape.165.refs_2_, ...), custom_call_target="tpu_custom_call" | custom-call | flops 188743680 | bytes 2359296 | tf_op jit(solution)/shard_map/self_forward/pallas_call | solution.py:687
  106.8 4.8 %collective-permute-done.15.refs_8_.refs_15_ = bf16[192,1024]{1,0:T(8,128)(2,1)S(1)} collective-permute-done((bf16[192,1024]{1,0:T(8,128)(2,1)}, bf16[192,1024]{1,0:T(8,128)(2,1)S(1)}, u32[]{:S(2)}, u32[]{:S(2)}) %collective-permute-start.15) | collective-permute-done | bytes 393248 | tf_op jit(solution)/shard_map/ppermute | solution.py:493
  112.3 2.7 collective-permute-start.22
  119.1 4.4 %collective-permute-done.22.refs_9_.refs_16_ = bf16[192,1024]{1,0:T(8,128)(2,1)S(1)} collective-permute-done((bf16[192,1024]{1,0:T(8,128)(2,1)S(1)}, bf16[192,1024]{1,0:T(8,128)(2,1)S(1)}, u32[]{:S(2)}, u32[]{:S(2)}) %collective-permute-start.22) | collective-permute-done | bytes 393248 | tf_op jit(solution)/shard_map/ppermute | solution.py:493
  124.4 3.3 collective-permute-done.19.refs_11_
  133.2 14.9 %cross_forward.1 = (bf16[4,128,192]{2,1,0:T(8,128)(2,1)}, bf16[4,384,1024]{2,1,0:T(8,128)(2,1)}, bf16[4,128,192]{2,1,0:T(8,128)(2,1)}, f32[12,128,1]{2,1,0:T(8,1...) custom-call(s32[12]{0:T(128)} %concatenate.25.refs_0_.meta, f32[4,2,192]{2,1,0:T(2,128)} %reshape.162.refs_1_, ...), custom_call_target="tpu_custom_call" | custom-call | flops 377487360 | bytes 2359296 | tf_op jit(solution)/shard_map/cross_forward/pallas_call | solution.py:706
  149.0 19.3 %ffn_both.1 = (bf16[128,768]{1,0:T(8,128)(2,1)}, f32[128,768]{1,0:T(8,128)}, f32[16,768]{1,0:T(8,128)}, bf16[8,2,192,768]{3,2,1,0:T(8,128)(2,1)}, bf16[8,2,192,768]{3,2,1,0:T(8,128)(2,1)}) custom-call(s32[12]{0:T(128)} %concatenate.25.refs_0_.meta, f32[128,768]{1,0:T(8,128)} %get-tuple-element.208.refs_1_, f32[128,768]{1,0:T(8,128)} %get-tuple-element.209.refs_2_, ...), custom_call_target="tpu_custom_call" | custom-call | flops 471859200 | bytes 4718592 | tf_op jit(solution)/shard_map/ffn_both/pallas_call | solution.py:732
  168.8 3.4 collective-permute-start.29
  172.2 18.7 %cross_back.1 = (bf16[4,192,1024]{2,1,0:T(8,128)(2,1)}, bf16[4,384,1024]{2,1,0:T(8,128)(2,1)}, bf16[4,128,192]{2,1,0:T(8,128)(2,1)}, f32[128,768]{1,0:T(8,128)}, f32[8,768]{1,0:T(8,128)}, /*index=5*/f32[4,2,192]{2,1,0:T(2,128)}) custom-call(s32[12]{0:T(128)} %concatenate.25.refs_0_.meta, f32[128,768]{1,0:T(8,128)} %get-tuple-element.216.refs_1_.refs_5_, ...), custom_call_target="tpu_custom_call" | custom-call | flops 471859200 | bytes 3538944 | tf_op jit(solution)/shard_map/cross_back/pallas_call | solution.py:758
  191.8 4.0 %add_convert_fusion.1 = bf16[6,2,192,768]{3,2,1,0:T(8,128)(2,1)S(1)} fusion(bf16[8,2,192,768]{3,2,1,0:T(8,128)(2,1)} %collective-permute-done.27, bf16[8,2,192,768]{3,2,1,0:T(8,128)(2,1)} %get-tuple-element.213), kind=kLoop, calls=%fused_computation.1 | loop fusion | flops 7077888 | bytes 10616832 | tf_op jit(solution)/shard_map/convert_element_type | solution.py:525
  203.2 23.0 %head_back.1 = (f32[128,768]{1,0:T(8,128)}, f32[24,768]{1,0:T(8,128)}, bf16[8,2,192,768]{3,2,1,0:T(8,128)(2,1)}, bf16[8,2,192,768]{3,2,1,0:T(8,128)(2,1)}) custom-call(s32[12]{0:T(128)} %concatenate.25.refs_0_.meta, f32[128,768]{1,0:T(8,128)} %get-tuple-element.229.refs_1_, bf16[128,768]{1,0:T(8,128)(2,1)} %constant_dynamic-slice_fusion.1.refs_1_.refs_2_, ...), custom_call_target="tpu_custom_call" | custom-call | flops 566231040 | bytes 7077888 | tf_op jit(solution)/shard_map/head_back/pallas_call | solution.py:800
  228.1 3.0 collective-permute-start.38
  236.7 8.3 %collective-permute-done.39.refs_3_ = bf16[192,1024]{1,0:T(8,128)(2,1)S(1)} collective-permute-done((bf16[192,1024]{1,0:T(8,128)(2,1)S(1)}, bf16[192,1024]{1,0:T(8,128)(2,1)S(1)}, u32[]{:S(2)}, u32[]{:S(2)}) %collective-permute-start.39) | collective-permute-done | bytes 393248 | tf_op jit(solution)/shard_map/ppermute | solution.py:493
  247.3 4.7 %add_convert_fusion = bf16[6,2,192,768]{3,2,1,0:T(8,128)(2,1)S(1)} fusion(bf16[8,2,192,768]{3,2,1,0:T(8,128)(2,1)S(1)} %collective-permute-done.37, bf16[8,2,192,768]{3,2,1,0:T(8,128)(2,1)} %get-tuple-element.242), kind=kLoop, calls=%fused_computation | loop fusion | flops 7077888 | bytes 10616832 | tf_op jit(solution)/shard_map/convert_element_type | solution.py:525
  264.8 3.2 join_memory.1
  268.0 5.0 %collective-permute-done.44 = bf16[192,768]{1,0:T(8,128)(2,1)S(1)} collective-permute-done((bf16[192,768]{1,0:T(8,128)(2,1)}, bf16[192,768]{1,0:T(8,128)(2,1)S(1)}, u32[]{:S(2)}, u32[]{:S(2)}) %collective-permute-start.44) | collective-permute-done | bytes 294944 | tf_op jit(solution)/shard_map/ppermute | solution.py:493
  273.0 12.5 %collective-permute-done.45 = bf16[192,768]{1,0:T(8,128)(2,1)S(1)} collective-permute-done((bf16[192,768]{1,0:T(8,128)(2,1)}, bf16[192,768]{1,0:T(8,128)(2,1)S(1)}, u32[]{:S(2)}, u32[]{:S(2)}) %collective-permute-start.45) | collective-permute-done | bytes 294944 | tf_op jit(solution)/shard_map/ppermute | solution.py:493
  294.2 4.6 %collective-permute-done.49.refs_2_ = bf16[128,768]{1,0:T(8,128)(2,1)S(1)} collective-permute-done((bf16[128,768]{1,0:T(8,128)(2,1)S(1)}, bf16[128,768]{1,0:T(8,128)(2,1)S(1)}, u32[]{:S(2)}, u32[]{:S(2)}) %collective-permute-start.49) | collective-permute-done | bytes 196640 | tf_op jit(solution)/shard_map/ppermute | solution.py:493
  298.8 5.6 %collective-permute-done.50.refs_3_ = bf16[128,768]{1,0:T(8,128)(2,1)S(1)} collective-permute-done((bf16[128,768]{1,0:T(8,128)(2,1)S(1)}, bf16[128,768]{1,0:T(8,128)(2,1)S(1)}, u32[]{:S(2)}, u32[]{:S(2)}) %collective-permute-start.50) | collective-permute-done | bytes 196640 | tf_op jit(solution)/shard_map/ppermute | solution.py:493
  304.4 2.6 fusion
  312.8 10.0 %collective-permute-done.53 = bf16[192,768]{1,0:T(8,128)(2,1)S(1)} collective-permute-done((bf16[192,768]{1,0:T(8,128)(2,1)S(1)}, bf16[192,768]{1,0:T(8,128)(2,1)S(1)}, u32[]{:S(2)}, u32[]{:S(2)}) %collective-permute-start.53) | collective-permute-done | bytes 294944 | tf_op jit(solution)/shard_map/ppermute | solution.py:493
  327.1 8.7 %collective-permute-done.55 = bf16[192,768]{1,0:T(8,128)(2,1)S(1)} collective-permute-done((bf16[192,768]{1,0:T(8,128)(2,1)S(1)}, bf16[192,768]{1,0:T(8,128)(2,1)S(1)}, u32[]{:S(2)}, u32[]{:S(2)}) %collective-permute-start.55) | collective-permute-done | bytes 294944 | tf_op jit(solution)/shard_map/ppermute | solution.py:493
  340.9 5.3 %collective-permute-done.58.refs_1_ = bf16[192,768]{1,0:T(8,128)(2,1)S(1)} collective-permute-done((bf16[192,768]{1,0:T(8,128)(2,1)S(1)}, bf16[192,768]{1,0:T(8,128)(2,1)S(1)}, u32[]{:S(2)}, u32[]{:S(2)}) %collective-permute-start.58) | collective-permute-done | bytes 294944 | tf_op jit(solution)/shard_map/ppermute | solution.py:490
  350.1 4.3 %finish_ffn.1 = (f32[768,768]{1,0:T(8,128)}, f32[768,768]{1,0:T(8,128)}) custom-call(s32[12]{0:T(128)} %concatenate.25.refs_0_.meta, bf16[192,768]{1,0:T(8,128)(2,1)} %copy-done.14, bf16[192,768]{1,0:T(8,128)(2,1)} %copy-done.17, bf16[192,768]{1,0:T(8,128)(2,1)} %copy-done.18, bf16[96,768]{1,0:T(8,128)(2,1)} %copy-done.30, bf16[96,768]{1,0:T(8,128)(2,1)} %copy-done.31, ...), custom_call_target="tpu_custom_call" | custom-call | bytes 294912 | tf_op jit(solution)/shard_map/finish_ffn/pallas_call | solution.py:890
  358.5 3.9 %collective-permute-done.66 = f32[24,768]{1,0:T(8,128)S(1)} collective-permute-done((f32[24,768]{1,0:T(8,128)S(1)}, f32[24,768]{1,0:T(8,128)S(1)}, u32[]{:S(2)}, u32[]{:S(2)}) %collective-permute-start.66) | collective-permute-done | bytes 73760 | tf_op jit(solution)/shard_map/ppermute | solution.py:490
  367.4 4.4 %finish_heads.1 = (f32[576,768]{1,0:T(8,128)}, f32[192,768]{1,0:T(8,128)}, f32[192,768]{1,0:T(8,128)}, f32[192,768]{1,0:T(8,128)}, f32[384,768]{1,0:T(8,128)}) custom-call(s32[12]{0:T(128)} %concatenate.25.refs_0_.meta, bf16[192,768]{1,0:T(8,128)(2,1)} %copy-done.23, bf16[192,768]{1,0:T(8,128)(2,1)} %copy-done.15, bf16[192,768]{1,0:T(8,128)(2,1)} %copy-done.16, ...), custom_call_target="tpu_custom_call" | custom-call | bytes 294912 | tf_op jit(solution)/shard_map/finish_heads/pallas_call | solution.py:912
  (307 shorter events, 122.5 us)
Async XLA Ops:
  4.7 22.7 %collective-permute-start.1 = (bf16[208,768]{1,0:T(8,128)(2,1)S(1)}, bf16[208,768]{1,0:T(8,128)(2,1)S(1)}, u32[]{:S(2)}, u32[]{:S(2)}) collective-permute-start(bf16[208,768]{1,0:T(8,128)(2,1)S(1)} %concatenate.29), channel_id=1, source_target_pairs={{0,2},{1,3},{2,0},{3,1},{4,6},{5,7},{6,4},{7,5},{8,10},{9,11},{10,... | collective-permute-start | bytes 958472 | tf_op jit(solution)/shard_map/ppermute | solution.py:493
  7.2 27.1 %collective-permute-start = (bf16[208,768]{1,0:T(8,128)(2,1)S(1)}, bf16[208,768]{1,0:T(8,128)(2,1)S(1)}, u32[]{:S(2)}, u32[]{:S(2)}) collective-permute-start(bf16[208,768]{1,0:T(8,128)(2,1)S(1)} %concatenate.29), channel_id=1, source_target_pairs={{0,1},{1,2},{2,3},{3,0},{4,5},{5,6},{6,7},{7,4},{8,9},{9,10},{10,1... | collective-permute-start | bytes 958472 | tf_op jit(solution)/shard_map/ppermute | solution.py:493
  35.1 32.9 %collective-permute-start.3 = (bf16[3,192,768]{2,1,0:T(8,128)(2,1)S(1)}, bf16[3,192,768]{2,1,0:T(8,128)(2,1)S(1)}, u32[]{:S(2)}, u32[]{:S(2)}) collective-permute-start(bf16[3,192,768]{2,1,0:T(8,128)(2,1)S(1)} %pad_maximum_fusion.refs_6_.refs_10_.refs_7_.refs_17_), channel_id=1, source_target_pairs={{0,8},{4,12},{8,0},{12,4},{16,24},{20,28},{24,16},{28,20},{1,9},{5... | collective-permute-start | bytes 2654216 | tf_op jit(solution)/shard_map/ppermute | solution.py:490
  36.4 31.6 %collective-permute-start.4 = (bf16[3,192,768]{2,1,0:T(8,128)(2,1)S(1)}, bf16[3,192,768]{2,1,0:T(8,128)(2,1)S(1)}, u32[]{:S(2)}, u32[]{:S(2)}) collective-permute-start(bf16[3,192,768]{2,1,0:T(8,128)(2,1)S(1)} %pad_maximum_fusion.refs_6_.refs_10_.refs_7_.refs_17_), channel_id=1, source_target_pairs={{0,16},{4,20},{8,24},{12,28},{16,0},{20,4},{24,8},{28,12},{1,17},{... | collective-permute-start | bytes 2654216 | tf_op jit(solution)/shard_map/ppermute | solution.py:490
  41.5 23.7 %collective-permute-start.6 = (bf16[192,768]{1,0:T(8,128)(2,1)}, bf16[192,768]{1,0:T(8,128)(2,1)}, u32[]{:S(2)}, u32[]{:S(2)}) collective-permute-start(bf16[192,768]{1,0:T(8,128)(2,1)} %pad_maximum_fusion.2), channel_id=1, source_target_pairs={{0,2},{1,3},{2,0},{3,1},{4,6},{5,7},{6,4},{7,5},{8,10},{9,11},{10,... | collective-permute-start | bytes 884744 | tf_op jit(solution)/shard_map/ppermute | solution.py:493
  42.7 25.2 %collective-permute-start.7 = (bf16[192,768]{1,0:T(8,128)(2,1)}, bf16[192,768]{1,0:T(8,128)(2,1)}, u32[]{:S(2)}, u32[]{:S(2)}) collective-permute-start(bf16[192,768]{1,0:T(8,128)(2,1)} %pad_maximum_fusion.2), channel_id=1, source_target_pairs={{0,3},{1,0},{2,1},{3,2},{4,7},{5,4},{6,5},{7,6},{8,11},{9,8},{10,9... | collective-permute-start | bytes 884744 | tf_op jit(solution)/shard_map/ppermute | solution.py:493
  88.7 23.0 %collective-permute-start.13 = (bf16[3,192,768]{2,1,0:T(8,128)(2,1)}, bf16[3,192,768]{2,1,0:T(8,128)(2,1)}, u32[]{:S(2)}, u32[]{:S(2)}) collective-permute-start(bf16[3,192,768]{2,1,0:T(8,128)(2,1)} %pad_maximum_fusion.1.refs_8_), channel_id=1, source_target_pairs={{0,8},{4,12},{8,0},{12,4},{16,24},{20,28},{24,16},{28,20},{1,9},{5... | collective-permute-start | bytes 2654216 | tf_op jit(solution)/shard_map/ppermute | solution.py:490
  89.9 21.8 %collective-permute-start.14 = (bf16[3,192,768]{2,1,0:T(8,128)(2,1)}, bf16[3,192,768]{2,1,0:T(8,128)(2,1)}, u32[]{:S(2)}, u32[]{:S(2)}) collective-permute-start(bf16[3,192,768]{2,1,0:T(8,128)(2,1)} %pad_maximum_fusion.1.refs_8_), channel_id=1, source_target_pairs={{0,16},{4,20},{8,24},{12,28},{16,0},{20,4},{24,8},{28,12},{1,17},{... | collective-permute-start | bytes 2654216 | tf_op jit(solution)/shard_map/ppermute | solution.py:490
  92.7 19.0 %collective-permute-start.15 = (bf16[192,1024]{1,0:T(8,128)(2,1)}, bf16[192,1024]{1,0:T(8,128)(2,1)S(1)}, u32[]{:S(2)}, u32[]{:S(2)}) collective-permute-start(bf16[192,1024]{1,0:T(8,128)(2,1)} %get-tuple-element.180), channel_id=1, source_target_pairs={{0,2},{1,3},{2,0},{3,1},{4,6},{5,7},{6,4},{7,5},{8,10},{9,11},{10,... | collective-permute-start | bytes 1179656 | tf_op jit(solution)/shard_map/ppermute | solution.py:493
  111.6 17.0 %collective-permute-start.21 = (bf16[3,192,768]{2,1,0:T(8,128)(2,1)S(1)}, bf16[3,192,768]{2,1,0:T(8,128)(2,1)S(1)}, u32[]{:S(2)}, u32[]{:S(2)}) collective-permute-start(bf16[3,192,768]{2,1,0:T(8,128)(2,1)S(1)} %copy-done.13), channel_id=1, source_target_pairs={{0,4},{4,0},{8,12},{12,8},{16,20},{20,16},{24,28},{28,24},{1,5},{5... | collective-permute-start | bytes 2654216 | tf_op jit(solution)/shard_map/ppermute | solution.py:490
  118.1 29.9 %collective-permute-start.23 = (bf16[3,192,768]{2,1,0:T(8,128)(2,1)}, bf16[3,192,768]{2,1,0:T(8,128)(2,1)}, u32[]{:S(2)}, u32[]{:S(2)}) collective-permute-start(bf16[3,192,768]{2,1,0:T(8,128)(2,1)} %collective-permute-done.13.refs_9_), channel_id=1, source_target_pairs={{0,4},{4,0},{8,12},{12,8},{16,20},{20,16},{24,28},{28,24},{1,5},{5... | collective-permute-start | bytes 2654216 | tf_op jit(solution)/shard_map/ppermute | solution.py:490
  123.5 24.6 %collective-permute-start.24 = (bf16[3,192,768]{2,1,0:T(8,128)(2,1)}, bf16[3,192,768]{2,1,0:T(8,128)(2,1)}, u32[]{:S(2)}, u32[]{:S(2)}) collective-permute-start(bf16[3,192,768]{2,1,0:T(8,128)(2,1)} %collective-permute-done.14.refs_10_), channel_id=1, source_target_pairs={{0,4},{4,0},{8,12},{12,8},{16,20},{20,16},{24,28},{28,24},{1,5},{5... | collective-permute-start | bytes 2654216 | tf_op jit(solution)/shard_map/ppermute | solution.py:490
  128.7 19.4 %collective-permute-start.25 = (bf16[3,96,768]{2,1,0:T(8,128)(2,1)}, bf16[3,96,768]{2,1,0:T(8,128)(2,1)S(1)}, u32[]{:S(2)}, u32[]{:S(2)}) collective-permute-start(bf16[3,96,768]{2,1,0:T(8,128)(2,1)} %collective-permute-done.19.refs_11_), channel_id=1, source_target_pairs={{0,4},{4,0},{8,12},{12,8},{16,20},{20,16},{24,28},{28,24},{1,5},{5... | collective-permute-start | bytes 1327112 | tf_op jit(solution)/shard_map/ppermute | solution.py:490
  130.2 17.9 %collective-permute-start.26 = (bf16[3,96,768]{2,1,0:T(8,128)(2,1)}, bf16[3,96,768]{2,1,0:T(8,128)(2,1)S(1)}, u32[]{:S(2)}, u32[]{:S(2)}) collective-permute-start(bf16[3,96,768]{2,1,0:T(8,128)(2,1)} %collective-permute-done.20.refs_12_), channel_id=1, source_target_pairs={{0,4},{4,0},{8,12},{12,8},{16,20},{20,16},{24,28},{28,24},{1,5},{5... | collective-permute-start | bytes 1327112 | tf_op jit(solution)/shard_map/ppermute | solution.py:490
  168.3 22.7 %collective-permute-start.27 = (bf16[8,2,192,768]{3,2,1,0:T(8,128)(2,1)}, bf16[8,2,192,768]{3,2,1,0:T(8,128)(2,1)}, u32[]{:S(2)}, u32[]{:S(2)}) collective-permute-start(bf16[8,2,192,768]{3,2,1,0:T(8,128)(2,1)} %get-tuple-element.214), channel_id=1, source_target_pairs={{0,4},{4,0},{8,12},{12,8},{16,20},{20,16},{24,28},{28,24},{1,5},{5... | collective-permute-start | bytes 14155784 | tf_op jit(solution)/shard_map/ppermute | solution.py:490
  168.8 22.2 %collective-permute-start.28 = (bf16[128,768]{1,0:T(8,128)(2,1)}, bf16[128,768]{1,0:T(8,128)(2,1)S(1)}, u32[]{:S(2)}, u32[]{:S(2)}) collective-permute-start(bf16[128,768]{1,0:T(8,128)(2,1)} %get-tuple-element.260.refs_0_), channel_id=1, source_target_pairs={{0,1},{1,2},{2,3},{3,0},{4,5},{5,6},{6,7},{7,4},{8,9},{9,10},{10,1... | collective-permute-start | bytes 589832 | tf_op jit(solution)/shard_map/ppermute | solution.py:493
  168.8 22.2 %collective-permute-start.29 = (bf16[128,768]{1,0:T(8,128)(2,1)}, bf16[128,768]{1,0:T(8,128)(2,1)S(1)}, u32[]{:S(2)}, u32[]{:S(2)}) collective-permute-start(bf16[128,768]{1,0:T(8,128)(2,1)} %get-tuple-element.260.refs_0_), channel_id=1, source_target_pairs={{0,2},{1,3},{2,0},{3,1},{4,6},{5,7},{6,4},{7,5},{8,10},{9,11},{10,... | collective-permute-start | bytes 589832 | tf_op jit(solution)/shard_map/ppermute | solution.py:493
  172.2 18.8 %collective-permute-start.30 = (bf16[128,768]{1,0:T(8,128)(2,1)}, bf16[128,768]{1,0:T(8,128)(2,1)S(1)}, u32[]{:S(2)}, u32[]{:S(2)}) collective-permute-start(bf16[128,768]{1,0:T(8,128)(2,1)} %get-tuple-element.260.refs_0_), channel_id=1, source_target_pairs={{0,3},{1,0},{2,1},{3,2},{4,7},{5,4},{6,5},{7,6},{8,11},{9,8},{10,9... | collective-permute-start | bytes 589832 | tf_op jit(solution)/shard_map/ppermute | solution.py:493
  197.4 28.8 %collective-permute-start.31 = (bf16[2,2,192,768]{3,2,1,0:T(8,128)(2,1)}, bf16[2,2,192,768]{3,2,1,0:T(8,128)(2,1)}, u32[]{:S(2)}, u32[]{:S(2)}) collective-permute-start(bf16[2,2,192,768]{3,2,1,0:T(8,128)(2,1)} %get-tuple-element.331), channel_id=1, source_target_pairs={{0,8},{4,12},{8,0},{12,4},{16,24},{20,28},{24,16},{28,20},{1,9},{5... | collective-permute-start | bytes 3538952 | tf_op jit(solution)/shard_map/ppermute | solution.py:490
  198.6 27.6 %collective-permute-start.32 = (bf16[2,2,192,768]{3,2,1,0:T(8,128)(2,1)}, bf16[2,2,192,768]{3,2,1,0:T(8,128)(2,1)}, u32[]{:S(2)}, u32[]{:S(2)}) collective-permute-start(bf16[2,2,192,768]{3,2,1,0:T(8,128)(2,1)} %get-tuple-element.330), channel_id=1, source_target_pairs={{0,16},{4,20},{8,24},{12,28},{16,0},{20,4},{24,8},{28,12},{1,17},{... | collective-permute-start | bytes 3538952 | tf_op jit(solution)/shard_map/ppermute | solution.py:490
  199.9 26.3 %collective-permute-start.33 = (bf16[192,1024]{1,0:T(8,128)(2,1)}, bf16[192,1024]{1,0:T(8,128)(2,1)S(1)}, u32[]{:S(2)}, u32[]{:S(2)}) collective-permute-start(bf16[192,1024]{1,0:T(8,128)(2,1)} %get-tuple-element.333), channel_id=1, source_target_pairs={{0,1},{1,2},{2,3},{3,0},{4,5},{5,6},{6,7},{7,4},{8,9},{9,10},{10,1... | collective-permute-start | bytes 1179656 | tf_op jit(solution)/shard_map/ppermute | solution.py:493
  201.4 24.9 %collective-permute-start.34 = (bf16[192,1024]{1,0:T(8,128)(2,1)}, bf16[192,1024]{1,0:T(8,128)(2,1)}, u32[]{:S(2)}, u32[]{:S(2)}) collective-permute-start(bf16[192,1024]{1,0:T(8,128)(2,1)} %get-tuple-element.332), channel_id=1, source_target_pairs={{0,2},{1,3},{2,0},{3,1},{4,6},{5,7},{6,4},{7,5},{8,10},{9,11},{10,... | collective-permute-start | bytes 1179656 | tf_op jit(solution)/shard_map/ppermute | solution.py:493
  226.3 21.0 %collective-permute-start.37 = (bf16[8,2,192,768]{3,2,1,0:T(8,128)(2,1)}, bf16[8,2,192,768]{3,2,1,0:T(8,128)(2,1)S(1)}, u32[]{:S(2)}, u32[]{:S(2)}) collective-permute-start(bf16[8,2,192,768]{3,2,1,0:T(8,128)(2,1)} %get-tuple-element.245), channel_id=1, source_target_pairs={{0,4},{4,0},{8,12},{12,8},{16,20},{20,16},{24,28},{28,24},{1,5},{5... | collective-permute-start | bytes 14155784 | tf_op jit(solution)/shard_map/ppermute | solution.py:490
  232.6 14.6 %collective-permute-start.35 = (bf16[2,192,768]{2,1,0:T(8,128)(2,1)S(1)}, bf16[2,192,768]{2,1,0:T(8,128)(2,1)S(1)}, u32[]{:S(2)}, u32[]{:S(2)}) collective-permute-start(bf16[2,192,768]{2,1,0:T(8,128)(2,1)S(1)} %get-tuple-element.329), channel_id=1, source_target_pairs={{0,8},{4,12},{8,0},{12,4},{16,24},{20,28},{24,16},{28,20},{1,9},{5... | collective-permute-start | bytes 1769480 | tf_op jit(solution)/shard_map/ppermute | solution.py:490
  235.3 20.7 %collective-permute-start.43 = (f32[24,768]{1,0:T(8,128)S(1)}, f32[24,768]{1,0:T(8,128)S(1)}, u32[]{:S(2)}, u32[]{:S(2)}) collective-permute-start(f32[24,768]{1,0:T(8,128)S(1)} %add.221), channel_id=1, source_target_pairs={{0,2},{1,3},{2,0},{3,1},{4,6},{5,7},{6,4},{7,5},{8,10},{9,11},{10,... | collective-permute-start | bytes 221192 | tf_op jit(solution)/shard_map/ppermute | solution.py:496
  253.6 33.8 %collective-permute-start.40 = (bf16[2,2,192,768]{3,2,1,0:T(8,128)(2,1)}, bf16[2,2,192,768]{3,2,1,0:T(8,128)(2,1)}, u32[]{:S(2)}, u32[]{:S(2)}) collective-permute-start(bf16[2,2,192,768]{3,2,1,0:T(8,128)(2,1)} %get-tuple-element.327), channel_id=1, source_target_pairs={{0,8},{4,12},{8,0},{12,4},{16,24},{20,28},{24,16},{28,20},{1,9},{5... | collective-permute-start | bytes 3538952 | tf_op jit(solution)/shard_map/ppermute | solution.py:490
  254.7 32.7 %collective-permute-start.41 = (bf16[2,2,192,768]{3,2,1,0:T(8,128)(2,1)}, bf16[2,2,192,768]{3,2,1,0:T(8,128)(2,1)}, u32[]{:S(2)}, u32[]{:S(2)}) collective-permute-start(bf16[2,2,192,768]{3,2,1,0:T(8,128)(2,1)} %get-tuple-element.326), channel_id=1, source_target_pairs={{0,16},{4,20},{8,24},{12,28},{16,0},{20,4},{24,8},{28,12},{1,17},{... | collective-permute-start | bytes 3538952 | tf_op jit(solution)/shard_map/ppermute | solution.py:490
  260.4 25.1 %collective-permute-start.45 = (bf16[192,768]{1,0:T(8,128)(2,1)}, bf16[192,768]{1,0:T(8,128)(2,1)S(1)}, u32[]{:S(2)}, u32[]{:S(2)}) collective-permute-start(bf16[192,768]{1,0:T(8,128)(2,1)} %get-tuple-element.341), channel_id=1, source_target_pairs={{0,1},{1,2},{2,3},{3,0},{4,5},{5,6},{6,7},{7,4},{8,9},{9,10},{10,1... | collective-permute-start | bytes 884744 | tf_op jit(solution)/shard_map/ppermute | solution.py:493
  262.3 25.1 %collective-permute-start.42 = (bf16[192,768]{1,0:T(8,128)(2,1)}, bf16[192,768]{1,0:T(8,128)(2,1)}, u32[]{:S(2)}, u32[]{:S(2)}) collective-permute-start(bf16[192,768]{1,0:T(8,128)(2,1)} %fusion.14), channel_id=1, source_target_pairs={{0,3},{1,0},{2,1},{3,2},{4,7},{5,4},{6,5},{7,6},{8,11},{9,8},{10,9... | collective-permute-start | bytes 884744 | tf_op jit(solution)/shard_map/ppermute | solution.py:493
  288.9 15.5 %collective-permute-start.46 = (bf16[2,192,768]{2,1,0:T(8,128)(2,1)S(1)}, bf16[2,192,768]{2,1,0:T(8,128)(2,1)S(1)}, u32[]{:S(2)}, u32[]{:S(2)}) collective-permute-start(bf16[2,192,768]{2,1,0:T(8,128)(2,1)S(1)} %get-tuple-element.325), channel_id=1, source_target_pairs={{0,8},{4,12},{8,0},{12,4},{16,24},{20,28},{24,16},{28,20},{1,9},{5... | collective-permute-start | bytes 1769480 | tf_op jit(solution)/shard_map/ppermute | solution.py:490
  289.3 15.1 %collective-permute-start.47 = (bf16[2,192,768]{2,1,0:T(8,128)(2,1)S(1)}, bf16[2,192,768]{2,1,0:T(8,128)(2,1)S(1)}, u32[]{:S(2)}, u32[]{:S(2)}) collective-permute-start(bf16[2,192,768]{2,1,0:T(8,128)(2,1)S(1)} %get-tuple-element.324), channel_id=1, source_target_pairs={{0,16},{4,20},{8,24},{12,28},{16,0},{20,4},{24,8},{28,12},{1,17},{... | collective-permute-start | bytes 1769480 | tf_op jit(solution)/shard_map/ppermute | solution.py:490
  307.3 15.6 %collective-permute-start.53 = (bf16[192,768]{1,0:T(8,128)(2,1)S(1)}, bf16[192,768]{1,0:T(8,128)(2,1)S(1)}, u32[]{:S(2)}, u32[]{:S(2)}) collective-permute-start(bf16[192,768]{1,0:T(8,128)(2,1)S(1)} %fusion.15), channel_id=1, source_target_pairs={{0,3},{1,0},{2,1},{3,2},{4,7},{5,4},{6,5},{7,6},{8,11},{9,8},{10,9... | collective-permute-start | bytes 884744 | tf_op jit(solution)/shard_map/ppermute | solution.py:493
  (88 other events, 891.5 us)

commit v4 on v3

--- a/solution.py
+++ b/solution.py
@@ -58,16 +58,17 @@
     return found, places
 
 
-def fetch(pieces, place, target, low, high, sem):
+def fetch(pieces, place, target, low, high, sems):
     size = high - low
     blocks, rows = pieces[0].shape[:2]
     half = rows // 2
-    for beside in (0, 1):
-        whole = pieces[5 * beside : 5 * beside + 3]
-        split = pieces[5 * beside + 3 : 5 * beside + 5]
-        for offset in range(4):
-            row = (place ^ (offset + 4 * beside)) * size
-            for block in range(blocks):
+    for block in range(blocks):
+        sem = sems.at[block + 1]
+        for beside in (0, 1):
+            whole = pieces[5 * beside : 5 * beside + 3]
+            split = pieces[5 * beside + 3 : 5 * beside + 5]
+            for offset in range(4):
+                row = (place ^ (offset + 4 * beside)) * size
                 if offset < 3:
                     source = whole[offset].at[block, pl.ds(low, size)]
                     to = target.at[block + 1, pl.ds(pl.multiple_of(row, 16), size)]
@@ -81,9 +82,12 @@
                     pltpu.make_async_copy(source, to, sem).start()
 
 
-def fetch_own(source, target, low, sem):
-    size = source.shape[0]
-    pltpu.make_async_copy(source, target.at[0, pl.ds(low, size)], sem).start()
+def fetch_own(sources, target, sems):
+    row = 0
+    for source in sources:
+        size = source.shape[0]
+        pltpu.make_async_copy(source, target.at[0, pl.ds(row, size)], sems.at[0]).start()
+        row += size
 
 
 def arrive(target, sem):
@@ -116,14 +120,13 @@
     pieces, (own_self, own_sp) = refs[:10], refs[10:12]
     qkv, low, z1, first = refs[12:16]
     ws, acc, sems = refs[16:]
+    fetch_own((own_self, own_sp), ws, sems.at[0])
     fetch(pieces, meta[0], ws, 0, 96, sems.at[0])
-    fetch_own(own_self, ws, 0, sems.at[0])
-    fetch_own(own_sp, ws, 3 * local, sems.at[0])
     allowed = self_mask(meta, nseg, x_ref.shape[0])
     acc[...] = x_ref[...].astype(F32) + ob[0:1]
-    arrive(ws, sems.at[0])
 
     def step(z, carry):
+        arrive(ws.at[z], sems.at[0, z])
         flat = nt(x_ref[...], ws[z, : 3 * local])
         rows = sb[z]
         qkv[z, :, :local] = ((flat[:, :local] + rows[0:1]) * scaling).astype(BF16)
@@ -134,7 +137,7 @@
             scores = nt(qkv[z, :, at : at + HD], qkv[z, :, local + at : local + at + HD])
             scores = jnp.where(allowed, scores, NEG_FILL)
             weights = jnp.exp(scores - jnp.max(scores, -1, keepdims=True))
-            probs = (weights / jnp.sum(weights, -1, keepdims=True)).astype(BF16)
+            probs = (weights * (1.0 / jnp.sum(weights, -1, keepdims=True))).astype(BF16)
             out = nn(probs, qkv[z, :, 2 * local + at : 2 * local + at + HD])
             low[z, :, at : at + HD] = out.astype(BF16)
         acc[...] += nn(low[z], ws[z, 3 * local :])
@@ -154,11 +157,8 @@
 
 
 def fetch_cross(pieces, owns, place, target, sem):
+    fetch_own(owns, target, sem)
     fetch(pieces, place, target, 96, 192, sem)
-    row = 0
-    for own in owns:
-        fetch_own(own, target, row, sem)
-        row += own.shape[0]
 
 
 def cross_forward(dims, meta, cb, ob, gain, bias, first, *refs):
@@ -166,30 +166,32 @@
     blocks, pieces, owns = refs[:mp], refs[mp : mp + 10], refs[mp + 10 : mp + 13]
     cq, kv, low, total, z2, second = refs[mp + 13 : mp + 19]
     wc, mem, acc, sems = refs[mp + 19 :]
+    fetch_memory(blocks, meta[1], mem, sems.at[1, 0])
     fetch_cross(pieces, owns, meta[0], wc, sems.at[0])
-    fetch_memory(blocks, meta[1], mem, sems.at[1])
     allowed = cross_mask(meta, nseg, first.shape[0], mem.shape[1])
     acc[...] = first[...] + ob[1:2]
     first_low = first[...].astype(BF16)
-    arrive(wc, sems.at[0])
-    arrive(mem, sems.at[1])
+    arrive(mem, sems.at[1, 0])
 
     def step(z, carry):
+        arrive(wc.at[z], sems.at[0, z])
         rows = cb[z]
         cq[z] = ((nt(first_low, wc[z, :local]) + rows[0:1]) * scaling).astype(BF16)
         flat = nn(wc[z, 2 * local :], mem[...])
         column = jnp.swapaxes(jnp.broadcast_to(rows[1:2], (8, local)), 0, 1)[:, :1]
-        kv[z, :local] = flat[:local].astype(BF16)
-        kv[z, local:] = (flat[local:] + column).astype(BF16)
+        keys = flat[:local].astype(BF16)
+        values = (flat[local:] + column).astype(BF16)
+        kv[z, :local] = keys
+        kv[z, local:] = values
         for i in range(heads):
             at = HD * i
-            scores = nn(cq[z, :, at : at + HD], kv[z, at : at + HD])
+            scores = nn(cq[z, :, at : at + HD], keys[at : at + HD])
             scores = jnp.where(allowed, scores, NEG_FILL)
             peak = jnp.max(scores, -1, keepdims=True)
             weights = jnp.exp(scores - peak)
             mass = jnp.sum(weights, -1, keepdims=True)
-            probs = (weights / mass).astype(BF16)
-            low[z, :, at : at + HD] = nt(probs, kv[z, local + at : local + at + HD]).astype(BF16)
+            probs = (weights * (1.0 / mass)).astype(BF16)
+            low[z, :, at : at + HD] = nt(probs, values[at : at + HD]).astype(BF16)
             total[z * heads + i] = peak + jnp.log(mass)
         acc[...] += nn(low[z], wc[z, local : 2 * local])
         return carry
@@ -200,40 +202,50 @@
     second[...] = unit * gain[1:2] + bias[1:2]
 
 
-def put_slots(beside, mine, place, z, base, size, source):
+def put_slots(beside, mine, place, z, base, source, sem):
     half = lax.div(z, 2)
     at = lax.rem(z, 2)
+    size = source.shape[0] // SUB
     for offset in range(4):
         slot = slot_of(offset, half)
         for target, flip in ((mine, 0), (beside, 4)):
             row = pl.multiple_of((place ^ (offset + flip)) * size, 16)
-            target[slot, at, base : base + size] = source[pl.ds(row, size)].astype(BF16)
+            to = target.at[slot, at, pl.ds(base, size)]
+            pltpu.make_async_copy(source.at[pl.ds(row, size)], to, sem).start()
 
 
 def ffn_both(dims, meta, second, z2, grad, ib, ob, gain, bias, *refs):
     mp, local, heads, scaling, nseg = dims
     pieces, (own_in, own_out) = refs[:10], refs[10:12]
-    result, dz2, sums, beside, mine = refs[12:17]
-    win, wout, acc, act, slope, dw, sems = refs[17:]
+    result, dz2, sums, shared, own_half = refs[12:17]
+    win, wout, acc, act, slope, low, sems = refs[17:]
     place = meta[0]
+    width = second.shape[1]
+    half = width // 2
+    mine = pl.multiple_of(lax.div(place, 4) * half, 128)
+    other = pl.multiple_of((1 - lax.div(place, 4)) * half, 128)
+    fetch_own((own_in,), win, sems.at[0])
+    fetch_own((own_out,), wout, sems.at[1])
     fetch(pieces, place, win, 0, 96, sems.at[0])
-    fetch_own(own_in, win, 0, sems.at[0])
     fetch(pieces, place, wout, 96, 192, sems.at[1])
-    fetch_own(own_out, wout, 0, sems.at[1])
     acc[...] = second[...] + ob[2:3]
-    second_low = second[...].astype(BF16)
-    arrive(win, sems.at[0])
-    arrive(wout, sems.at[1])
+    low[...] = second[...].astype(BF16)
+    own_half[0] = low[:, pl.ds(mine, half)]
+    shared[0, :, width:] = low[:, pl.ds(other, half)]
 
     def forward(z, carry):
-        inner = nn(second_low, win[z]) + ib[z]
+        arrive(win.at[z], sems.at[0, z])
+        arrive(wout.at[z], sems.at[1, z])
+        inner = nn(low[...], win[z]) + ib[z]
         share = 0.5 * (1.0 + lax.erf(inner * ROOT_HALF))
         act[z] = (inner * share).astype(BF16)
+        own_half[z + 1] = act[z, :, pl.ds(mine, half)]
+        shared[z + 1, :, width:] = act[z, :, pl.ds(other, half)]
         slope[z] = share + inner * (ROOT_TWO_PI * jnp.exp(-0.5 * inner * inner))
         acc[...] += nn(act[z], wout[z])
         return carry
 
-    lax.fori_loop(0, mp, forward, 0)
+    lax.fori_loop(0, mp, forward, 0, unroll=True)
     unit, inverse = normed(acc[...])
     result[...] = (unit * gain[2:3] + bias[2:3]).astype(BF16)
     out_grad = grad[...].astype(F32)
@@ -243,6 +255,7 @@
     sums[1:2] = row_sum(out_grad * unit)
     sums[2:3] = row_sum(out_grad)
     third_low = third.astype(BF16)
+    shared[0, :, :width] = third_low
     acc[...] = third
 
     def backward(z, carry):
@@ -250,13 +263,10 @@
         sums[pl.ds(8 + z, 1)] = row_sum(inner)
         inner_low = inner.astype(BF16)
         acc[...] += nt(inner_low, win[z])
-        dw[...] = tn(second_low, inner_low)
-        put_slots(beside, mine, place, z, 0, 96, dw)
-        dw[...] = tn(act[z], third_low)
-        put_slots(beside, mine, place, z, 96, 96, dw)
+        shared[z + 1, :, :width] = inner_low
         return carry
 
-    lax.fori_loop(0, mp, backward, 0)
+    lax.fori_loop(0, mp, backward, 0, unroll=True)
     unit, inverse = normed(z2[...])
     grad_rows = acc[...]
     values = norm_back(unit, inverse, gain[1:2], grad_rows)
@@ -266,21 +276,52 @@
     sums[5:6] = row_sum(grad_rows)
 
 
+def ffn_weights(dims, meta, shared, own_half, theirs, to_two, to_four, rest, rows, dw, sems):
+    mp = dims[0]
+    slots = shared.shape[1]
+    width = rows.shape[2] - own_half.shape[2]
+    for i in range(mp + 1):
+        sem = sems.at[i % mp, i // mp]
+        part = rows.at[i, pl.ds(0, slots)]
+        pltpu.make_async_copy(shared.at[i, :, pl.ds(0, width)], part.at[:, pl.ds(0, width)], sem).start()
+        pltpu.make_async_copy(own_half.at[i], part.at[:, pl.ds(width, width // 2)], sem).start()
+        pltpu.make_async_copy(theirs.at[i], rows.at[i, pl.ds(slots, slots)], sem).start()
+    arrive(rows.at[0], sems.at[0, 0])
+    for z in range(mp):
+        i = z + 1
+        arrive(rows.at[i], sems.at[i % mp, i // mp])
+        dw[z, 0] = tn(rows[0, :, width:], rows[i, :, :width]).astype(BF16)
+        dw[z, 1] = tn(rows[i, :, width:], rows[0, :, :width]).astype(BF16)
+        size = dw.shape[2] // 4
+        for offset in range(4):
+            slot = SLOTS.index((offset, z // 2))
+            if slot < 4:
+                target = (to_two, to_four)[slot // 2].at[slot % 2, z % 2]
+            else:
+                target = rest.at[slot - 4, z % 2]
+            row = pl.multiple_of(((meta[0] ^ offset) & 3) * size, 16)
+            for j in (0, 1):
+                source = dw.at[z, j, pl.ds(row, size)]
+                pltpu.make_async_copy(source, target.at[pl.ds(j * size, size)], sems.at[0, 2]).start()
+    arrive(dw, sems.at[0, 2])
+
+
 def cross_back(dims, meta, dz2, cq, total, z1, gain, *refs):
     mp, local, heads, scaling, nseg = dims
     kv_ref, pieces, owns = refs[0], refs[1:11], refs[11:14]
-    mem_out, kv_low, dcq, dz1, sums, sums_local = refs[14:20]
-    wc, kv, dmem, acc, dout, sems = refs[20:]
+    mem_out, (kv_low, dcq, dz1, sums, sums_local) = refs[14 : 14 + mp], refs[14 + mp : 19 + mp]
+    wc, kv, dmem, acc, dout, sems = refs[19 + mp :]
+    for z in range(mp):
+        pltpu.make_async_copy(kv_ref.at[z], kv.at[z], sems.at[1, z]).start()
     fetch_cross(pieces, owns, meta[0], wc, sems.at[0])
-    pltpu.make_async_copy(kv_ref, kv, sems.at[1]).start()
     allowed = cross_mask(meta, nseg, dz2.shape[0], kv.shape[2])
     dz2_low = dz2[...].astype(BF16)
     acc[...] = dz2[...]
     dmem[...] = jnp.zeros_like(dmem)
-    arrive(wc, sems.at[0])
-    arrive(kv, sems.at[1])
 
     def step(z, carry):
+        arrive(wc.at[z], sems.at[0, z])
+        arrive(kv.at[z], sems.at[1, z])
         dout[...] = nt(dz2_low, wc[z, local : 2 * local]).astype(BF16)
         for i in range(heads):
             at = HD * i
@@ -308,7 +349,7 @@
     lax.fori_loop(0, mp, step, 0)
     for block in range(mp):
         row = pl.multiple_of(lax.rem(meta[1] + block, mp) * local, 16)
-        mem_out[block] = dmem[pl.ds(row, local)].astype(BF16)
+        mem_out[block][...] = dmem[pl.ds(row, local)].astype(BF16)
     unit, inverse = normed(z1[...])
     grad_rows = acc[...]
     values = norm_back(unit, inverse, gain[0:1], grad_rows)
@@ -328,21 +369,21 @@
     dx, small, beside, mine = refs[13 + mp : 17 + mp]
     ws, kv, mem, acc, dout, dqkv, dw, sums_local, sems = refs[17 + mp :]
     place = meta[0]
+    fetch_own((own_self, own_sp), ws, sems.at[0])
     fetch(pieces, place, ws, 0, 96, sems.at[0])
-    fetch_own(own_self, ws, 0, sems.at[0])
-    fetch_own(own_sp, ws, 3 * local, sems.at[0])
-    pltpu.make_async_copy(kv_ref, kv, sems.at[1]).start()
-    fetch_memory(blocks, meta[1], mem, sems.at[2])
+    fetch_memory(blocks, meta[1], mem, sems.at[2, 0])
+    for z in range(mp):
+        pltpu.make_async_copy(kv_ref.at[z], kv.at[z], sems.at[1, z]).start()
     allowed = self_mask(meta, nseg, x_ref.shape[0])
     dz1_low = dz1[...].astype(BF16)
     dz2_low = dz2[...].astype(BF16)
     first_low = first[...].astype(BF16)
     acc[...] = dz1[...]
-    arrive(ws, sems.at[0])
-    arrive(kv, sems.at[1])
-    arrive(mem, sems.at[2])
+    arrive(mem, sems.at[2, 0])
 
     def step(z, carry):
+        arrive(ws.at[z], sems.at[0, z])
+        arrive(kv.at[z], sems.at[1, z])
         dout[...] = nt(dz1_low, ws[z, 3 * local :]).astype(BF16)
         for i in range(heads):
             at = HD * i
@@ -352,7 +393,7 @@
             grad = dout[:, at : at + HD]
             scores = jnp.where(allowed, nt(query, key), NEG_FILL)
             weights = jnp.exp(scores - jnp.max(scores, -1, keepdims=True))
-            probs = weights / jnp.sum(weights, -1, keepdims=True)
+            probs = weights * (1.0 / jnp.sum(weights, -1, keepdims=True))
             prob_grad = nt(grad, value)
             offset = jnp.sum(probs * prob_grad, -1, keepdims=True)
             score_grad = (probs * (prob_grad - offset)).astype(BF16)
@@ -364,13 +405,13 @@
             sums_local[z, 0:1, at : at + HD] = row_sum(query_grad)
             sums_local[z, 1:2, at : at + HD] = row_sum(value_grad)
         acc[...] += nn(dqkv[...], ws[z, : 3 * local])
-        dw[: 3 * local] = tn(dqkv[...], x_ref[...])
-        dw[3 * local :] = tn(self_low[z], dz1_low)
-        put_slots(beside, mine, place, z, 0, 96, dw)
-        dw[:local] = tn(dcq[z], first_low)
-        dw[local : 2 * local] = tn(cross_low[z], dz2_low)
-        dw[2 * local :] = nt(kv[z], mem[...])
-        put_slots(beside, mine, place, z, 96, 96, dw)
+        dw[z, 0, : 3 * local] = tn(dqkv[...], x_ref[...]).astype(BF16)
+        dw[z, 0, 3 * local :] = tn(self_low[z], dz1_low).astype(BF16)
+        put_slots(beside, mine, place, z, 0, dw.at[z, 0], sems.at[3, 0])
+        dw[z, 1, :local] = tn(dcq[z], first_low).astype(BF16)
+        dw[z, 1, local : 2 * local] = tn(cross_low[z], dz2_low).astype(BF16)
+        dw[z, 1, 2 * local :] = nt(kv[z], mem[...]).astype(BF16)
+        put_slots(beside, mine, place, z, 96, dw.at[z, 1], sems.at[3, 0])
         return carry
 
     lax.fori_loop(0, mp, step, 0)
@@ -389,25 +430,25 @@
         return carry
 
     lax.fori_loop(0, mp, collect, 0)
-
-
-def place_rows(place, ranges, low, over_two, over_four, near, far, across):
-    half = near.shape[0]
-    rows = low.shape[0]
+    arrive(dw, sems.at[3, 0])
+
+
+def place_rows(place, ranges, pieces):
+    half = pieces[3].shape[0]
 
     def taken(offset, start, size):
-        if offset >= 4:
-            return across[pl.ds((offset - 4) * rows + start, size)]
+        mine = pieces[5 * (offset // 4) :]
+        offset = offset % 4
         if offset < 3:
-            return (low, over_two, over_four)[offset][pl.ds(start, size)]
+            return mine[offset][pl.ds(start, size)]
         if start < half:
-            return near[pl.ds(start, size)]
-        return far[pl.ds(start - half, size)]
+            return mine[3][pl.ds(start, size)]
+        return mine[4][pl.ds(start - half, size)]
 
     for offset in range(8):
         position = place ^ offset
         for start, size, targets in ranges:
-            if offset == 3 and start < half < start + size:
+            if offset % 4 == 3 and start < half < start + size:
                 parts = ((start, half - start), (half, start + size - half))
             else:
                 parts = ((start, size),)
@@ -425,13 +466,29 @@
                     first += count
 
 
-def finish_heads(meta, *refs):
-    place_rows(meta[0], ((0, 96, refs[6:8]), (96, 96, refs[8:])), *refs[:6])
+def finish_heads(meta, small, *refs):
+    place_rows(meta[0], ((0, 96, refs[10:12]), (96, 96, refs[12:15])), refs[:10])
+    shared, sharded = refs[15:18], refs[18:]
+    for i, target in enumerate(shared):
+        for j, row in enumerate((0, 6, 3)):
+            target[j : j + 1] = small[row + i : row + i + 1]
+    row = 9 + 2 * meta[1]
+    local = sharded[0].shape[1]
+    for i in (0, 1):
+        for j in (0, 1):
+            at = (2 * i + j) * local
+            sharded[i][j : j + 1] = small[pl.ds(row, 1), at : at + local]
+    sharded[2][...] = small[pl.ds(row + 1, 1)].reshape(sharded[2].shape)
 
 
 def finish_ffn(meta, *refs):
     gi, go = refs[6:]
-    place_rows(meta[0], ((0, 96, (gi,)), (96, 96, (go,))), *refs[:6])
+    pieces, joined = list(refs[:5]), refs[5]
+    row = 0
+    for piece in refs[:5]:
+        pieces.append(joined.at[pl.ds(row, piece.shape[0])])
+        row += piece.shape[0]
+    place_rows(meta[0], ((0, 96, (gi,)), (96, 96, (go,))), pieces)
 
 
 def join_columns(meta, *refs):
@@ -467,12 +524,12 @@
 META = pl.BlockSpec(memory_space=pltpu.SMEM)
 
 
-def call(kernel, in_specs, outs, scratch, flops, moved, name):
+def call(kernel, in_specs, outs, scratch, flops, moved, name, written=0):
     return pl.pallas_call(
         kernel,
         out_shape=outs,
         in_specs=in_specs,
-        out_specs=in_vmem(len(outs)),
+        out_specs=in_vmem(len(outs) - written) + in_place(written),
         scratch_shapes=scratch,
         name=name,
         compiler_params=pltpu.CompilerParams(vmem_limit_bytes=60 * 1024 * 1024),
@@ -520,33 +577,24 @@
         return found
 
     class Group:
-        def __init__(self, *pairs):
-            self.pairs = pairs
-            self.low = self.summed(slice(0, 6)).astype(BF16)
-
-        def summed(self, slots):
-            parts = [
-                mine[slots].astype(F32) + other[slots].astype(F32) for other, mine in self.pairs
-            ]
-            return parts[0] if len(parts) == 1 else jnp.concatenate(parts, axis=-2)
-
-        def first(self):
-            return swap(self.low[0:2], 2), swap(self.low[2:4], 4)
+        def __init__(self, summed):
+            self.summed = summed
 
         def second(self, from_two, from_four):
-            late_four = (self.low[5].astype(F32) + from_two[0].astype(F32)).astype(BF16)
-            late_two = (self.low[4].astype(F32) + from_four[0].astype(F32)).astype(BF16)
+            late_two = (self.summed(4) + from_four[0].astype(F32)).astype(BF16)
+            late_four = (self.summed(5) + from_two[0].astype(F32)).astype(BF16)
             return late_two, late_four
 
         def third(self, from_two, from_four, late_two, late_four):
-            top = self.summed(6) + from_two[1].astype(F32) + late_four.astype(F32)
-            end = self.summed(7) + from_four[1].astype(F32) + late_two.astype(F32)
-            bit = SUB
-            while bit < dp:
-                top = top + swap(top, bit)
-                end = end + swap(end, bit)
-                bit *= 2
-            blocks = [top[0], top[1], end[0], end[1]]
+            blocks = []
+            for slot, near, late in ((6, from_two, late_four), (7, from_four, late_two)):
+                for i in (0, 1):
+                    total = self.summed(slot, i) + near[1, i].astype(F32) + late[i].astype(F32)
+                    bit = SUB
+                    while bit < dp:
+                        total = total + swap(total, bit)
+                        bit *= 2
+                    blocks.append(total)
             return blocks[0], [block.astype(BF16) for block in blocks[1:]]
 
     def line_sum(total, sent):
@@ -640,9 +688,21 @@
         head_near = near_chips(head_own)
         ffn_piece = after(ffn_piece, *head_line)
         ffn_line = [shift(ffn_piece, step) for step in range(1, mp)]
-        head_own, head_near, ffn_line, memory_blocks = meet(
-            head_own, head_near, ffn_line, memory_blocks
-        )
+        biases = [bias]
+        for piece in head_line:
+            term = piece[rows : rows + bias_rows].reshape(3, -1, width).astype(F32)
+            biases.append((term[0] + term[1]) + term[2])
+        biases = jnp.stack(biases).reshape(mp, -1)
+        self_bias = biases[:, : 2 * local].reshape(mp, 2, local)
+        cross_bias = biases[:, 2 * local : 4 * local].reshape(mp, 2, local)
+        inner_bias = biases[:, None, 4 * local :]
+        hidden_row = row_of(hidden, slots)
+        grad_row = row_of(out_grad, slots)
+        early = (meta, self_bias, cross_bias, inner_bias, hidden_row, grad_row)
+        head_own, head_near, ffn_line, memory_blocks, early = meet(
+            head_own, head_near, ffn_line, memory_blocks, early
+        )
+        meta, self_bias, cross_bias, inner_bias, hidden_row, grad_row = early
         head_far = far_chips(*head_near)
         head_beside = [swap(head_own, 1), swap(head_near[0], 1)]
         memory_blocks[1] = shift(memory_blocks[1], 1)
@@ -654,20 +714,9 @@
         head_pieces = (head_own, *head_near, *head_far, *head_beside)
         ffn_near = near_chips(ffn_own)
         memory_blocks[2] = shift(memory_blocks[2], 2)
-        biases = [bias]
-        for piece in head_line:
-            term = piece[rows : rows + bias_rows].reshape(3, -1, width).astype(F32)
-            biases.append((term[0] + term[1]) + term[2])
-        biases = jnp.stack(biases).reshape(mp, -1)
-
-        self_bias = biases[:, : 2 * local].reshape(mp, 2, local)
-        cross_bias = biases[:, 2 * local : 4 * local].reshape(mp, 2, local)
-        inner_bias = biases[:, None, 4 * local :]
-        hidden_row = row_of(hidden, slots)
-        grad_row = row_of(out_grad, slots)
         params = (out_biases, norm_gains, norm_biases)
-        dma = pltpu.SemaphoreType.DMA((2,))
-        square = VMEM((width, width), F32)
+        dma = pltpu.SemaphoreType.DMA((4, mp))
+        squares = VMEM((mp, 2, width, width), BF16)
         weights_shape = VMEM((mp, 4 * local, width), BF16)
         flat_shape = VMEM((slots, width), F32)
         kv_shape = VMEM((mp, 2 * local, mem_slots), BF16)
@@ -729,15 +778,16 @@
             cross_proj,
             own_kv,
         )
-        result, dz2, ffn_sums, ffn_beside, ffn_mine = call(
+        shared_shape = (mp + 1, slots, width + width // 2)
+        result, dz2, ffn_sums, ffn_shared, ffn_half = call(
             bound(ffn_both),
             [META] + in_vmem(7) + in_place(12),
             (
                 shaped((slots, width), BF16),
                 row_shape,
                 shaped((16, width)),
-                ffn_slots,
-                ffn_slots,
+                shaped(shared_shape, BF16),
+                shaped((mp + 1, slots, width // 2), BF16),
             ),
             [
                 VMEM((mp, width, inner), BF16),
@@ -745,21 +795,20 @@
                 flat_shape,
                 VMEM((mp, slots, inner), BF16),
                 VMEM((mp, slots, inner), F32),
-                square,
+                VMEM((slots, width), BF16),
                 dma,
             ],
-            50 * matmul,
-            16 * plain,
+            40 * matmul,
+            10 * plain,
             "ffn_both",
         )(meta, second, z2, grad_row, inner_bias, *params, *ffn_pieces, ffn_in, ffn_out)
-        ffn_other = swap(ffn_beside, 1)
+        ffn_theirs = swap(ffn_shared, 1)
         result_blocks = spread_line(result)
-
-        memory_grads, kv_low, cross_dq, dz1, cross_sums, cross_local = call(
+        *memory_grads, kv_low, cross_dq, dz1, cross_sums, cross_local = call(
             bound(cross_back),
             [META] + in_vmem(5) + in_place(14),
             (
-                shaped((mp, local, mem_slots), BF16),
+                *[shaped((local, mem_slots), BF16)] * mp,
                 shaped((mp, 2 * local, mem_slots), BF16),
                 low_shape,
                 row_shape,
@@ -790,13 +839,28 @@
             cross_proj,
             own_kv,
         )
-        ffn_other, result_blocks, memory_grads, kv_low, dz1 = meet(
-            ffn_other, result_blocks, memory_grads, kv_low, dz1
-        )
-        ffn_group = Group((ffn_other, ffn_mine))
-        ffn_group.low, dz1, memory_grads = meet(ffn_group.low, dz1, memory_grads)
-        ffn_from = ffn_group.first()
-        memory_out = [memory_grads[0]] + [shift(memory_grads[step], step) for step in (1, 2)]
+        result_blocks, memory_grads, kv_low, dz1, ffn_theirs = meet(
+            result_blocks, memory_grads, kv_low, dz1, ffn_theirs
+        )
+        memory_out = [memory_grads[0]]
+        memory_out += [shift(memory_grads[step], step) for step in (1, 2)]
+        pair_slots = shaped((2, 2, 2 * width // SUB, width), BF16)
+        to_two, to_four, ffn_rest = call(
+            bound(ffn_weights),
+            [META] + in_place(3),
+            (pair_slots, pair_slots, shaped((4, 2, 2 * width // SUB, width), BF16)),
+            [
+                VMEM((mp + 1, 2 * slots, width + width // 2), BF16),
+                VMEM((mp, 2, width // 2, width), BF16),
+                dma,
+            ],
+            16 * matmul,
+            8 * plain,
+            "ffn_weights",
+            3,
+        )(meta, ffn_shared, ffn_half, ffn_theirs)
+        ffn_from = swap(to_two, 2), swap(to_four, 4)
+        dz1 = after(dz1, to_two)
         hidden_grad, small, head_beside, head_mine = call(
             bound(head_back),
             [META] + in_vmem(11) + in_place(mp + 13),
@@ -808,13 +872,14 @@
                 flat_shape,
                 VMEM((slots, local), BF16),
                 VMEM((slots, 3 * local), BF16),
-                square,
+                squares,
                 VMEM((mp, 2, local), F32),
-                pltpu.SemaphoreType.DMA((3,)),
+                dma,
             ],
             60 * matmul,
             24 * plain,
             "head_back",
+            2,
         )(
             meta,
             dz1,
@@ -834,59 +899,73 @@
             own_self,
             self_proj,
         )
-        ffn_from, memory_out, memory_grads, hidden_grad, small, head_beside, head_mine = meet(
-            ffn_from, memory_out, memory_grads, hidden_grad, small, head_beside, head_mine
-        )
+        ffn_from, memory_out, memory_last, hidden_grad, small, head_beside, head_mine = meet(
+            ffn_from, memory_out, memory_grads[3], hidden_grad, small, head_beside, head_mine
+        )
+        head_other = swap(head_beside, 1)
+        ffn_group = Group(lambda slot, *at: ffn_rest[(slot - 4, *at)].astype(F32))
         late_two, late_four = ffn_group.second(*ffn_from)
-        head_other = swap(head_beside, 1)
+        ffn_late = swap(late_two, 2), swap(late_four, 4)
+        memory_out.append(shift(memory_last, 3))
         small = small + flip(small, 1)
-        memory_out.append(shift(after(memory_grads[3], small), 3))
-        ffn_late = swap(late_two, 2), swap(late_four, 4)
-        ffn_late, head_other, memory_out = meet(ffn_late, head_other, memory_out)
-        head_group = Group((head_other, head_mine))
-        head_from = head_group.first()
+        head_other, ffn_late, memory_out, small = meet(head_other, ffn_late, memory_out, small)
+        ffn_total, ffn_blocks = ffn_group.third(*ffn_from, *ffn_late)
+
+        def head_summed(*slots):
+            return head_mine[slots].astype(F32) + head_other[slots].astype(F32)
+
+        head_group = Group(head_summed)
+        head_from = (
+            swap(head_summed(slice(0, 2)).astype(BF16), 2),
+            swap(head_summed(slice(2, 4)).astype(BF16), 4),
+        )
+        ffn_sent = [shift(ffn_blocks[step - 1], -step) for step in range(1, mp)]
+
+        def joined(kernel, blocks, shape, dtype, name):
+            return call(
+                kernel, [META] + in_vmem(mp), (shaped(shape, dtype),), [], 0, 2 * plain, name
+            )(meta, *blocks)[0]
+
+        rows_shape = (mp * slots, width)
+        memory_grad = joined(
+            join_columns, memory_out, (local, mp * mem_slots), F32, "join_memory"
+        )
+        result = joined(join_rows, result_blocks, rows_shape, BF16, "join_result")
+        head_from, ffn_sent, memory_grad, result, hidden_grad = meet(
+            head_from, ffn_sent, memory_grad, result, hidden_grad
+        )
+        late_two, late_four = head_group.second(*head_from)
+        head_late = swap(late_two, 2), swap(late_four, 4)
         bit = 2
         while bit < mp:
             small = small + flip(small, bit)
             bit *= 2
-        ffn_late = after(ffn_late[0], small), ffn_late[1]
-        ffn_total, ffn_blocks = ffn_group.third(*ffn_from, *ffn_late)
-        ffn_sent = [shift(ffn_blocks[step - 1], -step) for step in range(1, mp)]
-
-        def joined(kernel, blocks, shape, dtype, name):
-            return call(
-                kernel, [META] + in_vmem(mp), (shaped(shape, dtype),), [], 0, 2 * plain, name
-            )(meta, *blocks)[0]
-
-        rows_shape = (mp * slots, width)
-        memory_grad = joined(
-            join_columns, memory_out, (local, mp * mem_slots), F32, "join_memory"
-        )
-        result = joined(join_rows, result_blocks, rows_shape, BF16, "join_result")
-        head_from, ffn_sent, memory_grad, result, hidden_grad = meet(
-            head_from, ffn_sent, memory_grad, result, hidden_grad
-        )
-        late_two, late_four = head_group.second(*head_from)
-        head_late = swap(late_two, 2), swap(late_four, 4)
-        hidden_blocks = spread_line(hidden_grad.astype(BF16))
         ffn_low = line_sum(ffn_total, ffn_sent)
-        head_late, hidden_blocks, ffn_low, small = meet(head_late, hidden_blocks, ffn_low, small)
+        small = small + swap(small, 1)
+        bit = SUB
+        while bit < dp:
+            small = small + swap(small, bit)
+            bit *= 2
+        head_late, ffn_low, small = meet(head_late, ffn_low, small)
         head_total, head_blocks = head_group.third(*head_from, *head_late)
+        head_sent = [shift(head_blocks[step - 1], -step) for step in range(1, mp)]
         ffn_near = near_chips(ffn_low)
-        head_sent = [shift(head_blocks[0], -1), shift(head_blocks[2], -3)]
-        ffn_near, head_sent, head_blocks = meet(ffn_near, head_sent, head_blocks)
+        small, *ffn_near = meet(small, *ffn_near)
+        small = small + swap(small, 2)
+        small = small + swap(small, 4)
+        ffn_near[0], _ = meet(ffn_near[0], head_sent[0])
         ffn_far = far_chips(*ffn_near)
-        head_sent.append(shift(head_blocks[1], -2))
-        hidden_grad = joined(join_rows, hidden_blocks, rows_shape, F32, "join_hidden")
-        head_sent, ffn_near, ffn_far, small, hidden_grad = meet(
-            head_sent, ffn_near, ffn_far, small, hidden_grad
+        hidden_low = hidden_grad.astype(BF16)
+        ffn_reduced = (ffn_low, *ffn_near, *ffn_far)
+        ffn_joined = jnp.concatenate(ffn_reduced)
+        head_sent, ffn_reduced, ffn_joined, small, hidden_low = meet(
+            head_sent, ffn_reduced, ffn_joined, small, hidden_low
         )
         head_low = line_sum(head_total, head_sent)
         head_near = near_chips(head_low)
-        ffn_reduced = (ffn_low, *ffn_near, *ffn_far)
-        ffn_reduced += (swap(jnp.concatenate(ffn_reduced), 1),)
-        small = small + swap(small, 1)
-        head_near, ffn_reduced, small = meet(head_near, ffn_reduced, small)
+        hidden_blocks = [hidden_low, shift(hidden_low, 1), None, shift(hidden_low, 3)]
+        ffn_joined = swap(ffn_joined, 1)
+        head_near, ffn_joined, hidden_blocks = meet(head_near, ffn_joined, hidden_blocks)
         grad_in, grad_out = call(
             finish_ffn,
             [META] + in_vmem(6),
@@ -895,52 +974,52 @@
             0,
             plain,
             "finish_ffn",
-        )(meta, *ffn_reduced)
+        )(meta, *ffn_reduced, ffn_joined)
+        hidden_blocks[2] = shift(hidden_blocks[0], 2)
         head_far = far_chips(*head_near)
-        small = small + swap(small, 2)
-        head_far, small, grad_in, grad_out = meet(head_far, small, grad_in, grad_out)
-        head_reduced = (head_low, *head_near, *head_far)
-        head_reduced += (swap(jnp.concatenate(head_reduced), 1),)
-        small = small + swap(small, 4)
-        bit = SUB
-        while bit < dp:
-            small = small + swap(small, bit)
-            bit *= 2
-        sharded = lax.dynamic_index_in_dim(
-            small[9 : 9 + 2 * mp].reshape(mp, -1), line, 0, keepdims=False
-        )
-        grad_self, grad_sp, grad_cq, grad_cp, grad_kv = call(
+        head_beside = [swap(piece, 1) for piece in (head_low, *head_near)]
+        head_far, head_beside, grad_in, grad_out, hidden_blocks = meet(
+            head_far, head_beside, grad_in, grad_out, hidden_blocks
+        )
+        hidden_grad = joined(join_rows, hidden_blocks, rows_shape, F32, "join_hidden")
+        head_beside += [swap(piece, 1) for piece in head_far]
+        finished = call(
             finish_heads,
-            [META] + in_vmem(6),
+            [META] + in_vmem(11),
             (
                 shaped((3 * local, width)),
                 shaped((local, width)),
                 shaped((local, width)),
                 shaped((local, width)),
                 shaped((2 * local, width)),
+                shaped((3, width)),
+                shaped((3, width)),
+                shaped((3, width)),
+                shaped((2, local)),
+                shaped((2, local)),
+                shaped((inner,)),
             ),
             [],
             0,
             plain,
             "finish_heads",
-        )(meta, *head_reduced)
+        )(meta, small, head_low, *head_near, *head_far, *head_beside)
+        grad_self, grad_sp, grad_cq, grad_cp, grad_kv = finished[:5]
         return (
             result,
             hidden_grad,
             memory_grad.T,
             jnp.swapaxes(grad_self.reshape(3, local, width), 1, 2),
-            sharded[: 2 * local].reshape(2, local),
+            finished[8],
             grad_sp,
             grad_cq.T,
             jnp.swapaxes(grad_kv.reshape(2, local, width), 1, 2),
-            sharded[2 * local : 4 * local].reshape(2, local),
+            finished[9],
             grad_cp,
             grad_in,
-            sharded[4 * local :],
+            finished[10],
             grad_out,
-            jnp.stack([small[0], small[6], small[3]]),
-            jnp.stack([small[1], small[7], small[4]]),
-            jnp.stack([small[2], small[8], small[5]]),
+            *finished[5:8],
         )
 
     return jax.shard_map(

time: 376 us -> 348 us (0.926)
  starting transfers between devices: 61.5 us -> 79.5 us
  waiting for transfers between devices: 146 us -> 128 us
  local copies, waits for them, and re-layouts: 32.8 us -> 18.9 us
  Pallas kernels: 102 us -> 92.2 us
  other arithmetic: 27.9 us -> 22.2 us
    ppermute x24, waiting for transfers between devices: 126 us -> 98.8 us  [shift(): return lax.ppermute(value, 'mp', [(i, (i + step) % mp) for i in range(mp)])]
    ppermute x41 -> x45, starting transfers between devices: 32.7 us -> 48.7 us  [swap(): return lax.ppermute(value, 'dp', [(i, i ^ bit) for i in range(dp)])]
    ppermute x2, waiting for transfers between devices: 0.01 us -> 13.9 us  [flip(): return lax.ppermute(value, 'mp', [(i, i ^ bit) for i in range(mp)])]
    pallas_call x1, Pallas kernels: 19.3 us -> 10.4 us  [body(): call(bound(ffn_both), [META] + in_vmem(7) + in_place(12), (shaped((slots,...]
    another operation x5 -> x0, other arithmetic: 6.99 us -> none
    ppermute x24, starting transfers between devices: 24.4 us -> 29.8 us  [shift(): return lax.ppermute(value, 'mp', [(i, (i + step) % mp) for i in range(mp)])]
    ppermute x41 -> x45, waiting for transfers between devices: 20.6 us -> 15.5 us  [swap(): return lax.ppermute(value, 'dp', [(i, i ^ bit) for i in range(dp)])]
    pallas_call x2 -> x3, Pallas kernels: 23.2 us -> 28.1 us  [the longest x1 18.6 us: body(): call(bound(cross_back), [META] + in_vmem(5) + in_place(14), (*[shaped((lo...]
  transfers between devices with their start and end apart: 67 -> 71, of which waited for: 30 -> 27; matrix products, arithmetic and copies ran while one was open for 11% -> 7% of each run, Pallas kernels for 21% -> 21%
where the time goes in v4:
time: 348 us; the launch traced here: 343 us
  waiting for transfers between devices  128 us (37%)
  Pallas kernels  92.2 us (26%)
  starting transfers between devices  79.5 us (23%)
  other arithmetic  22.2 us (6%)
  local copies, waits for them, and re-layouts  18.9 us (5%)
    ppermute x24, waiting for transfers between devices, shift(): return lax.ppermute(value, 'mp', [(i, (i + step) % mp) for i in range(mp)])  98.8 us
    ppermute x45, starting transfers between devices, swap(): return lax.ppermute(value, 'dp', [(i, i ^ bit) for i in range(dp)])  48.7 us
    ppermute x24, starting transfers between devices, shift(): return lax.ppermute(value, 'mp', [(i, (i + step) % mp) for i in range(mp)])  29.8 us
    pallas_call x1, Pallas kernels, body(): call(bound(head_back), [META] + in_vmem(11) + in_place(mp + 13), (row_sha...  19.4 us
    pallas_call x1, Pallas kernels, body(): call(bound(cross_back), [META] + in_vmem(5) + in_place(14), (*[shaped((lo...  18.6 us
    ppermute x45, waiting for transfers between devices, swap(): return lax.ppermute(value, 'dp', [(i, i ^ bit) for i in range(dp)])  15.5 us
    ppermute x2, waiting for transfers between devices, flip(): return lax.ppermute(value, 'mp', [(i, i ^ bit) for i in range(mp)])  13.9 us
    pallas_call x1, Pallas kernels, body(): call(bound(cross_forward), [META] + in_vmem(5) + in_place(mp + 13), (low_...  13.8 us
  transfers between devices with their start and end apart: 71, of which 27 were waited for; matrix products, arithmetic and copies ran while one was open for 7% of the time, Pallas kernels for 21%

profile of v4, /device:TPU:9, one launch (start us, length us, event | category | flops | bytes accessed | tf_op | source)
XLA Modules:
  0.0 342.8 jit_solution(17419030525866224424)
XLA Ops:
  17.9 9.4 %collective-permute-done.1 = bf16[208,768]{1,0:T(8,128)(2,1)S(1)} collective-permute-done((bf16[208,768]{1,0:T(8,128)(2,1)S(1)}, bf16[208,768]{1,0:T(8,128)(2,1)S(1)}, u32[]{:S(2)}, u32[]{:S(2)}) %collective-permute-start.1) | collective-permute-done | bytes 319520 | tf_op jit(solution)/shard_map/ppermute | solution.py:550
  27.3 6.8 %collective-permute-done = bf16[208,768]{1,0:T(8,128)(2,1)S(1)} collective-permute-done((bf16[208,768]{1,0:T(8,128)(2,1)S(1)}, bf16[208,768]{1,0:T(8,128)(2,1)S(1)}, u32[]{:S(2)}, u32[]{:S(2)}) %collective-permute-start) | collective-permute-done | bytes 319520 | tf_op jit(solution)/shard_map/ppermute | solution.py:550
  43.1 11.1 %collective-permute-done.6 = bf16[192,768]{1,0:T(8,128)(2,1)} collective-permute-done((bf16[192,768]{1,0:T(8,128)(2,1)}, bf16[192,768]{1,0:T(8,128)(2,1)}, u32[]{:S(2)}, u32[]{:S(2)}) %collective-permute-start.6) | collective-permute-done | bytes 294944 | tf_op jit(solution)/shard_map/ppermute | solution.py:550
  54.2 6.3 %collective-permute-done.5 = bf16[192,768]{1,0:T(8,128)(2,1)} collective-permute-done((bf16[192,768]{1,0:T(8,128)(2,1)}, bf16[192,768]{1,0:T(8,128)(2,1)}, u32[]{:S(2)}, u32[]{:S(2)}) %collective-permute-start.5) | collective-permute-done | bytes 294944 | tf_op jit(solution)/shard_map/ppermute | solution.py:550
  68.1 8.1 %collective-permute-done.12.refs_7_.refs_14_ = bf16[192,1024]{1,0:T(8,128)(2,1)S(1)} collective-permute-done((bf16[192,1024]{1,0:T(8,128)(2,1)}, bf16[192,1024]{1,0:T(8,128)(2,1)S(1)}, u32[]{:S(2)}, u32[]{:S(2)}) %collective-permute-start.12) | collective-permute-done | bytes 393248 | tf_op jit(solution)/shard_map/ppermute | solution.py:550
  84.5 8.4 %self_forward.1 = (bf16[4,128,576]{2,1,0:T(8,128)(2,1)}, bf16[4,128,192]{2,1,0:T(8,128)(2,1)}, f32[128,768]{1,0:T(8,128)}, f32[128,768]{1,0:T(8,128)}) custom-call(s32[12]{0:T(128)} %concatenate.27.refs_0_.meta, bf16[128,768]{1,0:T(8,128)(2,1)} %get-tuple-element.202.refs_1_.refs_2_, f32[4,2,192]{2,1,0:T(2,128)} %reshape.174.refs_2_, f32[3,768]{1,0:T(4,128)} %refs_5_.4, ...), custom_call_target="tpu_custom_call" | custom-call | flops 188743680 | bytes 2359296 | tf_op jit(solution)/shard_map/self_forward/pallas_call | solution.py:736
  92.9 7.9 %collective-permute-done.15.refs_8_.refs_15_ = bf16[192,1024]{1,0:T(8,128)(2,1)} collective-permute-done((bf16[192,1024]{1,0:T(8,128)(2,1)}, bf16[192,1024]{1,0:T(8,128)(2,1)}, u32[]{:S(2)}, u32[]{:S(2)}) %collective-permute-start.15) | collective-permute-done | bytes 393248 | tf_op jit(solution)/shard_map/ppermute | solution.py:550
  103.0 3.3 collective-permute-start.22
  109.8 5.4 %collective-permute-done.22.refs_9_.refs_16_ = bf16[192,1024]{1,0:T(8,128)(2,1)S(1)} collective-permute-done((bf16[192,1024]{1,0:T(8,128)(2,1)}, bf16[192,1024]{1,0:T(8,128)(2,1)S(1)}, u32[]{:S(2)}, u32[]{:S(2)}) %collective-permute-start.22) | collective-permute-done | bytes 393248 | tf_op jit(solution)/shard_map/ppermute | solution.py:550
  115.9 3.1 collective-permute-done.19.refs_11_
  120.5 13.8 %cross_forward.1 = (bf16[4,128,192]{2,1,0:T(8,128)(2,1)}, bf16[4,384,1024]{2,1,0:T(8,128)(2,1)}, bf16[4,128,192]{2,1,0:T(8,128)(2,1)}, f32[12,128,1]{2,1,0:T(8,1...) custom-call(s32[12]{0:T(128)} %concatenate.27.refs_0_.meta, f32[4,2,192]{2,1,0:T(2,128)} %reshape.175.refs_1_, ...), custom_call_target="tpu_custom_call" | custom-call | flops 377487360 | bytes 2359296 | tf_op jit(solution)/shard_map/cross_forward/pallas_call | solution.py:755
  135.4 10.4 %ffn_both.1 = (bf16[128,768]{1,0:T(8,128)(2,1)}, f32[128,768]{1,0:T(8,128)}, f32[16,768]{1,0:T(8,128)}, bf16[5,128,1152]{2,1,0:T(8,128)(2,1)}, bf16[5,128,384]{2,1,0:T(8,128)(2,1)}) custom-call(s32[12]{0:T(128)} %concatenate.27.refs_0_.meta, f32[128,768]{1,0:T(8,128)} %get-tuple-element.230.refs_1_, f32[128,768]{1,0:T(8,128)} %get-tuple-element.231.refs_2_, ...), custom_call_target="tpu_custom_call" | custom-call | flops 377487360 | bytes 2949120 | tf_op jit(solution)/shard_map/ffn_both/pallas_call | solution.py:782
  147.8 18.6 %cross_back.1 = (bf16[192,1024]{1,0:T(8,128)(2,1)}, bf16[192,1024]{1,0:T(8,128)(2,1)}, bf16[192,1024]{1,0:T(8,128)(2,1)}, bf16[192,1024]{1,0:T(8,128)(2,1)}, bf1...) custom-call(s32[12]{0:T(128)} %concatenate.27.refs_0_.meta, ...), custom_call_target="tpu_custom_call" | custom-call | flops 471859200 | bytes 3538944 | tf_op jit(solution)/shard_map/cross_back/pallas_call | solution.py:807
  167.6 5.1 %ffn_weights.1 = (bf16[2,2,192,768]{3,2,1,0:T(8,128)(2,1)}, bf16[2,2,192,768]{3,2,1,0:T(8,128)(2,1)}, bf16[4,2,192,768]{3,2,1,0:T(8,128)(2,1)}) custom-call(s32[12]{0:T(128)} %concatenate.27.refs_0_.meta, bf16[5,128,1152]{2,1,0:T(8,128)(2,1)} %get-tuple-element.237.refs_1_, bf16[5,128,384]{2,1,0:T(8,128)(2,1)} %get-tuple-element.238.refs_2_, ...), custom_call_target="tpu_custom_call" | custom-call | flops 150994944 | bytes 2359296 | tf_op jit(solution)/shard_map/ffn_weights/pallas_call | solution.py:848
  178.5 19.4 %head_back.1 = (f32[128,768]{1,0:T(8,128)}, f32[24,768]{1,0:T(8,128)}, bf16[8,2,192,768]{3,2,1,0:T(8,128)(2,1)}, bf16[8,2,192,768]{3,2,1,0:T(8,128)(2,1)}) custom-call(s32[12]{0:T(128)} %concatenate.27.refs_0_.meta, f32[128,768]{1,0:T(8,128)} %get-tuple-element.259.refs_1_, bf16[128,768]{1,0:T(8,128)(2,1)} %get-tuple-element.202.refs_1_.refs_2_, ...), custom_call_target="tpu_custom_call" | custom-call | flops 566231040 | bytes 7077888 | tf_op jit(solution)/shard_map/head_back/pallas_call | solution.py:864
  205.6 3.4 collective-permute-start.38
  210.0 9.8 %collective-permute-done.39 = f32[24,768]{1,0:T(8,128)S(1)} collective-permute-done((f32[24,768]{1,0:T(8,128)S(1)}, f32[24,768]{1,0:T(8,128)S(1)}, u32[]{:S(2)}, u32[]{:S(2)}) %collective-permute-start.39) | collective-permute-done | bytes 73760 | tf_op jit(solution)/shard_map/ppermute | solution.py:553
  221.1 5.3 %add_convert_fusion = (bf16[2,2,192,768]{3,2,1,0:T(8,128)(2,1)}, bf16[2,2,192,768]{3,2,1,0:T(8,128)(2,1)}) fusion(bf16[8,2,192,768]{3,2,1,0:T(8,128)(2,1)S(1)} %collective-permute-done.35, bf16[8,2,192,768]{3,2,1,0:T(8,128)(2,1)} %get-tuple-element.272), kind=kLoop, calls=%fused_computation | loop fusion | flops 4718592 | bytes 7077888 | tf_op jit(solution)/shard_map/convert_element_type | solution.py:920
  230.4 3.6 %collective-permute-start.43 = (bf16[192,768]{1,0:T(8,128)(2,1)S(1)}, bf16[192,768]{1,0:T(8,128)(2,1)}, u32[]{:S(2)}, u32[]{:S(2)}) collective-permute-start(bf16[192,768]{1,0:T(8,128)(2,1)S(1)} %get-tuple-element.360), channel_id=1, source_target_pairs={{0,2},{1,3},{2,0},{3,1},{4,6},{5,7},{6,4},{7,5},{8,10},{9,11},{10,... | collective-permute-start | bytes 884744 | tf_op jit(solution)/shard_map/ppermute | solution.py:550
  236.2 3.2 join_memory.1
  239.4 14.3 %collective-permute-done.43 = bf16[192,768]{1,0:T(8,128)(2,1)} collective-permute-done((bf16[192,768]{1,0:T(8,128)(2,1)S(1)}, bf16[192,768]{1,0:T(8,128)(2,1)}, u32[]{:S(2)}, u32[]{:S(2)}) %collective-permute-start.43) | collective-permute-done | bytes 294944 | tf_op jit(solution)/shard_map/ppermute | solution.py:550
  253.8 4.7 %collective-permute-done.42 = bf16[192,768]{1,0:T(8,128)(2,1)} collective-permute-done((bf16[192,768]{1,0:T(8,128)(2,1)S(1)}, bf16[192,768]{1,0:T(8,128)(2,1)}, u32[]{:S(2)}, u32[]{:S(2)}) %collective-permute-start.42) | collective-permute-done | bytes 294944 | tf_op jit(solution)/shard_map/ppermute | solution.py:550
  262.4 4.1 %collective-permute-done.47 = f32[24,768]{1,0:T(8,128)S(1)} collective-permute-done((f32[24,768]{1,0:T(8,128)S(1)}, f32[24,768]{1,0:T(8,128)S(1)}, u32[]{:S(2)}, u32[]{:S(2)}) %collective-permute-start.47) | collective-permute-done | bytes 73760 | tf_op jit(solution)/shard_map/ppermute | solution.py:553
  266.5 3.4 %collective-permute-start.48 = (f32[24,768]{1,0:T(8,128)S(1)}, f32[24,768]{1,0:T(8,128)S(1)}, u32[]{:S(2)}, u32[]{:S(2)}) collective-permute-start(f32[24,768]{1,0:T(8,128)S(1)} %add.287), channel_id=1, source_target_pairs={{0,4},{4,0},{8,12},{12,8},{16,20},{20,16},{24,28},{28,24},{1,5},{5... | collective-permute-start | bytes 221192 | tf_op jit(solution)/shard_map/ppermute | solution.py:547
  281.0 6.3 %collective-permute-done.49 = bf16[192,768]{1,0:T(8,128)(2,1)S(1)} collective-permute-done((bf16[192,768]{1,0:T(8,128)(2,1)S(1)}, bf16[192,768]{1,0:T(8,128)(2,1)S(1)}, u32[]{:S(2)}, u32[]{:S(2)}) %collective-permute-start.49) | collective-permute-done | bytes 294944 | tf_op jit(solution)/shard_map/ppermute | solution.py:550
  291.3 3.1 collective-permute-done.57
  295.1 5.8 %collective-permute-done.50 = bf16[192,768]{1,0:T(8,128)(2,1)S(1)} collective-permute-done((bf16[192,768]{1,0:T(8,128)(2,1)S(1)}, bf16[192,768]{1,0:T(8,128)(2,1)S(1)}, u32[]{:S(2)}, u32[]{:S(2)}) %collective-permute-start.50) | collective-permute-done | bytes 294944 | tf_op jit(solution)/shard_map/ppermute | solution.py:550
  300.9 11.9 %collective-permute-start.60 = (bf16[768,768]{1,0:T(8,128)(2,1)S(1)}, bf16[768,768]{1,0:T(8,128)(2,1)S(1)}, u32[]{:S(2)}, u32[]{:S(2)}) collective-permute-start(bf16[768,768]{1,0:T(8,128)(2,1)S(1)} %constant_dynamic-update-slice_fusion.1), channel_id=1, source_target_pairs={{0,4},{4,0},{8,12},{12,8},{16,20},{20,16},{24,28},{28,24},{1,5},{5... | collective-permute-start | bytes 3538952 | tf_op jit(solution)/shard_map/ppermute | solution.py:547
  316.3 7.1 %collective-permute-done.62.refs_3_ = bf16[128,768]{1,0:T(8,128)(2,1)S(1)} collective-permute-done((bf16[128,768]{1,0:T(8,128)(2,1)S(1)}, bf16[128,768]{1,0:T(8,128)(2,1)S(1)}, u32[]{:S(2)}, u32[]{:S(2)}) %collective-permute-start.62) | collective-permute-done | bytes 196640 | tf_op jit(solution)/shard_map/ppermute | solution.py:550
  326.0 4.3 %finish_ffn.1 = (f32[768,768]{1,0:T(8,128)}, f32[768,768]{1,0:T(8,128)}) custom-call(s32[12]{0:T(128)} %concatenate.27.refs_0_.meta, bf16[192,768]{1,0:T(8,128)(2,1)} %copy-done.11, bf16[192,768]{1,0:T(8,128)(2,1)} %copy-done.15, bf16[192,768]{1,0:T(8,128)(2,1)} %copy-done.14, bf16[96,768]{1,0:T(8,128)(2,1)} %copy-done.28, bf16[96,768]{1,0:T(8,128)(2,1)} %copy-done.29, ...), custom_call_target="tpu_custom_call" | custom-call | bytes 294912 | tf_op jit(solution)/shard_map/finish_ffn/pallas_call | solution.py:969
  330.3 3.0 collective-permute-done.68.refs_2_
  338.2 4.4 %finish_heads.1 = (f32[576,768]{1,0:T(8,128)}, f32[192,768]{1,0:T(8,128)}, f32[192,768]{1,0:T(8,128)}, f32[192,768]{1,0:T(8,128)}, f32[384,768]{1,0:T(8,128)}, /...) custom-call(s32[12]{0:T(128)} %concatenate.27.refs_0_.meta, ...), custom_call_target="tpu_custom_call" | custom-call | bytes 294912 | tf_op jit(solution)/shard_map/finish_heads/pallas_call | solution.py:986
  (292 shorter events, 106.1 us)
Async XLA Ops:
  4.7 22.7 %collective-permute-start.1 = (bf16[208,768]{1,0:T(8,128)(2,1)S(1)}, bf16[208,768]{1,0:T(8,128)(2,1)S(1)}, u32[]{:S(2)}, u32[]{:S(2)}) collective-permute-start(bf16[208,768]{1,0:T(8,128)(2,1)S(1)} %concatenate.25), channel_id=1, source_target_pairs={{0,2},{1,3},{2,0},{3,1},{4,6},{5,7},{6,4},{7,5},{8,10},{9,11},{10,... | collective-permute-start | bytes 958472 | tf_op jit(solution)/shard_map/ppermute | solution.py:550
  7.1 27.1 %collective-permute-start = (bf16[208,768]{1,0:T(8,128)(2,1)S(1)}, bf16[208,768]{1,0:T(8,128)(2,1)S(1)}, u32[]{:S(2)}, u32[]{:S(2)}) collective-permute-start(bf16[208,768]{1,0:T(8,128)(2,1)S(1)} %concatenate.25), channel_id=1, source_target_pairs={{0,1},{1,2},{2,3},{3,0},{4,5},{5,6},{6,7},{7,4},{8,9},{9,10},{10,1... | collective-permute-start | bytes 958472 | tf_op jit(solution)/shard_map/ppermute | solution.py:550
  34.8 19.4 %collective-permute-start.6 = (bf16[192,768]{1,0:T(8,128)(2,1)}, bf16[192,768]{1,0:T(8,128)(2,1)}, u32[]{:S(2)}, u32[]{:S(2)}) collective-permute-start(bf16[192,768]{1,0:T(8,128)(2,1)} %pad_maximum_fusion.2), channel_id=1, source_target_pairs={{0,2},{1,3},{2,0},{3,1},{4,6},{5,7},{6,4},{7,5},{8,10},{9,11},{10,... | collective-permute-start | bytes 884744 | tf_op jit(solution)/shard_map/ppermute | solution.py:550
  37.6 23.0 %collective-permute-start.5 = (bf16[192,768]{1,0:T(8,128)(2,1)}, bf16[192,768]{1,0:T(8,128)(2,1)}, u32[]{:S(2)}, u32[]{:S(2)}) collective-permute-start(bf16[192,768]{1,0:T(8,128)(2,1)} %pad_maximum_fusion.2), channel_id=1, source_target_pairs={{0,1},{1,2},{2,3},{3,0},{4,5},{5,6},{6,7},{7,4},{8,9},{9,10},{10,1... | collective-permute-start | bytes 884744 | tf_op jit(solution)/shard_map/ppermute | solution.py:550
  37.8 22.8 %collective-permute-start.4 = (bf16[3,192,768]{2,1,0:T(8,128)(2,1)S(1)}, bf16[3,192,768]{2,1,0:T(8,128)(2,1)S(1)}, u32[]{:S(2)}, u32[]{:S(2)}) collective-permute-start(bf16[3,192,768]{2,1,0:T(8,128)(2,1)S(1)} %pad_maximum_fusion.refs_6_.refs_10_.refs_7_.refs_17_), channel_id=1, source_target_pairs={{0,16},{4,20},{8,24},{12,28},{16,0},{20,4},{24,8},{28,12},{1,17},{... | collective-permute-start | bytes 2654216 | tf_op jit(solution)/shard_map/ppermute | solution.py:547
  39.1 21.5 %collective-permute-start.3 = (bf16[3,192,768]{2,1,0:T(8,128)(2,1)S(1)}, bf16[3,192,768]{2,1,0:T(8,128)(2,1)S(1)}, u32[]{:S(2)}, u32[]{:S(2)}) collective-permute-start(bf16[3,192,768]{2,1,0:T(8,128)(2,1)S(1)} %pad_maximum_fusion.refs_6_.refs_10_.refs_7_.refs_17_), channel_id=1, source_target_pairs={{0,8},{4,12},{8,0},{12,4},{16,24},{20,28},{24,16},{28,20},{1,9},{5... | collective-permute-start | bytes 2654216 | tf_op jit(solution)/shard_map/ppermute | solution.py:547
  60.5 15.7 %collective-permute-start.10 = (bf16[3,192,768]{2,1,0:T(8,128)(2,1)S(1)}, bf16[3,192,768]{2,1,0:T(8,128)(2,1)S(1)}, u32[]{:S(2)}, u32[]{:S(2)}) collective-permute-start(bf16[3,192,768]{2,1,0:T(8,128)(2,1)S(1)} %pad_maximum_fusion.refs_6_.refs_10_.refs_7_.refs_17_), channel_id=1, source_target_pairs={{0,4},{4,0},{8,12},{12,8},{16,20},{20,16},{24,28},{28,24},{1,5},{5... | collective-permute-start | bytes 2654216 | tf_op jit(solution)/shard_map/ppermute | solution.py:547
  80.4 21.4 %collective-permute-start.14 = (bf16[3,192,768]{2,1,0:T(8,128)(2,1)}, bf16[3,192,768]{2,1,0:T(8,128)(2,1)S(1)}, u32[]{:S(2)}, u32[]{:S(2)}) collective-permute-start(bf16[3,192,768]{2,1,0:T(8,128)(2,1)} %pad_maximum_fusion.1.refs_8_), channel_id=1, source_target_pairs={{0,16},{4,20},{8,24},{12,28},{16,0},{20,4},{24,8},{28,12},{1,17},{... | collective-permute-start | bytes 2654216 | tf_op jit(solution)/shard_map/ppermute | solution.py:547
  80.6 21.2 %collective-permute-start.13 = (bf16[3,192,768]{2,1,0:T(8,128)(2,1)}, bf16[3,192,768]{2,1,0:T(8,128)(2,1)}, u32[]{:S(2)}, u32[]{:S(2)}) collective-permute-start(bf16[3,192,768]{2,1,0:T(8,128)(2,1)} %pad_maximum_fusion.1.refs_8_), channel_id=1, source_target_pairs={{0,8},{4,12},{8,0},{12,4},{16,24},{20,28},{24,16},{28,20},{1,9},{5... | collective-permute-start | bytes 2654216 | tf_op jit(solution)/shard_map/ppermute | solution.py:547
  82.2 18.6 %collective-permute-start.15 = (bf16[192,1024]{1,0:T(8,128)(2,1)}, bf16[192,1024]{1,0:T(8,128)(2,1)}, u32[]{:S(2)}, u32[]{:S(2)}) collective-permute-start(bf16[192,1024]{1,0:T(8,128)(2,1)} %get-tuple-element.200), channel_id=1, source_target_pairs={{0,2},{1,3},{2,0},{3,1},{4,6},{5,7},{6,4},{7,5},{8,10},{9,11},{10,... | collective-permute-start | bytes 1179656 | tf_op jit(solution)/shard_map/ppermute | solution.py:550
  101.8 17.2 %collective-permute-start.21 = (bf16[3,192,768]{2,1,0:T(8,128)(2,1)}, bf16[3,192,768]{2,1,0:T(8,128)(2,1)S(1)}, u32[]{:S(2)}, u32[]{:S(2)}) collective-permute-start(bf16[3,192,768]{2,1,0:T(8,128)(2,1)} %pad_maximum_fusion.1.refs_8_), channel_id=1, source_target_pairs={{0,4},{4,0},{8,12},{12,8},{16,20},{20,16},{24,28},{28,24},{1,5},{5... | collective-permute-start | bytes 2654216 | tf_op jit(solution)/shard_map/ppermute | solution.py:547
  108.9 25.4 %collective-permute-start.24 = (bf16[3,192,768]{2,1,0:T(8,128)(2,1)S(1)}, bf16[3,192,768]{2,1,0:T(8,128)(2,1)S(1)}, u32[]{:S(2)}, u32[]{:S(2)}) collective-permute-start(bf16[3,192,768]{2,1,0:T(8,128)(2,1)S(1)} %collective-permute-done.14.refs_10_), channel_id=1, source_target_pairs={{0,4},{4,0},{8,12},{12,8},{16,20},{20,16},{24,28},{28,24},{1,5},{5... | collective-permute-start | bytes 2654216 | tf_op jit(solution)/shard_map/ppermute | solution.py:547
  115.1 19.2 %collective-permute-start.23 = (bf16[3,192,768]{2,1,0:T(8,128)(2,1)}, bf16[3,192,768]{2,1,0:T(8,128)(2,1)}, u32[]{:S(2)}, u32[]{:S(2)}) collective-permute-start(bf16[3,192,768]{2,1,0:T(8,128)(2,1)} %collective-permute-done.13.refs_9_), channel_id=1, source_target_pairs={{0,4},{4,0},{8,12},{12,8},{16,20},{20,16},{24,28},{28,24},{1,5},{5... | collective-permute-start | bytes 2654216 | tf_op jit(solution)/shard_map/ppermute | solution.py:547
  119.0 15.3 %collective-permute-start.25 = (bf16[3,96,768]{2,1,0:T(8,128)(2,1)S(1)}, bf16[3,96,768]{2,1,0:T(8,128)(2,1)S(1)}, u32[]{:S(2)}, u32[]{:S(2)}) collective-permute-start(bf16[3,96,768]{2,1,0:T(8,128)(2,1)S(1)} %collective-permute-done.19.refs_11_), channel_id=1, source_target_pairs={{0,4},{4,0},{8,12},{12,8},{16,20},{20,16},{24,28},{28,24},{1,5},{5... | collective-permute-start | bytes 1327112 | tf_op jit(solution)/shard_map/ppermute | solution.py:547
  145.8 20.6 %collective-permute-start.30 = (bf16[5,128,1152]{2,1,0:T(8,128)(2,1)}, bf16[5,128,1152]{2,1,0:T(8,128)(2,1)S(1)}, u32[]{:S(2)}, u32[]{:S(2)}) collective-permute-start(bf16[5,128,1152]{2,1,0:T(8,128)(2,1)} %get-tuple-element.237.refs_1_), channel_id=1, source_target_pairs={{0,4},{4,0},{8,12},{12,8},{16,20},{20,16},{24,28},{28,24},{1,5},{5... | collective-permute-start | bytes 4423688 | tf_op jit(solution)/shard_map/ppermute | solution.py:547
  146.3 20.1 %collective-permute-start.29 = (bf16[128,768]{1,0:T(8,128)(2,1)}, bf16[128,768]{1,0:T(8,128)(2,1)S(1)}, u32[]{:S(2)}, u32[]{:S(2)}) collective-permute-start(bf16[128,768]{1,0:T(8,128)(2,1)} %get-tuple-element.289.refs_0_), channel_id=1, source_target_pairs={{0,3},{1,0},{2,1},{3,2},{4,7},{5,4},{6,5},{7,6},{8,11},{9,8},{10,9... | collective-permute-start | bytes 589832 | tf_op jit(solution)/shard_map/ppermute | solution.py:550
  146.6 19.8 %collective-permute-start.28 = (bf16[128,768]{1,0:T(8,128)(2,1)}, bf16[128,768]{1,0:T(8,128)(2,1)S(1)}, u32[]{:S(2)}, u32[]{:S(2)}) collective-permute-start(bf16[128,768]{1,0:T(8,128)(2,1)} %get-tuple-element.289.refs_0_), channel_id=1, source_target_pairs={{0,2},{1,3},{2,0},{3,1},{4,6},{5,7},{6,4},{7,5},{8,10},{9,11},{10,... | collective-permute-start | bytes 589832 | tf_op jit(solution)/shard_map/ppermute | solution.py:550
  146.6 19.8 %collective-permute-start.27 = (bf16[128,768]{1,0:T(8,128)(2,1)}, bf16[128,768]{1,0:T(8,128)(2,1)S(1)}, u32[]{:S(2)}, u32[]{:S(2)}) collective-permute-start(bf16[128,768]{1,0:T(8,128)(2,1)} %get-tuple-element.289.refs_0_), channel_id=1, source_target_pairs={{0,1},{1,2},{2,3},{3,0},{4,5},{5,6},{6,7},{7,4},{8,9},{9,10},{10,1... | collective-permute-start | bytes 589832 | tf_op jit(solution)/shard_map/ppermute | solution.py:550
  172.7 27.6 %collective-permute-start.32 = (bf16[2,2,192,768]{3,2,1,0:T(8,128)(2,1)}, bf16[2,2,192,768]{3,2,1,0:T(8,128)(2,1)}, u32[]{:S(2)}, u32[]{:S(2)}) collective-permute-start(bf16[2,2,192,768]{3,2,1,0:T(8,128)(2,1)} %get-tuple-element.253), channel_id=1, source_target_pairs={{0,16},{4,20},{8,24},{12,28},{16,0},{20,4},{24,8},{28,12},{1,17},{... | collective-permute-start | bytes 3538952 | tf_op jit(solution)/shard_map/ppermute | solution.py:547
  174.0 26.4 %collective-permute-start.31 = (bf16[2,2,192,768]{3,2,1,0:T(8,128)(2,1)}, bf16[2,2,192,768]{3,2,1,0:T(8,128)(2,1)S(1)}, u32[]{:S(2)}, u32[]{:S(2)}) collective-permute-start(bf16[2,2,192,768]{3,2,1,0:T(8,128)(2,1)} %get-tuple-element.252), channel_id=1, source_target_pairs={{0,8},{4,12},{8,0},{12,4},{16,24},{20,28},{24,16},{28,20},{1,9},{5... | collective-permute-start | bytes 3538952 | tf_op jit(solution)/shard_map/ppermute | solution.py:547
  175.2 22.7 %collective-permute-start.33 = (bf16[192,1024]{1,0:T(8,128)(2,1)}, bf16[192,1024]{1,0:T(8,128)(2,1)}, u32[]{:S(2)}, u32[]{:S(2)}) collective-permute-start(bf16[192,1024]{1,0:T(8,128)(2,1)} %get-tuple-element.255), channel_id=1, source_target_pairs={{0,1},{1,2},{2,3},{3,0},{4,5},{5,6},{6,7},{7,4},{8,9},{9,10},{10,1... | collective-permute-start | bytes 1179656 | tf_op jit(solution)/shard_map/ppermute | solution.py:550
  176.4 23.9 %collective-permute-start.34 = (bf16[192,1024]{1,0:T(8,128)(2,1)}, bf16[192,1024]{1,0:T(8,128)(2,1)}, u32[]{:S(2)}, u32[]{:S(2)}) collective-permute-start(bf16[192,1024]{1,0:T(8,128)(2,1)} %get-tuple-element.256), channel_id=1, source_target_pairs={{0,2},{1,3},{2,0},{3,1},{4,6},{5,7},{6,4},{7,5},{8,10},{9,11},{10,... | collective-permute-start | bytes 1179656 | tf_op jit(solution)/shard_map/ppermute | solution.py:550
  200.5 20.7 %collective-permute-start.35 = (bf16[8,2,192,768]{3,2,1,0:T(8,128)(2,1)}, bf16[8,2,192,768]{3,2,1,0:T(8,128)(2,1)S(1)}, u32[]{:S(2)}, u32[]{:S(2)}) collective-permute-start(bf16[8,2,192,768]{3,2,1,0:T(8,128)(2,1)} %get-tuple-element.273), channel_id=1, source_target_pairs={{0,4},{4,0},{8,12},{12,8},{16,20},{20,16},{24,28},{28,24},{1,5},{5... | collective-permute-start | bytes 14155784 | tf_op jit(solution)/shard_map/ppermute | solution.py:547
  204.4 16.0 %collective-permute-start.37 = (bf16[2,192,768]{2,1,0:T(8,128)(2,1)S(1)}, bf16[2,192,768]{2,1,0:T(8,128)(2,1)S(1)}, u32[]{:S(2)}, u32[]{:S(2)}) collective-permute-start(bf16[2,192,768]{2,1,0:T(8,128)(2,1)S(1)} %get-tuple-element.362), channel_id=1, source_target_pairs={{0,16},{4,20},{8,24},{12,28},{16,0},{20,4},{24,8},{28,12},{1,17},{... | collective-permute-start | bytes 1769480 | tf_op jit(solution)/shard_map/ppermute | solution.py:547
  204.7 15.7 %collective-permute-start.36 = (bf16[2,192,768]{2,1,0:T(8,128)(2,1)S(1)}, bf16[2,192,768]{2,1,0:T(8,128)(2,1)S(1)}, u32[]{:S(2)}, u32[]{:S(2)}) collective-permute-start(bf16[2,192,768]{2,1,0:T(8,128)(2,1)S(1)} %get-tuple-element.363), channel_id=1, source_target_pairs={{0,8},{4,12},{8,0},{12,4},{16,24},{20,28},{24,16},{28,20},{1,9},{5... | collective-permute-start | bytes 1769480 | tf_op jit(solution)/shard_map/ppermute | solution.py:547
  226.4 32.1 %collective-permute-start.41 = (bf16[2,2,192,768]{3,2,1,0:T(8,128)(2,1)}, bf16[2,2,192,768]{3,2,1,0:T(8,128)(2,1)}, u32[]{:S(2)}, u32[]{:S(2)}) collective-permute-start(bf16[2,2,192,768]{3,2,1,0:T(8,128)(2,1)} %get-tuple-element.357), channel_id=1, source_target_pairs={{0,16},{4,20},{8,24},{12,28},{16,0},{20,4},{24,8},{28,12},{1,17},{... | collective-permute-start | bytes 3538952 | tf_op jit(solution)/shard_map/ppermute | solution.py:547
  227.7 30.8 %collective-permute-start.40 = (bf16[2,2,192,768]{3,2,1,0:T(8,128)(2,1)}, bf16[2,2,192,768]{3,2,1,0:T(8,128)(2,1)S(1)}, u32[]{:S(2)}, u32[]{:S(2)}) collective-permute-start(bf16[2,2,192,768]{3,2,1,0:T(8,128)(2,1)} %get-tuple-element.358), channel_id=1, source_target_pairs={{0,8},{4,12},{8,0},{12,4},{16,24},{20,28},{24,16},{28,20},{1,9},{5... | collective-permute-start | bytes 3538952 | tf_op jit(solution)/shard_map/ppermute | solution.py:547
  230.4 23.4 %collective-permute-start.43 = (bf16[192,768]{1,0:T(8,128)(2,1)S(1)}, bf16[192,768]{1,0:T(8,128)(2,1)}, u32[]{:S(2)}, u32[]{:S(2)}) collective-permute-start(bf16[192,768]{1,0:T(8,128)(2,1)S(1)} %get-tuple-element.360), channel_id=1, source_target_pairs={{0,2},{1,3},{2,0},{3,1},{4,6},{5,7},{6,4},{7,5},{8,10},{9,11},{10,... | collective-permute-start | bytes 884744 | tf_op jit(solution)/shard_map/ppermute | solution.py:550
  234.0 24.5 %collective-permute-start.42 = (bf16[192,768]{1,0:T(8,128)(2,1)S(1)}, bf16[192,768]{1,0:T(8,128)(2,1)}, u32[]{:S(2)}, u32[]{:S(2)}) collective-permute-start(bf16[192,768]{1,0:T(8,128)(2,1)S(1)} %get-tuple-element.361), channel_id=1, source_target_pairs={{0,3},{1,0},{2,1},{3,2},{4,7},{5,4},{6,5},{7,6},{8,11},{9,8},{10,9... | collective-permute-start | bytes 884744 | tf_op jit(solution)/shard_map/ppermute | solution.py:550
  278.5 16.6 %collective-permute-start.51 = (bf16[192,768]{1,0:T(8,128)(2,1)S(1)}, bf16[192,768]{1,0:T(8,128)(2,1)S(1)}, u32[]{:S(2)}, u32[]{:S(2)}) collective-permute-start(bf16[192,768]{1,0:T(8,128)(2,1)S(1)} %get-tuple-element.352), channel_id=1, source_target_pairs={{0,1},{1,2},{2,3},{3,0},{4,5},{5,6},{6,7},{7,4},{8,9},{9,10},{10,1... | collective-permute-start | bytes 884744 | tf_op jit(solution)/shard_map/ppermute | solution.py:550
  280.0 20.8 %collective-permute-start.50 = (bf16[192,768]{1,0:T(8,128)(2,1)S(1)}, bf16[192,768]{1,0:T(8,128)(2,1)S(1)}, u32[]{:S(2)}, u32[]{:S(2)}) collective-permute-start(bf16[192,768]{1,0:T(8,128)(2,1)S(1)} %get-tuple-element.353), channel_id=1, source_target_pairs={{0,2},{1,3},{2,0},{3,1},{4,6},{5,7},{6,4},{7,5},{8,10},{9,11},{10,... | collective-permute-start | bytes 884744 | tf_op jit(solution)/shard_map/ppermute | solution.py:550
  300.9 23.5 %collective-permute-start.60 = (bf16[768,768]{1,0:T(8,128)(2,1)S(1)}, bf16[768,768]{1,0:T(8,128)(2,1)S(1)}, u32[]{:S(2)}, u32[]{:S(2)}) collective-permute-start(bf16[768,768]{1,0:T(8,128)(2,1)S(1)} %constant_dynamic-update-slice_fusion.1), channel_id=1, source_target_pairs={{0,4},{4,0},{8,12},{12,8},{16,20},{20,16},{24,28},{28,24},{1,5},{5... | collective-permute-start | bytes 3538952 | tf_op jit(solution)/shard_map/ppermute | solution.py:547
  (92 other events, 863.8 us)

commit v5 on v4

--- a/solution.py
+++ b/solution.py
@@ -94,6 +94,30 @@
     pltpu.make_async_copy(target, target, sem).wait()
 
 
+def fetch_halves(pieces, owns, place, target, sems):
+    own_cq, own_cp, own_kv = owns
+    size = own_cq.shape[0]
+    pltpu.make_async_copy(own_cq, target.at[0, 0, pl.ds(0, size)], sems.at[0, 0]).start()
+    pltpu.make_async_copy(own_cp, target.at[0, 0, pl.ds(size, size)], sems.at[0, 0]).start()
+    pltpu.make_async_copy(own_kv, target.at[1, 0], sems.at[1, 0]).start()
+    blocks, rows = pieces[0].shape[:2]
+    size = rows // 2
+    for block in range(blocks):
+        for index in range(8):
+            offset = index % 4
+            mine = pieces[5 * (index // 4) :]
+            position = place ^ index
+            plane = lax.div(position, 4)
+            row = pl.multiple_of(lax.rem(position, 4) * size, 16)
+            if offset < 3:
+                source = mine[offset].at[block, pl.ds(size, size)]
+            else:
+                at = 2 * block + 1
+                source = mine[3 + at // blocks].at[at % blocks]
+            to = target.at[plane, block + 1, pl.ds(row, size)]
+            pltpu.make_async_copy(source, to, sems.at[plane, block + 1]).start()
+
+
 def fetch_memory(blocks, line, target, sem):
     count = len(blocks)
     for step, block in enumerate(blocks):
@@ -149,6 +173,19 @@
     first[...] = unit * gain[0:1] + bias[0:1]
 
 
+def put_heads(target, source, heads):
+    rows = source.shape[0]
+    for i in range(heads):
+        columns = slice(HD * i, HD * (i + 1))
+        target[rows * i : rows * (i + 1), columns] = source[:, columns]
+
+
+def masked(scores, allowed):
+    shape = scores.shape
+    scores = scores.reshape((-1,) + allowed.shape)
+    return jnp.where(allowed[None], scores, NEG_FILL).reshape(shape)
+
+
 def cross_mask(meta, nseg, slots, mem_slots):
     query_segment, _ = segments(meta, 4, nseg, (slots, 1), 0)
     key_segment, key_place = segments(meta, 4 + nseg, nseg, (1, mem_slots), 1)
@@ -164,35 +201,40 @@
 def cross_forward(dims, meta, cb, ob, gain, bias, first, *refs):
     mp, local, heads, scaling, nseg = dims
     blocks, pieces, owns = refs[:mp], refs[mp : mp + 10], refs[mp + 10 : mp + 13]
-    cq, kv, low, total, z2, second = refs[mp + 13 : mp + 19]
-    wc, mem, acc, sems = refs[mp + 19 :]
+    cq, low, total, z2, second, kv = refs[mp + 13 : mp + 19]
+    wc, mem, acc, stacked, both, sems = refs[mp + 19 :]
     fetch_memory(blocks, meta[1], mem, sems.at[1, 0])
     fetch_cross(pieces, owns, meta[0], wc, sems.at[0])
-    allowed = cross_mask(meta, nseg, first.shape[0], mem.shape[1])
+    slots = first.shape[0]
+    allowed = cross_mask(meta, nseg, slots, mem.shape[1])
     acc[...] = first[...] + ob[1:2]
+    stacked[...] = jnp.zeros_like(stacked)
     first_low = first[...].astype(BF16)
     arrive(mem, sems.at[1, 0])
 
     def step(z, carry):
         arrive(wc.at[z], sems.at[0, z])
         rows = cb[z]
-        cq[z] = ((nt(first_low, wc[z, :local]) + rows[0:1]) * scaling).astype(BF16)
+        query = ((nt(first_low, wc[z, :local]) + rows[0:1]) * scaling).astype(BF16)
+        cq[z] = query
+        put_heads(stacked, query, heads)
         flat = nn(wc[z, 2 * local :], mem[...])
         column = jnp.swapaxes(jnp.broadcast_to(rows[1:2], (8, local)), 0, 1)[:, :1]
         keys = flat[:local].astype(BF16)
         values = (flat[local:] + column).astype(BF16)
-        kv[z, :local] = keys
-        kv[z, local:] = values
+        both[z, :local] = keys
+        both[z, local:] = values
+        pltpu.make_async_copy(both.at[z], kv.at[z], sems.at[2, 0]).start()
+        scores = masked(nn(stacked[...], keys), allowed)
+        peak = jnp.max(scores, -1, keepdims=True)
+        weights = jnp.exp(scores - peak)
+        mass = jnp.sum(weights, -1, keepdims=True)
+        probs = (weights * (1.0 / mass)).astype(BF16)
+        total[z] = peak + jnp.log(mass)
+        out = nt(probs, values)
         for i in range(heads):
-            at = HD * i
-            scores = nn(cq[z, :, at : at + HD], keys[at : at + HD])
-            scores = jnp.where(allowed, scores, NEG_FILL)
-            peak = jnp.max(scores, -1, keepdims=True)
-            weights = jnp.exp(scores - peak)
-            mass = jnp.sum(weights, -1, keepdims=True)
-            probs = (weights * (1.0 / mass)).astype(BF16)
-            low[z, :, at : at + HD] = nt(probs, values[at : at + HD]).astype(BF16)
-            total[z * heads + i] = peak + jnp.log(mass)
+            columns = slice(HD * i, HD * (i + 1))
+            low[z, :, columns] = out[slots * i : slots * (i + 1), columns].astype(BF16)
         acc[...] += nn(low[z], wc[z, local : 2 * local])
         return carry
 
@@ -200,6 +242,7 @@
     z2[...] = acc[...]
     unit, _ = normed(acc[...])
     second[...] = unit * gain[1:2] + bias[1:2]
+    arrive(both, sems.at[2, 0])
 
 
 def put_slots(beside, mine, place, z, base, source, sem):
@@ -309,47 +352,55 @@
 def cross_back(dims, meta, dz2, cq, total, z1, gain, *refs):
     mp, local, heads, scaling, nseg = dims
     kv_ref, pieces, owns = refs[0], refs[1:11], refs[11:14]
-    mem_out, (kv_low, dcq, dz1, sums, sums_local) = refs[14 : 14 + mp], refs[14 + mp : 19 + mp]
-    wc, kv, dmem, acc, dout, sems = refs[19 + mp :]
+    dcq, dz1, sums, sums_local, kv_low = refs[14:19]
+    mem_out = refs[19 : 19 + mp]
+    wc, kv, kv_grad, dmem, acc, queries, grads, sems = refs[19 + mp :]
     for z in range(mp):
-        pltpu.make_async_copy(kv_ref.at[z], kv.at[z], sems.at[1, z]).start()
-    fetch_cross(pieces, owns, meta[0], wc, sems.at[0])
-    allowed = cross_mask(meta, nseg, dz2.shape[0], kv.shape[2])
+        pltpu.make_async_copy(kv_ref.at[z], kv.at[z], sems.at[2, z]).start()
+    fetch_halves(pieces, owns, meta[0], wc, sems)
+    slots = dz2.shape[0]
+    allowed = cross_mask(meta, nseg, slots, kv.shape[2])
+    queries[...] = jnp.zeros_like(queries)
+    grads[...] = jnp.zeros_like(grads)
     dz2_low = dz2[...].astype(BF16)
     acc[...] = dz2[...]
-    dmem[...] = jnp.zeros_like(dmem)
 
     def step(z, carry):
-        arrive(wc.at[z], sems.at[0, z])
-        arrive(kv.at[z], sems.at[1, z])
-        dout[...] = nt(dz2_low, wc[z, local : 2 * local]).astype(BF16)
+        arrive(wc.at[0, z], sems.at[0, z])
+        arrive(wc.at[1, z], sems.at[1, z])
+        arrive(kv.at[z], sems.at[2, z])
+        put_heads(queries, cq[z], heads)
+        grad = nt(dz2_low, wc[0, z, local:]).astype(BF16)
+        put_heads(grads, grad, heads)
+        keys, values = kv[z, :local], kv[z, local:]
+        probs = jnp.exp(masked(nn(queries[...], keys), allowed) - total[z])
+        probs_low = probs.astype(BF16)
+        prob_grad = nn(grads[...], values)
+        offset = jnp.sum(probs * prob_grad, -1, keepdims=True)
+        score_grad = (probs * (prob_grad - offset)).astype(BF16)
+        kv_grad[z, :local] = tn(queries[...], score_grad).astype(BF16)
+        kv_grad[z, local:] = tn(grads[...], probs_low).astype(BF16)
+        pltpu.make_async_copy(kv_grad.at[z], kv_low.at[z], sems.at[3, 0]).start()
+        mass = jnp.sum(probs_low.astype(F32), -1, keepdims=True)
+        query_grad = nt(score_grad, keys) * scaling
         for i in range(heads):
-            at = HD * i
-            query = cq[z, :, at : at + HD]
-            key = kv[z, at : at + HD]
-            value = kv[z, local + at : local + at + HD]
-            grad = dout[:, at : at + HD]
-            scores = jnp.where(allowed, nn(query, key), NEG_FILL)
-            probs = jnp.exp(scores - total[z * heads + i])
-            probs_low = probs.astype(BF16)
-            prob_grad = nn(grad, value)
-            offset = jnp.sum(probs * prob_grad, -1, keepdims=True)
-            score_grad = (probs * (prob_grad - offset)).astype(BF16)
-            kv_low[z, at : at + HD] = tn(query, score_grad).astype(BF16)
-            kv_low[z, local + at : local + at + HD] = tn(grad, probs_low).astype(BF16)
-            mass = jnp.sum(probs_low.astype(F32), -1, keepdims=True)
-            query_grad = nt(score_grad, key) * scaling
-            dcq[z, :, at : at + HD] = query_grad.astype(BF16)
-            sums_local[z, 0:1, at : at + HD] = row_sum(query_grad)
-            sums_local[z, 1:2, at : at + HD] = row_sum(mass * grad.astype(F32))
-        acc[...] += nn(dcq[z], wc[z, :local])
-        dmem[...] += tn(wc[z, 2 * local :], kv_low[z])
+            columns = slice(HD * i, HD * (i + 1))
+            rows = slice(slots * i, slots * (i + 1))
+            part = query_grad[rows, columns]
+            dcq[z, :, columns] = part.astype(BF16)
+            sums_local[z, 0:1, columns] = row_sum(part)
+            sums_local[z, 1:2, columns] = row_sum(mass[rows] * grad[:, columns].astype(F32))
+        acc[...] += nn(dcq[z], wc[0, z, :local])
         return carry
 
     lax.fori_loop(0, mp, step, 0)
+    depth = mp * kv_grad.shape[1]
+    product = tn(wc[1].reshape(depth, wc.shape[3]), kv_grad[...].reshape(depth, kv.shape[2]))
+    dmem[...] = product.astype(BF16)
     for block in range(mp):
         row = pl.multiple_of(lax.rem(meta[1] + block, mp) * local, 16)
-        mem_out[block][...] = dmem[pl.ds(row, local)].astype(BF16)
+        source = dmem.at[pl.ds(row, local)]
+        pltpu.make_async_copy(source, mem_out[block], sems.at[3, 1]).start()
     unit, inverse = normed(z1[...])
     grad_rows = acc[...]
     values = norm_back(unit, inverse, gain[0:1], grad_rows)
@@ -358,6 +409,8 @@
     sums[0:1] = row_sum(values)
     sums[1:2] = row_sum(grad_rows * unit)
     sums[2:3] = row_sum(grad_rows)
+    arrive(kv_grad, sems.at[3, 0])
+    arrive(dmem, sems.at[3, 1])
 
 
 def head_back(dims, meta, dz1, x_ref, qkv, self_low, dz2, first, dcq, cross_low, *refs):
@@ -489,6 +542,20 @@
         pieces.append(joined.at[pl.ds(row, piece.shape[0])])
         row += piece.shape[0]
     place_rows(meta[0], ((0, 96, (gi,)), (96, 96, (go,))), pieces)
+
+
+def add_slots(mine, other, to_two, to_four, left, right, out, sems):
+    count = out.shape[0]
+    for i in range(count):
+        pltpu.make_async_copy(mine.at[i], left.at[i], sems.at[0, i]).start()
+        pltpu.make_async_copy(other.at[i], right.at[i], sems.at[1, i]).start()
+    for i in range(count):
+        arrive(left.at[i], sems.at[0, i])
+        arrive(right.at[i], sems.at[1, i])
+        out[i] = (left[i].astype(F32) + right[i].astype(F32)).astype(BF16)
+        target = (to_two, to_four)[i // 2].at[i % 2]
+        pltpu.make_async_copy(out.at[i], target, sems.at[2, 0]).start()
+    arrive(out, sems.at[2, 0])
 
 
 def join_columns(meta, *refs):
@@ -720,6 +787,7 @@
         weights_shape = VMEM((mp, 4 * local, width), BF16)
         flat_shape = VMEM((slots, width), F32)
         kv_shape = VMEM((mp, 2 * local, mem_slots), BF16)
+        stack_shape = VMEM((heads * slots, local), BF16)
         row_shape = shaped((slots, width))
         low_shape = shaped((mp, slots, local), BF16)
         head_slots = shaped((8, 2, 4 * local // SUB, width), BF16)
@@ -752,21 +820,29 @@
         )
         ffn_beside += [swap(piece, 1) for piece in (*ffn_near, *ffn_far)]
         ffn_pieces = (ffn_own, *ffn_near, *ffn_far, *ffn_beside)
-        cross_q, kv, cross_low, cross_total, z2, second = call(
+        cross_q, cross_low, cross_total, z2, second, kv = call(
             bound(cross_forward),
             [META] + in_vmem(5) + in_place(mp + 13),
             (
                 low_shape,
-                shaped((mp, 2 * local, mem_slots), BF16),
                 low_shape,
-                shaped((mp * heads, slots, 1)),
+                shaped((mp, heads * slots, 1)),
                 row_shape,
                 row_shape,
+                shaped((mp, 2 * local, mem_slots), BF16),
             ),
-            [weights_shape, VMEM((width, mem_slots), BF16), flat_shape, dma],
+            [
+                weights_shape,
+                VMEM((width, mem_slots), BF16),
+                flat_shape,
+                stack_shape,
+                kv_shape,
+                dma,
+            ],
             40 * matmul,
             8 * plain,
             "cross_forward",
+            1,
         )(
             meta,
             cross_bias,
@@ -804,28 +880,31 @@
         )(meta, second, z2, grad_row, inner_bias, *params, *ffn_pieces, ffn_in, ffn_out)
         ffn_theirs = swap(ffn_shared, 1)
         result_blocks = spread_line(result)
-        *memory_grads, kv_low, cross_dq, dz1, cross_sums, cross_local = call(
+        cross_dq, dz1, cross_sums, cross_local, kv_low, *memory_grads = call(
             bound(cross_back),
             [META] + in_vmem(5) + in_place(14),
             (
-                *[shaped((local, mem_slots), BF16)] * mp,
-                shaped((mp, 2 * local, mem_slots), BF16),
                 low_shape,
                 row_shape,
                 shaped((8, width)),
                 shaped((mp, 2, local)),
+                shaped((mp, 2 * local, mem_slots), BF16),
+                *[shaped((local, mem_slots), BF16)] * mp,
             ),
             [
-                weights_shape,
+                VMEM((2, mp, 2 * local, width), BF16),
                 kv_shape,
-                VMEM((width, mem_slots), F32),
+                kv_shape,
+                VMEM((width, mem_slots), BF16),
                 flat_shape,
-                VMEM((slots, local), BF16),
+                stack_shape,
+                stack_shape,
                 dma,
             ],
             50 * matmul,
             12 * plain,
             "cross_back",
+            1 + mp,
         )(
             meta,
             dz2,
@@ -915,10 +994,18 @@
             return head_mine[slots].astype(F32) + head_other[slots].astype(F32)
 
         head_group = Group(head_summed)
-        head_from = (
-            swap(head_summed(slice(0, 2)).astype(BF16), 2),
-            swap(head_summed(slice(2, 4)).astype(BF16), 4),
-        )
+        four_slots = VMEM((4, 2, 2 * width // SUB, width), BF16)
+        to_two, to_four = call(
+            add_slots,
+            in_place(2),
+            (pair_slots, pair_slots),
+            [four_slots, four_slots, four_slots, dma],
+            0,
+            4 * plain,
+            "add_slots",
+            2,
+        )(head_mine, head_other)
+        head_from = swap(to_two, 2), swap(to_four, 4)
         ffn_sent = [shift(ffn_blocks[step - 1], -step) for step in range(1, mp)]
 
         def joined(kernel, blocks, shape, dtype, name):
@@ -936,6 +1023,9 @@
         )
         late_two, late_four = head_group.second(*head_from)
         head_late = swap(late_two, 2), swap(late_four, 4)
+        hidden_low = hidden_grad.astype(BF16)
+        hidden_blocks = [hidden_low, shift(hidden_low, 1), None, shift(hidden_low, 3)]
+        small = after(small, hidden_blocks[1])
         bit = 2
         while bit < mp:
             small = small + flip(small, bit)
@@ -946,7 +1036,9 @@
         while bit < dp:
             small = small + swap(small, bit)
             bit *= 2
-        head_late, ffn_low, small = meet(head_late, ffn_low, small)
+        head_late, ffn_low, small, hidden_blocks = meet(
+            head_late, ffn_low, small, hidden_blocks
+        )
         head_total, head_blocks = head_group.third(*head_from, *head_late)
         head_sent = [shift(head_blocks[step - 1], -step) for step in range(1, mp)]
         ffn_near = near_chips(ffn_low)
@@ -955,15 +1047,14 @@
         small = small + swap(small, 4)
         ffn_near[0], _ = meet(ffn_near[0], head_sent[0])
         ffn_far = far_chips(*ffn_near)
-        hidden_low = hidden_grad.astype(BF16)
         ffn_reduced = (ffn_low, *ffn_near, *ffn_far)
         ffn_joined = jnp.concatenate(ffn_reduced)
-        head_sent, ffn_reduced, ffn_joined, small, hidden_low = meet(
-            head_sent, ffn_reduced, ffn_joined, small, hidden_low
+        head_sent, ffn_reduced, ffn_joined, small, hidden_blocks = meet(
+            head_sent, ffn_reduced, ffn_joined, small, hidden_blocks
         )
         head_low = line_sum(head_total, head_sent)
         head_near = near_chips(head_low)
-        hidden_blocks = [hidden_low, shift(hidden_low, 1), None, shift(hidden_low, 3)]
+        hidden_blocks[2] = shift(hidden_blocks[0], 2)
         ffn_joined = swap(ffn_joined, 1)
         head_near, ffn_joined, hidden_blocks = meet(head_near, ffn_joined, hidden_blocks)
         grad_in, grad_out = call(
@@ -975,13 +1066,12 @@
             plain,
             "finish_ffn",
         )(meta, *ffn_reduced, ffn_joined)
-        hidden_blocks[2] = shift(hidden_blocks[0], 2)
+        hidden_grad = joined(join_rows, hidden_blocks, rows_shape, F32, "join_hidden")
         head_far = far_chips(*head_near)
         head_beside = [swap(piece, 1) for piece in (head_low, *head_near)]
-        head_far, head_beside, grad_in, grad_out, hidden_blocks = meet(
-            head_far, head_beside, grad_in, grad_out, hidden_blocks
-        )
-        hidden_grad = joined(join_rows, hidden_blocks, rows_shape, F32, "join_hidden")
+        head_far, head_beside, grad_in, grad_out, hidden_grad = meet(
+            head_far, head_beside, grad_in, grad_out, hidden_grad
+        )
         head_beside += [swap(piece, 1) for piece in head_far]
         finished = call(
             finish_heads,

time: 348 us -> 341 us (0.980); the launches traced: 343 us -> 340 us
  other arithmetic: 22.2 us -> 17.3 us
    convert_element_type x1 -> x0, other arithmetic: 5.3 us -> none  [body(): head_summed(slice(2, 4)).astype(BF16)]
    ppermute x24, starting transfers between devices: 29.8 us -> 34.8 us  [shift(): return lax.ppermute(value, 'mp', [(i, (i + step) % mp) for i in range(mp)])]
    pallas_call x1 -> x2, Pallas kernels: 18.6 us -> 20.7 us  [the longest x1 17.2 us: body(): call(bound(cross_back), [META] + in_vmem(5) + in_place(14), (low_shape, r...]
where the time goes in v5:
time: 341 us; the launch traced here: 340 us
  waiting for transfers between devices  126 us (37%)
  Pallas kernels  93.8 us (28%)
  starting transfers between devices  81.9 us (24%)
  local copies, waits for them, and re-layouts  18.5 us (5%)
  other arithmetic  17.3 us (5%)
    ppermute x24, waiting for transfers between devices, shift(): return lax.ppermute(value, 'mp', [(i, (i + step) % mp) for i in range(mp)])  99.4 us
    ppermute x45, starting transfers between devices, swap(): return lax.ppermute(value, 'dp', [(i, i ^ bit) for i in range(dp)])  46.4 us
    ppermute x24, starting transfers between devices, shift(): return lax.ppermute(value, 'mp', [(i, (i + step) % mp) for i in range(mp)])  34.8 us
    pallas_call x1, Pallas kernels, body(): call(bound(head_back), [META] + in_vmem(11) + in_place(mp + 13), (row_sha...  19.4 us
    pallas_call x1, Pallas kernels, body(): call(bound(cross_back), [META] + in_vmem(5) + in_place(14), (low_shape, r...  17.2 us
    ppermute x45, waiting for transfers between devices, swap(): return lax.ppermute(value, 'dp', [(i, i ^ bit) for i in range(dp)])  14 us
    pallas_call x1, Pallas kernels, body(): call(bound(cross_forward), [META] + in_vmem(5) + in_place(mp + 13), (low_...  13.3 us
    ppermute x2, waiting for transfers between devices, flip(): return lax.ppermute(value, 'mp', [(i, i ^ bit) for i in range(mp)])  12.9 us
  transfers between devices with their start and end apart: 71, of which 27 were waited for; matrix products, arithmetic and copies ran while one was open for 7% of the time, Pallas kernels for 21%

profile of v5, /device:TPU:9, one launch (start us, length us, event | category | flops | bytes accessed | tf_op | source)
XLA Modules:
  0.0 339.7 jit_solution(13536128430931224721)
XLA Ops:
  17.9 9.5 %collective-permute-done.1 = bf16[208,768]{1,0:T(8,128)(2,1)S(1)} collective-permute-done((bf16[208,768]{1,0:T(8,128)(2,1)S(1)}, bf16[208,768]{1,0:T(8,128)(2,1)S(1)}, u32[]{:S(2)}, u32[]{:S(2)}) %collective-permute-start.1) | collective-permute-done | bytes 319520 | tf_op jit(solution)/shard_map/ppermute | solution.py:617
  27.3 6.8 %collective-permute-done = bf16[208,768]{1,0:T(8,128)(2,1)S(1)} collective-permute-done((bf16[208,768]{1,0:T(8,128)(2,1)S(1)}, bf16[208,768]{1,0:T(8,128)(2,1)S(1)}, u32[]{:S(2)}, u32[]{:S(2)}) %collective-permute-start) | collective-permute-done | bytes 319520 | tf_op jit(solution)/shard_map/ppermute | solution.py:617
  43.1 11.1 %collective-permute-done.6 = bf16[192,768]{1,0:T(8,128)(2,1)} collective-permute-done((bf16[192,768]{1,0:T(8,128)(2,1)}, bf16[192,768]{1,0:T(8,128)(2,1)}, u32[]{:S(2)}, u32[]{:S(2)}) %collective-permute-start.6) | collective-permute-done | bytes 294944 | tf_op jit(solution)/shard_map/ppermute | solution.py:617
  54.2 6.3 %collective-permute-done.5 = bf16[192,768]{1,0:T(8,128)(2,1)} collective-permute-done((bf16[192,768]{1,0:T(8,128)(2,1)}, bf16[192,768]{1,0:T(8,128)(2,1)}, u32[]{:S(2)}, u32[]{:S(2)}) %collective-permute-start.5) | collective-permute-done | bytes 294944 | tf_op jit(solution)/shard_map/ppermute | solution.py:617
  68.1 8.1 %collective-permute-done.12.refs_7_.refs_14_ = bf16[192,1024]{1,0:T(8,128)(2,1)S(1)} collective-permute-done((bf16[192,1024]{1,0:T(8,128)(2,1)}, bf16[192,1024]{1,0:T(8,128)(2,1)S(1)}, u32[]{:S(2)}, u32[]{:S(2)}) %collective-permute-start.12) | collective-permute-done | bytes 393248 | tf_op jit(solution)/shard_map/ppermute | solution.py:617
  84.5 8.4 %self_forward.1 = (bf16[4,128,576]{2,1,0:T(8,128)(2,1)}, bf16[4,128,192]{2,1,0:T(8,128)(2,1)}, f32[128,768]{1,0:T(8,128)}, f32[128,768]{1,0:T(8,128)}) custom-call(s32[12]{0:T(128)} %concatenate.27.refs_0_.meta, bf16[128,768]{1,0:T(8,128)(2,1)} %get-tuple-element.208.refs_1_.refs_2_, f32[4,2,192]{2,1,0:T(2,128)} %reshape.174.refs_2_, f32[3,768]{1,0:T(4,128)} %refs_5_.4, ...), custom_call_target="tpu_custom_call" | custom-call | flops 188743680 | bytes 2359296 | tf_op jit(solution)/shard_map/self_forward/pallas_call | solution.py:804
  92.9 7.9 %collective-permute-done.15.refs_8_.refs_15_ = bf16[192,1024]{1,0:T(8,128)(2,1)} collective-permute-done((bf16[192,1024]{1,0:T(8,128)(2,1)}, bf16[192,1024]{1,0:T(8,128)(2,1)}, u32[]{:S(2)}, u32[]{:S(2)}) %collective-permute-start.15) | collective-permute-done | bytes 393248 | tf_op jit(solution)/shard_map/ppermute | solution.py:617
  103.0 3.3 collective-permute-start.22
  109.8 5.4 %collective-permute-done.22.refs_9_.refs_16_ = bf16[192,1024]{1,0:T(8,128)(2,1)S(1)} collective-permute-done((bf16[192,1024]{1,0:T(8,128)(2,1)}, bf16[192,1024]{1,0:T(8,128)(2,1)S(1)}, u32[]{:S(2)}, u32[]{:S(2)}) %collective-permute-start.22) | collective-permute-done | bytes 393248 | tf_op jit(solution)/shard_map/ppermute | solution.py:617
  115.9 3.1 collective-permute-done.19.refs_11_
  120.5 13.3 %cross_forward.1 = (bf16[4,128,192]{2,1,0:T(8,128)(2,1)}, bf16[4,128,192]{2,1,0:T(8,128)(2,1)}, f32[4,384,1]{2,1,0:T(8,128)}, f32[128,768]{1,0:T(8,128)}, f32[12...) custom-call(s32[12]{0:T(128)} %concatenate.27.refs_0_.meta, f32[4,2,192]{2,1,0:T(2,128)} %reshape.175.refs_1_, ...), custom_call_target="tpu_custom_call" | custom-call | flops 377487360 | bytes 2359296 | tf_op jit(solution)/shard_map/cross_forward/pallas_call | solution.py:823
  134.9 10.4 %ffn_both.1 = (bf16[128,768]{1,0:T(8,128)(2,1)}, f32[128,768]{1,0:T(8,128)}, f32[16,768]{1,0:T(8,128)}, bf16[5,128,1152]{2,1,0:T(8,128)(2,1)}, bf16[5,128,384]{2,1,0:T(8,128)(2,1)}) custom-call(s32[12]{0:T(128)} %concatenate.27.refs_0_.meta, f32[128,768]{1,0:T(8,128)} %get-tuple-element.236.refs_1_, f32[128,768]{1,0:T(8,128)} %get-tuple-element.237.refs_2_, ...), custom_call_target="tpu_custom_call" | custom-call | flops 377487360 | bytes 2949120 | tf_op jit(solution)/shard_map/ffn_both/pallas_call | solution.py:858
  147.3 17.2 %cross_back.1 = (bf16[4,128,192]{2,1,0:T(8,128)(2,1)}, f32[128,768]{1,0:T(8,128)}, f32[8,768]{1,0:T(8,128)}, f32[4,2,192]{2,1,0:T(2,128)}, bf16[4,384,1024]{2,1,...) custom-call(s32[12]{0:T(128)} %concatenate.27.refs_0_.meta, ...), custom_call_target="tpu_custom_call" | custom-call | flops 471859200 | bytes 3538944 | tf_op jit(solution)/shard_map/cross_back/pallas_call | solution.py:883
  165.8 5.1 %ffn_weights.1 = (bf16[2,2,192,768]{3,2,1,0:T(8,128)(2,1)}, bf16[2,2,192,768]{3,2,1,0:T(8,128)(2,1)}, bf16[4,2,192,768]{3,2,1,0:T(8,128)(2,1)}) custom-call(s32[12]{0:T(128)} %concatenate.27.refs_0_.meta, bf16[5,128,1152]{2,1,0:T(8,128)(2,1)} %get-tuple-element.243.refs_1_, bf16[5,128,384]{2,1,0:T(8,128)(2,1)} %get-tuple-element.244.refs_2_, ...), custom_call_target="tpu_custom_call" | custom-call | flops 150994944 | bytes 2359296 | tf_op jit(solution)/shard_map/ffn_weights/pallas_call | solution.py:927
  177.0 19.4 %head_back.1 = (f32[128,768]{1,0:T(8,128)}, f32[24,768]{1,0:T(8,128)}, bf16[8,2,192,768]{3,2,1,0:T(8,128)(2,1)}, bf16[8,2,192,768]{3,2,1,0:T(8,128)(2,1)}) custom-call(s32[12]{0:T(128)} %concatenate.27.refs_0_.meta, f32[128,768]{1,0:T(8,128)} %get-tuple-element.265.refs_1_, bf16[128,768]{1,0:T(8,128)(2,1)} %get-tuple-element.208.refs_1_.refs_2_, ...), custom_call_target="tpu_custom_call" | custom-call | flops 566231040 | bytes 7077888 | tf_op jit(solution)/shard_map/head_back/pallas_call | solution.py:943
  203.7 3.7 %collective-permute-start.38 = (bf16[192,1024]{1,0:T(8,128)(2,1)S(1)}, bf16[192,1024]{1,0:T(8,128)(2,1)S(1)}, u32[]{:S(2)}, u32[]{:S(2)}) collective-permute-start(bf16[192,1024]{1,0:T(8,128)(2,1)S(1)} %copy-done.49), channel_id=1, source_target_pairs={{0,3},{1,0},{2,1},{3,2},{4,7},{5,4},{6,5},{7,6},{8,11},{9,8},{10,9... | collective-permute-start | bytes 1179656 | tf_op jit(solution)/shard_map/ppermute | solution.py:617
  208.1 9.9 %collective-permute-done.39 = f32[24,768]{1,0:T(8,128)S(1)} collective-permute-done((f32[24,768]{1,0:T(8,128)S(1)}, f32[24,768]{1,0:T(8,128)S(1)}, u32[]{:S(2)}, u32[]{:S(2)}) %collective-permute-start.39) | collective-permute-done | bytes 73760 | tf_op jit(solution)/shard_map/ppermute | solution.py:620
  219.4 3.5 %add_slots.1 = (bf16[2,2,192,768]{3,2,1,0:T(8,128)(2,1)}, bf16[2,2,192,768]{3,2,1,0:T(8,128)(2,1)}) custom-call(bf16[8,2,192,768]{3,2,1,0:T(8,128)(2,1)} %get-tuple-element.278.mine, bf16[8,2,192,768]{3,2,1,0:T(8,128)(2,1)} %collective-permute-done.35.other), custom_call_target="tpu_custom_call" | custom-call | bytes 1179648 | tf_op jit(solution)/shard_map/add_slots/pallas_call | solution.py:998
  227.1 3.9 %collective-permute-start.43 = (bf16[192,768]{1,0:T(8,128)(2,1)S(1)}, bf16[192,768]{1,0:T(8,128)(2,1)}, u32[]{:S(2)}, u32[]{:S(2)}) collective-permute-start(bf16[192,768]{1,0:T(8,128)(2,1)S(1)} %get-tuple-element.370), channel_id=1, source_target_pairs={{0,2},{1,3},{2,0},{3,1},{4,6},{5,7},{6,4},{7,5},{8,10},{9,11},{10,... | collective-permute-start | bytes 884744 | tf_op jit(solution)/shard_map/ppermute | solution.py:617
  233.2 3.2 join_memory.1
  236.4 14.2 %collective-permute-done.43 = bf16[192,768]{1,0:T(8,128)(2,1)} collective-permute-done((bf16[192,768]{1,0:T(8,128)(2,1)S(1)}, bf16[192,768]{1,0:T(8,128)(2,1)}, u32[]{:S(2)}, u32[]{:S(2)}) %collective-permute-start.43) | collective-permute-done | bytes 294944 | tf_op jit(solution)/shard_map/ppermute | solution.py:617
  250.6 4.9 %collective-permute-done.42 = bf16[192,768]{1,0:T(8,128)(2,1)} collective-permute-done((bf16[192,768]{1,0:T(8,128)(2,1)S(1)}, bf16[192,768]{1,0:T(8,128)(2,1)}, u32[]{:S(2)}, u32[]{:S(2)}) %collective-permute-start.42) | collective-permute-done | bytes 294944 | tf_op jit(solution)/shard_map/ppermute | solution.py:617
  259.7 4.8 %collective-permute-done.47.refs_1_ = bf16[128,768]{1,0:T(8,128)(2,1)S(1)} collective-permute-done((bf16[128,768]{1,0:T(8,128)(2,1)S(1)}, bf16[128,768]{1,0:T(8,128)(2,1)S(1)}, u32[]{:S(2)}, u32[]{:S(2)}) %collective-permute-start.47) | collective-permute-done | bytes 196640 | tf_op jit(solution)/shard_map/ppermute | solution.py:617
  265.7 3.0 collective-permute-done.48
  268.7 4.5 %collective-permute-start.49 = (f32[24,768]{1,0:T(8,128)S(1)}, f32[24,768]{1,0:T(8,128)S(1)}, u32[]{:S(2)}, u32[]{:S(2)}) collective-permute-start(f32[24,768]{1,0:T(8,128)S(1)} %add.279), channel_id=1, source_target_pairs={{0,4},{4,0},{8,12},{12,8},{16,20},{20,16},{24,28},{28,24},{1,5},{5... | collective-permute-start | bytes 221192 | tf_op jit(solution)/shard_map/ppermute | solution.py:614
  279.9 4.1 %collective-permute-start.52 = (bf16[192,768]{1,0:T(8,128)(2,1)S(1)}, bf16[192,768]{1,0:T(8,128)(2,1)S(1)}, u32[]{:S(2)}, u32[]{:S(2)}) collective-permute-start(bf16[192,768]{1,0:T(8,128)(2,1)S(1)} %get-tuple-element.365), channel_id=1, source_target_pairs={{0,2},{1,3},{2,0},{3,1},{4,6},{5,7},{6,4},{7,5},{8,10},{9,11},{10,... | collective-permute-start | bytes 884744 | tf_op jit(solution)/shard_map/ppermute | solution.py:617
  290.3 3.1 collective-permute-done.59
  294.2 10.1 %collective-permute-done.52 = bf16[192,768]{1,0:T(8,128)(2,1)S(1)} collective-permute-done((bf16[192,768]{1,0:T(8,128)(2,1)S(1)}, bf16[192,768]{1,0:T(8,128)(2,1)S(1)}, u32[]{:S(2)}, u32[]{:S(2)}) %collective-permute-start.52) | collective-permute-done | bytes 294944 | tf_op jit(solution)/shard_map/ppermute | solution.py:617
  304.3 6.8 %collective-permute-start.62 = (bf16[768,768]{1,0:T(8,128)(2,1)S(1)}, bf16[768,768]{1,0:T(8,128)(2,1)S(1)}, u32[]{:S(2)}, u32[]{:S(2)}) collective-permute-start(bf16[768,768]{1,0:T(8,128)(2,1)S(1)} %constant_dynamic-update-slice_fusion.1), channel_id=1, source_target_pairs={{0,4},{4,0},{8,12},{12,8},{16,20},{20,16},{24,28},{28,24},{1,5},{5... | collective-permute-start | bytes 3538952 | tf_op jit(solution)/shard_map/ppermute | solution.py:614
  314.6 6.2 %collective-permute-done.63.refs_2_ = bf16[128,768]{1,0:T(8,128)(2,1)S(1)} collective-permute-done((bf16[128,768]{1,0:T(8,128)(2,1)S(1)}, bf16[128,768]{1,0:T(8,128)(2,1)S(1)}, u32[]{:S(2)}, u32[]{:S(2)}) %collective-permute-start.63) | collective-permute-done | bytes 196640 | tf_op jit(solution)/shard_map/ppermute | solution.py:617
  327.4 4.3 %finish_ffn.1 = (f32[768,768]{1,0:T(8,128)}, f32[768,768]{1,0:T(8,128)}) custom-call(s32[12]{0:T(128)} %concatenate.27.refs_0_.meta, bf16[192,768]{1,0:T(8,128)(2,1)} %copy-done.10, bf16[192,768]{1,0:T(8,128)(2,1)} %copy-done.14, bf16[192,768]{1,0:T(8,128)(2,1)} %copy-done.13, bf16[96,768]{1,0:T(8,128)(2,1)} %copy-done.27, bf16[96,768]{1,0:T(8,128)(2,1)} %copy-done.28, ...), custom_call_target="tpu_custom_call" | custom-call | bytes 294912 | tf_op jit(solution)/shard_map/finish_ffn/pallas_call | solution.py:1060
  335.1 4.4 %finish_heads.1 = (f32[576,768]{1,0:T(8,128)}, f32[192,768]{1,0:T(8,128)}, f32[192,768]{1,0:T(8,128)}, f32[192,768]{1,0:T(8,128)}, f32[384,768]{1,0:T(8,128)}, /...) custom-call(s32[12]{0:T(128)} %concatenate.27.refs_0_.meta, ...), custom_call_target="tpu_custom_call" | custom-call | bytes 294912 | tf_op jit(solution)/shard_map/finish_heads/pallas_call | solution.py:1076
  (290 shorter events, 108.0 us)
Async XLA Ops:
  4.7 22.7 %collective-permute-start.1 = (bf16[208,768]{1,0:T(8,128)(2,1)S(1)}, bf16[208,768]{1,0:T(8,128)(2,1)S(1)}, u32[]{:S(2)}, u32[]{:S(2)}) collective-permute-start(bf16[208,768]{1,0:T(8,128)(2,1)S(1)} %concatenate.25), channel_id=1, source_target_pairs={{0,2},{1,3},{2,0},{3,1},{4,6},{5,7},{6,4},{7,5},{8,10},{9,11},{10,... | collective-permute-start | bytes 958472 | tf_op jit(solution)/shard_map/ppermute | solution.py:617
  7.1 27.1 %collective-permute-start = (bf16[208,768]{1,0:T(8,128)(2,1)S(1)}, bf16[208,768]{1,0:T(8,128)(2,1)S(1)}, u32[]{:S(2)}, u32[]{:S(2)}) collective-permute-start(bf16[208,768]{1,0:T(8,128)(2,1)S(1)} %concatenate.25), channel_id=1, source_target_pairs={{0,1},{1,2},{2,3},{3,0},{4,5},{5,6},{6,7},{7,4},{8,9},{9,10},{10,1... | collective-permute-start | bytes 958472 | tf_op jit(solution)/shard_map/ppermute | solution.py:617
  34.8 19.4 %collective-permute-start.6 = (bf16[192,768]{1,0:T(8,128)(2,1)}, bf16[192,768]{1,0:T(8,128)(2,1)}, u32[]{:S(2)}, u32[]{:S(2)}) collective-permute-start(bf16[192,768]{1,0:T(8,128)(2,1)} %pad_maximum_fusion.2), channel_id=1, source_target_pairs={{0,2},{1,3},{2,0},{3,1},{4,6},{5,7},{6,4},{7,5},{8,10},{9,11},{10,... | collective-permute-start | bytes 884744 | tf_op jit(solution)/shard_map/ppermute | solution.py:617
  37.6 23.0 %collective-permute-start.5 = (bf16[192,768]{1,0:T(8,128)(2,1)}, bf16[192,768]{1,0:T(8,128)(2,1)}, u32[]{:S(2)}, u32[]{:S(2)}) collective-permute-start(bf16[192,768]{1,0:T(8,128)(2,1)} %pad_maximum_fusion.2), channel_id=1, source_target_pairs={{0,1},{1,2},{2,3},{3,0},{4,5},{5,6},{6,7},{7,4},{8,9},{9,10},{10,1... | collective-permute-start | bytes 884744 | tf_op jit(solution)/shard_map/ppermute | solution.py:617
  37.8 22.8 %collective-permute-start.4 = (bf16[3,192,768]{2,1,0:T(8,128)(2,1)S(1)}, bf16[3,192,768]{2,1,0:T(8,128)(2,1)S(1)}, u32[]{:S(2)}, u32[]{:S(2)}) collective-permute-start(bf16[3,192,768]{2,1,0:T(8,128)(2,1)S(1)} %pad_maximum_fusion.refs_6_.refs_10_.refs_7_.refs_17_), channel_id=1, source_target_pairs={{0,16},{4,20},{8,24},{12,28},{16,0},{20,4},{24,8},{28,12},{1,17},{... | collective-permute-start | bytes 2654216 | tf_op jit(solution)/shard_map/ppermute | solution.py:614
  39.1 21.5 %collective-permute-start.3 = (bf16[3,192,768]{2,1,0:T(8,128)(2,1)S(1)}, bf16[3,192,768]{2,1,0:T(8,128)(2,1)S(1)}, u32[]{:S(2)}, u32[]{:S(2)}) collective-permute-start(bf16[3,192,768]{2,1,0:T(8,128)(2,1)S(1)} %pad_maximum_fusion.refs_6_.refs_10_.refs_7_.refs_17_), channel_id=1, source_target_pairs={{0,8},{4,12},{8,0},{12,4},{16,24},{20,28},{24,16},{28,20},{1,9},{5... | collective-permute-start | bytes 2654216 | tf_op jit(solution)/shard_map/ppermute | solution.py:614
  80.4 21.4 %collective-permute-start.14 = (bf16[3,192,768]{2,1,0:T(8,128)(2,1)}, bf16[3,192,768]{2,1,0:T(8,128)(2,1)S(1)}, u32[]{:S(2)}, u32[]{:S(2)}) collective-permute-start(bf16[3,192,768]{2,1,0:T(8,128)(2,1)} %pad_maximum_fusion.1.refs_8_), channel_id=1, source_target_pairs={{0,16},{4,20},{8,24},{12,28},{16,0},{20,4},{24,8},{28,12},{1,17},{... | collective-permute-start | bytes 2654216 | tf_op jit(solution)/shard_map/ppermute | solution.py:614
  80.6 21.2 %collective-permute-start.13 = (bf16[3,192,768]{2,1,0:T(8,128)(2,1)}, bf16[3,192,768]{2,1,0:T(8,128)(2,1)}, u32[]{:S(2)}, u32[]{:S(2)}) collective-permute-start(bf16[3,192,768]{2,1,0:T(8,128)(2,1)} %pad_maximum_fusion.1.refs_8_), channel_id=1, source_target_pairs={{0,8},{4,12},{8,0},{12,4},{16,24},{20,28},{24,16},{28,20},{1,9},{5... | collective-permute-start | bytes 2654216 | tf_op jit(solution)/shard_map/ppermute | solution.py:614
  82.2 18.6 %collective-permute-start.15 = (bf16[192,1024]{1,0:T(8,128)(2,1)}, bf16[192,1024]{1,0:T(8,128)(2,1)}, u32[]{:S(2)}, u32[]{:S(2)}) collective-permute-start(bf16[192,1024]{1,0:T(8,128)(2,1)} %get-tuple-element.206), channel_id=1, source_target_pairs={{0,2},{1,3},{2,0},{3,1},{4,6},{5,7},{6,4},{7,5},{8,10},{9,11},{10,... | collective-permute-start | bytes 1179656 | tf_op jit(solution)/shard_map/ppermute | solution.py:617
  101.8 17.2 %collective-permute-start.21 = (bf16[3,192,768]{2,1,0:T(8,128)(2,1)}, bf16[3,192,768]{2,1,0:T(8,128)(2,1)S(1)}, u32[]{:S(2)}, u32[]{:S(2)}) collective-permute-start(bf16[3,192,768]{2,1,0:T(8,128)(2,1)} %pad_maximum_fusion.1.refs_8_), channel_id=1, source_target_pairs={{0,4},{4,0},{8,12},{12,8},{16,20},{20,16},{24,28},{28,24},{1,5},{5... | collective-permute-start | bytes 2654216 | tf_op jit(solution)/shard_map/ppermute | solution.py:614
  108.9 24.9 %collective-permute-start.24 = (bf16[3,192,768]{2,1,0:T(8,128)(2,1)S(1)}, bf16[3,192,768]{2,1,0:T(8,128)(2,1)S(1)}, u32[]{:S(2)}, u32[]{:S(2)}) collective-permute-start(bf16[3,192,768]{2,1,0:T(8,128)(2,1)S(1)} %collective-permute-done.14.refs_10_), channel_id=1, source_target_pairs={{0,4},{4,0},{8,12},{12,8},{16,20},{20,16},{24,28},{28,24},{1,5},{5... | collective-permute-start | bytes 2654216 | tf_op jit(solution)/shard_map/ppermute | solution.py:614
  115.1 18.7 %collective-permute-start.23 = (bf16[3,192,768]{2,1,0:T(8,128)(2,1)}, bf16[3,192,768]{2,1,0:T(8,128)(2,1)}, u32[]{:S(2)}, u32[]{:S(2)}) collective-permute-start(bf16[3,192,768]{2,1,0:T(8,128)(2,1)} %collective-permute-done.13.refs_9_), channel_id=1, source_target_pairs={{0,4},{4,0},{8,12},{12,8},{16,20},{20,16},{24,28},{28,24},{1,5},{5... | collective-permute-start | bytes 2654216 | tf_op jit(solution)/shard_map/ppermute | solution.py:614
  145.3 19.3 %collective-permute-start.30 = (bf16[5,128,1152]{2,1,0:T(8,128)(2,1)}, bf16[5,128,1152]{2,1,0:T(8,128)(2,1)S(1)}, u32[]{:S(2)}, u32[]{:S(2)}) collective-permute-start(bf16[5,128,1152]{2,1,0:T(8,128)(2,1)} %get-tuple-element.243.refs_1_), channel_id=1, source_target_pairs={{0,4},{4,0},{8,12},{12,8},{16,20},{20,16},{24,28},{28,24},{1,5},{5... | collective-permute-start | bytes 4423688 | tf_op jit(solution)/shard_map/ppermute | solution.py:614
  145.8 18.7 %collective-permute-start.29 = (bf16[128,768]{1,0:T(8,128)(2,1)}, bf16[128,768]{1,0:T(8,128)(2,1)S(1)}, u32[]{:S(2)}, u32[]{:S(2)}) collective-permute-start(bf16[128,768]{1,0:T(8,128)(2,1)} %get-tuple-element.297.refs_0_), channel_id=1, source_target_pairs={{0,3},{1,0},{2,1},{3,2},{4,7},{5,4},{6,5},{7,6},{8,11},{9,8},{10,9... | collective-permute-start | bytes 589832 | tf_op jit(solution)/shard_map/ppermute | solution.py:617
  146.0 18.5 %collective-permute-start.28 = (bf16[128,768]{1,0:T(8,128)(2,1)}, bf16[128,768]{1,0:T(8,128)(2,1)S(1)}, u32[]{:S(2)}, u32[]{:S(2)}) collective-permute-start(bf16[128,768]{1,0:T(8,128)(2,1)} %get-tuple-element.297.refs_0_), channel_id=1, source_target_pairs={{0,2},{1,3},{2,0},{3,1},{4,6},{5,7},{6,4},{7,5},{8,10},{9,11},{10,... | collective-permute-start | bytes 589832 | tf_op jit(solution)/shard_map/ppermute | solution.py:617
  146.0 18.5 %collective-permute-start.27 = (bf16[128,768]{1,0:T(8,128)(2,1)}, bf16[128,768]{1,0:T(8,128)(2,1)S(1)}, u32[]{:S(2)}, u32[]{:S(2)}) collective-permute-start(bf16[128,768]{1,0:T(8,128)(2,1)} %get-tuple-element.297.refs_0_), channel_id=1, source_target_pairs={{0,1},{1,2},{2,3},{3,0},{4,5},{5,6},{6,7},{7,4},{8,9},{9,10},{10,1... | collective-permute-start | bytes 589832 | tf_op jit(solution)/shard_map/ppermute | solution.py:617
  170.8 27.6 %collective-permute-start.32 = (bf16[2,2,192,768]{3,2,1,0:T(8,128)(2,1)}, bf16[2,2,192,768]{3,2,1,0:T(8,128)(2,1)}, u32[]{:S(2)}, u32[]{:S(2)}) collective-permute-start(bf16[2,2,192,768]{3,2,1,0:T(8,128)(2,1)} %get-tuple-element.259), channel_id=1, source_target_pairs={{0,16},{4,20},{8,24},{12,28},{16,0},{20,4},{24,8},{28,12},{1,17},{... | collective-permute-start | bytes 3538952 | tf_op jit(solution)/shard_map/ppermute | solution.py:614
  172.2 26.5 %collective-permute-start.31 = (bf16[2,2,192,768]{3,2,1,0:T(8,128)(2,1)}, bf16[2,2,192,768]{3,2,1,0:T(8,128)(2,1)S(1)}, u32[]{:S(2)}, u32[]{:S(2)}) collective-permute-start(bf16[2,2,192,768]{3,2,1,0:T(8,128)(2,1)} %get-tuple-element.258), channel_id=1, source_target_pairs={{0,8},{4,12},{8,0},{12,4},{16,24},{20,28},{24,16},{28,20},{1,9},{5... | collective-permute-start | bytes 3538952 | tf_op jit(solution)/shard_map/ppermute | solution.py:614
  173.4 23.0 %collective-permute-start.33 = (bf16[192,1024]{1,0:T(8,128)(2,1)}, bf16[192,1024]{1,0:T(8,128)(2,1)}, u32[]{:S(2)}, u32[]{:S(2)}) collective-permute-start(bf16[192,1024]{1,0:T(8,128)(2,1)} %get-tuple-element.261), channel_id=1, source_target_pairs={{0,1},{1,2},{2,3},{3,0},{4,5},{5,6},{6,7},{7,4},{8,9},{9,10},{10,1... | collective-permute-start | bytes 1179656 | tf_op jit(solution)/shard_map/ppermute | solution.py:617
  174.5 23.9 %collective-permute-start.34 = (bf16[192,1024]{1,0:T(8,128)(2,1)}, bf16[192,1024]{1,0:T(8,128)(2,1)}, u32[]{:S(2)}, u32[]{:S(2)}) collective-permute-start(bf16[192,1024]{1,0:T(8,128)(2,1)} %get-tuple-element.262), channel_id=1, source_target_pairs={{0,2},{1,3},{2,0},{3,1},{4,6},{5,7},{6,4},{7,5},{8,10},{9,11},{10,... | collective-permute-start | bytes 1179656 | tf_op jit(solution)/shard_map/ppermute | solution.py:617
  198.6 20.7 %collective-permute-start.35 = (bf16[8,2,192,768]{3,2,1,0:T(8,128)(2,1)}, bf16[8,2,192,768]{3,2,1,0:T(8,128)(2,1)}, u32[]{:S(2)}, u32[]{:S(2)}) collective-permute-start(bf16[8,2,192,768]{3,2,1,0:T(8,128)(2,1)} %get-tuple-element.279), channel_id=1, source_target_pairs={{0,4},{4,0},{8,12},{12,8},{16,20},{20,16},{24,28},{28,24},{1,5},{5... | collective-permute-start | bytes 14155784 | tf_op jit(solution)/shard_map/ppermute | solution.py:614
  202.5 16.1 %collective-permute-start.37 = (bf16[2,192,768]{2,1,0:T(8,128)(2,1)S(1)}, bf16[2,192,768]{2,1,0:T(8,128)(2,1)}, u32[]{:S(2)}, u32[]{:S(2)}) collective-permute-start(bf16[2,192,768]{2,1,0:T(8,128)(2,1)S(1)} %get-tuple-element.372), channel_id=1, source_target_pairs={{0,16},{4,20},{8,24},{12,28},{16,0},{20,4},{24,8},{28,12},{1,17},{... | collective-permute-start | bytes 1769480 | tf_op jit(solution)/shard_map/ppermute | solution.py:614
  202.8 15.8 %collective-permute-start.36 = (bf16[2,192,768]{2,1,0:T(8,128)(2,1)S(1)}, bf16[2,192,768]{2,1,0:T(8,128)(2,1)}, u32[]{:S(2)}, u32[]{:S(2)}) collective-permute-start(bf16[2,192,768]{2,1,0:T(8,128)(2,1)S(1)} %get-tuple-element.373), channel_id=1, source_target_pairs={{0,8},{4,12},{8,0},{12,4},{16,24},{20,28},{24,16},{28,20},{1,9},{5... | collective-permute-start | bytes 1769480 | tf_op jit(solution)/shard_map/ppermute | solution.py:614
  222.8 32.7 %collective-permute-start.40 = (bf16[2,2,192,768]{3,2,1,0:T(8,128)(2,1)}, bf16[2,2,192,768]{3,2,1,0:T(8,128)(2,1)S(1)}, u32[]{:S(2)}, u32[]{:S(2)}) collective-permute-start(bf16[2,2,192,768]{3,2,1,0:T(8,128)(2,1)} %get-tuple-element.289), channel_id=1, source_target_pairs={{0,8},{4,12},{8,0},{12,4},{16,24},{20,28},{24,16},{28,20},{1,9},{5... | collective-permute-start | bytes 3538952 | tf_op jit(solution)/shard_map/ppermute | solution.py:614
  223.5 32.1 %collective-permute-start.41 = (bf16[2,2,192,768]{3,2,1,0:T(8,128)(2,1)}, bf16[2,2,192,768]{3,2,1,0:T(8,128)(2,1)}, u32[]{:S(2)}, u32[]{:S(2)}) collective-permute-start(bf16[2,2,192,768]{3,2,1,0:T(8,128)(2,1)} %get-tuple-element.290), channel_id=1, source_target_pairs={{0,16},{4,20},{8,24},{12,28},{16,0},{20,4},{24,8},{28,12},{1,17},{... | collective-permute-start | bytes 3538952 | tf_op jit(solution)/shard_map/ppermute | solution.py:614
  227.1 23.5 %collective-permute-start.43 = (bf16[192,768]{1,0:T(8,128)(2,1)S(1)}, bf16[192,768]{1,0:T(8,128)(2,1)}, u32[]{:S(2)}, u32[]{:S(2)}) collective-permute-start(bf16[192,768]{1,0:T(8,128)(2,1)S(1)} %get-tuple-element.370), channel_id=1, source_target_pairs={{0,2},{1,3},{2,0},{3,1},{4,6},{5,7},{6,4},{7,5},{8,10},{9,11},{10,... | collective-permute-start | bytes 884744 | tf_op jit(solution)/shard_map/ppermute | solution.py:617
  231.0 24.5 %collective-permute-start.42 = (bf16[192,768]{1,0:T(8,128)(2,1)S(1)}, bf16[192,768]{1,0:T(8,128)(2,1)}, u32[]{:S(2)}, u32[]{:S(2)}) collective-permute-start(bf16[192,768]{1,0:T(8,128)(2,1)S(1)} %get-tuple-element.371), channel_id=1, source_target_pairs={{0,3},{1,0},{2,1},{3,2},{4,7},{5,4},{6,5},{7,6},{8,11},{9,8},{10,9... | collective-permute-start | bytes 884744 | tf_op jit(solution)/shard_map/ppermute | solution.py:617
  257.8 17.1 %collective-permute-start.46 = (bf16[2,192,768]{2,1,0:T(8,128)(2,1)S(1)}, bf16[2,192,768]{2,1,0:T(8,128)(2,1)S(1)}, u32[]{:S(2)}, u32[]{:S(2)}) collective-permute-start(bf16[2,192,768]{2,1,0:T(8,128)(2,1)S(1)} %get-tuple-element.367), channel_id=1, source_target_pairs={{0,16},{4,20},{8,24},{12,28},{16,0},{20,4},{24,8},{28,12},{1,17},{... | collective-permute-start | bytes 1769480 | tf_op jit(solution)/shard_map/ppermute | solution.py:614
  258.1 16.7 %collective-permute-start.45 = (bf16[2,192,768]{2,1,0:T(8,128)(2,1)S(1)}, bf16[2,192,768]{2,1,0:T(8,128)(2,1)S(1)}, u32[]{:S(2)}, u32[]{:S(2)}) collective-permute-start(bf16[2,192,768]{2,1,0:T(8,128)(2,1)S(1)} %get-tuple-element.368), channel_id=1, source_target_pairs={{0,8},{4,12},{8,0},{12,4},{16,24},{20,28},{24,16},{28,20},{1,9},{5... | collective-permute-start | bytes 1769480 | tf_op jit(solution)/shard_map/ppermute | solution.py:614
  279.9 24.4 %collective-permute-start.52 = (bf16[192,768]{1,0:T(8,128)(2,1)S(1)}, bf16[192,768]{1,0:T(8,128)(2,1)S(1)}, u32[]{:S(2)}, u32[]{:S(2)}) collective-permute-start(bf16[192,768]{1,0:T(8,128)(2,1)S(1)} %get-tuple-element.365), channel_id=1, source_target_pairs={{0,2},{1,3},{2,0},{3,1},{4,6},{5,7},{6,4},{7,5},{8,10},{9,11},{10,... | collective-permute-start | bytes 884744 | tf_op jit(solution)/shard_map/ppermute | solution.py:617
  304.3 16.9 %collective-permute-start.62 = (bf16[768,768]{1,0:T(8,128)(2,1)S(1)}, bf16[768,768]{1,0:T(8,128)(2,1)S(1)}, u32[]{:S(2)}, u32[]{:S(2)}) collective-permute-start(bf16[768,768]{1,0:T(8,128)(2,1)S(1)} %constant_dynamic-update-slice_fusion.1), channel_id=1, source_target_pairs={{0,4},{4,0},{8,12},{12,8},{16,20},{20,16},{24,28},{28,24},{1,5},{5... | collective-permute-start | bytes 3538952 | tf_op jit(solution)/shard_map/ppermute | solution.py:614
  314.1 17.6 %collective-permute-start.66 = (bf16[192,768]{1,0:T(8,128)(2,1)S(1)}, bf16[192,768]{1,0:T(8,128)(2,1)S(1)}, u32[]{:S(2)}, u32[]{:S(2)}) collective-permute-start(bf16[192,768]{1,0:T(8,128)(2,1)S(1)} %fusion.10.refs_0_), channel_id=1, source_target_pairs={{0,4},{4,0},{8,12},{12,8},{16,20},{20,16},{24,28},{28,24},{1,5},{5... | collective-permute-start | bytes 884744 | tf_op jit(solution)/shard_map/ppermute | solution.py:614
  (91 other events, 873.8 us)

commit v6 on v5

--- a/solution.py
+++ b/solution.py
@@ -474,7 +474,7 @@
     small[3:9] = ffn_sums[0:6]
 
     def collect(z, carry):
-        row = 9 + 2 * lax.rem(meta[1] + mp - z, mp)
+        row = 9 + 2 * (meta[1] ^ z)
         for i, part in enumerate((sums_local, cross_local)):
             for j in (0, 1):
                 at = (2 * i + j) * local
@@ -749,12 +749,12 @@
             lax.dynamic_slice_in_dim(memory_t, ((line + step) % mp) * mem_slots, mem_slots, 1)
             for step in range(mp)
         ]
-        head_line = [shift(head_piece, step) for step in range(1, mp)]
+        head_line = [flip(head_piece, step) for step in range(1, mp)]
         rows = head_piece.shape[0] - 16
         head_own = jnp.stack([piece[:rows] for piece in head_line])
         head_near = near_chips(head_own)
         ffn_piece = after(ffn_piece, *head_line)
-        ffn_line = [shift(ffn_piece, step) for step in range(1, mp)]
+        ffn_line = [flip(ffn_piece, step) for step in range(1, mp)]
         biases = [bias]
         for piece in head_line:
             term = piece[rows : rows + bias_rows].reshape(3, -1, width).astype(F32)
@@ -985,15 +985,8 @@
         ffn_group = Group(lambda slot, *at: ffn_rest[(slot - 4, *at)].astype(F32))
         late_two, late_four = ffn_group.second(*ffn_from)
         ffn_late = swap(late_two, 2), swap(late_four, 4)
-        memory_out.append(shift(memory_last, 3))
         small = small + flip(small, 1)
-        head_other, ffn_late, memory_out, small = meet(head_other, ffn_late, memory_out, small)
-        ffn_total, ffn_blocks = ffn_group.third(*ffn_from, *ffn_late)
-
-        def head_summed(*slots):
-            return head_mine[slots].astype(F32) + head_other[slots].astype(F32)
-
-        head_group = Group(head_summed)
+        memory_out.append(shift(after(memory_last, small), 3))
         four_slots = VMEM((4, 2, 2 * width // SUB, width), BF16)
         to_two, to_four = call(
             add_slots,
@@ -1005,8 +998,17 @@
             "add_slots",
             2,
         )(head_mine, head_other)
+        to_two, to_four, head_other, ffn_late, memory_out, small = meet(
+            to_two, to_four, head_other, ffn_late, memory_out, small
+        )
+        ffn_total, ffn_blocks = ffn_group.third(*ffn_from, *ffn_late)
+
+        def head_summed(*slots):
+            return head_mine[slots].astype(F32) + head_other[slots].astype(F32)
+
+        head_group = Group(head_summed)
         head_from = swap(to_two, 2), swap(to_four, 4)
-        ffn_sent = [shift(ffn_blocks[step - 1], -step) for step in range(1, mp)]
+        ffn_sent = [flip(ffn_blocks[step - 1], step) for step in range(1, mp)]
 
         def joined(kernel, blocks, shape, dtype, name):
             return call(
@@ -1040,7 +1042,8 @@
             head_late, ffn_low, small, hidden_blocks
         )
         head_total, head_blocks = head_group.third(*head_from, *head_late)
-        head_sent = [shift(head_blocks[step - 1], -step) for step in range(1, mp)]
+        ffn_low, head_blocks = meet(ffn_low, head_blocks)
+        head_sent = [flip(head_blocks[step - 1], step) for step in range(1, mp)]
         ffn_near = near_chips(ffn_low)
         small, *ffn_near = meet(small, *ffn_near)
         small = small + swap(small, 2)
@@ -1056,7 +1059,6 @@
         head_near = near_chips(head_low)
         hidden_blocks[2] = shift(hidden_blocks[0], 2)
         ffn_joined = swap(ffn_joined, 1)
-        head_near, ffn_joined, hidden_blocks = meet(head_near, ffn_joined, hidden_blocks)
         grad_in, grad_out = call(
             finish_ffn,
             [META] + in_vmem(6),
@@ -1066,12 +1068,13 @@
             plain,
             "finish_ffn",
         )(meta, *ffn_reduced, ffn_joined)
+        head_near, grad_in, grad_out, hidden_blocks = meet(
+            head_near, grad_in, grad_out, hidden_blocks
+        )
         hidden_grad = joined(join_rows, hidden_blocks, rows_shape, F32, "join_hidden")
         head_far = far_chips(*head_near)
         head_beside = [swap(piece, 1) for piece in (head_low, *head_near)]
-        head_far, head_beside, grad_in, grad_out, hidden_grad = meet(
-            head_far, head_beside, grad_in, grad_out, hidden_grad
-        )
+        head_far, head_beside, hidden_grad = meet(head_far, head_beside, hidden_grad)
         head_beside += [swap(piece, 1) for piece in head_far]
         finished = call(
             finish_heads,

time: 341 us -> 335 us (0.982)
  waiting for transfers between devices: 126 us -> 116 us
    ppermute x24 -> x12, waiting for transfers between devices: 99.4 us -> 36.2 us  [shift(): return lax.ppermute(value, 'mp', [(i, (i + step) % mp) for i in range(mp)])]
    ppermute x2 -> x14, waiting for transfers between devices: 12.9 us -> 65.9 us  [flip(): return lax.ppermute(value, 'mp', [(i, i ^ bit) for i in range(mp)])]
    ppermute x2 -> x14, starting transfers between devices: 0.74 us -> 20.9 us  [flip(): return lax.ppermute(value, 'mp', [(i, i ^ bit) for i in range(mp)])]
    ppermute x24 -> x12, starting transfers between devices: 34.8 us -> 17 us  [shift(): return lax.ppermute(value, 'mp', [(i, (i + step) % mp) for i in range(mp)])]
  transfers between devices with their start and end apart: 71 -> 71, of which waited for: 27 -> 28; matrix products, arithmetic and copies ran while one was open for 7% -> 7% of each run, Pallas kernels for 21% -> 22%
where the time goes in v6:
time: 335 us; the launch traced here: 331 us
  waiting for transfers between devices  116 us (35%)
  Pallas kernels  93.8 us (28%)
  starting transfers between devices  81.8 us (24%)
  local copies, waits for them, and re-layouts  18.7 us (6%)
  other arithmetic  18.4 us (5%)
    ppermute x14, waiting for transfers between devices, flip(): return lax.ppermute(value, 'mp', [(i, i ^ bit) for i in range(mp)])  65.9 us
    ppermute x45, starting transfers between devices, swap(): return lax.ppermute(value, 'dp', [(i, i ^ bit) for i in range(dp)])  43.9 us
    ppermute x12, waiting for transfers between devices, shift(): return lax.ppermute(value, 'mp', [(i, (i + step) % mp) for i in range(mp)])  36.2 us
    ppermute x14, starting transfers between devices, flip(): return lax.ppermute(value, 'mp', [(i, i ^ bit) for i in range(mp)])  20.9 us
    pallas_call x1, Pallas kernels, body(): call(bound(head_back), [META] + in_vmem(11) + in_place(mp + 13), (row_sha...  19.4 us
    pallas_call x1, Pallas kernels, body(): call(bound(cross_back), [META] + in_vmem(5) + in_place(14), (low_shape, r...  17.2 us
    ppermute x12, starting transfers between devices, shift(): return lax.ppermute(value, 'mp', [(i, (i + step) % mp) for i in range(mp)])  17 us
    ppermute x45, waiting for transfers between devices, swap(): return lax.ppermute(value, 'dp', [(i, i ^ bit) for i in range(dp)])  14.4 us
  transfers between devices with their start and end apart: 71, of which 28 were waited for; matrix products, arithmetic and copies ran while one was open for 7% of the time, Pallas kernels for 22%

profile of v6, /device:TPU:9, one launch (start us, length us, event | category | flops | bytes accessed | tf_op | source)
XLA Modules:
  0.0 330.8 jit_solution(5408169208218664758)
XLA Ops:
  16.6 10.3 %collective-permute-done.2 = bf16[208,768]{1,0:T(8,128)(2,1)S(1)} collective-permute-done((bf16[208,768]{1,0:T(8,128)(2,1)S(1)}, bf16[208,768]{1,0:T(8,128)(2,1)S(1)}, u32[]{:S(2)}, u32[]{:S(2)}) %collective-permute-start.2) | collective-permute-done | bytes 319520 | tf_op jit(solution)/shard_map/ppermute | solution.py:620
  26.9 5.7 %collective-permute-done.1 = bf16[208,768]{1,0:T(8,128)(2,1)S(1)} collective-permute-done((bf16[208,768]{1,0:T(8,128)(2,1)S(1)}, bf16[208,768]{1,0:T(8,128)(2,1)S(1)}, u32[]{:S(2)}, u32[]{:S(2)}) %collective-permute-start.1) | collective-permute-done | bytes 319520 | tf_op jit(solution)/shard_map/ppermute | solution.py:620
  33.1 4.0 %collective-permute-start.6 = (bf16[192,768]{1,0:T(8,128)(2,1)}, bf16[192,768]{1,0:T(8,128)(2,1)}, u32[]{:S(2)}, u32[]{:S(2)}) collective-permute-start(bf16[192,768]{1,0:T(8,128)(2,1)} %pad_maximum_fusion.2), channel_id=1, source_target_pairs={{0,2},{1,3},{2,0},{3,1},{4,6},{5,7},{6,4},{7,5},{8,10},{9,11},{10,... | collective-permute-start | bytes 884744 | tf_op jit(solution)/shard_map/ppermute | solution.py:620
  42.6 9.4 %collective-permute-done.7 = bf16[192,768]{1,0:T(8,128)(2,1)} collective-permute-done((bf16[192,768]{1,0:T(8,128)(2,1)}, bf16[192,768]{1,0:T(8,128)(2,1)}, u32[]{:S(2)}, u32[]{:S(2)}) %collective-permute-start.7) | collective-permute-done | bytes 294944 | tf_op jit(solution)/shard_map/ppermute | solution.py:620
  52.0 5.4 %collective-permute-done.6 = bf16[192,768]{1,0:T(8,128)(2,1)} collective-permute-done((bf16[192,768]{1,0:T(8,128)(2,1)}, bf16[192,768]{1,0:T(8,128)(2,1)}, u32[]{:S(2)}, u32[]{:S(2)}) %collective-permute-start.6) | collective-permute-done | bytes 294944 | tf_op jit(solution)/shard_map/ppermute | solution.py:620
  57.5 3.1 collective-permute-start.10
  65.6 8.5 %collective-permute-done.12.refs_7_.refs_14_ = bf16[192,1024]{1,0:T(8,128)(2,1)S(1)} collective-permute-done((bf16[192,1024]{1,0:T(8,128)(2,1)}, bf16[192,1024]{1,0:T(8,128)(2,1)S(1)}, u32[]{:S(2)}, u32[]{:S(2)}) %collective-permute-start.12) | collective-permute-done | bytes 393248 | tf_op jit(solution)/shard_map/ppermute | solution.py:617
  82.5 8.4 %self_forward.1 = (bf16[4,128,576]{2,1,0:T(8,128)(2,1)}, bf16[4,128,192]{2,1,0:T(8,128)(2,1)}, f32[128,768]{1,0:T(8,128)}, f32[128,768]{1,0:T(8,128)}) custom-call(s32[12]{0:T(128)} %concatenate.27.refs_0_.meta, bf16[128,768]{1,0:T(8,128)(2,1)} %get-tuple-element.214.refs_1_.refs_2_, f32[4,2,192]{2,1,0:T(2,128)} %reshape.174.refs_2_, f32[3,768]{1,0:T(4,128)} %refs_5_.4, ...), custom_call_target="tpu_custom_call" | custom-call | flops 188743680 | bytes 2359296 | tf_op jit(solution)/shard_map/self_forward/pallas_call | solution.py:804
  90.9 8.0 %collective-permute-done.15.refs_8_.refs_15_ = bf16[192,1024]{1,0:T(8,128)(2,1)} collective-permute-done((bf16[192,1024]{1,0:T(8,128)(2,1)}, bf16[192,1024]{1,0:T(8,128)(2,1)}, u32[]{:S(2)}, u32[]{:S(2)}) %collective-permute-start.15) | collective-permute-done | bytes 393248 | tf_op jit(solution)/shard_map/ppermute | solution.py:617
  100.8 3.3 collective-permute-start.22
  107.5 5.4 %collective-permute-done.22.refs_9_.refs_16_ = bf16[192,1024]{1,0:T(8,128)(2,1)S(1)} collective-permute-done((bf16[192,1024]{1,0:T(8,128)(2,1)}, bf16[192,1024]{1,0:T(8,128)(2,1)S(1)}, u32[]{:S(2)}, u32[]{:S(2)}) %collective-permute-start.22) | collective-permute-done | bytes 393248 | tf_op jit(solution)/shard_map/ppermute | solution.py:617
  113.7 3.1 collective-permute-done.19.refs_11_
  118.2 13.3 %cross_forward.1 = (bf16[4,128,192]{2,1,0:T(8,128)(2,1)}, bf16[4,128,192]{2,1,0:T(8,128)(2,1)}, f32[4,384,1]{2,1,0:T(8,128)}, f32[128,768]{1,0:T(8,128)}, f32[12...) custom-call(s32[12]{0:T(128)} %concatenate.27.refs_0_.meta, f32[4,2,192]{2,1,0:T(2,128)} %reshape.175.refs_1_, ...), custom_call_target="tpu_custom_call" | custom-call | flops 377487360 | bytes 2359296 | tf_op jit(solution)/shard_map/cross_forward/pallas_call | solution.py:823
  132.6 10.4 %ffn_both.1 = (bf16[128,768]{1,0:T(8,128)(2,1)}, f32[128,768]{1,0:T(8,128)}, f32[16,768]{1,0:T(8,128)}, bf16[5,128,1152]{2,1,0:T(8,128)(2,1)}, bf16[5,128,384]{2,1,0:T(8,128)(2,1)}) custom-call(s32[12]{0:T(128)} %concatenate.27.refs_0_.meta, f32[128,768]{1,0:T(8,128)} %get-tuple-element.242.refs_1_, f32[128,768]{1,0:T(8,128)} %get-tuple-element.243.refs_2_, ...), custom_call_target="tpu_custom_call" | custom-call | flops 377487360 | bytes 2949120 | tf_op jit(solution)/shard_map/ffn_both/pallas_call | solution.py:858
  145.7 17.2 %cross_back.1 = (bf16[4,128,192]{2,1,0:T(8,128)(2,1)}, f32[128,768]{1,0:T(8,128)}, f32[8,768]{1,0:T(8,128)}, f32[4,2,192]{2,1,0:T(2,128)}, bf16[4,384,1024]{2,1,...) custom-call(s32[12]{0:T(128)} %concatenate.27.refs_0_.meta, ...), custom_call_target="tpu_custom_call" | custom-call | flops 471859200 | bytes 3538944 | tf_op jit(solution)/shard_map/cross_back/pallas_call | solution.py:883
  164.1 5.1 %ffn_weights.1 = (bf16[2,2,192,768]{3,2,1,0:T(8,128)(2,1)}, bf16[2,2,192,768]{3,2,1,0:T(8,128)(2,1)}, bf16[4,2,192,768]{3,2,1,0:T(8,128)(2,1)}) custom-call(s32[12]{0:T(128)} %concatenate.27.refs_0_.meta, bf16[5,128,1152]{2,1,0:T(8,128)(2,1)} %get-tuple-element.249.refs_1_, bf16[5,128,384]{2,1,0:T(8,128)(2,1)} %get-tuple-element.250.refs_2_, ...), custom_call_target="tpu_custom_call" | custom-call | flops 150994944 | bytes 2359296 | tf_op jit(solution)/shard_map/ffn_weights/pallas_call | solution.py:927
  174.7 19.4 %head_back.1 = (f32[128,768]{1,0:T(8,128)}, f32[24,768]{1,0:T(8,128)}, bf16[8,2,192,768]{3,2,1,0:T(8,128)(2,1)}, bf16[8,2,192,768]{3,2,1,0:T(8,128)(2,1)}) custom-call(s32[12]{0:T(128)} %concatenate.27.refs_0_.meta, f32[128,768]{1,0:T(8,128)} %get-tuple-element.271.refs_1_, bf16[128,768]{1,0:T(8,128)(2,1)} %get-tuple-element.214.refs_1_.refs_2_, ...), custom_call_target="tpu_custom_call" | custom-call | flops 566231040 | bytes 7077888 | tf_op jit(solution)/shard_map/head_back/pallas_call | solution.py:943
  202.6 3.3 %collective-permute-start.38 = (f32[24,768]{1,0:T(8,128)S(1)}, f32[24,768]{1,0:T(8,128)S(1)}, u32[]{:S(2)}, u32[]{:S(2)}) collective-permute-start(f32[24,768]{1,0:T(8,128)S(1)} %copy-done.47), channel_id=1, source_target_pairs={{0,1},{1,0},{2,3},{3,2},{4,5},{5,4},{6,7},{7,6},{8,9},{9,8},{10,11... | collective-permute-start | bytes 221192 | tf_op jit(solution)/shard_map/ppermute | solution.py:620
  210.2 3.5 %add_slots.1 = (bf16[2,2,192,768]{3,2,1,0:T(8,128)(2,1)}, bf16[2,2,192,768]{3,2,1,0:T(8,128)(2,1)}) custom-call(bf16[8,2,192,768]{3,2,1,0:T(8,128)(2,1)} %get-tuple-element.284.mine, bf16[8,2,192,768]{3,2,1,0:T(8,128)(2,1)} %collective-permute-done.35.other), custom_call_target="tpu_custom_call" | custom-call | bytes 1179648 | tf_op jit(solution)/shard_map/add_slots/pallas_call | solution.py:991
  213.7 4.6 %collective-permute-done.39.refs_3_ = bf16[192,1024]{1,0:T(8,128)(2,1)} collective-permute-done((bf16[192,1024]{1,0:T(8,128)(2,1)}, bf16[192,1024]{1,0:T(8,128)(2,1)}, u32[]{:S(2)}, u32[]{:S(2)}) %collective-permute-start.39) | collective-permute-done | bytes 393248 | tf_op jit(solution)/shard_map/ppermute | solution.py:617
  223.2 3.3 collective-permute-start.43
  228.6 3.2 join_memory.1
  231.8 10.1 %collective-permute-done.44 = bf16[192,768]{1,0:T(8,128)(2,1)} collective-permute-done((bf16[192,768]{1,0:T(8,128)(2,1)}, bf16[192,768]{1,0:T(8,128)(2,1)}, u32[]{:S(2)}, u32[]{:S(2)}) %collective-permute-start.44) | collective-permute-done | bytes 294944 | tf_op jit(solution)/shard_map/ppermute | solution.py:620
  242.0 4.3 %collective-permute-done.43 = bf16[192,768]{1,0:T(8,128)(2,1)} collective-permute-done((bf16[192,768]{1,0:T(8,128)(2,1)S(1)}, bf16[192,768]{1,0:T(8,128)(2,1)}, u32[]{:S(2)}, u32[]{:S(2)}) %collective-permute-start.43) | collective-permute-done | bytes 294944 | tf_op jit(solution)/shard_map/ppermute | solution.py:620
  251.2 5.4 %collective-permute-done.47.refs_1_ = bf16[128,768]{1,0:T(8,128)(2,1)S(1)} collective-permute-done((bf16[128,768]{1,0:T(8,128)(2,1)S(1)}, bf16[128,768]{1,0:T(8,128)(2,1)S(1)}, u32[]{:S(2)}, u32[]{:S(2)}) %collective-permute-start.47) | collective-permute-done | bytes 196640 | tf_op jit(solution)/shard_map/ppermute | solution.py:617
  261.5 5.1 %collective-permute-start.49 = (f32[24,768]{1,0:T(8,128)S(1)}, f32[24,768]{1,0:T(8,128)S(1)}, u32[]{:S(2)}, u32[]{:S(2)}) collective-permute-start(f32[24,768]{1,0:T(8,128)S(1)} %add.279), channel_id=1, source_target_pairs={{0,4},{4,0},{8,12},{12,8},{16,20},{20,16},{24,28},{28,24},{1,5},{5... | collective-permute-start | bytes 221192 | tf_op jit(solution)/shard_map/ppermute | solution.py:614
  272.8 3.8 %collective-permute-start.51 = (bf16[192,768]{1,0:T(8,128)(2,1)S(1)}, bf16[192,768]{1,0:T(8,128)(2,1)S(1)}, u32[]{:S(2)}, u32[]{:S(2)}) collective-permute-start(bf16[192,768]{1,0:T(8,128)(2,1)S(1)} %get-tuple-element.323), channel_id=1, source_target_pairs={{0,1},{1,0},{2,3},{3,2},{4,5},{5,4},{6,7},{7,6},{8,9},{9,8},{10,11... | collective-permute-start | bytes 884744 | tf_op jit(solution)/shard_map/ppermute | solution.py:620
  277.9 9.3 %collective-permute-done.51 = bf16[192,768]{1,0:T(8,128)(2,1)S(1)} collective-permute-done((bf16[192,768]{1,0:T(8,128)(2,1)S(1)}, bf16[192,768]{1,0:T(8,128)(2,1)S(1)}, u32[]{:S(2)}, u32[]{:S(2)}) %collective-permute-start.51) | collective-permute-done | bytes 294944 | tf_op jit(solution)/shard_map/ppermute | solution.py:620
  291.0 3.2 collective-permute-done.59
  295.0 7.6 %collective-permute-done.53 = bf16[192,768]{1,0:T(8,128)(2,1)S(1)} collective-permute-done((bf16[192,768]{1,0:T(8,128)(2,1)S(1)}, bf16[192,768]{1,0:T(8,128)(2,1)S(1)}, u32[]{:S(2)}, u32[]{:S(2)}) %collective-permute-start.53) | collective-permute-done | bytes 294944 | tf_op jit(solution)/shard_map/ppermute | solution.py:620
  308.3 4.3 %finish_ffn.1 = (f32[768,768]{1,0:T(8,128)}, f32[768,768]{1,0:T(8,128)}) custom-call(s32[12]{0:T(128)} %concatenate.27.refs_0_.meta, bf16[192,768]{1,0:T(8,128)(2,1)} %copy-done.10, bf16[192,768]{1,0:T(8,128)(2,1)} %copy-done.14, bf16[192,768]{1,0:T(8,128)(2,1)} %copy-done.13, bf16[96,768]{1,0:T(8,128)(2,1)} %copy-done.27, bf16[96,768]{1,0:T(8,128)(2,1)} %copy-done.28, ...), custom_call_target="tpu_custom_call" | custom-call | bytes 294912 | tf_op jit(solution)/shard_map/finish_ffn/pallas_call | solution.py:1062
  326.2 4.4 %finish_heads.1 = (f32[576,768]{1,0:T(8,128)}, f32[192,768]{1,0:T(8,128)}, f32[192,768]{1,0:T(8,128)}, f32[192,768]{1,0:T(8,128)}, f32[384,768]{1,0:T(8,128)}, /...) custom-call(s32[12]{0:T(128)} %concatenate.27.refs_0_.meta, ...), custom_call_target="tpu_custom_call" | custom-call | bytes 294912 | tf_op jit(solution)/shard_map/finish_heads/pallas_call | solution.py:1079
  (286 shorter events, 113.8 us)
Async XLA Ops:
  4.6 22.3 %collective-permute-start.2 = (bf16[208,768]{1,0:T(8,128)(2,1)S(1)}, bf16[208,768]{1,0:T(8,128)(2,1)S(1)}, u32[]{:S(2)}, u32[]{:S(2)}) collective-permute-start(bf16[208,768]{1,0:T(8,128)(2,1)S(1)} %concatenate.25), channel_id=1, source_target_pairs={{0,3},{1,2},{2,1},{3,0},{4,7},{5,6},{6,5},{7,4},{8,11},{9,10},{10,... | collective-permute-start | bytes 958472 | tf_op jit(solution)/shard_map/ppermute | solution.py:620
  6.0 26.7 %collective-permute-start.1 = (bf16[208,768]{1,0:T(8,128)(2,1)S(1)}, bf16[208,768]{1,0:T(8,128)(2,1)S(1)}, u32[]{:S(2)}, u32[]{:S(2)}) collective-permute-start(bf16[208,768]{1,0:T(8,128)(2,1)S(1)} %concatenate.25), channel_id=1, source_target_pairs={{0,2},{1,3},{2,0},{3,1},{4,6},{5,7},{6,4},{7,5},{8,10},{9,11},{10,... | collective-permute-start | bytes 958472 | tf_op jit(solution)/shard_map/ppermute | solution.py:620
  7.0 25.6 %collective-permute-start = (bf16[208,768]{1,0:T(8,128)(2,1)S(1)}, bf16[208,768]{1,0:T(8,128)(2,1)S(1)}, u32[]{:S(2)}, u32[]{:S(2)}) collective-permute-start(bf16[208,768]{1,0:T(8,128)(2,1)S(1)} %concatenate.25), channel_id=1, source_target_pairs={{0,1},{1,0},{2,3},{3,2},{4,5},{5,4},{6,7},{7,6},{8,9},{9,8},{10,11... | collective-permute-start | bytes 958472 | tf_op jit(solution)/shard_map/ppermute | solution.py:620
  32.7 19.3 %collective-permute-start.7 = (bf16[192,768]{1,0:T(8,128)(2,1)}, bf16[192,768]{1,0:T(8,128)(2,1)}, u32[]{:S(2)}, u32[]{:S(2)}) collective-permute-start(bf16[192,768]{1,0:T(8,128)(2,1)} %pad_maximum_fusion.2), channel_id=1, source_target_pairs={{0,3},{1,2},{2,1},{3,0},{4,7},{5,6},{6,5},{7,4},{8,11},{9,10},{10,... | collective-permute-start | bytes 884744 | tf_op jit(solution)/shard_map/ppermute | solution.py:620
  33.1 24.4 %collective-permute-start.6 = (bf16[192,768]{1,0:T(8,128)(2,1)}, bf16[192,768]{1,0:T(8,128)(2,1)}, u32[]{:S(2)}, u32[]{:S(2)}) collective-permute-start(bf16[192,768]{1,0:T(8,128)(2,1)} %pad_maximum_fusion.2), channel_id=1, source_target_pairs={{0,2},{1,3},{2,0},{3,1},{4,6},{5,7},{6,4},{7,5},{8,10},{9,11},{10,... | collective-permute-start | bytes 884744 | tf_op jit(solution)/shard_map/ppermute | solution.py:620
  37.1 20.4 %collective-permute-start.5 = (bf16[192,768]{1,0:T(8,128)(2,1)}, bf16[192,768]{1,0:T(8,128)(2,1)}, u32[]{:S(2)}, u32[]{:S(2)}) collective-permute-start(bf16[192,768]{1,0:T(8,128)(2,1)} %pad_maximum_fusion.2), channel_id=1, source_target_pairs={{0,1},{1,0},{2,3},{3,2},{4,5},{5,4},{6,7},{7,6},{8,9},{9,8},{10,11... | collective-permute-start | bytes 884744 | tf_op jit(solution)/shard_map/ppermute | solution.py:620
  37.3 20.2 %collective-permute-start.4 = (bf16[3,192,768]{2,1,0:T(8,128)(2,1)S(1)}, bf16[3,192,768]{2,1,0:T(8,128)(2,1)S(1)}, u32[]{:S(2)}, u32[]{:S(2)}) collective-permute-start(bf16[3,192,768]{2,1,0:T(8,128)(2,1)S(1)} %pad_maximum_fusion.refs_6_.refs_10_.refs_7_.refs_17_), channel_id=1, source_target_pairs={{0,16},{4,20},{8,24},{12,28},{16,0},{20,4},{24,8},{28,12},{1,17},{... | collective-permute-start | bytes 2654216 | tf_op jit(solution)/shard_map/ppermute | solution.py:614
  38.6 18.9 %collective-permute-start.3 = (bf16[3,192,768]{2,1,0:T(8,128)(2,1)S(1)}, bf16[3,192,768]{2,1,0:T(8,128)(2,1)S(1)}, u32[]{:S(2)}, u32[]{:S(2)}) collective-permute-start(bf16[3,192,768]{2,1,0:T(8,128)(2,1)S(1)} %pad_maximum_fusion.refs_6_.refs_10_.refs_7_.refs_17_), channel_id=1, source_target_pairs={{0,8},{4,12},{8,0},{12,4},{16,24},{20,28},{24,16},{28,20},{1,9},{5... | collective-permute-start | bytes 2654216 | tf_op jit(solution)/shard_map/ppermute | solution.py:614
  78.2 21.4 %collective-permute-start.14 = (bf16[3,192,768]{2,1,0:T(8,128)(2,1)}, bf16[3,192,768]{2,1,0:T(8,128)(2,1)S(1)}, u32[]{:S(2)}, u32[]{:S(2)}) collective-permute-start(bf16[3,192,768]{2,1,0:T(8,128)(2,1)} %pad_maximum_fusion.1.refs_8_), channel_id=1, source_target_pairs={{0,16},{4,20},{8,24},{12,28},{16,0},{20,4},{24,8},{28,12},{1,17},{... | collective-permute-start | bytes 2654216 | tf_op jit(solution)/shard_map/ppermute | solution.py:614
  78.4 21.2 %collective-permute-start.13 = (bf16[3,192,768]{2,1,0:T(8,128)(2,1)}, bf16[3,192,768]{2,1,0:T(8,128)(2,1)}, u32[]{:S(2)}, u32[]{:S(2)}) collective-permute-start(bf16[3,192,768]{2,1,0:T(8,128)(2,1)} %pad_maximum_fusion.1.refs_8_), channel_id=1, source_target_pairs={{0,8},{4,12},{8,0},{12,4},{16,24},{20,28},{24,16},{28,20},{1,9},{5... | collective-permute-start | bytes 2654216 | tf_op jit(solution)/shard_map/ppermute | solution.py:614
  80.0 18.9 %collective-permute-start.15 = (bf16[192,1024]{1,0:T(8,128)(2,1)}, bf16[192,1024]{1,0:T(8,128)(2,1)}, u32[]{:S(2)}, u32[]{:S(2)}) collective-permute-start(bf16[192,1024]{1,0:T(8,128)(2,1)} %get-tuple-element.212), channel_id=1, source_target_pairs={{0,2},{1,3},{2,0},{3,1},{4,6},{5,7},{6,4},{7,5},{8,10},{9,11},{10,... | collective-permute-start | bytes 1179656 | tf_op jit(solution)/shard_map/ppermute | solution.py:617
  99.6 17.2 %collective-permute-start.21 = (bf16[3,192,768]{2,1,0:T(8,128)(2,1)}, bf16[3,192,768]{2,1,0:T(8,128)(2,1)S(1)}, u32[]{:S(2)}, u32[]{:S(2)}) collective-permute-start(bf16[3,192,768]{2,1,0:T(8,128)(2,1)} %pad_maximum_fusion.1.refs_8_), channel_id=1, source_target_pairs={{0,4},{4,0},{8,12},{12,8},{16,20},{20,16},{24,28},{28,24},{1,5},{5... | collective-permute-start | bytes 2654216 | tf_op jit(solution)/shard_map/ppermute | solution.py:614
  106.7 24.9 %collective-permute-start.24 = (bf16[3,192,768]{2,1,0:T(8,128)(2,1)S(1)}, bf16[3,192,768]{2,1,0:T(8,128)(2,1)S(1)}, u32[]{:S(2)}, u32[]{:S(2)}) collective-permute-start(bf16[3,192,768]{2,1,0:T(8,128)(2,1)S(1)} %collective-permute-done.14.refs_10_), channel_id=1, source_target_pairs={{0,4},{4,0},{8,12},{12,8},{16,20},{20,16},{24,28},{28,24},{1,5},{5... | collective-permute-start | bytes 2654216 | tf_op jit(solution)/shard_map/ppermute | solution.py:614
  112.9 18.7 %collective-permute-start.23 = (bf16[3,192,768]{2,1,0:T(8,128)(2,1)}, bf16[3,192,768]{2,1,0:T(8,128)(2,1)}, u32[]{:S(2)}, u32[]{:S(2)}) collective-permute-start(bf16[3,192,768]{2,1,0:T(8,128)(2,1)} %collective-permute-done.13.refs_9_), channel_id=1, source_target_pairs={{0,4},{4,0},{8,12},{12,8},{16,20},{20,16},{24,28},{28,24},{1,5},{5... | collective-permute-start | bytes 2654216 | tf_op jit(solution)/shard_map/ppermute | solution.py:614
  143.0 19.9 %collective-permute-start.30 = (bf16[5,128,1152]{2,1,0:T(8,128)(2,1)}, bf16[5,128,1152]{2,1,0:T(8,128)(2,1)S(1)}, u32[]{:S(2)}, u32[]{:S(2)}) collective-permute-start(bf16[5,128,1152]{2,1,0:T(8,128)(2,1)} %get-tuple-element.249.refs_1_), channel_id=1, source_target_pairs={{0,4},{4,0},{8,12},{12,8},{16,20},{20,16},{24,28},{28,24},{1,5},{5... | collective-permute-start | bytes 4423688 | tf_op jit(solution)/shard_map/ppermute | solution.py:614
  143.5 19.4 %collective-permute-start.29 = (bf16[128,768]{1,0:T(8,128)(2,1)}, bf16[128,768]{1,0:T(8,128)(2,1)S(1)}, u32[]{:S(2)}, u32[]{:S(2)}) collective-permute-start(bf16[128,768]{1,0:T(8,128)(2,1)} %get-tuple-element.305.refs_0_), channel_id=1, source_target_pairs={{0,3},{1,0},{2,1},{3,2},{4,7},{5,4},{6,5},{7,6},{8,11},{9,8},{10,9... | collective-permute-start | bytes 589832 | tf_op jit(solution)/shard_map/ppermute | solution.py:617
  144.5 18.4 %collective-permute-start.28 = (bf16[128,768]{1,0:T(8,128)(2,1)}, bf16[128,768]{1,0:T(8,128)(2,1)S(1)}, u32[]{:S(2)}, u32[]{:S(2)}) collective-permute-start(bf16[128,768]{1,0:T(8,128)(2,1)} %get-tuple-element.305.refs_0_), channel_id=1, source_target_pairs={{0,2},{1,3},{2,0},{3,1},{4,6},{5,7},{6,4},{7,5},{8,10},{9,11},{10,... | collective-permute-start | bytes 589832 | tf_op jit(solution)/shard_map/ppermute | solution.py:617
  144.5 18.4 %collective-permute-start.27 = (bf16[128,768]{1,0:T(8,128)(2,1)}, bf16[128,768]{1,0:T(8,128)(2,1)S(1)}, u32[]{:S(2)}, u32[]{:S(2)}) collective-permute-start(bf16[128,768]{1,0:T(8,128)(2,1)} %get-tuple-element.305.refs_0_), channel_id=1, source_target_pairs={{0,1},{1,2},{2,3},{3,0},{4,5},{5,6},{6,7},{7,4},{8,9},{9,10},{10,1... | collective-permute-start | bytes 589832 | tf_op jit(solution)/shard_map/ppermute | solution.py:617
  169.3 26.9 %collective-permute-start.32 = (bf16[2,2,192,768]{3,2,1,0:T(8,128)(2,1)}, bf16[2,2,192,768]{3,2,1,0:T(8,128)(2,1)}, u32[]{:S(2)}, u32[]{:S(2)}) collective-permute-start(bf16[2,2,192,768]{3,2,1,0:T(8,128)(2,1)} %get-tuple-element.265), channel_id=1, source_target_pairs={{0,16},{4,20},{8,24},{12,28},{16,0},{20,4},{24,8},{28,12},{1,17},{... | collective-permute-start | bytes 3538952 | tf_op jit(solution)/shard_map/ppermute | solution.py:614
  170.0 26.4 %collective-permute-start.31 = (bf16[2,2,192,768]{3,2,1,0:T(8,128)(2,1)}, bf16[2,2,192,768]{3,2,1,0:T(8,128)(2,1)S(1)}, u32[]{:S(2)}, u32[]{:S(2)}) collective-permute-start(bf16[2,2,192,768]{3,2,1,0:T(8,128)(2,1)} %get-tuple-element.264), channel_id=1, source_target_pairs={{0,8},{4,12},{8,0},{12,4},{16,24},{20,28},{24,16},{28,20},{1,9},{5... | collective-permute-start | bytes 3538952 | tf_op jit(solution)/shard_map/ppermute | solution.py:614
  171.0 23.1 %collective-permute-start.33 = (bf16[192,1024]{1,0:T(8,128)(2,1)}, bf16[192,1024]{1,0:T(8,128)(2,1)}, u32[]{:S(2)}, u32[]{:S(2)}) collective-permute-start(bf16[192,1024]{1,0:T(8,128)(2,1)} %get-tuple-element.267), channel_id=1, source_target_pairs={{0,1},{1,2},{2,3},{3,0},{4,5},{5,6},{6,7},{7,4},{8,9},{9,10},{10,1... | collective-permute-start | bytes 1179656 | tf_op jit(solution)/shard_map/ppermute | solution.py:617
  172.2 23.9 %collective-permute-start.34 = (bf16[192,1024]{1,0:T(8,128)(2,1)}, bf16[192,1024]{1,0:T(8,128)(2,1)}, u32[]{:S(2)}, u32[]{:S(2)}) collective-permute-start(bf16[192,1024]{1,0:T(8,128)(2,1)} %get-tuple-element.268), channel_id=1, source_target_pairs={{0,2},{1,3},{2,0},{3,1},{4,6},{5,7},{6,4},{7,5},{8,10},{9,11},{10,... | collective-permute-start | bytes 1179656 | tf_op jit(solution)/shard_map/ppermute | solution.py:617
  201.2 17.1 %collective-permute-start.37 = (bf16[2,192,768]{2,1,0:T(8,128)(2,1)}, bf16[2,192,768]{2,1,0:T(8,128)(2,1)}, u32[]{:S(2)}, u32[]{:S(2)}) collective-permute-start(bf16[2,192,768]{2,1,0:T(8,128)(2,1)} %get-tuple-element.384), channel_id=1, source_target_pairs={{0,16},{4,20},{8,24},{12,28},{16,0},{20,4},{24,8},{28,12},{1,17},{... | collective-permute-start | bytes 1769480 | tf_op jit(solution)/shard_map/ppermute | solution.py:614
  218.3 28.0 %collective-permute-start.40 = (bf16[2,2,192,768]{3,2,1,0:T(8,128)(2,1)}, bf16[2,2,192,768]{3,2,1,0:T(8,128)(2,1)S(1)}, u32[]{:S(2)}, u32[]{:S(2)}) collective-permute-start(bf16[2,2,192,768]{3,2,1,0:T(8,128)(2,1)} %get-tuple-element.297), channel_id=1, source_target_pairs={{0,8},{4,12},{8,0},{12,4},{16,24},{20,28},{24,16},{28,20},{1,9},{5... | collective-permute-start | bytes 3538952 | tf_op jit(solution)/shard_map/ppermute | solution.py:614
  219.5 26.8 %collective-permute-start.41 = (bf16[2,2,192,768]{3,2,1,0:T(8,128)(2,1)}, bf16[2,2,192,768]{3,2,1,0:T(8,128)(2,1)}, u32[]{:S(2)}, u32[]{:S(2)}) collective-permute-start(bf16[2,2,192,768]{3,2,1,0:T(8,128)(2,1)} %get-tuple-element.298), channel_id=1, source_target_pairs={{0,16},{4,20},{8,24},{12,28},{16,0},{20,4},{24,8},{28,12},{1,17},{... | collective-permute-start | bytes 3538952 | tf_op jit(solution)/shard_map/ppermute | solution.py:614
  223.2 18.8 %collective-permute-start.44 = (bf16[192,768]{1,0:T(8,128)(2,1)}, bf16[192,768]{1,0:T(8,128)(2,1)}, u32[]{:S(2)}, u32[]{:S(2)}) collective-permute-start(bf16[192,768]{1,0:T(8,128)(2,1)} %get-tuple-element.381), channel_id=1, source_target_pairs={{0,3},{1,2},{2,1},{3,0},{4,7},{5,6},{6,5},{7,4},{8,11},{9,10},{10,... | collective-permute-start | bytes 884744 | tf_op jit(solution)/shard_map/ppermute | solution.py:620
  223.2 23.1 %collective-permute-start.43 = (bf16[192,768]{1,0:T(8,128)(2,1)S(1)}, bf16[192,768]{1,0:T(8,128)(2,1)}, u32[]{:S(2)}, u32[]{:S(2)}) collective-permute-start(bf16[192,768]{1,0:T(8,128)(2,1)S(1)} %get-tuple-element.382), channel_id=1, source_target_pairs={{0,2},{1,3},{2,0},{3,1},{4,6},{5,7},{6,4},{7,5},{8,10},{9,11},{10,... | collective-permute-start | bytes 884744 | tf_op jit(solution)/shard_map/ppermute | solution.py:620
  226.4 19.9 %collective-permute-start.42 = (bf16[192,768]{1,0:T(8,128)(2,1)S(1)}, bf16[192,768]{1,0:T(8,128)(2,1)}, u32[]{:S(2)}, u32[]{:S(2)}) collective-permute-start(bf16[192,768]{1,0:T(8,128)(2,1)S(1)} %get-tuple-element.383), channel_id=1, source_target_pairs={{0,1},{1,0},{2,3},{3,2},{4,5},{5,4},{6,7},{7,6},{8,9},{9,8},{10,11... | collective-permute-start | bytes 884744 | tf_op jit(solution)/shard_map/ppermute | solution.py:620
  248.5 19.7 %collective-permute-start.46 = (bf16[2,192,768]{2,1,0:T(8,128)(2,1)S(1)}, bf16[2,192,768]{2,1,0:T(8,128)(2,1)S(1)}, u32[]{:S(2)}, u32[]{:S(2)}) collective-permute-start(bf16[2,192,768]{2,1,0:T(8,128)(2,1)S(1)} %get-tuple-element.379), channel_id=1, source_target_pairs={{0,16},{4,20},{8,24},{12,28},{16,0},{20,4},{24,8},{28,12},{1,17},{... | collective-permute-start | bytes 1769480 | tf_op jit(solution)/shard_map/ppermute | solution.py:614
  248.7 19.5 %collective-permute-start.45 = (bf16[2,192,768]{2,1,0:T(8,128)(2,1)S(1)}, bf16[2,192,768]{2,1,0:T(8,128)(2,1)S(1)}, u32[]{:S(2)}, u32[]{:S(2)}) collective-permute-start(bf16[2,192,768]{2,1,0:T(8,128)(2,1)S(1)} %get-tuple-element.380), channel_id=1, source_target_pairs={{0,8},{4,12},{8,0},{12,4},{16,24},{20,28},{24,16},{28,20},{1,9},{5... | collective-permute-start | bytes 1769480 | tf_op jit(solution)/shard_map/ppermute | solution.py:614
  276.7 18.3 %collective-permute-start.52 = (bf16[192,768]{1,0:T(8,128)(2,1)S(1)}, bf16[192,768]{1,0:T(8,128)(2,1)S(1)}, u32[]{:S(2)}, u32[]{:S(2)}) collective-permute-start(bf16[192,768]{1,0:T(8,128)(2,1)S(1)} %get-tuple-element.324), channel_id=1, source_target_pairs={{0,2},{1,3},{2,0},{3,1},{4,6},{5,7},{6,4},{7,5},{8,10},{9,11},{10,... | collective-permute-start | bytes 884744 | tf_op jit(solution)/shard_map/ppermute | solution.py:620
  276.7 25.9 %collective-permute-start.53 = (bf16[192,768]{1,0:T(8,128)(2,1)S(1)}, bf16[192,768]{1,0:T(8,128)(2,1)S(1)}, u32[]{:S(2)}, u32[]{:S(2)}) collective-permute-start(bf16[192,768]{1,0:T(8,128)(2,1)S(1)} %get-tuple-element.325), channel_id=1, source_target_pairs={{0,3},{1,2},{2,1},{3,0},{4,7},{5,6},{6,5},{7,4},{8,11},{9,10},{10,... | collective-permute-start | bytes 884744 | tf_op jit(solution)/shard_map/ppermute | solution.py:620
  (89 other events, 824.4 us)

commit v7 on v6

--- a/solution.py
+++ b/solution.py
@@ -591,6 +591,9 @@
 META = pl.BlockSpec(memory_space=pltpu.SMEM)
 
 
+ROOM = dict(finish_heads=14, finish_ffn=14, join_result=14, join_hidden=14, join_memory=14)
+
+
 def call(kernel, in_specs, outs, scratch, flops, moved, name, written=0):
     return pl.pallas_call(
         kernel,
@@ -599,7 +602,7 @@
         out_specs=in_vmem(len(outs) - written) + in_place(written),
         scratch_shapes=scratch,
         name=name,
-        compiler_params=pltpu.CompilerParams(vmem_limit_bytes=60 * 1024 * 1024),
+        compiler_params=pltpu.CompilerParams(vmem_limit_bytes=ROOM.get(name, 60) * 1024 * 1024),
         cost_estimate=pl.CostEstimate(
             flops=flops // 16, bytes_accessed=moved // 4, transcendentals=0
         ),

time: 335 us -> 330 us (0.985)
  waiting for transfers between devices: 116 us -> 122 us
  Pallas kernels: 93.8 us -> 89.5 us
  transfers between devices with their start and end apart: 71 -> 71, of which waited for: 28 -> 30; matrix products, arithmetic and copies ran while one was open for 7% -> 7% of each run, Pallas kernels for 22% -> 22%
where the time goes in v7:
time: 330 us; the launch traced here: 326 us
  waiting for transfers between devices  122 us (37%)
  Pallas kernels  89.5 us (27%)
  starting transfers between devices  81.2 us (25%)
  local copies, waits for them, and re-layouts  16.6 us (5%)
  other arithmetic  15.9 us (5%)
    ppermute x14, waiting for transfers between devices, flip(): return lax.ppermute(value, 'mp', [(i, i ^ bit) for i in range(mp)])  68.1 us
    ppermute x45, starting transfers between devices, swap(): return lax.ppermute(value, 'dp', [(i, i ^ bit) for i in range(dp)])  44 us
    ppermute x12, waiting for transfers between devices, shift(): return lax.ppermute(value, 'mp', [(i, (i + step) % mp) for i in range(mp)])  38.1 us
    ppermute x14, starting transfers between devices, flip(): return lax.ppermute(value, 'mp', [(i, i ^ bit) for i in range(mp)])  20.8 us
    pallas_call x1, Pallas kernels, body(): call(bound(head_back), [META] + in_vmem(11) + in_place(mp + 13), (row_sha...  19.4 us
    pallas_call x1, Pallas kernels, body(): call(bound(cross_back), [META] + in_vmem(5) + in_place(14), (low_shape, r...  17.1 us
    ppermute x12, starting transfers between devices, shift(): return lax.ppermute(value, 'mp', [(i, (i + step) % mp) for i in range(mp)])  16.3 us
    ppermute x45, waiting for transfers between devices, swap(): return lax.ppermute(value, 'dp', [(i, i ^ bit) for i in range(dp)])  15.3 us
  transfers between devices with their start and end apart: 71, of which 30 were waited for; matrix products, arithmetic and copies ran while one was open for 7% of the time, Pallas kernels for 22%

profile of v7, /device:TPU:9, one launch (start us, length us, event | category | flops | bytes accessed | tf_op | source)
XLA Modules:
  0.0 326.1 jit_solution(14975085222767133008)
XLA Ops:
  16.7 10.2 %collective-permute-done.2 = bf16[208,768]{1,0:T(8,128)(2,1)S(1)} collective-permute-done((bf16[208,768]{1,0:T(8,128)(2,1)S(1)}, bf16[208,768]{1,0:T(8,128)(2,1)S(1)}, u32[]{:S(2)}, u32[]{:S(2)}) %collective-permute-start.2) | collective-permute-done | bytes 319520 | tf_op jit(solution)/shard_map/ppermute | solution.py:623
  26.9 5.7 %collective-permute-done.1 = bf16[208,768]{1,0:T(8,128)(2,1)S(1)} collective-permute-done((bf16[208,768]{1,0:T(8,128)(2,1)S(1)}, bf16[208,768]{1,0:T(8,128)(2,1)S(1)}, u32[]{:S(2)}, u32[]{:S(2)}) %collective-permute-start.1) | collective-permute-done | bytes 319520 | tf_op jit(solution)/shard_map/ppermute | solution.py:623
  33.1 4.0 %collective-permute-start.6 = (bf16[192,768]{1,0:T(8,128)(2,1)}, bf16[192,768]{1,0:T(8,128)(2,1)}, u32[]{:S(2)}, u32[]{:S(2)}) collective-permute-start(bf16[192,768]{1,0:T(8,128)(2,1)} %pad_maximum_fusion.2), channel_id=1, source_target_pairs={{0,2},{1,3},{2,0},{3,1},{4,6},{5,7},{6,4},{7,5},{8,10},{9,11},{10,... | collective-permute-start | bytes 884744 | tf_op jit(solution)/shard_map/ppermute | solution.py:623
  42.6 9.4 %collective-permute-done.7 = bf16[192,768]{1,0:T(8,128)(2,1)} collective-permute-done((bf16[192,768]{1,0:T(8,128)(2,1)}, bf16[192,768]{1,0:T(8,128)(2,1)}, u32[]{:S(2)}, u32[]{:S(2)}) %collective-permute-start.7) | collective-permute-done | bytes 294944 | tf_op jit(solution)/shard_map/ppermute | solution.py:623
  52.0 5.4 %collective-permute-done.6 = bf16[192,768]{1,0:T(8,128)(2,1)} collective-permute-done((bf16[192,768]{1,0:T(8,128)(2,1)}, bf16[192,768]{1,0:T(8,128)(2,1)}, u32[]{:S(2)}, u32[]{:S(2)}) %collective-permute-start.6) | collective-permute-done | bytes 294944 | tf_op jit(solution)/shard_map/ppermute | solution.py:623
  57.5 3.1 collective-permute-start.10
  65.6 8.5 %collective-permute-done.12.refs_7_.refs_14_ = bf16[192,1024]{1,0:T(8,128)(2,1)S(1)} collective-permute-done((bf16[192,1024]{1,0:T(8,128)(2,1)}, bf16[192,1024]{1,0:T(8,128)(2,1)S(1)}, u32[]{:S(2)}, u32[]{:S(2)}) %collective-permute-start.12) | collective-permute-done | bytes 393248 | tf_op jit(solution)/shard_map/ppermute | solution.py:620
  82.4 8.5 %self_forward.1 = (bf16[4,128,576]{2,1,0:T(8,128)(2,1)}, bf16[4,128,192]{2,1,0:T(8,128)(2,1)}, f32[128,768]{1,0:T(8,128)}, f32[128,768]{1,0:T(8,128)}) custom-call(s32[12]{0:T(128)} %concatenate.27.refs_0_.meta, bf16[128,768]{1,0:T(8,128)(2,1)} %get-tuple-element.214.refs_1_.refs_2_, f32[4,2,192]{2,1,0:T(2,128)} %reshape.174.refs_2_, f32[3,768]{1,0:T(4,128)} %refs_5_.4, ...), custom_call_target="tpu_custom_call" | custom-call | flops 188743680 | bytes 2359296 | tf_op jit(solution)/shard_map/self_forward/pallas_call | solution.py:807
  90.9 7.8 %collective-permute-done.15.refs_8_.refs_15_ = bf16[192,1024]{1,0:T(8,128)(2,1)S(1)} collective-permute-done((bf16[192,1024]{1,0:T(8,128)(2,1)}, bf16[192,1024]{1,0:T(8,128)(2,1)S(1)}, u32[]{:S(2)}, u32[]{:S(2)}) %collective-permute-start.15) | collective-permute-done | bytes 393248 | tf_op jit(solution)/shard_map/ppermute | solution.py:620
  100.8 3.3 collective-permute-start.22
  107.6 5.4 %collective-permute-done.22.refs_9_.refs_16_ = bf16[192,1024]{1,0:T(8,128)(2,1)S(1)} collective-permute-done((bf16[192,1024]{1,0:T(8,128)(2,1)}, bf16[192,1024]{1,0:T(8,128)(2,1)S(1)}, u32[]{:S(2)}, u32[]{:S(2)}) %collective-permute-start.22) | collective-permute-done | bytes 393248 | tf_op jit(solution)/shard_map/ppermute | solution.py:620
  113.7 3.1 collective-permute-done.19.refs_11_
  118.2 13.3 %cross_forward.1 = (bf16[4,128,192]{2,1,0:T(8,128)(2,1)}, bf16[4,128,192]{2,1,0:T(8,128)(2,1)}, f32[4,384,1]{2,1,0:T(8,128)}, f32[128,768]{1,0:T(8,128)}, f32[12...) custom-call(s32[12]{0:T(128)} %concatenate.27.refs_0_.meta, f32[4,2,192]{2,1,0:T(2,128)} %reshape.175.refs_1_, ...), custom_call_target="tpu_custom_call" | custom-call | flops 377487360 | bytes 2359296 | tf_op jit(solution)/shard_map/cross_forward/pallas_call | solution.py:826
  132.5 10.4 %ffn_both.1 = (bf16[128,768]{1,0:T(8,128)(2,1)}, f32[128,768]{1,0:T(8,128)}, f32[16,768]{1,0:T(8,128)}, bf16[5,128,1152]{2,1,0:T(8,128)(2,1)}, bf16[5,128,384]{2,1,0:T(8,128)(2,1)}) custom-call(s32[12]{0:T(128)} %concatenate.27.refs_0_.meta, f32[128,768]{1,0:T(8,128)} %get-tuple-element.242.refs_1_, f32[128,768]{1,0:T(8,128)} %get-tuple-element.243.refs_2_, ...), custom_call_target="tpu_custom_call" | custom-call | flops 377487360 | bytes 2949120 | tf_op jit(solution)/shard_map/ffn_both/pallas_call | solution.py:861
  145.4 17.1 %cross_back.1 = (bf16[4,128,192]{2,1,0:T(8,128)(2,1)}, f32[128,768]{1,0:T(8,128)}, f32[8,768]{1,0:T(8,128)}, f32[4,2,192]{2,1,0:T(2,128)}, bf16[4,384,1024]{2,1,...) custom-call(s32[12]{0:T(128)} %concatenate.27.refs_0_.meta, ...), custom_call_target="tpu_custom_call" | custom-call | flops 471859200 | bytes 3538944 | tf_op jit(solution)/shard_map/cross_back/pallas_call | solution.py:886
  163.7 5.2 %ffn_weights.1 = (bf16[2,2,192,768]{3,2,1,0:T(8,128)(2,1)}, bf16[2,2,192,768]{3,2,1,0:T(8,128)(2,1)}, bf16[4,2,192,768]{3,2,1,0:T(8,128)(2,1)}) custom-call(s32[12]{0:T(128)} %concatenate.27.refs_0_.meta, bf16[5,128,1152]{2,1,0:T(8,128)(2,1)} %get-tuple-element.249.refs_1_, bf16[5,128,384]{2,1,0:T(8,128)(2,1)} %get-tuple-element.250.refs_2_, ...), custom_call_target="tpu_custom_call" | custom-call | flops 150994944 | bytes 2359296 | tf_op jit(solution)/shard_map/ffn_weights/pallas_call | solution.py:930
  174.6 19.4 %head_back.1 = (f32[128,768]{1,0:T(8,128)}, f32[24,768]{1,0:T(8,128)}, bf16[8,2,192,768]{3,2,1,0:T(8,128)(2,1)}, bf16[8,2,192,768]{3,2,1,0:T(8,128)(2,1)}) custom-call(s32[12]{0:T(128)} %concatenate.27.refs_0_.meta, f32[128,768]{1,0:T(8,128)} %get-tuple-element.271.refs_1_, bf16[128,768]{1,0:T(8,128)(2,1)} %get-tuple-element.214.refs_1_.refs_2_, ...), custom_call_target="tpu_custom_call" | custom-call | flops 566231040 | bytes 7077888 | tf_op jit(solution)/shard_map/head_back/pallas_call | solution.py:946
  202.4 3.2 collective-permute-start.38
  209.8 3.5 %add_slots.1 = (bf16[2,2,192,768]{3,2,1,0:T(8,128)(2,1)}, bf16[2,2,192,768]{3,2,1,0:T(8,128)(2,1)}) custom-call(bf16[8,2,192,768]{3,2,1,0:T(8,128)(2,1)} %get-tuple-element.284.mine, bf16[8,2,192,768]{3,2,1,0:T(8,128)(2,1)} %collective-permute-done.35.other), custom_call_target="tpu_custom_call" | custom-call | bytes 1179648 | tf_op jit(solution)/shard_map/add_slots/pallas_call | solution.py:994
  213.3 4.9 %collective-permute-done.39.refs_3_ = bf16[192,1024]{1,0:T(8,128)(2,1)S(1)} collective-permute-done((bf16[192,1024]{1,0:T(8,128)(2,1)}, bf16[192,1024]{1,0:T(8,128)(2,1)S(1)}, u32[]{:S(2)}, u32[]{:S(2)}) %collective-permute-start.39) | collective-permute-done | bytes 393248 | tf_op jit(solution)/shard_map/ppermute | solution.py:620
  222.6 3.3 %collective-permute-start.43 = (bf16[192,768]{1,0:T(8,128)(2,1)S(1)}, bf16[192,768]{1,0:T(8,128)(2,1)S(1)}, u32[]{:S(2)}, u32[]{:S(2)}) collective-permute-start(bf16[192,768]{1,0:T(8,128)(2,1)S(1)} %get-tuple-element.382), channel_id=1, source_target_pairs={{0,2},{1,3},{2,0},{3,1},{4,6},{5,7},{6,4},{7,5},{8,10},{9,11},{10,... | collective-permute-start | bytes 884744 | tf_op jit(solution)/shard_map/ppermute | solution.py:623
  229.8 11.8 %collective-permute-done.44 = bf16[192,768]{1,0:T(8,128)(2,1)S(1)} collective-permute-done((bf16[192,768]{1,0:T(8,128)(2,1)S(1)}, bf16[192,768]{1,0:T(8,128)(2,1)S(1)}, u32[]{:S(2)}, u32[]{:S(2)}) %collective-permute-start.44) | collective-permute-done | bytes 294944 | tf_op jit(solution)/shard_map/ppermute | solution.py:623
  241.5 4.1 %collective-permute-done.43 = bf16[192,768]{1,0:T(8,128)(2,1)S(1)} collective-permute-done((bf16[192,768]{1,0:T(8,128)(2,1)S(1)}, bf16[192,768]{1,0:T(8,128)(2,1)S(1)}, u32[]{:S(2)}, u32[]{:S(2)}) %collective-permute-start.43) | collective-permute-done | bytes 294944 | tf_op jit(solution)/shard_map/ppermute | solution.py:623
  250.0 5.3 %collective-permute-done.47.refs_1_ = bf16[128,768]{1,0:T(8,128)(2,1)S(1)} collective-permute-done((bf16[128,768]{1,0:T(8,128)(2,1)S(1)}, bf16[128,768]{1,0:T(8,128)(2,1)S(1)}, u32[]{:S(2)}, u32[]{:S(2)}) %collective-permute-start.47) | collective-permute-done | bytes 196640 | tf_op jit(solution)/shard_map/ppermute | solution.py:620
  260.1 5.2 %collective-permute-start.49 = (f32[24,768]{1,0:T(8,128)S(1)}, f32[24,768]{1,0:T(8,128)S(1)}, u32[]{:S(2)}, u32[]{:S(2)}) collective-permute-start(f32[24,768]{1,0:T(8,128)S(1)} %add.279), channel_id=1, source_target_pairs={{0,4},{4,0},{8,12},{12,8},{16,20},{20,16},{24,28},{28,24},{1,5},{5... | collective-permute-start | bytes 221192 | tf_op jit(solution)/shard_map/ppermute | solution.py:617
  270.6 3.8 %collective-permute-start.51 = (bf16[192,768]{1,0:T(8,128)(2,1)S(1)}, bf16[192,768]{1,0:T(8,128)(2,1)S(1)}, u32[]{:S(2)}, u32[]{:S(2)}) collective-permute-start(bf16[192,768]{1,0:T(8,128)(2,1)S(1)} %get-tuple-element.323), channel_id=1, source_target_pairs={{0,1},{1,0},{2,3},{3,2},{4,5},{5,4},{6,7},{7,6},{8,9},{9,8},{10,11... | collective-permute-start | bytes 884744 | tf_op jit(solution)/shard_map/ppermute | solution.py:623
  275.7 9.5 %collective-permute-done.51 = bf16[192,768]{1,0:T(8,128)(2,1)S(1)} collective-permute-done((bf16[192,768]{1,0:T(8,128)(2,1)S(1)}, bf16[192,768]{1,0:T(8,128)(2,1)S(1)}, u32[]{:S(2)}, u32[]{:S(2)}) %collective-permute-start.51) | collective-permute-done | bytes 294944 | tf_op jit(solution)/shard_map/ppermute | solution.py:623
  289.0 3.2 collective-permute-done.59
  292.3 7.9 %collective-permute-done.53 = bf16[192,768]{1,0:T(8,128)(2,1)S(1)} collective-permute-done((bf16[192,768]{1,0:T(8,128)(2,1)S(1)}, bf16[192,768]{1,0:T(8,128)(2,1)S(1)}, u32[]{:S(2)}, u32[]{:S(2)}) %collective-permute-start.53) | collective-permute-done | bytes 294944 | tf_op jit(solution)/shard_map/ppermute | solution.py:623
  305.1 3.1 finish_ffn.1
  308.2 4.4 %collective-permute-done.63.refs_2_ = bf16[128,768]{1,0:T(8,128)(2,1)S(1)} collective-permute-done((bf16[128,768]{1,0:T(8,128)(2,1)S(1)}, bf16[128,768]{1,0:T(8,128)(2,1)S(1)}, u32[]{:S(2)}, u32[]{:S(2)}) %collective-permute-start.63) | collective-permute-done | bytes 196640 | tf_op jit(solution)/shard_map/ppermute | solution.py:620
  322.8 3.3 %finish_heads.1 = (f32[576,768]{1,0:T(8,128)}, f32[192,768]{1,0:T(8,128)}, f32[192,768]{1,0:T(8,128)}, f32[192,768]{1,0:T(8,128)}, f32[384,768]{1,0:T(8,128)}, /...) custom-call(s32[12]{0:T(128)S(1)} %copy-done.2, ...), custom_call_target="tpu_custom_call" | custom-call | bytes 294912 | tf_op jit(solution)/shard_map/finish_heads/pallas_call | solution.py:1082
  (248 shorter events, 108.4 us)
Async XLA Ops:
  4.6 22.3 %collective-permute-start.2 = (bf16[208,768]{1,0:T(8,128)(2,1)S(1)}, bf16[208,768]{1,0:T(8,128)(2,1)S(1)}, u32[]{:S(2)}, u32[]{:S(2)}) collective-permute-start(bf16[208,768]{1,0:T(8,128)(2,1)S(1)} %concatenate.25), channel_id=1, source_target_pairs={{0,3},{1,2},{2,1},{3,0},{4,7},{5,6},{6,5},{7,4},{8,11},{9,10},{10,... | collective-permute-start | bytes 958472 | tf_op jit(solution)/shard_map/ppermute | solution.py:623
  6.0 26.7 %collective-permute-start.1 = (bf16[208,768]{1,0:T(8,128)(2,1)S(1)}, bf16[208,768]{1,0:T(8,128)(2,1)S(1)}, u32[]{:S(2)}, u32[]{:S(2)}) collective-permute-start(bf16[208,768]{1,0:T(8,128)(2,1)S(1)} %concatenate.25), channel_id=1, source_target_pairs={{0,2},{1,3},{2,0},{3,1},{4,6},{5,7},{6,4},{7,5},{8,10},{9,11},{10,... | collective-permute-start | bytes 958472 | tf_op jit(solution)/shard_map/ppermute | solution.py:623
  7.0 25.6 %collective-permute-start = (bf16[208,768]{1,0:T(8,128)(2,1)S(1)}, bf16[208,768]{1,0:T(8,128)(2,1)S(1)}, u32[]{:S(2)}, u32[]{:S(2)}) collective-permute-start(bf16[208,768]{1,0:T(8,128)(2,1)S(1)} %concatenate.25), channel_id=1, source_target_pairs={{0,1},{1,0},{2,3},{3,2},{4,5},{5,4},{6,7},{7,6},{8,9},{9,8},{10,11... | collective-permute-start | bytes 958472 | tf_op jit(solution)/shard_map/ppermute | solution.py:623
  32.7 19.3 %collective-permute-start.7 = (bf16[192,768]{1,0:T(8,128)(2,1)}, bf16[192,768]{1,0:T(8,128)(2,1)}, u32[]{:S(2)}, u32[]{:S(2)}) collective-permute-start(bf16[192,768]{1,0:T(8,128)(2,1)} %pad_maximum_fusion.2), channel_id=1, source_target_pairs={{0,3},{1,2},{2,1},{3,0},{4,7},{5,6},{6,5},{7,4},{8,11},{9,10},{10,... | collective-permute-start | bytes 884744 | tf_op jit(solution)/shard_map/ppermute | solution.py:623
  33.1 24.4 %collective-permute-start.6 = (bf16[192,768]{1,0:T(8,128)(2,1)}, bf16[192,768]{1,0:T(8,128)(2,1)}, u32[]{:S(2)}, u32[]{:S(2)}) collective-permute-start(bf16[192,768]{1,0:T(8,128)(2,1)} %pad_maximum_fusion.2), channel_id=1, source_target_pairs={{0,2},{1,3},{2,0},{3,1},{4,6},{5,7},{6,4},{7,5},{8,10},{9,11},{10,... | collective-permute-start | bytes 884744 | tf_op jit(solution)/shard_map/ppermute | solution.py:623
  37.1 20.4 %collective-permute-start.5 = (bf16[192,768]{1,0:T(8,128)(2,1)}, bf16[192,768]{1,0:T(8,128)(2,1)}, u32[]{:S(2)}, u32[]{:S(2)}) collective-permute-start(bf16[192,768]{1,0:T(8,128)(2,1)} %pad_maximum_fusion.2), channel_id=1, source_target_pairs={{0,1},{1,0},{2,3},{3,2},{4,5},{5,4},{6,7},{7,6},{8,9},{9,8},{10,11... | collective-permute-start | bytes 884744 | tf_op jit(solution)/shard_map/ppermute | solution.py:623
  37.3 20.2 %collective-permute-start.4 = (bf16[3,192,768]{2,1,0:T(8,128)(2,1)S(1)}, bf16[3,192,768]{2,1,0:T(8,128)(2,1)S(1)}, u32[]{:S(2)}, u32[]{:S(2)}) collective-permute-start(bf16[3,192,768]{2,1,0:T(8,128)(2,1)S(1)} %pad_maximum_fusion.refs_6_.refs_10_.refs_7_.refs_17_), channel_id=1, source_target_pairs={{0,16},{4,20},{8,24},{12,28},{16,0},{20,4},{24,8},{28,12},{1,17},{... | collective-permute-start | bytes 2654216 | tf_op jit(solution)/shard_map/ppermute | solution.py:617
  38.6 18.9 %collective-permute-start.3 = (bf16[3,192,768]{2,1,0:T(8,128)(2,1)S(1)}, bf16[3,192,768]{2,1,0:T(8,128)(2,1)S(1)}, u32[]{:S(2)}, u32[]{:S(2)}) collective-permute-start(bf16[3,192,768]{2,1,0:T(8,128)(2,1)S(1)} %pad_maximum_fusion.refs_6_.refs_10_.refs_7_.refs_17_), channel_id=1, source_target_pairs={{0,8},{4,12},{8,0},{12,4},{16,24},{20,28},{24,16},{28,20},{1,9},{5... | collective-permute-start | bytes 2654216 | tf_op jit(solution)/shard_map/ppermute | solution.py:617
  78.2 21.4 %collective-permute-start.14 = (bf16[3,192,768]{2,1,0:T(8,128)(2,1)}, bf16[3,192,768]{2,1,0:T(8,128)(2,1)S(1)}, u32[]{:S(2)}, u32[]{:S(2)}) collective-permute-start(bf16[3,192,768]{2,1,0:T(8,128)(2,1)} %pad_maximum_fusion.1.refs_8_), channel_id=1, source_target_pairs={{0,16},{4,20},{8,24},{12,28},{16,0},{20,4},{24,8},{28,12},{1,17},{... | collective-permute-start | bytes 2654216 | tf_op jit(solution)/shard_map/ppermute | solution.py:617
  78.4 21.2 %collective-permute-start.13 = (bf16[3,192,768]{2,1,0:T(8,128)(2,1)}, bf16[3,192,768]{2,1,0:T(8,128)(2,1)}, u32[]{:S(2)}, u32[]{:S(2)}) collective-permute-start(bf16[3,192,768]{2,1,0:T(8,128)(2,1)} %pad_maximum_fusion.1.refs_8_), channel_id=1, source_target_pairs={{0,8},{4,12},{8,0},{12,4},{16,24},{20,28},{24,16},{28,20},{1,9},{5... | collective-permute-start | bytes 2654216 | tf_op jit(solution)/shard_map/ppermute | solution.py:617
  80.0 18.7 %collective-permute-start.15 = (bf16[192,1024]{1,0:T(8,128)(2,1)}, bf16[192,1024]{1,0:T(8,128)(2,1)S(1)}, u32[]{:S(2)}, u32[]{:S(2)}) collective-permute-start(bf16[192,1024]{1,0:T(8,128)(2,1)} %get-tuple-element.212), channel_id=1, source_target_pairs={{0,2},{1,3},{2,0},{3,1},{4,6},{5,7},{6,4},{7,5},{8,10},{9,11},{10,... | collective-permute-start | bytes 1179656 | tf_op jit(solution)/shard_map/ppermute | solution.py:620
  99.6 17.2 %collective-permute-start.21 = (bf16[3,192,768]{2,1,0:T(8,128)(2,1)}, bf16[3,192,768]{2,1,0:T(8,128)(2,1)S(1)}, u32[]{:S(2)}, u32[]{:S(2)}) collective-permute-start(bf16[3,192,768]{2,1,0:T(8,128)(2,1)} %pad_maximum_fusion.1.refs_8_), channel_id=1, source_target_pairs={{0,4},{4,0},{8,12},{12,8},{16,20},{20,16},{24,28},{28,24},{1,5},{5... | collective-permute-start | bytes 2654216 | tf_op jit(solution)/shard_map/ppermute | solution.py:617
  106.7 24.9 %collective-permute-start.24 = (bf16[3,192,768]{2,1,0:T(8,128)(2,1)S(1)}, bf16[3,192,768]{2,1,0:T(8,128)(2,1)S(1)}, u32[]{:S(2)}, u32[]{:S(2)}) collective-permute-start(bf16[3,192,768]{2,1,0:T(8,128)(2,1)S(1)} %collective-permute-done.14.refs_10_), channel_id=1, source_target_pairs={{0,4},{4,0},{8,12},{12,8},{16,20},{20,16},{24,28},{28,24},{1,5},{5... | collective-permute-start | bytes 2654216 | tf_op jit(solution)/shard_map/ppermute | solution.py:617
  112.9 18.7 %collective-permute-start.23 = (bf16[3,192,768]{2,1,0:T(8,128)(2,1)}, bf16[3,192,768]{2,1,0:T(8,128)(2,1)}, u32[]{:S(2)}, u32[]{:S(2)}) collective-permute-start(bf16[3,192,768]{2,1,0:T(8,128)(2,1)} %collective-permute-done.13.refs_9_), channel_id=1, source_target_pairs={{0,4},{4,0},{8,12},{12,8},{16,20},{20,16},{24,28},{28,24},{1,5},{5... | collective-permute-start | bytes 2654216 | tf_op jit(solution)/shard_map/ppermute | solution.py:617
  142.9 19.7 %collective-permute-start.30 = (bf16[5,128,1152]{2,1,0:T(8,128)(2,1)}, bf16[5,128,1152]{2,1,0:T(8,128)(2,1)S(1)}, u32[]{:S(2)}, u32[]{:S(2)}) collective-permute-start(bf16[5,128,1152]{2,1,0:T(8,128)(2,1)} %get-tuple-element.249.refs_1_), channel_id=1, source_target_pairs={{0,4},{4,0},{8,12},{12,8},{16,20},{20,16},{24,28},{28,24},{1,5},{5... | collective-permute-start | bytes 4423688 | tf_op jit(solution)/shard_map/ppermute | solution.py:617
  143.4 19.1 %collective-permute-start.29 = (bf16[128,768]{1,0:T(8,128)(2,1)}, bf16[128,768]{1,0:T(8,128)(2,1)S(1)}, u32[]{:S(2)}, u32[]{:S(2)}) collective-permute-start(bf16[128,768]{1,0:T(8,128)(2,1)} %get-tuple-element.305.refs_0_), channel_id=1, source_target_pairs={{0,3},{1,0},{2,1},{3,2},{4,7},{5,4},{6,5},{7,6},{8,11},{9,8},{10,9... | collective-permute-start | bytes 589832 | tf_op jit(solution)/shard_map/ppermute | solution.py:620
  144.2 18.3 %collective-permute-start.28 = (bf16[128,768]{1,0:T(8,128)(2,1)}, bf16[128,768]{1,0:T(8,128)(2,1)S(1)}, u32[]{:S(2)}, u32[]{:S(2)}) collective-permute-start(bf16[128,768]{1,0:T(8,128)(2,1)} %get-tuple-element.305.refs_0_), channel_id=1, source_target_pairs={{0,2},{1,3},{2,0},{3,1},{4,6},{5,7},{6,4},{7,5},{8,10},{9,11},{10,... | collective-permute-start | bytes 589832 | tf_op jit(solution)/shard_map/ppermute | solution.py:620
  144.2 18.3 %collective-permute-start.27 = (bf16[128,768]{1,0:T(8,128)(2,1)}, bf16[128,768]{1,0:T(8,128)(2,1)S(1)}, u32[]{:S(2)}, u32[]{:S(2)}) collective-permute-start(bf16[128,768]{1,0:T(8,128)(2,1)} %get-tuple-element.305.refs_0_), channel_id=1, source_target_pairs={{0,1},{1,2},{2,3},{3,0},{4,5},{5,6},{6,7},{7,4},{8,9},{9,10},{10,1... | collective-permute-start | bytes 589832 | tf_op jit(solution)/shard_map/ppermute | solution.py:620
  168.9 27.0 %collective-permute-start.32 = (bf16[2,2,192,768]{3,2,1,0:T(8,128)(2,1)}, bf16[2,2,192,768]{3,2,1,0:T(8,128)(2,1)}, u32[]{:S(2)}, u32[]{:S(2)}) collective-permute-start(bf16[2,2,192,768]{3,2,1,0:T(8,128)(2,1)} %get-tuple-element.265), channel_id=1, source_target_pairs={{0,16},{4,20},{8,24},{12,28},{16,0},{20,4},{24,8},{28,12},{1,17},{... | collective-permute-start | bytes 3538952 | tf_op jit(solution)/shard_map/ppermute | solution.py:617
  169.7 26.4 %collective-permute-start.31 = (bf16[2,2,192,768]{3,2,1,0:T(8,128)(2,1)}, bf16[2,2,192,768]{3,2,1,0:T(8,128)(2,1)}, u32[]{:S(2)}, u32[]{:S(2)}) collective-permute-start(bf16[2,2,192,768]{3,2,1,0:T(8,128)(2,1)} %get-tuple-element.264), channel_id=1, source_target_pairs={{0,8},{4,12},{8,0},{12,4},{16,24},{20,28},{24,16},{28,20},{1,9},{5... | collective-permute-start | bytes 3538952 | tf_op jit(solution)/shard_map/ppermute | solution.py:617
  170.9 23.2 %collective-permute-start.33 = (bf16[192,1024]{1,0:T(8,128)(2,1)}, bf16[192,1024]{1,0:T(8,128)(2,1)S(1)}, u32[]{:S(2)}, u32[]{:S(2)}) collective-permute-start(bf16[192,1024]{1,0:T(8,128)(2,1)} %get-tuple-element.267), channel_id=1, source_target_pairs={{0,1},{1,2},{2,3},{3,0},{4,5},{5,6},{6,7},{7,4},{8,9},{9,10},{10,1... | collective-permute-start | bytes 1179656 | tf_op jit(solution)/shard_map/ppermute | solution.py:620
  172.1 23.8 %collective-permute-start.34 = (bf16[192,1024]{1,0:T(8,128)(2,1)S(1)}, bf16[192,1024]{1,0:T(8,128)(2,1)S(1)}, u32[]{:S(2)}, u32[]{:S(2)}) collective-permute-start(bf16[192,1024]{1,0:T(8,128)(2,1)S(1)} %copy-done.28), channel_id=1, source_target_pairs={{0,2},{1,3},{2,0},{3,1},{4,6},{5,7},{6,4},{7,5},{8,10},{9,11},{10,... | collective-permute-start | bytes 1179656 | tf_op jit(solution)/shard_map/ppermute | solution.py:620
  201.0 17.2 %collective-permute-start.37 = (bf16[2,192,768]{2,1,0:T(8,128)(2,1)}, bf16[2,192,768]{2,1,0:T(8,128)(2,1)}, u32[]{:S(2)}, u32[]{:S(2)}) collective-permute-start(bf16[2,192,768]{2,1,0:T(8,128)(2,1)} %get-tuple-element.384), channel_id=1, source_target_pairs={{0,16},{4,20},{8,24},{12,28},{16,0},{20,4},{24,8},{28,12},{1,17},{... | collective-permute-start | bytes 1769480 | tf_op jit(solution)/shard_map/ppermute | solution.py:617
  218.2 27.4 %collective-permute-start.40 = (bf16[2,2,192,768]{3,2,1,0:T(8,128)(2,1)}, bf16[2,2,192,768]{3,2,1,0:T(8,128)(2,1)S(1)}, u32[]{:S(2)}, u32[]{:S(2)}) collective-permute-start(bf16[2,2,192,768]{3,2,1,0:T(8,128)(2,1)} %get-tuple-element.297), channel_id=1, source_target_pairs={{0,8},{4,12},{8,0},{12,4},{16,24},{20,28},{24,16},{28,20},{1,9},{5... | collective-permute-start | bytes 3538952 | tf_op jit(solution)/shard_map/ppermute | solution.py:617
  219.5 26.1 %collective-permute-start.41 = (bf16[2,2,192,768]{3,2,1,0:T(8,128)(2,1)}, bf16[2,2,192,768]{3,2,1,0:T(8,128)(2,1)S(1)}, u32[]{:S(2)}, u32[]{:S(2)}) collective-permute-start(bf16[2,2,192,768]{3,2,1,0:T(8,128)(2,1)} %get-tuple-element.298), channel_id=1, source_target_pairs={{0,16},{4,20},{8,24},{12,28},{16,0},{20,4},{24,8},{28,12},{1,17},{... | collective-permute-start | bytes 3538952 | tf_op jit(solution)/shard_map/ppermute | solution.py:617
  222.5 19.0 %collective-permute-start.44 = (bf16[192,768]{1,0:T(8,128)(2,1)S(1)}, bf16[192,768]{1,0:T(8,128)(2,1)S(1)}, u32[]{:S(2)}, u32[]{:S(2)}) collective-permute-start(bf16[192,768]{1,0:T(8,128)(2,1)S(1)} %get-tuple-element.381), channel_id=1, source_target_pairs={{0,3},{1,2},{2,1},{3,0},{4,7},{5,6},{6,5},{7,4},{8,11},{9,10},{10,... | collective-permute-start | bytes 884744 | tf_op jit(solution)/shard_map/ppermute | solution.py:623
  222.6 23.0 %collective-permute-start.43 = (bf16[192,768]{1,0:T(8,128)(2,1)S(1)}, bf16[192,768]{1,0:T(8,128)(2,1)S(1)}, u32[]{:S(2)}, u32[]{:S(2)}) collective-permute-start(bf16[192,768]{1,0:T(8,128)(2,1)S(1)} %get-tuple-element.382), channel_id=1, source_target_pairs={{0,2},{1,3},{2,0},{3,1},{4,6},{5,7},{6,4},{7,5},{8,10},{9,11},{10,... | collective-permute-start | bytes 884744 | tf_op jit(solution)/shard_map/ppermute | solution.py:623
  225.8 19.8 %collective-permute-start.42 = (bf16[192,768]{1,0:T(8,128)(2,1)S(1)}, bf16[192,768]{1,0:T(8,128)(2,1)S(1)}, u32[]{:S(2)}, u32[]{:S(2)}) collective-permute-start(bf16[192,768]{1,0:T(8,128)(2,1)S(1)} %get-tuple-element.383), channel_id=1, source_target_pairs={{0,1},{1,0},{2,3},{3,2},{4,5},{5,4},{6,7},{7,6},{8,9},{9,8},{10,11... | collective-permute-start | bytes 884744 | tf_op jit(solution)/shard_map/ppermute | solution.py:623
  247.3 19.3 %collective-permute-start.46 = (bf16[2,192,768]{2,1,0:T(8,128)(2,1)S(1)}, bf16[2,192,768]{2,1,0:T(8,128)(2,1)S(1)}, u32[]{:S(2)}, u32[]{:S(2)}) collective-permute-start(bf16[2,192,768]{2,1,0:T(8,128)(2,1)S(1)} %get-tuple-element.379), channel_id=1, source_target_pairs={{0,16},{4,20},{8,24},{12,28},{16,0},{20,4},{24,8},{28,12},{1,17},{... | collective-permute-start | bytes 1769480 | tf_op jit(solution)/shard_map/ppermute | solution.py:617
  248.0 18.7 %collective-permute-start.45 = (bf16[2,192,768]{2,1,0:T(8,128)(2,1)S(1)}, bf16[2,192,768]{2,1,0:T(8,128)(2,1)S(1)}, u32[]{:S(2)}, u32[]{:S(2)}) collective-permute-start(bf16[2,192,768]{2,1,0:T(8,128)(2,1)S(1)} %get-tuple-element.380), channel_id=1, source_target_pairs={{0,8},{4,12},{8,0},{12,4},{16,24},{20,28},{24,16},{28,20},{1,9},{5... | collective-permute-start | bytes 1769480 | tf_op jit(solution)/shard_map/ppermute | solution.py:617
  274.4 17.8 %collective-permute-start.52 = (bf16[192,768]{1,0:T(8,128)(2,1)S(1)}, bf16[192,768]{1,0:T(8,128)(2,1)S(1)}, u32[]{:S(2)}, u32[]{:S(2)}) collective-permute-start(bf16[192,768]{1,0:T(8,128)(2,1)S(1)} %get-tuple-element.324), channel_id=1, source_target_pairs={{0,2},{1,3},{2,0},{3,1},{4,6},{5,7},{6,4},{7,5},{8,10},{9,11},{10,... | collective-permute-start | bytes 884744 | tf_op jit(solution)/shard_map/ppermute | solution.py:623
  274.4 25.8 %collective-permute-start.53 = (bf16[192,768]{1,0:T(8,128)(2,1)S(1)}, bf16[192,768]{1,0:T(8,128)(2,1)S(1)}, u32[]{:S(2)}, u32[]{:S(2)}) collective-permute-start(bf16[192,768]{1,0:T(8,128)(2,1)S(1)} %get-tuple-element.325), channel_id=1, source_target_pairs={{0,3},{1,2},{2,1},{3,0},{4,7},{5,6},{6,5},{7,4},{8,11},{9,10},{10,... | collective-permute-start | bytes 884744 | tf_op jit(solution)/shard_map/ppermute | solution.py:623
  (70 other events, 654.5 us)

commit v8 on v7

--- a/solution.py
+++ b/solution.py
@@ -1030,7 +1030,7 @@
         head_late = swap(late_two, 2), swap(late_four, 4)
         hidden_low = hidden_grad.astype(BF16)
         hidden_blocks = [hidden_low, shift(hidden_low, 1), None, shift(hidden_low, 3)]
-        small = after(small, hidden_blocks[1])
+        small = after(small, hidden_blocks[3])
         bit = 2
         while bit < mp:
             small = small + flip(small, bit)

time: 330 us -> 330 us (level)
  waiting for transfers between devices: 122 us -> 115 us
  starting transfers between devices: 81.2 us -> 87 us
    ppermute x45, starting transfers between devices: 44 us -> 49.5 us  [swap(): return lax.ppermute(value, 'dp', [(i, i ^ bit) for i in range(dp)])]
    ppermute x14, waiting for transfers between devices: 68.1 us -> 63.7 us  [flip(): return lax.ppermute(value, 'mp', [(i, i ^ bit) for i in range(mp)])]
where the time goes in v8:
time: 330 us; the launch traced here: 325 us
  waiting for transfers between devices  115 us (35%)
  Pallas kernels  89.5 us (27%)
  starting transfers between devices  87 us (26%)
  local copies, waits for them, and re-layouts  16.6 us (5%)
  other arithmetic  15.9 us (5%)
    ppermute x14, waiting for transfers between devices, flip(): return lax.ppermute(value, 'mp', [(i, i ^ bit) for i in range(mp)])  63.7 us
    ppermute x45, starting transfers between devices, swap(): return lax.ppermute(value, 'dp', [(i, i ^ bit) for i in range(dp)])  49.5 us
    ppermute x12, waiting for transfers between devices, shift(): return lax.ppermute(value, 'mp', [(i, (i + step) % mp) for i in range(mp)])  35.6 us
    ppermute x14, starting transfers between devices, flip(): return lax.ppermute(value, 'mp', [(i, i ^ bit) for i in range(mp)])  20.9 us
    pallas_call x1, Pallas kernels, body(): call(bound(head_back), [META] + in_vmem(11) + in_place(mp + 13), (row_sha...  19.4 us
    pallas_call x1, Pallas kernels, body(): call(bound(cross_back), [META] + in_vmem(5) + in_place(14), (low_shape, r...  17.1 us
    ppermute x12, starting transfers between devices, shift(): return lax.ppermute(value, 'mp', [(i, (i + step) % mp) for i in range(mp)])  16.6 us
    ppermute x45, waiting for transfers between devices, swap(): return lax.ppermute(value, 'dp', [(i, i ^ bit) for i in range(dp)])  15.7 us
  transfers between devices with their start and end apart: 71, of which 30 were waited for; matrix products, arithmetic and copies ran while one was open for 7% of the time, Pallas kernels for 22%

profile of v8, /device:TPU:9, one launch (start us, length us, event | category | flops | bytes accessed | tf_op | source)
XLA Modules:
  0.0 325.3 jit_solution(9142238313228361353)
XLA Ops:
  16.7 10.2 %collective-permute-done.2 = bf16[208,768]{1,0:T(8,128)(2,1)S(1)} collective-permute-done((bf16[208,768]{1,0:T(8,128)(2,1)S(1)}, bf16[208,768]{1,0:T(8,128)(2,1)S(1)}, u32[]{:S(2)}, u32[]{:S(2)}) %collective-permute-start.2) | collective-permute-done | bytes 319520 | tf_op jit(solution)/shard_map/ppermute | solution.py:623
  26.9 5.7 %collective-permute-done.1 = bf16[208,768]{1,0:T(8,128)(2,1)S(1)} collective-permute-done((bf16[208,768]{1,0:T(8,128)(2,1)S(1)}, bf16[208,768]{1,0:T(8,128)(2,1)S(1)}, u32[]{:S(2)}, u32[]{:S(2)}) %collective-permute-start.1) | collective-permute-done | bytes 319520 | tf_op jit(solution)/shard_map/ppermute | solution.py:623
  33.1 4.0 %collective-permute-start.6 = (bf16[192,768]{1,0:T(8,128)(2,1)}, bf16[192,768]{1,0:T(8,128)(2,1)}, u32[]{:S(2)}, u32[]{:S(2)}) collective-permute-start(bf16[192,768]{1,0:T(8,128)(2,1)} %pad_maximum_fusion.2), channel_id=1, source_target_pairs={{0,2},{1,3},{2,0},{3,1},{4,6},{5,7},{6,4},{7,5},{8,10},{9,11},{10,... | collective-permute-start | bytes 884744 | tf_op jit(solution)/shard_map/ppermute | solution.py:623
  42.6 9.4 %collective-permute-done.7 = bf16[192,768]{1,0:T(8,128)(2,1)} collective-permute-done((bf16[192,768]{1,0:T(8,128)(2,1)}, bf16[192,768]{1,0:T(8,128)(2,1)}, u32[]{:S(2)}, u32[]{:S(2)}) %collective-permute-start.7) | collective-permute-done | bytes 294944 | tf_op jit(solution)/shard_map/ppermute | solution.py:623
  52.0 5.4 %collective-permute-done.6 = bf16[192,768]{1,0:T(8,128)(2,1)} collective-permute-done((bf16[192,768]{1,0:T(8,128)(2,1)}, bf16[192,768]{1,0:T(8,128)(2,1)}, u32[]{:S(2)}, u32[]{:S(2)}) %collective-permute-start.6) | collective-permute-done | bytes 294944 | tf_op jit(solution)/shard_map/ppermute | solution.py:623
  57.5 3.1 collective-permute-start.10
  65.6 8.5 %collective-permute-done.12.refs_7_.refs_14_ = bf16[192,1024]{1,0:T(8,128)(2,1)S(1)} collective-permute-done((bf16[192,1024]{1,0:T(8,128)(2,1)}, bf16[192,1024]{1,0:T(8,128)(2,1)S(1)}, u32[]{:S(2)}, u32[]{:S(2)}) %collective-permute-start.12) | collective-permute-done | bytes 393248 | tf_op jit(solution)/shard_map/ppermute | solution.py:620
  82.4 8.5 %self_forward.1 = (bf16[4,128,576]{2,1,0:T(8,128)(2,1)}, bf16[4,128,192]{2,1,0:T(8,128)(2,1)}, f32[128,768]{1,0:T(8,128)}, f32[128,768]{1,0:T(8,128)}) custom-call(s32[12]{0:T(128)} %concatenate.27.refs_0_.meta, bf16[128,768]{1,0:T(8,128)(2,1)} %get-tuple-element.214.refs_1_.refs_2_, f32[4,2,192]{2,1,0:T(2,128)} %reshape.174.refs_2_, f32[3,768]{1,0:T(4,128)} %refs_5_.4, ...), custom_call_target="tpu_custom_call" | custom-call | flops 188743680 | bytes 2359296 | tf_op jit(solution)/shard_map/self_forward/pallas_call | solution.py:807
  90.9 7.8 %collective-permute-done.15.refs_8_.refs_15_ = bf16[192,1024]{1,0:T(8,128)(2,1)S(1)} collective-permute-done((bf16[192,1024]{1,0:T(8,128)(2,1)}, bf16[192,1024]{1,0:T(8,128)(2,1)S(1)}, u32[]{:S(2)}, u32[]{:S(2)}) %collective-permute-start.15) | collective-permute-done | bytes 393248 | tf_op jit(solution)/shard_map/ppermute | solution.py:620
  100.8 3.3 %collective-permute-start.22 = (bf16[192,1024]{1,0:T(8,128)(2,1)}, bf16[192,1024]{1,0:T(8,128)(2,1)S(1)}, u32[]{:S(2)}, u32[]{:S(2)}) collective-permute-start(bf16[192,1024]{1,0:T(8,128)(2,1)} %get-tuple-element.235), channel_id=1, source_target_pairs={{0,3},{1,0},{2,1},{3,2},{4,7},{5,4},{6,5},{7,6},{8,11},{9,8},{10,9... | collective-permute-start | bytes 1179656 | tf_op jit(solution)/shard_map/ppermute | solution.py:620
  107.6 5.4 %collective-permute-done.22.refs_9_.refs_16_ = bf16[192,1024]{1,0:T(8,128)(2,1)S(1)} collective-permute-done((bf16[192,1024]{1,0:T(8,128)(2,1)}, bf16[192,1024]{1,0:T(8,128)(2,1)S(1)}, u32[]{:S(2)}, u32[]{:S(2)}) %collective-permute-start.22) | collective-permute-done | bytes 393248 | tf_op jit(solution)/shard_map/ppermute | solution.py:620
  113.7 3.1 collective-permute-done.19.refs_11_
  118.2 13.3 %cross_forward.1 = (bf16[4,128,192]{2,1,0:T(8,128)(2,1)}, bf16[4,128,192]{2,1,0:T(8,128)(2,1)}, f32[4,384,1]{2,1,0:T(8,128)}, f32[128,768]{1,0:T(8,128)}, f32[12...) custom-call(s32[12]{0:T(128)} %concatenate.27.refs_0_.meta, f32[4,2,192]{2,1,0:T(2,128)} %reshape.175.refs_1_, ...), custom_call_target="tpu_custom_call" | custom-call | flops 377487360 | bytes 2359296 | tf_op jit(solution)/shard_map/cross_forward/pallas_call | solution.py:826
  132.5 10.4 %ffn_both.1 = (bf16[128,768]{1,0:T(8,128)(2,1)}, f32[128,768]{1,0:T(8,128)}, f32[16,768]{1,0:T(8,128)}, bf16[5,128,1152]{2,1,0:T(8,128)(2,1)}, bf16[5,128,384]{2,1,0:T(8,128)(2,1)}) custom-call(s32[12]{0:T(128)} %concatenate.27.refs_0_.meta, f32[128,768]{1,0:T(8,128)} %get-tuple-element.242.refs_1_, f32[128,768]{1,0:T(8,128)} %get-tuple-element.243.refs_2_, ...), custom_call_target="tpu_custom_call" | custom-call | flops 377487360 | bytes 2949120 | tf_op jit(solution)/shard_map/ffn_both/pallas_call | solution.py:861
  145.4 17.1 %cross_back.1 = (bf16[4,128,192]{2,1,0:T(8,128)(2,1)}, f32[128,768]{1,0:T(8,128)}, f32[8,768]{1,0:T(8,128)}, f32[4,2,192]{2,1,0:T(2,128)}, bf16[4,384,1024]{2,1,...) custom-call(s32[12]{0:T(128)} %concatenate.27.refs_0_.meta, ...), custom_call_target="tpu_custom_call" | custom-call | flops 471859200 | bytes 3538944 | tf_op jit(solution)/shard_map/cross_back/pallas_call | solution.py:886
  163.7 5.2 %ffn_weights.1 = (bf16[2,2,192,768]{3,2,1,0:T(8,128)(2,1)}, bf16[2,2,192,768]{3,2,1,0:T(8,128)(2,1)}, bf16[4,2,192,768]{3,2,1,0:T(8,128)(2,1)}) custom-call(s32[12]{0:T(128)} %concatenate.27.refs_0_.meta, bf16[5,128,1152]{2,1,0:T(8,128)(2,1)} %get-tuple-element.249.refs_1_, bf16[5,128,384]{2,1,0:T(8,128)(2,1)} %get-tuple-element.250.refs_2_, ...), custom_call_target="tpu_custom_call" | custom-call | flops 150994944 | bytes 2359296 | tf_op jit(solution)/shard_map/ffn_weights/pallas_call | solution.py:930
  174.6 19.4 %head_back.1 = (f32[128,768]{1,0:T(8,128)}, f32[24,768]{1,0:T(8,128)}, bf16[8,2,192,768]{3,2,1,0:T(8,128)(2,1)}, bf16[8,2,192,768]{3,2,1,0:T(8,128)(2,1)}) custom-call(s32[12]{0:T(128)} %concatenate.27.refs_0_.meta, f32[128,768]{1,0:T(8,128)} %get-tuple-element.271.refs_1_, bf16[128,768]{1,0:T(8,128)(2,1)} %get-tuple-element.214.refs_1_.refs_2_, ...), custom_call_target="tpu_custom_call" | custom-call | flops 566231040 | bytes 7077888 | tf_op jit(solution)/shard_map/head_back/pallas_call | solution.py:946
  202.4 3.2 collective-permute-start.38
  209.8 3.5 %add_slots.1 = (bf16[2,2,192,768]{3,2,1,0:T(8,128)(2,1)}, bf16[2,2,192,768]{3,2,1,0:T(8,128)(2,1)}) custom-call(bf16[8,2,192,768]{3,2,1,0:T(8,128)(2,1)} %get-tuple-element.284.mine, bf16[8,2,192,768]{3,2,1,0:T(8,128)(2,1)} %collective-permute-done.35.other), custom_call_target="tpu_custom_call" | custom-call | bytes 1179648 | tf_op jit(solution)/shard_map/add_slots/pallas_call | solution.py:994
  213.3 4.9 %collective-permute-done.39.refs_3_ = bf16[192,1024]{1,0:T(8,128)(2,1)S(1)} collective-permute-done((bf16[192,1024]{1,0:T(8,128)(2,1)}, bf16[192,1024]{1,0:T(8,128)(2,1)S(1)}, u32[]{:S(2)}, u32[]{:S(2)}) %collective-permute-start.39) | collective-permute-done | bytes 393248 | tf_op jit(solution)/shard_map/ppermute | solution.py:620
  222.6 3.3 %collective-permute-start.43 = (bf16[192,768]{1,0:T(8,128)(2,1)S(1)}, bf16[192,768]{1,0:T(8,128)(2,1)S(1)}, u32[]{:S(2)}, u32[]{:S(2)}) collective-permute-start(bf16[192,768]{1,0:T(8,128)(2,1)S(1)} %get-tuple-element.382), channel_id=1, source_target_pairs={{0,2},{1,3},{2,0},{3,1},{4,6},{5,7},{6,4},{7,5},{8,10},{9,11},{10,... | collective-permute-start | bytes 884744 | tf_op jit(solution)/shard_map/ppermute | solution.py:623
  229.8 11.8 %collective-permute-done.44 = bf16[192,768]{1,0:T(8,128)(2,1)S(1)} collective-permute-done((bf16[192,768]{1,0:T(8,128)(2,1)S(1)}, bf16[192,768]{1,0:T(8,128)(2,1)S(1)}, u32[]{:S(2)}, u32[]{:S(2)}) %collective-permute-start.44) | collective-permute-done | bytes 294944 | tf_op jit(solution)/shard_map/ppermute | solution.py:623
  241.5 4.1 %collective-permute-done.43 = bf16[192,768]{1,0:T(8,128)(2,1)S(1)} collective-permute-done((bf16[192,768]{1,0:T(8,128)(2,1)S(1)}, bf16[192,768]{1,0:T(8,128)(2,1)S(1)}, u32[]{:S(2)}, u32[]{:S(2)}) %collective-permute-start.43) | collective-permute-done | bytes 294944 | tf_op jit(solution)/shard_map/ppermute | solution.py:623
  248.3 3.5 %collective-permute-start.47 = (bf16[128,768]{1,0:T(8,128)(2,1)S(1)}, bf16[128,768]{1,0:T(8,128)(2,1)S(1)}, u32[]{:S(2)}, u32[]{:S(2)}) collective-permute-start(bf16[128,768]{1,0:T(8,128)(2,1)S(1)} %convert_element_type.308.refs_0_), channel_id=1, source_target_pairs={{0,3},{1,0},{2,1},{3,2},{4,7},{5,4},{6,5},{7,6},{8,11},{9,8},{10,9... | collective-permute-start | bytes 589832 | tf_op jit(solution)/shard_map/ppermute | solution.py:620
  254.5 3.3 %collective-permute-start.48 = (f32[24,768]{1,0:T(8,128)S(1)}, f32[24,768]{1,0:T(8,128)S(1)}, u32[]{:S(2)}, u32[]{:S(2)}) collective-permute-start(f32[24,768]{1,0:T(8,128)S(1)} %copy-done.26), channel_id=1, source_target_pairs={{0,2},{1,3},{2,0},{3,1},{4,6},{5,7},{6,4},{7,5},{8,10},{9,11},{10,... | collective-permute-start | bytes 221192 | tf_op jit(solution)/shard_map/ppermute | solution.py:623
  260.4 5.6 %collective-permute-start.49 = (f32[24,768]{1,0:T(8,128)S(1)}, f32[24,768]{1,0:T(8,128)S(1)}, u32[]{:S(2)}, u32[]{:S(2)}) collective-permute-start(f32[24,768]{1,0:T(8,128)S(1)} %add.279), channel_id=1, source_target_pairs={{0,4},{4,0},{8,12},{12,8},{16,20},{20,16},{24,28},{28,24},{1,5},{5... | collective-permute-start | bytes 221192 | tf_op jit(solution)/shard_map/ppermute | solution.py:617
  276.9 4.5 %collective-permute-done.51 = bf16[192,768]{1,0:T(8,128)(2,1)S(1)} collective-permute-done((bf16[192,768]{1,0:T(8,128)(2,1)S(1)}, bf16[192,768]{1,0:T(8,128)(2,1)S(1)}, u32[]{:S(2)}, u32[]{:S(2)}) %collective-permute-start.51) | collective-permute-done | bytes 294944 | tf_op jit(solution)/shard_map/ppermute | solution.py:623
  290.6 7.8 %collective-permute-done.53 = bf16[192,768]{1,0:T(8,128)(2,1)S(1)} collective-permute-done((bf16[192,768]{1,0:T(8,128)(2,1)S(1)}, bf16[192,768]{1,0:T(8,128)(2,1)S(1)}, u32[]{:S(2)}, u32[]{:S(2)}) %collective-permute-start.53) | collective-permute-done | bytes 294944 | tf_op jit(solution)/shard_map/ppermute | solution.py:623
  298.4 3.2 collective-permute-start.62
  305.3 3.1 finish_ffn.1
  308.5 4.5 %collective-permute-done.63.refs_2_ = bf16[128,768]{1,0:T(8,128)(2,1)S(1)} collective-permute-done((bf16[128,768]{1,0:T(8,128)(2,1)S(1)}, bf16[128,768]{1,0:T(8,128)(2,1)S(1)}, u32[]{:S(2)}, u32[]{:S(2)}) %collective-permute-start.63) | collective-permute-done | bytes 196640 | tf_op jit(solution)/shard_map/ppermute | solution.py:620
  322.0 3.3 %finish_heads.1 = (f32[576,768]{1,0:T(8,128)}, f32[192,768]{1,0:T(8,128)}, f32[192,768]{1,0:T(8,128)}, f32[192,768]{1,0:T(8,128)}, f32[384,768]{1,0:T(8,128)}, /...) custom-call(s32[12]{0:T(128)S(1)} %copy-done.2, ...), custom_call_target="tpu_custom_call" | custom-call | bytes 294912 | tf_op jit(solution)/shard_map/finish_heads/pallas_call | solution.py:1082
  (248 shorter events, 114.3 us)
Async XLA Ops:
  4.6 22.3 %collective-permute-start.2 = (bf16[208,768]{1,0:T(8,128)(2,1)S(1)}, bf16[208,768]{1,0:T(8,128)(2,1)S(1)}, u32[]{:S(2)}, u32[]{:S(2)}) collective-permute-start(bf16[208,768]{1,0:T(8,128)(2,1)S(1)} %concatenate.25), channel_id=1, source_target_pairs={{0,3},{1,2},{2,1},{3,0},{4,7},{5,6},{6,5},{7,4},{8,11},{9,10},{10,... | collective-permute-start | bytes 958472 | tf_op jit(solution)/shard_map/ppermute | solution.py:623
  6.0 26.7 %collective-permute-start.1 = (bf16[208,768]{1,0:T(8,128)(2,1)S(1)}, bf16[208,768]{1,0:T(8,128)(2,1)S(1)}, u32[]{:S(2)}, u32[]{:S(2)}) collective-permute-start(bf16[208,768]{1,0:T(8,128)(2,1)S(1)} %concatenate.25), channel_id=1, source_target_pairs={{0,2},{1,3},{2,0},{3,1},{4,6},{5,7},{6,4},{7,5},{8,10},{9,11},{10,... | collective-permute-start | bytes 958472 | tf_op jit(solution)/shard_map/ppermute | solution.py:623
  7.0 25.6 %collective-permute-start = (bf16[208,768]{1,0:T(8,128)(2,1)S(1)}, bf16[208,768]{1,0:T(8,128)(2,1)S(1)}, u32[]{:S(2)}, u32[]{:S(2)}) collective-permute-start(bf16[208,768]{1,0:T(8,128)(2,1)S(1)} %concatenate.25), channel_id=1, source_target_pairs={{0,1},{1,0},{2,3},{3,2},{4,5},{5,4},{6,7},{7,6},{8,9},{9,8},{10,11... | collective-permute-start | bytes 958472 | tf_op jit(solution)/shard_map/ppermute | solution.py:623
  32.7 19.3 %collective-permute-start.7 = (bf16[192,768]{1,0:T(8,128)(2,1)}, bf16[192,768]{1,0:T(8,128)(2,1)}, u32[]{:S(2)}, u32[]{:S(2)}) collective-permute-start(bf16[192,768]{1,0:T(8,128)(2,1)} %pad_maximum_fusion.2), channel_id=1, source_target_pairs={{0,3},{1,2},{2,1},{3,0},{4,7},{5,6},{6,5},{7,4},{8,11},{9,10},{10,... | collective-permute-start | bytes 884744 | tf_op jit(solution)/shard_map/ppermute | solution.py:623
  33.1 24.4 %collective-permute-start.6 = (bf16[192,768]{1,0:T(8,128)(2,1)}, bf16[192,768]{1,0:T(8,128)(2,1)}, u32[]{:S(2)}, u32[]{:S(2)}) collective-permute-start(bf16[192,768]{1,0:T(8,128)(2,1)} %pad_maximum_fusion.2), channel_id=1, source_target_pairs={{0,2},{1,3},{2,0},{3,1},{4,6},{5,7},{6,4},{7,5},{8,10},{9,11},{10,... | collective-permute-start | bytes 884744 | tf_op jit(solution)/shard_map/ppermute | solution.py:623
  37.1 20.4 %collective-permute-start.5 = (bf16[192,768]{1,0:T(8,128)(2,1)}, bf16[192,768]{1,0:T(8,128)(2,1)}, u32[]{:S(2)}, u32[]{:S(2)}) collective-permute-start(bf16[192,768]{1,0:T(8,128)(2,1)} %pad_maximum_fusion.2), channel_id=1, source_target_pairs={{0,1},{1,0},{2,3},{3,2},{4,5},{5,4},{6,7},{7,6},{8,9},{9,8},{10,11... | collective-permute-start | bytes 884744 | tf_op jit(solution)/shard_map/ppermute | solution.py:623
  37.3 20.2 %collective-permute-start.4 = (bf16[3,192,768]{2,1,0:T(8,128)(2,1)S(1)}, bf16[3,192,768]{2,1,0:T(8,128)(2,1)S(1)}, u32[]{:S(2)}, u32[]{:S(2)}) collective-permute-start(bf16[3,192,768]{2,1,0:T(8,128)(2,1)S(1)} %pad_maximum_fusion.refs_6_.refs_10_.refs_7_.refs_17_), channel_id=1, source_target_pairs={{0,16},{4,20},{8,24},{12,28},{16,0},{20,4},{24,8},{28,12},{1,17},{... | collective-permute-start | bytes 2654216 | tf_op jit(solution)/shard_map/ppermute | solution.py:617
  38.6 18.9 %collective-permute-start.3 = (bf16[3,192,768]{2,1,0:T(8,128)(2,1)S(1)}, bf16[3,192,768]{2,1,0:T(8,128)(2,1)S(1)}, u32[]{:S(2)}, u32[]{:S(2)}) collective-permute-start(bf16[3,192,768]{2,1,0:T(8,128)(2,1)S(1)} %pad_maximum_fusion.refs_6_.refs_10_.refs_7_.refs_17_), channel_id=1, source_target_pairs={{0,8},{4,12},{8,0},{12,4},{16,24},{20,28},{24,16},{28,20},{1,9},{5... | collective-permute-start | bytes 2654216 | tf_op jit(solution)/shard_map/ppermute | solution.py:617
  78.2 21.4 %collective-permute-start.14 = (bf16[3,192,768]{2,1,0:T(8,128)(2,1)}, bf16[3,192,768]{2,1,0:T(8,128)(2,1)S(1)}, u32[]{:S(2)}, u32[]{:S(2)}) collective-permute-start(bf16[3,192,768]{2,1,0:T(8,128)(2,1)} %pad_maximum_fusion.1.refs_8_), channel_id=1, source_target_pairs={{0,16},{4,20},{8,24},{12,28},{16,0},{20,4},{24,8},{28,12},{1,17},{... | collective-permute-start | bytes 2654216 | tf_op jit(solution)/shard_map/ppermute | solution.py:617
  78.4 21.2 %collective-permute-start.13 = (bf16[3,192,768]{2,1,0:T(8,128)(2,1)}, bf16[3,192,768]{2,1,0:T(8,128)(2,1)}, u32[]{:S(2)}, u32[]{:S(2)}) collective-permute-start(bf16[3,192,768]{2,1,0:T(8,128)(2,1)} %pad_maximum_fusion.1.refs_8_), channel_id=1, source_target_pairs={{0,8},{4,12},{8,0},{12,4},{16,24},{20,28},{24,16},{28,20},{1,9},{5... | collective-permute-start | bytes 2654216 | tf_op jit(solution)/shard_map/ppermute | solution.py:617
  80.0 18.7 %collective-permute-start.15 = (bf16[192,1024]{1,0:T(8,128)(2,1)}, bf16[192,1024]{1,0:T(8,128)(2,1)S(1)}, u32[]{:S(2)}, u32[]{:S(2)}) collective-permute-start(bf16[192,1024]{1,0:T(8,128)(2,1)} %get-tuple-element.212), channel_id=1, source_target_pairs={{0,2},{1,3},{2,0},{3,1},{4,6},{5,7},{6,4},{7,5},{8,10},{9,11},{10,... | collective-permute-start | bytes 1179656 | tf_op jit(solution)/shard_map/ppermute | solution.py:620
  99.6 17.2 %collective-permute-start.21 = (bf16[3,192,768]{2,1,0:T(8,128)(2,1)}, bf16[3,192,768]{2,1,0:T(8,128)(2,1)S(1)}, u32[]{:S(2)}, u32[]{:S(2)}) collective-permute-start(bf16[3,192,768]{2,1,0:T(8,128)(2,1)} %pad_maximum_fusion.1.refs_8_), channel_id=1, source_target_pairs={{0,4},{4,0},{8,12},{12,8},{16,20},{20,16},{24,28},{28,24},{1,5},{5... | collective-permute-start | bytes 2654216 | tf_op jit(solution)/shard_map/ppermute | solution.py:617
  106.7 24.9 %collective-permute-start.24 = (bf16[3,192,768]{2,1,0:T(8,128)(2,1)S(1)}, bf16[3,192,768]{2,1,0:T(8,128)(2,1)S(1)}, u32[]{:S(2)}, u32[]{:S(2)}) collective-permute-start(bf16[3,192,768]{2,1,0:T(8,128)(2,1)S(1)} %collective-permute-done.14.refs_10_), channel_id=1, source_target_pairs={{0,4},{4,0},{8,12},{12,8},{16,20},{20,16},{24,28},{28,24},{1,5},{5... | collective-permute-start | bytes 2654216 | tf_op jit(solution)/shard_map/ppermute | solution.py:617
  112.9 18.7 %collective-permute-start.23 = (bf16[3,192,768]{2,1,0:T(8,128)(2,1)}, bf16[3,192,768]{2,1,0:T(8,128)(2,1)}, u32[]{:S(2)}, u32[]{:S(2)}) collective-permute-start(bf16[3,192,768]{2,1,0:T(8,128)(2,1)} %collective-permute-done.13.refs_9_), channel_id=1, source_target_pairs={{0,4},{4,0},{8,12},{12,8},{16,20},{20,16},{24,28},{28,24},{1,5},{5... | collective-permute-start | bytes 2654216 | tf_op jit(solution)/shard_map/ppermute | solution.py:617
  142.9 19.7 %collective-permute-start.30 = (bf16[5,128,1152]{2,1,0:T(8,128)(2,1)}, bf16[5,128,1152]{2,1,0:T(8,128)(2,1)S(1)}, u32[]{:S(2)}, u32[]{:S(2)}) collective-permute-start(bf16[5,128,1152]{2,1,0:T(8,128)(2,1)} %get-tuple-element.249.refs_1_), channel_id=1, source_target_pairs={{0,4},{4,0},{8,12},{12,8},{16,20},{20,16},{24,28},{28,24},{1,5},{5... | collective-permute-start | bytes 4423688 | tf_op jit(solution)/shard_map/ppermute | solution.py:617
  143.4 19.1 %collective-permute-start.29 = (bf16[128,768]{1,0:T(8,128)(2,1)}, bf16[128,768]{1,0:T(8,128)(2,1)S(1)}, u32[]{:S(2)}, u32[]{:S(2)}) collective-permute-start(bf16[128,768]{1,0:T(8,128)(2,1)} %get-tuple-element.305.refs_0_), channel_id=1, source_target_pairs={{0,3},{1,0},{2,1},{3,2},{4,7},{5,4},{6,5},{7,6},{8,11},{9,8},{10,9... | collective-permute-start | bytes 589832 | tf_op jit(solution)/shard_map/ppermute | solution.py:620
  144.2 18.3 %collective-permute-start.28 = (bf16[128,768]{1,0:T(8,128)(2,1)}, bf16[128,768]{1,0:T(8,128)(2,1)S(1)}, u32[]{:S(2)}, u32[]{:S(2)}) collective-permute-start(bf16[128,768]{1,0:T(8,128)(2,1)} %get-tuple-element.305.refs_0_), channel_id=1, source_target_pairs={{0,2},{1,3},{2,0},{3,1},{4,6},{5,7},{6,4},{7,5},{8,10},{9,11},{10,... | collective-permute-start | bytes 589832 | tf_op jit(solution)/shard_map/ppermute | solution.py:620
  144.2 18.3 %collective-permute-start.27 = (bf16[128,768]{1,0:T(8,128)(2,1)}, bf16[128,768]{1,0:T(8,128)(2,1)S(1)}, u32[]{:S(2)}, u32[]{:S(2)}) collective-permute-start(bf16[128,768]{1,0:T(8,128)(2,1)} %get-tuple-element.305.refs_0_), channel_id=1, source_target_pairs={{0,1},{1,2},{2,3},{3,0},{4,5},{5,6},{6,7},{7,4},{8,9},{9,10},{10,1... | collective-permute-start | bytes 589832 | tf_op jit(solution)/shard_map/ppermute | solution.py:620
  168.9 27.0 %collective-permute-start.32 = (bf16[2,2,192,768]{3,2,1,0:T(8,128)(2,1)}, bf16[2,2,192,768]{3,2,1,0:T(8,128)(2,1)}, u32[]{:S(2)}, u32[]{:S(2)}) collective-permute-start(bf16[2,2,192,768]{3,2,1,0:T(8,128)(2,1)} %get-tuple-element.265), channel_id=1, source_target_pairs={{0,16},{4,20},{8,24},{12,28},{16,0},{20,4},{24,8},{28,12},{1,17},{... | collective-permute-start | bytes 3538952 | tf_op jit(solution)/shard_map/ppermute | solution.py:617
  169.7 26.4 %collective-permute-start.31 = (bf16[2,2,192,768]{3,2,1,0:T(8,128)(2,1)}, bf16[2,2,192,768]{3,2,1,0:T(8,128)(2,1)}, u32[]{:S(2)}, u32[]{:S(2)}) collective-permute-start(bf16[2,2,192,768]{3,2,1,0:T(8,128)(2,1)} %get-tuple-element.264), channel_id=1, source_target_pairs={{0,8},{4,12},{8,0},{12,4},{16,24},{20,28},{24,16},{28,20},{1,9},{5... | collective-permute-start | bytes 3538952 | tf_op jit(solution)/shard_map/ppermute | solution.py:617
  170.9 23.2 %collective-permute-start.33 = (bf16[192,1024]{1,0:T(8,128)(2,1)}, bf16[192,1024]{1,0:T(8,128)(2,1)S(1)}, u32[]{:S(2)}, u32[]{:S(2)}) collective-permute-start(bf16[192,1024]{1,0:T(8,128)(2,1)} %get-tuple-element.267), channel_id=1, source_target_pairs={{0,1},{1,2},{2,3},{3,0},{4,5},{5,6},{6,7},{7,4},{8,9},{9,10},{10,1... | collective-permute-start | bytes 1179656 | tf_op jit(solution)/shard_map/ppermute | solution.py:620
  172.1 23.8 %collective-permute-start.34 = (bf16[192,1024]{1,0:T(8,128)(2,1)S(1)}, bf16[192,1024]{1,0:T(8,128)(2,1)S(1)}, u32[]{:S(2)}, u32[]{:S(2)}) collective-permute-start(bf16[192,1024]{1,0:T(8,128)(2,1)S(1)} %copy-done.28), channel_id=1, source_target_pairs={{0,2},{1,3},{2,0},{3,1},{4,6},{5,7},{6,4},{7,5},{8,10},{9,11},{10,... | collective-permute-start | bytes 1179656 | tf_op jit(solution)/shard_map/ppermute | solution.py:620
  201.0 17.2 %collective-permute-start.37 = (bf16[2,192,768]{2,1,0:T(8,128)(2,1)}, bf16[2,192,768]{2,1,0:T(8,128)(2,1)}, u32[]{:S(2)}, u32[]{:S(2)}) collective-permute-start(bf16[2,192,768]{2,1,0:T(8,128)(2,1)} %get-tuple-element.384), channel_id=1, source_target_pairs={{0,16},{4,20},{8,24},{12,28},{16,0},{20,4},{24,8},{28,12},{1,17},{... | collective-permute-start | bytes 1769480 | tf_op jit(solution)/shard_map/ppermute | solution.py:617
  218.2 27.4 %collective-permute-start.40 = (bf16[2,2,192,768]{3,2,1,0:T(8,128)(2,1)}, bf16[2,2,192,768]{3,2,1,0:T(8,128)(2,1)S(1)}, u32[]{:S(2)}, u32[]{:S(2)}) collective-permute-start(bf16[2,2,192,768]{3,2,1,0:T(8,128)(2,1)} %get-tuple-element.297), channel_id=1, source_target_pairs={{0,8},{4,12},{8,0},{12,4},{16,24},{20,28},{24,16},{28,20},{1,9},{5... | collective-permute-start | bytes 3538952 | tf_op jit(solution)/shard_map/ppermute | solution.py:617
  219.5 26.1 %collective-permute-start.41 = (bf16[2,2,192,768]{3,2,1,0:T(8,128)(2,1)}, bf16[2,2,192,768]{3,2,1,0:T(8,128)(2,1)S(1)}, u32[]{:S(2)}, u32[]{:S(2)}) collective-permute-start(bf16[2,2,192,768]{3,2,1,0:T(8,128)(2,1)} %get-tuple-element.298), channel_id=1, source_target_pairs={{0,16},{4,20},{8,24},{12,28},{16,0},{20,4},{24,8},{28,12},{1,17},{... | collective-permute-start | bytes 3538952 | tf_op jit(solution)/shard_map/ppermute | solution.py:617
  222.5 19.0 %collective-permute-start.44 = (bf16[192,768]{1,0:T(8,128)(2,1)S(1)}, bf16[192,768]{1,0:T(8,128)(2,1)S(1)}, u32[]{:S(2)}, u32[]{:S(2)}) collective-permute-start(bf16[192,768]{1,0:T(8,128)(2,1)S(1)} %get-tuple-element.381), channel_id=1, source_target_pairs={{0,3},{1,2},{2,1},{3,0},{4,7},{5,6},{6,5},{7,4},{8,11},{9,10},{10,... | collective-permute-start | bytes 884744 | tf_op jit(solution)/shard_map/ppermute | solution.py:623
  222.6 23.0 %collective-permute-start.43 = (bf16[192,768]{1,0:T(8,128)(2,1)S(1)}, bf16[192,768]{1,0:T(8,128)(2,1)S(1)}, u32[]{:S(2)}, u32[]{:S(2)}) collective-permute-start(bf16[192,768]{1,0:T(8,128)(2,1)S(1)} %get-tuple-element.382), channel_id=1, source_target_pairs={{0,2},{1,3},{2,0},{3,1},{4,6},{5,7},{6,4},{7,5},{8,10},{9,11},{10,... | collective-permute-start | bytes 884744 | tf_op jit(solution)/shard_map/ppermute | solution.py:623
  225.8 19.8 %collective-permute-start.42 = (bf16[192,768]{1,0:T(8,128)(2,1)S(1)}, bf16[192,768]{1,0:T(8,128)(2,1)S(1)}, u32[]{:S(2)}, u32[]{:S(2)}) collective-permute-start(bf16[192,768]{1,0:T(8,128)(2,1)S(1)} %get-tuple-element.383), channel_id=1, source_target_pairs={{0,1},{1,0},{2,3},{3,2},{4,5},{5,4},{6,7},{7,6},{8,9},{9,8},{10,11... | collective-permute-start | bytes 884744 | tf_op jit(solution)/shard_map/ppermute | solution.py:623
  247.3 20.0 %collective-permute-start.46 = (bf16[2,192,768]{2,1,0:T(8,128)(2,1)S(1)}, bf16[2,192,768]{2,1,0:T(8,128)(2,1)S(1)}, u32[]{:S(2)}, u32[]{:S(2)}) collective-permute-start(bf16[2,192,768]{2,1,0:T(8,128)(2,1)S(1)} %get-tuple-element.379), channel_id=1, source_target_pairs={{0,16},{4,20},{8,24},{12,28},{16,0},{20,4},{24,8},{28,12},{1,17},{... | collective-permute-start | bytes 1769480 | tf_op jit(solution)/shard_map/ppermute | solution.py:617
  248.0 19.4 %collective-permute-start.45 = (bf16[2,192,768]{2,1,0:T(8,128)(2,1)S(1)}, bf16[2,192,768]{2,1,0:T(8,128)(2,1)S(1)}, u32[]{:S(2)}, u32[]{:S(2)}) collective-permute-start(bf16[2,192,768]{2,1,0:T(8,128)(2,1)S(1)} %get-tuple-element.380), channel_id=1, source_target_pairs={{0,8},{4,12},{8,0},{12,4},{16,24},{20,28},{24,16},{28,20},{1,9},{5... | collective-permute-start | bytes 1769480 | tf_op jit(solution)/shard_map/ppermute | solution.py:617
  272.5 18.1 %collective-permute-start.52 = (bf16[192,768]{1,0:T(8,128)(2,1)S(1)}, bf16[192,768]{1,0:T(8,128)(2,1)S(1)}, u32[]{:S(2)}, u32[]{:S(2)}) collective-permute-start(bf16[192,768]{1,0:T(8,128)(2,1)S(1)} %get-tuple-element.324), channel_id=1, source_target_pairs={{0,2},{1,3},{2,0},{3,1},{4,6},{5,7},{6,4},{7,5},{8,10},{9,11},{10,... | collective-permute-start | bytes 884744 | tf_op jit(solution)/shard_map/ppermute | solution.py:623
  274.4 24.0 %collective-permute-start.53 = (bf16[192,768]{1,0:T(8,128)(2,1)S(1)}, bf16[192,768]{1,0:T(8,128)(2,1)S(1)}, u32[]{:S(2)}, u32[]{:S(2)}) collective-permute-start(bf16[192,768]{1,0:T(8,128)(2,1)S(1)} %get-tuple-element.325), channel_id=1, source_target_pairs={{0,3},{1,2},{2,1},{3,0},{4,7},{5,6},{6,5},{7,4},{8,11},{9,10},{10,... | collective-permute-start | bytes 884744 | tf_op jit(solution)/shard_map/ppermute | solution.py:623
  (70 other events, 651.9 us)
